TPU v7x, 32 devices: a whole 2x2x4 slice. The times are simulated.
32 devices in a mesh: dp: 8 (over z, y), seq: 4 (over x, core).
Axes of the slice: x: 2, y: 2, z: 4, core: 2. Of those that a mesh axis runs over, the one named last changes fastest.
Arguments:
- tokens: bfloat16 [2, 16, 1024, 1024], P(None, 'dp', 'seq'), may hold values from -6 to 6
- cotangent: bfloat16 [2, 16, 1024, 1024], P(None, 'dp', 'seq'), may hold values from -6 to 6
- lengths: int32 [2, 16], P(None, 'dp'), may hold values from 256 to 1024, as said below
- buckets: int32 [2047], replicated, may hold values from 0 to 31
- norm1_gain: float32 [1024], P(('dp', 'seq')), may hold values from 0.5 to 1.5
- w_query: float32 [1024, 1024], P(('dp', 'seq')), may hold values from -0.09375 to 0.09375
- w_key: float32 [1024, 1024], P(('dp', 'seq')), may hold values from -0.09375 to 0.09375
- w_value: float32 [1024, 1024], P(('dp', 'seq')), may hold values from -0.1875 to 0.1875
- w_out: float32 [1024, 1024], P(('dp', 'seq')), may hold values from -0.75 to 0.75
- rel_table: float32 [512], P(('dp', 'seq')), may hold values from -4 to 4
- norm2_gain: float32 [1024], P(('dp', 'seq')), may hold values from 0.5 to 1.5
- w_in: float32 [1024, 4096], P(('dp', 'seq')), may hold values from -0.1875 to 0.1875
- w_back: float32 [4096, 1024], P(('dp', 'seq')), may hold values from -0.125 to 0.125
Outputs:
- layer_out: bfloat16 [2, 16, 1024, 1024], P(None, 'dp', 'seq')
- input_grad: bfloat16 [2, 16, 1024, 1024], P(None, 'dp', 'seq')
- grad_norm1_gain: float32 [1024], P(('dp', 'seq'))
- grad_w_query: float32 [1024, 1024], P(('dp', 'seq'))
- grad_w_key: float32 [1024, 1024], P(('dp', 'seq'))
- grad_w_value: float32 [1024, 1024], P(('dp', 'seq'))
- grad_w_out: float32 [1024, 1024], P(('dp', 'seq'))
- grad_rel_table: float32 [512], P(('dp', 'seq'))
- grad_norm2_gain: float32 [1024], P(('dp', 'seq'))
- grad_w_in: float32 [1024, 4096], P(('dp', 'seq'))
- grad_w_back: float32 [4096, 1024], P(('dp', 'seq'))
Inputs may be any that keep to these rules, and one draw needn't show every extreme that they name: `lengths`: in each micro-batch one sequence has exactly 1024 used slots and another exactly 256; used slots come first in a sequence.
All inputs are finite; a program needn't handle non-finite values.
Results may differ from a plain program's by a relative error of at most 0.03.
Values may be sent and summed in bfloat16 or wider, within the bound.
No kernel may reach another device: no remote copies, remote signals or barrier semaphores. Data moves between devices by JAX's collectives and lax.ppermute only.
A program may use at most 384 MiB of HBM per device.

v0:
```python
import jax
import jax.numpy as jnp
from jax import lax
from jax.sharding import PartitionSpec as P

HEADS = 16
DH = 64
BUCKETS = 32


epsilon = 1e-06
floor_score = -1e30
highest = lax.Precision.HIGHEST
root_coef = 0.7978845608
cubic_coef = 0.044715


def gelu_tanh(values):
    return (
        0.5
        * values
        * (1.0 + jnp.tanh(root_coef * (values + cubic_coef * values * values * values)))
    )


def gelu_slope(values):
    inner = jnp.tanh(root_coef * (values + cubic_coef * values * values * values))
    return 0.5 * (1.0 + inner) + 0.5 * values * (1.0 - inner * inner) * root_coef * (
        1.0 + 3.0 * cubic_coef * values * values
    )


def project(acts, weight):
    return jnp.einsum("srd,de->sre", acts, weight, preferred_element_type=jnp.float32)


def project_back(grads_in, weight):
    return jnp.einsum("sre,de->srd", grads_in, weight, preferred_element_type=jnp.float32)


def contract(acts, grads_in):
    return jnp.einsum("srd,sre->de", acts, grads_in, preferred_element_type=jnp.float32)


def rms_forward(values, gain):
    inverse = lax.rsqrt(jnp.mean(values * values, axis=-1, keepdims=True) + epsilon)
    normed = values * inverse
    return (normed, inverse, (normed * gain.astype(jnp.float32)).astype(jnp.bfloat16))


def rms_backward(grad_hidden, normed, inverse, gain):
    scaled = grad_hidden * gain.astype(jnp.float32)
    grad_values = inverse * (scaled - normed * jnp.mean(scaled * normed, axis=-1, keepdims=True))
    return (grad_values, jnp.sum(grad_hidden * normed, axis=(0, 1)))


def score_block(per_head_queries, per_head_keys, rel_bias, key_valid):
    scores = (
        jnp.einsum(
            "ofck,owck->ocfw", per_head_queries, per_head_keys, preferred_element_type=jnp.float32
        )
        + rel_bias[None]
    )
    return jnp.where(key_valid, scores, floor_score)


def offset_sums(grid, first_row, seq_len):
    head_count, row_count, key_count = grid.shape
    flipped = grid[:, ::-1, :]
    padded = jnp.pad(flipped, ((0, 0), (0, 0), (0, row_count)))
    wide_len = key_count + row_count
    skewed = padded.reshape(head_count, row_count * wide_len)[:, : row_count * (wide_len - 1)]
    skewed = skewed.reshape(head_count, row_count, wide_len - 1)
    column_sums = jnp.sum(skewed, axis=1)
    placed = jnp.zeros((head_count, 2 * seq_len - 1), jnp.float32)
    begin = seq_len - row_count - first_row
    return lax.dynamic_update_slice(placed, column_sums, (jnp.int32(0), begin))


def run_micro(inputs, incoming, seq_lens, attn_set, mlp_set, context):
    onehot, offsets, row_pos, key_pos, first_row, seq_len = context
    gain_one, query_w, key_w, value_w, out_w, bias_table = attn_set
    gain_two, in_w, return_projection_weight = mlp_set
    seq_count, row_count, model_width = inputs.shape
    values = inputs.astype(jnp.float32)
    normed_one, inverse_one, hidden_one = rms_forward(values, gain_one)
    queries = project(hidden_one, query_w).astype(jnp.bfloat16)
    keys_own = project(hidden_one, key_w).astype(jnp.bfloat16)
    values_own = project(hidden_one, value_w).astype(jnp.bfloat16)
    keys_all, values_all = (
        lax.all_gather(keys_own, "seq", axis=1, tiled=True),
        lax.all_gather(values_own, "seq", axis=1, tiled=True),
    )
    per_offset = jnp.dot(
        onehot, bias_table.reshape(BUCKETS, HEADS), preferred_element_type=jnp.float32
    )
    rel_bias = jnp.transpose(per_offset[offsets], (2, 0, 1))
    key_valid = (key_pos[None, :] < seq_lens[:, None])[:, None, None, :]
    per_head_queries = queries.reshape(seq_count, row_count, HEADS, DH)
    per_head_keys = keys_all.reshape(seq_count, seq_len, HEADS, DH)
    per_head_values = values_all.reshape(seq_count, seq_len, HEADS, DH)
    scores = score_block(per_head_queries, per_head_keys, rel_bias, key_valid)
    row_max = jnp.max(scores, axis=-1, keepdims=True)
    exp_scores = jnp.exp(scores - row_max)
    row_total = jnp.sum(exp_scores, axis=-1, keepdims=True)
    attn_probs = exp_scores / row_total
    log_total = row_max + jnp.log(row_total)
    reduced_precision_probs = attn_probs.astype(jnp.bfloat16)
    attended = jnp.einsum(
        "jfpe,jefn->jpfn",
        reduced_precision_probs,
        per_head_values,
        preferred_element_type=jnp.float32,
    )
    attended = attended.reshape(seq_count, row_count, model_width).astype(jnp.bfloat16)
    residual_mid = values + project(attended, out_w)
    normed_two, inverse_two, hidden_two = rms_forward(residual_mid, gain_two)
    pre_act = project(hidden_two, in_w)
    active = gelu_tanh(pre_act).astype(jnp.bfloat16)
    result = (residual_mid + project(active, return_projection_weight)).astype(jnp.bfloat16)
    row_valid = (row_pos[None, :] < seq_lens[:, None]).astype(jnp.float32)[:, :, None]
    grad_out = incoming.astype(jnp.float32) * row_valid
    grad_low = grad_out.astype(jnp.bfloat16)
    grad_back = contract(active, grad_low)
    gradient_active_rows = project_back(grad_low, return_projection_weight)
    grad_pre = (gradient_active_rows * gelu_slope(pre_act)).astype(jnp.bfloat16)
    grad_in = contract(hidden_two, grad_pre)
    grad_hidden_two = project_back(grad_pre, in_w)
    grad_mixed, grad_gain_two = rms_backward(grad_hidden_two, normed_two, inverse_two, gain_two)
    grad_mixed = grad_mixed + grad_out
    grad_branch = grad_mixed.astype(jnp.bfloat16)
    grad_outw = contract(attended, grad_branch)
    gradient_attended_values = project_back(grad_branch, out_w).astype(jnp.bfloat16)
    gradient_attended_values = gradient_attended_values.reshape(seq_count, row_count, HEADS, DH)
    scores = score_block(per_head_queries, per_head_keys, rel_bias, key_valid)
    attn_probs = jnp.exp(scores - log_total)
    reduced_precision_probs = attn_probs.astype(jnp.bfloat16)
    grad_probs = jnp.einsum(
        "ofck,owck->ocfw",
        gradient_attended_values,
        per_head_values,
        preferred_element_type=jnp.float32,
    )
    inner_sum = jnp.sum(attn_probs * grad_probs, axis=-1, keepdims=True)
    gradient_score_matrix = (attn_probs * (grad_probs - inner_sum)).astype(jnp.bfloat16)
    grad_query = jnp.einsum(
        "jfpe,jefn->jpfn", gradient_score_matrix, per_head_keys, preferred_element_type=jnp.float32
    )
    grad_query = grad_query.astype(jnp.bfloat16).reshape(seq_count, row_count, model_width)
    key_part = jnp.einsum(
        "eciv,eicq->evcq",
        gradient_score_matrix,
        per_head_queries,
        preferred_element_type=jnp.float32,
    )
    value_part = jnp.einsum(
        "eciv,eicq->evcq",
        reduced_precision_probs,
        gradient_attended_values,
        preferred_element_type=jnp.float32,
    )
    key_part = key_part.reshape(seq_count, seq_len, model_width)
    value_part = value_part.reshape(seq_count, seq_len, model_width)
    grad_key, grad_value = (
        lax.psum_scatter(
            key_part.astype(jnp.bfloat16), "seq", scatter_dimension=1, tiled=True
        ).astype(jnp.float32),
        lax.psum_scatter(
            value_part.astype(jnp.bfloat16), "seq", scatter_dimension=1, tiled=True
        ).astype(jnp.float32),
    )
    grad_key = grad_key.astype(jnp.bfloat16)
    grad_value = grad_value.astype(jnp.bfloat16)
    offset_grad = offset_sums(
        jnp.sum(gradient_score_matrix.astype(jnp.float32), axis=0), first_row, seq_len
    )
    grad_table = jnp.dot(onehot.astype(jnp.float32).T, offset_grad.T, precision=highest).reshape(-1)
    grad_qw = contract(hidden_one, grad_query)
    grad_kw = contract(hidden_one, grad_key)
    grad_vw = contract(hidden_one, grad_value)
    grad_hidden_one = (
        project_back(grad_query, query_w)
        + project_back(grad_key, key_w)
        + project_back(grad_value, value_w)
    )
    grad_values, grad_gain_one = rms_backward(grad_hidden_one, normed_one, inverse_one, gain_one)
    grad_values = grad_values + grad_mixed
    gradients = (
        grad_gain_one,
        grad_qw,
        grad_kw,
        grad_vw,
        grad_outw,
        grad_table,
        grad_gain_two,
        grad_in,
        grad_back,
    )
    return (result, grad_values.astype(jnp.bfloat16), gradients)


def local(
    tokens,
    cotangent,
    lengths,
    buckets,
    norm1_gain,
    w_query,
    w_key,
    w_value,
    w_out,
    rel_table,
    norm2_gain,
    w_in,
    w_back,
):
    micro_count, seq_count, row_count, model_width = tokens.shape
    seq_parts = lax.axis_size("seq")
    seq_len = row_count * seq_parts
    first_row = lax.axis_index("seq") * row_count
    row_pos = first_row + jnp.arange(row_count, dtype=jnp.int32)
    key_pos = jnp.arange(seq_len, dtype=jnp.int32)
    onehot = (buckets[:, None] == jnp.arange(BUCKETS, dtype=jnp.int32)[None, :]).astype(
        jnp.bfloat16
    )
    offsets = key_pos[None, :] - row_pos[:, None] + (seq_len - 1)
    context = (onehot, offsets, row_pos, key_pos, first_row, seq_len)
    outputs = []
    input_grads = []
    pending = None
    shard_sums = None
    for micro_step in range(micro_count):
        attn_set = (
            lax.all_gather(norm1_gain.astype(jnp.bfloat16), ("dp", "seq"), axis=0, tiled=True),
            lax.all_gather(w_query.astype(jnp.bfloat16), ("dp", "seq"), axis=0, tiled=True),
            lax.all_gather(w_key.astype(jnp.bfloat16), ("dp", "seq"), axis=0, tiled=True),
            lax.all_gather(w_value.astype(jnp.bfloat16), ("dp", "seq"), axis=0, tiled=True),
            lax.all_gather(w_out.astype(jnp.bfloat16), ("dp", "seq"), axis=0, tiled=True),
            lax.all_gather(rel_table.astype(jnp.bfloat16), ("dp", "seq"), axis=0, tiled=True),
        )
        mlp_set = (
            lax.all_gather(norm2_gain.astype(jnp.bfloat16), ("dp", "seq"), axis=0, tiled=True),
            lax.all_gather(w_in.astype(jnp.bfloat16), ("dp", "seq"), axis=0, tiled=True),
            lax.all_gather(w_back.astype(jnp.bfloat16), ("dp", "seq"), axis=0, tiled=True),
        )
        layer_part, grad_part, gradients = run_micro(
            tokens[micro_step],
            cotangent[micro_step],
            lengths[micro_step],
            attn_set,
            mlp_set,
            context,
        )
        outputs.append(layer_part)
        input_grads.append(grad_part)
        pending = gradients if pending is None else jax.tree.map(jnp.add, pending, gradients)
    shard_sums = (
        lax.psum_scatter(pending[0], ("dp", "seq"), scatter_dimension=0, tiled=True),
        lax.psum_scatter(pending[1], ("dp", "seq"), scatter_dimension=0, tiled=True),
        lax.psum_scatter(pending[2], ("dp", "seq"), scatter_dimension=0, tiled=True),
        lax.psum_scatter(pending[3], ("dp", "seq"), scatter_dimension=0, tiled=True),
        lax.psum_scatter(pending[4], ("dp", "seq"), scatter_dimension=0, tiled=True),
        lax.psum_scatter(pending[5], ("dp", "seq"), scatter_dimension=0, tiled=True),
        lax.psum_scatter(pending[6], ("dp", "seq"), scatter_dimension=0, tiled=True),
        lax.psum_scatter(pending[7], ("dp", "seq"), scatter_dimension=0, tiled=True),
        lax.psum_scatter(pending[8], ("dp", "seq"), scatter_dimension=0, tiled=True),
    )
    return (
        jnp.stack(outputs),
        jnp.stack(input_grads),
        shard_sums[0],
        shard_sums[1],
        shard_sums[2],
        shard_sums[3],
        shard_sums[4],
        shard_sums[5],
        shard_sums[6],
        shard_sums[7],
        shard_sums[8],
    )


def solution(mesh):
    return jax.shard_map(
        local,
        mesh=mesh,
        in_specs=(
            P(None, "dp", "seq", None),
            P(None, "dp", "seq", None),
            P(None, "dp"),
            P(),
            P(("dp", "seq")),
            P(("dp", "seq"), None),
            P(("dp", "seq"), None),
            P(("dp", "seq"), None),
            P(("dp", "seq"), None),
            P(("dp", "seq")),
            P(("dp", "seq")),
            P(("dp", "seq"), None),
            P(("dp", "seq"), None),
        ),
        out_specs=(
            P(None, "dp", "seq", None),
            P(None, "dp", "seq", None),
            P(("dp", "seq")),
            P(("dp", "seq"), None),
            P(("dp", "seq"), None),
            P(("dp", "seq"), None),
            P(("dp", "seq"), None),
            P(("dp", "seq")),
            P(("dp", "seq")),
            P(("dp", "seq"), None),
            P(("dp", "seq"), None),
        ),
        check_vma=False,
    )
```

profile of v0, /device:TPU:0, one launch (start us, length us, event | category | flops | bytes accessed | tf_op | source)
XLA Modules:
  0.0 2480.4 jit_solution(6824424981639617012)
XLA Ops:
  14.7 42.1 %all-reduce.9 = (bf16[1024]{0:T(1024)(128)(2,1)S(1)}, bf16[512]{0:T(512)(128)(2,1)S(1)}, bf16[1024]{0:T(1024)(128)(2,1)}) all-reduce(bf16[1024]{0:T(1024)(128)(2,1)S(1)} %dynamic-update-slice, bf16[512]{0:T(512)(128)(2,1)S(1)} %dynamic-update-slice.1, bf16[1024]{0:T(1024)(128)(2,1)S(1)} %dynamic-update-slice.2), channel_id=1, replica_groups=mesh['dp'=8,'seq'=4] {'dp','seq'}, use_global_device_ids=true, to_apply=%add.2 | all-reduce | flops 2560 | bytes 10240
  74.8 54.4 %all-gather.11.cloned.1.call-done = bf16[1024,1024]{1,0:T(8,128)(2,1)} async-done(((bf16[32,1024]{1,0:T(8,128)(2,1)}), bf16[1024,1024]{1,0:T(8,128)(2,1)}) %all-gather.11.cloned.1.call-update) | async-done | bytes 2097168 | tf_op jit(solution)/shard_map/all_gather | solution.py:237
  147.3 860.0 %gather_fusion = f32[262144,16]{1,0:T(8,128)} fusion(f32[2047,16]{1,0:T(8,128)S(1)} %fusion.160, s32[262144]{0:T(1024)S(1)} %broadcast_clamp_fusion), kind=kCustom, calls=%fused_computation | custom fusion | bytes 34603008 | tf_op jit(solution)/shard_map/gather | solution.py:97
  1007.3 75.5 %copy.97 = f32[256,1024,16]{1,0,2:T(8,128)} copy(f32[256,1024,16]{2,1,0:T(8,128)} %bitcast.9) | data formatting | bytes 33554432 | tf_op jit(solution)/shard_map/gather | solution.py:97
  1099.6 18.5 fusion.191
  1136.8 14.3 fusion
  1151.1 16.0 fusion.149
  1171.6 19.6 fusion.190
  1191.3 14.3 fusion.1
  1205.6 15.0 fusion.148
  1261.2 13.7 fusion.20
  1291.0 15.4 fusion.54
  1318.5 17.3 fusion.57
  1342.1 25.0 %multiply_reduce_fusion.1 = (f32[2,16,256]{2,1,0:T(8,128)S(1)}, f32[2,16,256,1024]{3,2,1,0:T(8,128)}) fusion(f32[2,16,256,1024]{3,2,1,0:T(8,128)} %get-tuple-element.48, f32[2,16,256]{2,1,0:T(8,128)S(1)} %log_add_fusion.1, bf16[2,256,16,64]{1,3,2,0:T(8,128)(2,1)S(1)} %bitcast.280, bf16[2,1024,16,64]{1,3,2,0:T(8,128)(2,1)} %bitcast.272), kind=kOutput, calls=%fused_computation.7 | convolution fusion | flops 1098899456 | bytes 72417280 | tf_op jit(solution)/shard_map/ofck,owck->ocfw/dot_general | solution.py:138
  1367.1 35.5 %convert_reduce_fusion.1 = (f32[16,256,1024]{2,1,0:T(8,128)}, bf16[2,16,256,1024]{3,2,1,0:T(8,128)(2,1)}) fusion(f32[2,16,256,1024]{3,2,1,0:T(8,128)} %get-tuple-element.53, f32[2,16,256]{2,1,0:T(8,128)S(1)} %get-tuple-element.52, f32[2,16,256,1024]{3,2,1,0:T(8,128)} %get-tuple-element.48, f32[2,16,256]{2,1,0:T(8,128)S(1)} %log_add_fusion.1), kind=kLoop, calls=%fused_computation.2 | loop fusion | flops 46137344 | bytes 100728832 | tf_op jit(solution)/shard_map/reduce_sum | solution.py:175
  1420.0 25.0 %multiply_reduce_fusion = (f32[2,16,256]{2,1,0:T(8,128)S(1)}, f32[2,16,256,1024]{3,2,1,0:T(8,128)}) fusion(f32[2,16,256,1024]{3,2,1,0:T(8,128)} %get-tuple-element.44, f32[2,16,256]{2,1,0:T(8,128)S(1)} %log_add_fusion, bf16[2,256,16,64]{1,3,2,0:T(8,128)(2,1)S(1)} %bitcast.278, bf16[2,1024,16,64]{1,3,2,0:T(8,128)(2,1)} %bitcast.270), kind=kOutput, calls=%fused_computation.4 | convolution fusion | flops 1098899456 | bytes 72417280 | tf_op jit(solution)/shard_map/ofck,owck->ocfw/dot_general | solution.py:138
  1445.1 35.1 %convert_reduce_fusion = (f32[16,256,1024]{2,1,0:T(8,128)}, bf16[2,16,256,1024]{3,2,1,0:T(8,128)(2,1)}) fusion(f32[2,16,256,1024]{3,2,1,0:T(8,128)} %get-tuple-element.55, f32[2,16,256]{2,1,0:T(8,128)S(1)} %get-tuple-element.54, f32[2,16,256,1024]{3,2,1,0:T(8,128)} %get-tuple-element.44, f32[2,16,256]{2,1,0:T(8,128)S(1)} %log_add_fusion), kind=kLoop, calls=%fused_computation.1 | loop fusion | flops 46137344 | bytes 100728832 | tf_op jit(solution)/shard_map/reduce_sum | solution.py:175
  1504.5 13.2 convolution_convert_fusion.3
  1562.9 13.5 fusion.174
  1589.6 15.2 fusion.161
  1604.8 14.8 bitcast_add_fusion
  1619.6 127.8 %rev.6 = f32[16,256,1024]{2,1,0:T(8,128)} reverse(f32[16,256,1024]{2,1,0:T(8,128)} %get-tuple-element.31), dimensions={1} | reverse | bytes 33554432 | tf_op jit(solution)/shard_map/rev | solution.py:69
  1754.4 14.5 copy.142
  1768.9 15.6 slice.34
  1784.5 38.0 %reshape.329 = f32[16,256,1279]{2,1,0:T(8,128)} reshape(f32[16,327424]{1,0:T(8,128)} %slice.34) | data formatting | bytes 41910272 | tf_op jit(solution)/shard_map/reshape | solution.py:73
  1822.5 127.7 %rev.7 = f32[16,256,1024]{2,1,0:T(8,128)} reverse(f32[16,256,1024]{2,1,0:T(8,128)} %get-tuple-element.29), dimensions={1} | reverse | bytes 33554432 | tf_op jit(solution)/shard_map/rev | solution.py:69
  1957.1 14.4 copy.143
  1971.4 15.7 slice.35
  1987.1 38.2 %reshape.331 = f32[16,256,1279]{2,1,0:T(8,128)} reshape(f32[16,327424]{1,0:T(8,128)} %slice.35) | data formatting | bytes 41910272 | tf_op jit(solution)/shard_map/reshape | solution.py:73
  2079.9 43.5 %all-reduce.8 = (f32[1024]{0:T(1024)S(1)}, f32[512]{0:T(512)S(1)}, f32[1024]{0:T(1024)S(1)}) all-reduce(f32[1024]{0:T(1024)S(1)} %add.276, f32[512]{0:T(512)S(1)} %add.283, f32[1024]{0:T(1024)S(1)} %add.284), channel_id=6, replica_groups=mesh['dp'=8,'seq'=4] {'dp','seq'}, use_global_device_ids=true, to_apply=%region_20.21.clone | all-reduce | flops 2560 | bytes 20480
  2130.9 154.5 %reduce-scatter.27.cloned.1.call-done = f32[32,4096]{1,0:T(8,128)} async-done(((f32[1024,4096]{1,0:T(8,128)}), f32[32,4096]{1,0:T(8,128)}) %reduce-scatter.27.cloned.1.call-update) | async-done | bytes 524304 | tf_op jit(solution)/shard_map/reduce_scatter | solution.py:265
  2285.4 187.9 %reduce-scatter.29.cloned.1.call-done = f32[128,1024]{1,0:T(8,128)} async-done(((f32[4096,1024]{1,0:T(8,128)}), f32[128,1024]{1,0:T(8,128)}) %reduce-scatter.29.cloned.1.call-update) | async-done | bytes 524304 | tf_op jit(solution)/shard_map/reduce_scatter | solution.py:266
  (304 shorter events, 333.7 us)
Async XLA Ops:
  7.2 63.4 %all-gather.17.cloned.1.call-start = ((), (), s32[]{:S(2)}) async-start(), calls=%async_computation.13 | async-start | bytes 2162688 | tf_op jit(solution)/shard_map/all_gather | solution.py:236
  8.8 120.5 %all-gather.11.cloned.1.call-start = ((), (), s32[]{:S(2)}) async-start(), calls=%async_computation.10 | async-start | bytes 2162688 | tf_op jit(solution)/shard_map/all_gather | solution.py:237
  10.4 1073.0 %all-gather.15.cloned.1.call-start = ((), (), s32[]{:S(2)}) async-start(), calls=%async_computation.12 | async-start | bytes 2162688 | tf_op jit(solution)/shard_map/all_gather | solution.py:235
  12.0 1081.0 %all-gather.19.cloned.1.call-start = ((), (), s32[]{:S(2)}) async-start(), calls=%async_computation.14 | async-start | bytes 5242880 | tf_op jit(solution)/shard_map/all_gather | solution.py:91
  56.8 80.4 %copy-start.38 = (f32[1024]{0:T(1024)}, f32[1024]{0:T(1024)S(1)}, u32[]{:S(2)}) copy-start(f32[1024]{0:T(1024)S(1)} %convert_element_type.265) | copy-start | bytes 12292
  58.8 70.4 %copy-start = (bf16[2,2,256,1024]{3,2,1,0:T(8,128)(2,1)S(1)}, bf16[2,2,256,1024]{3,2,1,0:T(8,128)(2,1)}, u32[]{:S(2)}) copy-start(bf16[2,2,256,1024]{3,2,1,0:T(8,128)(2,1)} %param.13) | copy-start | bytes 6291460
  58.9 74.3 %copy-start.56 = (f32[2,256]{1,0:T(2,128)}, f32[2,256]{1,0:T(2,128)S(1)}, u32[]{:S(2)}) copy-start(f32[2,256]{1,0:T(2,128)S(1)} %add_rsqrt_fusion.3) | copy-start | bytes 6148
  74.8 1043.3 %all-gather.13.cloned.1.call-start = ((), (), s32[]{:S(2)}) async-start(), calls=%async_computation.11 | async-start | bytes 5242880 | tf_op jit(solution)/shard_map/all_gather | solution.py:92
  133.2 991.2 %all-gather.29.cloned.1.call-start = ((), (), s32[]{:S(2)}) async-start(), calls=%async_computation.19 | async-start | bytes 5242880 | tf_op jit(solution)/shard_map/all_gather | solution.py:91
  137.2 993.4 %all-gather.27.cloned.1.call-start = ((), (), s32[]{:S(2)}) async-start(), calls=%async_computation.18 | async-start | bytes 5242880 | tf_op jit(solution)/shard_map/all_gather | solution.py:92
  141.2 1025.9 %all-gather.21.cloned.1.call-start = ((), (), s32[]{:S(2)}) async-start(), calls=%async_computation.15 | async-start | bytes 2162688 | tf_op jit(solution)/shard_map/all_gather | solution.py:238
  142.0 1083.3 %all-gather.23.cloned.1.call-start = ((), (), s32[]{:S(2)}) async-start(), calls=%async_computation.16 | async-start | bytes 8650752 | tf_op jit(solution)/shard_map/all_gather | solution.py:243
  142.8 1094.5 %all-gather.25.cloned.1.call-start = ((), (), s32[]{:S(2)}) async-start(), calls=%async_computation.17 | async-start | bytes 8650752 | tf_op jit(solution)/shard_map/all_gather | solution.py:244
  143.6 1397.4 %reduce-scatter.13.cloned.1.call-start = ((), (), s32[]{:S(2)}) async-start(), calls=%async_computation.21 | async-start | bytes 5242880 | tf_op jit(solution)/shard_map/reduce_scatter | solution.py:168
  1007.3 75.5 %copy-start.64 = (bf16[1024]{0:T(1024)(128)(2,1)S(1)}, bf16[1024]{0:T(1024)(128)(2,1)}, u32[]{:S(2)}) copy-start(bf16[1024]{0:T(1024)(128)(2,1)} %get-tuple-element.28) | copy-start | bytes 6148
  1007.3 76.1 %copy-start.1 = (bf16[2,2,256,1024]{3,2,1,0:T(8,128)(2,1)S(1)}, bf16[2,2,256,1024]{3,2,1,0:T(8,128)(2,1)}, u32[]{:S(2)}) copy-start(bf16[2,2,256,1024]{3,2,1,0:T(8,128)(2,1)} %param.13) | copy-start | bytes 6291460
  1007.3 76.1 %copy-start.39 = (f32[1024]{0:T(1024)S(1)}, f32[1024]{0:T(1024)}, u32[]{:S(2)}) copy-start(f32[1024]{0:T(1024)} %copy-done.38) | copy-start | bytes 12292
  1007.3 76.1 %copy-start.57 = (f32[2,256]{1,0:T(2,128)S(1)}, f32[2,256]{1,0:T(2,128)}, u32[]{:S(2)}) copy-start(f32[2,256]{1,0:T(2,128)} %copy-done.56) | copy-start | bytes 6148
  1093.0 78.6 %copy-start.11 = (bf16[2,256,1024]{1,2,0:T(8,128)(2,1)}, bf16[2,256,1024]{1,2,0:T(8,128)(2,1)S(1)}, u32[]{:S(2)}) copy-start(bf16[2,256,1024]{1,2,0:T(8,128)(2,1)S(1)} %copy.100) | copy-start | bytes 3145732
  1171.6 112.9 %copy-start.60 = (f32[2,256]{1,0:T(2,128)}, f32[2,256]{1,0:T(2,128)S(1)}, u32[]{:S(2)}) copy-start(f32[2,256]{1,0:T(2,128)S(1)} %add_rsqrt_fusion.2) | copy-start | bytes 6148
  1225.2 59.3 %copy-start.48 = (f32[2,256]{1,0:T(2,128)}, f32[2,256]{1,0:T(2,128)S(1)}, u32[]{:S(2)}) copy-start(f32[2,256]{1,0:T(2,128)S(1)} %add_rsqrt_fusion) | copy-start | bytes 6148
  1312.6 233.0 %reduce-scatter.17.cloned.1.call-start = ((), (), s32[]{:S(2)}) async-start(), calls=%async_computation.23 | async-start | bytes 5242880 | tf_op jit(solution)/shard_map/reduce_scatter | solution.py:168
  1342.1 209.6 %reduce-scatter.11.cloned.1.call-start = ((), (), s32[]{:S(2)}) async-start(), calls=%async_computation.20 | async-start | bytes 5242880 | tf_op jit(solution)/shard_map/reduce_scatter | solution.py:165
  1367.1 35.5 %copy-start.13 = (bf16[2,256,1024]{1,2,0:T(8,128)(2,1)S(1)}, bf16[2,256,1024]{1,2,0:T(8,128)(2,1)}, u32[]{:S(2)}) copy-start(bf16[2,256,1024]{1,2,0:T(8,128)(2,1)} %copy.94) | copy-start | bytes 3145732
  1419.8 136.5 %reduce-scatter.15.cloned.1.call-start = ((), (), s32[]{:S(2)}) async-start(), calls=%async_computation.22 | async-start | bytes 5242880 | tf_op jit(solution)/shard_map/reduce_scatter | solution.py:165
  1445.1 35.1 %copy-start.12 = (bf16[2,256,1024]{1,2,0:T(8,128)(2,1)S(1)}, bf16[2,256,1024]{1,2,0:T(8,128)(2,1)}, u32[]{:S(2)}) copy-start(bf16[2,256,1024]{1,2,0:T(8,128)(2,1)} %copy-done.11) | copy-start | bytes 3145732
  1497.2 633.7 %reduce-scatter.25.cloned.1.call-start = ((), (), s32[]{:S(2)}) async-start(), calls=%async_computation.27 | async-start | bytes 4325376 | tf_op jit(solution)/shard_map/reduce_scatter | solution.py:262
  1504.2 626.7 %reduce-scatter.19.cloned.1.call-start = ((), (), s32[]{:S(2)}) async-start(), calls=%async_computation.24 | async-start | bytes 4325376 | tf_op jit(solution)/shard_map/reduce_scatter | solution.py:259
  1540.5 590.4 %reduce-scatter.23.cloned.1.call-start = ((), (), s32[]{:S(2)}) async-start(), calls=%async_computation.26 | async-start | bytes 4325376 | tf_op jit(solution)/shard_map/reduce_scatter | solution.py:261
  1551.6 579.3 %reduce-scatter.21.cloned.1.call-start = ((), (), s32[]{:S(2)}) async-start(), calls=%async_computation.25 | async-start | bytes 4325376 | tf_op jit(solution)/shard_map/reduce_scatter | solution.py:260
  1562.3 723.1 %reduce-scatter.27.cloned.1.call-start = ((), (), s32[]{:S(2)}) async-start(), calls=%async_computation.28 | async-start | bytes 17301504 | tf_op jit(solution)/shard_map/reduce_scatter | solution.py:265
  1588.0 885.2 %reduce-scatter.29.cloned.1.call-start = ((), (), s32[]{:S(2)}) async-start(), calls=%async_computation.29 | async-start | bytes 17301504 | tf_op jit(solution)/shard_map/reduce_scatter | solution.py:266
  (59 other events, 410.8 us)
Sparse Core Ops, SparseCore 0:
  11.4 59.0 all-gather.16
  74.0 55.2 all-gather.10
  132.7 55.2 all-gather.14
  189.4 33.3 all-gather.18
  224.2 34.4 all-gather.12
  260.1 34.4 all-gather.28
  296.8 34.4 all-gather.26
  334.7 56.3 all-gather.20
  394.6 76.2 all-gather.22
  474.2 76.0 all-gather.24
  1312.8 43.3 reduce-scatter.12
  1358.7 44.5 reduce-scatter.16
  1419.9 43.7 reduce-scatter.10
  1497.4 43.1 reduce-scatter.14
  1543.3 140.9 reduce-scatter.24
  1686.9 136.7 reduce-scatter.18
  1826.5 136.7 reduce-scatter.22
  1966.0 137.1 reduce-scatter.20
  2106.1 179.2 reduce-scatter.26
  2288.1 185.1 reduce-scatter.28
where the time goes:
time: 2510 us; the launch traced here: 2480 us
  local copies, waits for them, and re-layouts  1410 us (56%)
  matrix products  421 us (17%)
  waiting for transfers between devices  409 us (16%)
  other arithmetic  138 us (5%)
  blocking collectives  85.7 us (3%)
    gather x2, local copies, waits for them, and re-layouts, run_micro(): rel_bias = jnp.transpose(per_offset[offsets], (2, 0, 1))  935 us
    rev x2, local copies, waits for them, and re-layouts, offset_sums(): flipped = grid[:, ::-1, :]  256 us
    reduce_scatter x1, waiting for transfers between devices, local(): lax.psum_scatter(pending[8], ('dp', 'seq'), scatter_dimension=0, tiled=True)  188 us
    reduce_scatter x1, waiting for transfers between devices, local(): lax.psum_scatter(pending[7], ('dp', 'seq'), scatter_dimension=0, tiled=True)  154 us
    dot_general x12, matrix products, contract(): jnp.einsum('srd,sre->de', acts, grads_in, preferred_element_type=jnp.floa...  90.2 us
    unnamed x2, blocking collectives  85.7 us
    reshape x2, local copies, waits for them, and re-layouts, offset_sums(): skewed = skewed.reshape(head_count, row_count, wide_len - 1)  76.2 us
    dot_general x12, matrix products, project(): jnp.einsum('srd,de->sre', acts, weight, preferred_element_type=jnp.float32)  72.7 us
  transfers between devices with their start and end apart: 20, of which 4 were waited for; matrix products, arithmetic and copies ran while one was open for 76% of the time, Pallas kernels for 0%

commit v1 on v0

--- a/solution.py
+++ b/solution.py
@@ -1,6 +1,10 @@
+import functools
+
 import jax
 import jax.numpy as jnp
 from jax import lax
+from jax.experimental import pallas as pl
+from jax.experimental.pallas import tpu as pltpu
 from jax.sharding import PartitionSpec as P
 
 HEADS = 16
@@ -280,9 +284,368 @@
     )
 
 
+NT = (((1,), (1,)), ((), ()))
+TN = (((0,), (0,)), ((), ()))
+STRIP = 128
+
+def _dot(a, b, dims=(((1,), (0,)), ((), ()))):
+    return lax.dot_general(a, b, dims, preferred_element_type=jnp.float32)
+
+def head_lanes(x, which, width=64):
+    lane = lax.broadcasted_iota(jnp.int32, (1, x.shape[1]), 1)
+    keep = (lane < width) if which == 0 else (lane >= width)
+    return jnp.where(keep, x, jnp.zeros_like(x))
+
+def skew(row, wide):
+    rows = jnp.broadcast_to(row, (STRIP, wide))
+    return pltpu.roll(rows, wide - (STRIP - 1), 1, stride=1, stride_axis=0)
+
+def fwd_kernel(len_ref, q_ref, k_ref, v_ref, t_ref, o_ref, lse_ref, strip, *, rows, seq_len):
+    wide = t_ref.shape[-1]
+    length = len_ref[0]
+    blocks = seq_len // rows
+    per = rows // STRIP
+    col_ok = lax.broadcasted_iota(jnp.int32, (1, seq_len), 1) < length
+    lane = lax.broadcasted_iota(jnp.int32, (1, 128), 1)
+    k2 = k_ref[...]
+    v2 = v_ref[...]
+    for a in range(2):
+        strip[a] = skew(t_ref[0, a:a + 1, :], wide)
+
+    def step(b, carry):
+        base = pl.multiple_of(b * rows, rows)
+        q2 = q_ref[pl.ds(base, rows), :]
+        outs, stats = [], []
+        for a in range(2):
+            scores = _dot(head_lanes(q2, a), k2, NT)
+            parts = []
+            for i in range(per):
+                off = pl.multiple_of((seq_len - STRIP) - (b * per + i) * STRIP, STRIP)
+                parts.append(strip[a, :, pl.ds(off, seq_len)])
+            bias = jnp.concatenate(parts, 0) if per > 1 else parts[0]
+            scores = jnp.where(col_ok, scores + bias, floor_score)
+            top = jnp.max(scores, axis=1, keepdims=True)
+            probs = jnp.exp(scores - top)
+            total = jnp.sum(probs, axis=1, keepdims=True)
+            out = _dot(probs.astype(jnp.bfloat16), v2)
+            outs.append(out * (1.0 / total))
+            stats.append(top + jnp.log(total))
+        o_ref[pl.ds(base, rows), :] = jnp.where(lane < 64, outs[0], outs[1]).astype(jnp.bfloat16)
+        lse_ref[0, pl.ds(base, rows), :] = jnp.where(lane < 64, stats[0], stats[1])
+        return carry
+
+    lax.fori_loop(0, blocks, step, 0, unroll=2)
+
+def attn_fwd(length, q, k, v, t, rows=256):
+    seq_len, width = q.shape
+    pairs = width // 128
+    wide = t.shape[-1]
+    blk = pl.BlockSpec((seq_len, 128), lambda p, n: (0, p))
+    return pl.pallas_call(
+        functools.partial(fwd_kernel, rows=rows, seq_len=seq_len),
+        out_shape=(jax.ShapeDtypeStruct((seq_len, width), jnp.bfloat16),
+                   jax.ShapeDtypeStruct((pairs, seq_len, 128), jnp.float32)),
+        grid_spec=pltpu.PrefetchScalarGridSpec(
+            num_scalar_prefetch=1, grid=(pairs,),
+            in_specs=[blk, blk, blk, pl.BlockSpec((1, 2, wide), lambda p, n: (p, 0, 0))],
+            out_specs=[blk, pl.BlockSpec((1, seq_len, 128), lambda p, n: (p, 0, 0))],
+            scratch_shapes=[pltpu.VMEM((2, STRIP, wide), jnp.float32)]),
+        compiler_params=pltpu.CompilerParams(vmem_limit_bytes=56 << 20),
+        cost_estimate=pl.CostEstimate(flops=4 * seq_len * seq_len * width * 4, bytes_accessed=seq_len * width * 12, transcendentals=seq_len * seq_len * 16),
+        name="attn_fwd",
+    )(length, q, k, v, t)
+
+def bwd_kernel(len_ref, q_ref, k_ref, v_ref, do_ref, o_ref, lse_ref, t_ref,
+               dq_ref, dk_ref, dv_ref, g_ref, strip, acc, dq_acc, *, rows, seq_len):
+    wide = t_ref.shape[-1]
+    length = len_ref[0]
+    blocks = seq_len // rows
+    per = rows // STRIP
+    lane = lax.broadcasted_iota(jnp.int32, (1, 128), 1)
+    q2 = q_ref[...]
+    do2 = do_ref[...]
+    prod = (do2.astype(jnp.float32) * o_ref[...].astype(jnp.float32)).T
+    stat = lse_ref[0].T
+    lse_rows = [stat[0:1, :], stat[64:65, :]]
+    delta_rows = [jnp.sum(prod[0:64], axis=0, keepdims=True), jnp.sum(prod[64:128], axis=0, keepdims=True)]
+    for a in range(2):
+        strip[a] = skew(t_ref[0, a:a + 1, :], wide)
+    acc[...] = jnp.zeros_like(acc)
+    dq_acc[...] = jnp.zeros_like(dq_acc)
+
+    def step(b, carry):
+        base = pl.multiple_of(b * rows, rows)
+        k2 = k_ref[pl.ds(base, rows), :]
+        v2 = v_ref[pl.ds(base, rows), :]
+        row_ok = (base + lax.broadcasted_iota(jnp.int32, (rows, 1), 0)) < length
+        dks, dvs = [], []
+        for a in range(2):
+            scores = _dot(head_lanes(k2, a), q2, NT)
+            offs = [pl.multiple_of((seq_len - STRIP) - (b * per + i) * STRIP, STRIP) for i in range(per)]
+            bias = [strip[a, :, pl.ds(off, seq_len)] for off in offs]
+            bias = jnp.concatenate(bias, 0) if per > 1 else bias[0]
+            probs = jnp.where(row_ok, jnp.exp(scores + bias - lse_rows[a]), 0.0)
+            grad_probs = _dot(head_lanes(v2, a), do2, NT)
+            grad_scores = probs * (grad_probs - delta_rows[a])
+            for i, off in enumerate(offs):
+                acc[a, :, pl.ds(off, seq_len)] += grad_scores[i * STRIP:(i + 1) * STRIP]
+            probs_b = probs.astype(jnp.bfloat16)
+            gs_b = grad_scores.astype(jnp.bfloat16)
+            dvs.append(_dot(probs_b, do2))
+            dks.append(_dot(gs_b, q2))
+            dq_acc[a] += _dot(gs_b, k2, TN)
+        dk_ref[pl.ds(base, rows), :] = jnp.where(lane < 64, dks[0], dks[1]).astype(jnp.bfloat16)
+        dv_ref[pl.ds(base, rows), :] = jnp.where(lane < 64, dvs[0], dvs[1]).astype(jnp.bfloat16)
+        return carry
+
+    lax.fori_loop(0, blocks, step, 0)
+    dq_ref[...] = jnp.where(lane < 64, dq_acc[0], dq_acc[1]).astype(jnp.bfloat16)
+    for a in range(2):
+        sums = acc[a]
+        half = STRIP
+        while half > 8:
+            half //= 2
+            sums = sums[:half] + pltpu.roll(sums[half:], wide - half, 1)
+        while half > 1:
+            half //= 2
+            sums = sums + pltpu.roll(pltpu.roll(sums, 8 - half, 0), wide - half, 1)
+        g_ref[0, a:a + 1, :] = pltpu.roll(sums, STRIP - 1, 1)[0:1]
+
+def attn_bwd(length, q, k, v, do, o, lse, trev, rows=256):
+    seq_len, width = q.shape
+    pairs = width // 128
+    wide = trev.shape[-1]
+    blk = pl.BlockSpec((seq_len, 128), lambda p, n: (0, p))
+    tb = pl.BlockSpec((1, 2, wide), lambda p, n: (p, 0, 0))
+    mat = jax.ShapeDtypeStruct((seq_len, width), jnp.bfloat16)
+    return pl.pallas_call(
+        functools.partial(bwd_kernel, rows=rows, seq_len=seq_len),
+        out_shape=(mat, mat, mat, jax.ShapeDtypeStruct((pairs, 2, wide), jnp.float32)),
+        grid_spec=pltpu.PrefetchScalarGridSpec(
+            num_scalar_prefetch=1, grid=(pairs,),
+            in_specs=[blk, blk, blk, blk, blk, pl.BlockSpec((1, seq_len, 128), lambda p, n: (p, 0, 0)), tb],
+            out_specs=[blk, blk, blk, tb],
+            scratch_shapes=[pltpu.VMEM((2, STRIP, wide), jnp.float32), pltpu.VMEM((2, STRIP, wide), jnp.float32),
+                            pltpu.VMEM((2, seq_len, 128), jnp.float32)]),
+        compiler_params=pltpu.CompilerParams(vmem_limit_bytes=56 << 20),
+        cost_estimate=pl.CostEstimate(flops=10 * seq_len * seq_len * width * 4, bytes_accessed=seq_len * width * 20, transcendentals=seq_len * seq_len * 16),
+        name="attn_bwd",
+    )(length, q, k, v, do, o, lse, trev)
+
+LIMIT = 58 << 20
+
+def qkv_kernel(x_ref, gain_ref, w_ref, h_ref, q_ref, k_ref, v_ref):
+    x = x_ref[...].astype(jnp.float32)
+    inverse = lax.rsqrt(jnp.mean(x * x, axis=1, keepdims=True) + epsilon)
+    hidden = (x * inverse * gain_ref[...]).astype(jnp.bfloat16)
+    h_ref[...] = hidden
+    width = x.shape[1]
+    for i, ref in enumerate((q_ref, k_ref, v_ref)):
+        ref[...] = _dot(hidden, w_ref[:, i * width:(i + 1) * width]).astype(jnp.bfloat16)
+
+def qkv_fwd(x, gain, w, rows=512):
+    total, width = x.shape
+    blk = pl.BlockSpec((rows, width), lambda i: (i, 0))
+    mat = jax.ShapeDtypeStruct((total, width), jnp.bfloat16)
+    return pl.pallas_call(
+        qkv_kernel, out_shape=(mat,) * 4, grid=(total // rows,),
+        in_specs=[blk, pl.BlockSpec((1, width), lambda i: (0, 0)),
+                  pl.BlockSpec((width, 3 * width), lambda i: (0, 0), pipeline_mode=pl.Buffered(1))],
+        out_specs=[blk] * 4,
+        compiler_params=pltpu.CompilerParams(vmem_limit_bytes=LIMIT),
+        cost_estimate=pl.CostEstimate(flops=6 * total * width * width, bytes_accessed=total * width * 10 + width * width * 6, transcendentals=0),
+        name="qkv_fwd",
+    )(x, gain, w)
+
+def gelu_both(v):
+    t = jnp.tanh(root_coef * (v + cubic_coef * v * v * v))
+    half = 0.5 * (1.0 + t)
+    slope = half + 0.5 * v * (1.0 - t * t) * (root_coef * (1.0 + 3.0 * cubic_coef * v * v))
+    return v * half, slope
+
+def mid_kernel(len_ref, x_ref, o_ref, g_ref, gain_ref, wo_ref, win_ref, wback_ref,
+               out_ref, gb_ref, do_ref, gwo_ref, gwin_ref, gwback_ref,
+               mixed, h2, h2t, acc, gh2, gm):
+    step = pl.program_id(0)
+    rows = x_ref.shape[0]
+
+    part = 256
+
+    @pl.when(step == 0)
+    def _():
+        def load(i, carry):
+            at = pl.ds(pl.multiple_of(i * part, part), part)
+            row_ok = i * part + lax.broadcasted_iota(jnp.int32, (part, 1), 0) < len_ref[0]
+            gm[at, :] = jnp.where(row_ok, g_ref[at, :], jnp.zeros((part, g_ref.shape[1]), jnp.bfloat16))
+            value = x_ref[at, :].astype(jnp.float32) + _dot(o_ref[at, :], wo_ref[...])
+            mixed[at, :] = value
+            acc[at, :] = value
+            inverse = lax.rsqrt(jnp.mean(value * value, axis=1, keepdims=True) + epsilon)
+            hidden = (value * inverse * gain_ref[...]).astype(jnp.bfloat16)
+            h2[at, :] = hidden
+            h2t[:, at] = hidden.T
+            gh2[at, :] = jnp.zeros_like(value)
+            return carry
+        lax.fori_loop(0, rows // part, load, 0)
+
+    pre = _dot(h2[...], win_ref[...])
+    grad_active = _dot(gm[...], wback_ref[...], NT)
+    act, slope = gelu_both(pre)
+    active = act.astype(jnp.bfloat16)
+    gpre = (grad_active * slope).astype(jnp.bfloat16)
+    acc[...] += _dot(active, wback_ref[...])
+    gwback_ref[...] = _dot(active, gm[...], TN).astype(jnp.bfloat16)
+    gwin_ref[...] = _dot(h2t[...], gpre).astype(jnp.bfloat16)
+    gh2[...] += _dot(gpre, win_ref[...], NT)
+
+    @pl.when(step == pl.num_programs(0) - 1)
+    def _():
+        def finish(i, carry):
+            at = pl.ds(pl.multiple_of(i * part, part), part)
+            out_ref[at, :] = acc[at, :].astype(jnp.bfloat16)
+            value = mixed[at, :]
+            inverse = lax.rsqrt(jnp.mean(value * value, axis=1, keepdims=True) + epsilon)
+            normed = value * inverse
+            scaled = gh2[at, :] * gain_ref[...]
+            grad = inverse * (scaled - normed * jnp.mean(scaled * normed, axis=1, keepdims=True)) + gm[at, :].astype(jnp.float32)
+            gb = grad.astype(jnp.bfloat16)
+            gb_ref[at, :] = gb
+            do_ref[at, :] = _dot(gb, wo_ref[...], NT).astype(jnp.bfloat16)
+            return carry
+        lax.fori_loop(0, rows // part, finish, 0)
+        gwo_ref[...] = _dot(o_ref[...], gb_ref[...], TN).astype(jnp.bfloat16)
+
+def mid(length, x, o, g, gain, wo, win, wback, cols=512):
+    rows, width = x.shape
+    ff = win.shape[1]
+    one = lambda shape: pl.BlockSpec(shape, lambda i, n: (0, 0), pipeline_mode=pl.Buffered(1))
+    res = one
+    mat = jax.ShapeDtypeStruct((rows, width), jnp.bfloat16)
+    return pl.pallas_call(
+        mid_kernel,
+        out_shape=(mat, mat, mat, jax.ShapeDtypeStruct((width, width), jnp.bfloat16),
+                   jax.ShapeDtypeStruct((width, ff), jnp.bfloat16), jax.ShapeDtypeStruct((ff, width), jnp.bfloat16)),
+        grid_spec=pltpu.PrefetchScalarGridSpec(
+            num_scalar_prefetch=1, grid=(ff // cols,),
+            in_specs=[one((rows, width)), one((rows, width)), one((rows, width)), one((1, width)), one((width, width)),
+                      pl.BlockSpec((width, cols), lambda i, n: (0, i)), pl.BlockSpec((cols, width), lambda i, n: (i, 0))],
+            out_specs=[res((rows, width)), res((rows, width)), res((rows, width)), res((width, width)),
+                       pl.BlockSpec((width, cols), lambda i, n: (0, i)), pl.BlockSpec((cols, width), lambda i, n: (i, 0))],
+            scratch_shapes=[pltpu.VMEM((rows, width), jnp.float32), pltpu.VMEM((rows, width), jnp.bfloat16),
+                            pltpu.VMEM((width, rows), jnp.bfloat16), pltpu.VMEM((rows, width), jnp.float32),
+                            pltpu.VMEM((rows, width), jnp.float32), pltpu.VMEM((rows, width), jnp.bfloat16)]),
+        compiler_params=pltpu.CompilerParams(vmem_limit_bytes=LIMIT),
+        cost_estimate=pl.CostEstimate(flops=12 * rows * width * ff + 6 * rows * width * width, bytes_accessed=rows * width * 12 + width * width * 4 + width * ff * 8, transcendentals=rows * ff),
+        name="mid",
+    )(length, x, o, g, gain, wo, win, wback)
+
+def gw_kernel(h_ref, dq_ref, dk_ref, dv_ref, out_ref):
+    for i, ref in enumerate((dq_ref, dk_ref, dv_ref)):
+        w = ref.shape[1]
+        out_ref[:, i * w:(i + 1) * w] = _dot(h_ref[...], ref[...], TN).astype(jnp.bfloat16)
+
+def qkv_gw(h, dq, dk, dv):
+    rows, width = h.shape
+    return pl.pallas_call(
+        gw_kernel, out_shape=jax.ShapeDtypeStruct((width, 3 * width), jnp.bfloat16),
+        compiler_params=pltpu.CompilerParams(vmem_limit_bytes=LIMIT),
+        cost_estimate=pl.CostEstimate(flops=6 * rows * width * width, bytes_accessed=rows * width * 8 + width * width * 6, transcendentals=0),
+        name="qkv_gw",
+    )(h, dq, dk, dv)
+
+def gx_kernel(x_ref, gb_ref, dq_ref, dk_ref, dv_ref, gain_ref, w_ref, out_ref):
+    width = x_ref.shape[1]
+    grad = _dot(dq_ref[...], w_ref[:, :width], NT)
+    grad += _dot(dk_ref[...], w_ref[:, width:2 * width], NT)
+    grad += _dot(dv_ref[...], w_ref[:, 2 * width:3 * width], NT)
+    x = x_ref[...].astype(jnp.float32)
+    inverse = lax.rsqrt(jnp.mean(x * x, axis=1, keepdims=True) + epsilon)
+    normed = x * inverse
+    scaled = grad * gain_ref[...]
+    out = inverse * (scaled - normed * jnp.mean(scaled * normed, axis=1, keepdims=True)) + gb_ref[...].astype(jnp.float32)
+    out_ref[...] = out.astype(jnp.bfloat16)
+
+def qkv_gx(x, gb, dq, dk, dv, gain, w, rows=512):
+    total, width = x.shape
+    blk = pl.BlockSpec((rows, width), lambda i: (i, 0))
+    return pl.pallas_call(
+        gx_kernel, out_shape=jax.ShapeDtypeStruct((total, width), jnp.bfloat16), grid=(total // rows,),
+        in_specs=[blk] * 5 + [pl.BlockSpec((1, width), lambda i: (0, 0)),
+                              pl.BlockSpec((width, 3 * width), lambda i: (0, 0), pipeline_mode=pl.Buffered(1))],
+        out_specs=blk,
+        compiler_params=pltpu.CompilerParams(vmem_limit_bytes=LIMIT),
+        cost_estimate=pl.CostEstimate(flops=6 * total * width * width, bytes_accessed=total * width * 12 + width * width * 6, transcendentals=0),
+        name="qkv_gx",
+    )(x, gb, dq, dk, dv, gain, w)
+def exchange(blocks):
+    parts = blocks.shape[0]
+    me = lax.axis_index("seq")
+    pick = lambda at: lax.dynamic_index_in_dim(blocks, at, 0, keepdims=True)
+    out = lax.dynamic_update_slice_in_dim(jnp.zeros_like(blocks), pick(me), me, 0)
+    for mask in range(1, parts):
+        came = lax.ppermute(pick(me ^ mask), "seq", [(i, i ^ mask) for i in range(parts)])
+        out = lax.dynamic_update_slice_in_dim(out, came, me ^ mask, 0)
+    return out
+
+
+def local_whole(tokens, cotangent, lengths, buckets, norm1_gain, w_query, w_key, w_value, w_out, rel_table, norm2_gain, w_in, w_back):
+    micro_count, seq_count, row_count, width = tokens.shape
+    parts = micro_count * seq_count
+    seq_len = parts * row_count
+    both = ("dp", "seq")
+    me = lax.axis_index("seq")
+    low = lambda v: v.astype(jnp.bfloat16)
+    own = norm1_gain.shape[0]
+    few = rel_table.shape[0]
+    small = jnp.stack([norm1_gain, norm2_gain, jnp.pad(rel_table, (0, own - few))], 1)
+    small = jnp.pad(low(small), ((0, 0), (0, 125)))
+    shard1 = jnp.concatenate([low(w_query), low(w_key), low(w_value), small], 1)
+    shard2 = jnp.concatenate([low(w_out), low(w_in)], 1)
+    full1 = lax.all_gather(shard1, both, axis=0, tiled=True)
+    x = exchange(tokens.reshape(parts, row_count, width)).reshape(seq_len, width)
+    full2 = lax.all_gather(shard2, both, axis=0, tiled=True)
+    full3 = lax.all_gather(low(w_back), both, axis=0, tiled=True)
+    g = exchange(cotangent.reshape(parts, row_count, width)).reshape(seq_len, width)
+    length = lax.dynamic_index_in_dim(lengths.reshape(parts), me, 0)
+
+    extra = full1[:, 3 * width:]
+    gain1 = extra[:, 0].astype(jnp.float32).reshape(1, width)
+    gain2 = extra[:, 1].astype(jnp.float32).reshape(1, width)
+    table = extra[:, 2].reshape(-1, own)[:, :few].reshape(BUCKETS, HEADS)
+    ids = jnp.arange(BUCKETS, dtype=jnp.int32)[:, None]
+    hot = low(jnp.pad(buckets, (0, 1), constant_values=-1)[None, :] == ids)
+    hot_back = low(jnp.pad(buckets[::-1], (0, 1), constant_values=-1)[None, :] == ids)
+    spread = lambda h: jnp.einsum("bh,bo->ho", table, h, preferred_element_type=jnp.float32).reshape(HEADS // 2, 2, -1)
+
+    hidden, q, k, v = qkv_fwd(x, gain1, full1)
+    attended, lse = attn_fwd(length, q, k, v, spread(hot))
+    out, gb, grad_attended, gwo, gwin, gwback = mid(length, x, attended, g, gain2, full2[:, :width], full2[:, width:], full3)
+    dq, dk, dv, g_off = attn_bwd(length, q, k, v, grad_attended, attended, lse, spread(hot_back))
+    g_table = jnp.dot(hot_back.astype(jnp.float32), g_off.reshape(HEADS, -1).T, precision=highest)
+    gw = qkv_gw(hidden, dq, dk, dv)
+    gx = qkv_gx(x, gb, dq, dk, dv, gain1, full1)
+    scatter = lambda v: lax.psum_scatter(v, both, scatter_dimension=0, tiled=True)
+    column = jnp.pad(g_table.reshape(-1, few), ((0, 0), (0, own - few))).reshape(-1, 1)
+    r2 = scatter(jnp.concatenate([gwo, gwin], 1)).astype(jnp.float32)
+    r3 = scatter(gwback).astype(jnp.float32)
+    r1 = scatter(jnp.concatenate([gw, jnp.pad(low(column), ((0, 0), (0, 127)))], 1)).astype(jnp.float32)
+    layer_out = exchange(out.reshape(parts, row_count, width)).reshape(tokens.shape)
+    input_grad = exchange(gx.reshape(parts, row_count, width)).reshape(tokens.shape)
+    up = lambda v: v.astype(jnp.float32)
+    g_gain1 = jnp.sum(up(shard1[:, :3 * width]) * r1[:, :3 * width], axis=1) / up(low(norm1_gain))
+    g_gain2 = jnp.sum(up(shard2[:, width:]) * r2[:, width:], axis=1) / up(low(norm2_gain))
+    return (layer_out, input_grad, g_gain1, r1[:, :width], r1[:, width:2 * width], r1[:, 2 * width:3 * width],
+            r2[:, :width], r1[:few, 3 * width], g_gain2, r2[:, width:], r3)
+
+
+def local_any(shape, tokens, *rest):
+    whole = tokens.shape[0] * tokens.shape[1] == shape[1] and tokens.shape[3] % 128 == 0
+    return (local_whole if whole else local)(tokens, *rest)
+
+
 def solution(mesh):
     return jax.shard_map(
-        local,
+        functools.partial(local_any, mesh.devices.shape),
         mesh=mesh,
         in_specs=(
             P(None, "dp", "seq", None),

time: 2510 us -> 900 us (0.36); the launches traced: 2480 us -> 899 us
  local copies, waits for them, and re-layouts: 1410 us -> 36.4 us
  matrix products: 421 us -> 0.56 us
  Pallas kernels: 0 us -> 239 us
  waiting for transfers between devices: 409 us -> 568 us
  other arithmetic: 138 us -> 31 us
  blocking collectives: 85.7 us -> 0 us
    gather x2 -> x0, local copies, waits for them, and re-layouts: 935 us -> none  [run_micro(): rel_bias = jnp.transpose(per_offset[offsets], (2, 0, 1))]
    dot_general x51 -> x3, matrix products: 421 us -> 0.56 us  [the longest x2 0.36 us: local_whole(): jnp.einsum('bh,bo->ho', table, h, preferred_element_type=jnp.float32)]
    rev x2 -> x0, local copies, waits for them, and re-layouts: 256 us -> none  [offset_sums(): flipped = grid[:, ::-1, :]]
    pallas_call x0 -> x6, Pallas kernels: none -> 239 us  [the longest x1 81.1 us: attn_bwd(): pl.pallas_call(functools.partial(bwd_kernel, rows=rows, seq_len=seq_len),...]
    ppermute x0 -> x12, waiting for transfers between devices: none -> 138 us  [exchange(): lax.ppermute(pick(me ^ mask), 'seq', [(i, i ^ mask) for i in range(parts)])]
    reduce_sum x7 -> x2, other arithmetic: 118 us -> 2.07 us  [the longest x1 1.9 us: local_whole(): jnp.sum(up(shard2[:, width:]) * r2[:, width:], axis=1) / up(low(norm2_gain))]
    unnamed x2 -> x0, blocking collectives: 85.7 us -> none
    reshape x3 -> x4, local copies, waits for them, and re-layouts: 76.2 us -> 2.56 us  [the longest x2 1.49 us: local_whole(): jnp.einsum('bh,bo->ho', table, h, preferred_element_type=jnp.float32)]
  transfers between devices with their start and end apart: 20 -> 18, of which waited for: 4 -> 14; matrix products, arithmetic and copies ran while one was open for 76% -> 5% of each run, Pallas kernels for 0% -> 8%
where the time goes in v1:
time: 900 us; the launch traced here: 899 us
  waiting for transfers between devices  568 us (63%)
  Pallas kernels  239 us (27%)
  local copies, waits for them, and re-layouts  36.4 us (4%)
  other arithmetic  31 us (3%)
  between operations  14.5 us (2%)
  starting transfers between devices  9.42 us (1%)
    reduce_scatter x3, waiting for transfers between devices, local_whole(): lax.psum_scatter(v, both, scatter_dimension=0, tiled=True)  317 us
    ppermute x12, waiting for transfers between devices, exchange(): lax.ppermute(pick(me ^ mask), 'seq', [(i, i ^ mask) for i in range(parts)])  138 us
    pallas_call x1, Pallas kernels, attn_bwd(): pl.pallas_call(functools.partial(bwd_kernel, rows=rows, seq_len=seq_len),...  81.1 us
    pallas_call x1, Pallas kernels, mid(): pl.pallas_call(mid_kernel, out_shape=(mat, mat, mat, jax.ShapeDtypeStruct...  76.4 us
    all_gather x1, waiting for transfers between devices, local_whole(): full3 = lax.all_gather(low(w_back), both, axis=0, tiled=True)  68 us
    pallas_call x1, Pallas kernels, attn_fwd(): pl.pallas_call(functools.partial(fwd_kernel, rows=rows, seq_len=seq_len),...  43.5 us
    all_gather x1, waiting for transfers between devices, local_whole(): full2 = lax.all_gather(shard2, both, axis=0, tiled=True)  29.2 us
  transfers between devices with their start and end apart: 18, of which 14 were waited for; matrix products, arithmetic and copies ran while one was open for 5% of the time, Pallas kernels for 8%

profile of v1, /device:TPU:0, one launch (start us, length us, event | category | flops | bytes accessed | tf_op | source)
XLA Modules:
  0.0 898.9 jit_solution(14977457723471980463)
XLA Ops:
  16.0 2.8 constant_dynamic-slice_fusion.5
  19.2 2.5 collective-permute-start.4
  24.9 1.9 collective-permute-start.1
  28.8 7.5 collective-permute-done.4
  37.4 13.6 %collective-permute-done.5 = bf16[1,256,1024]{2,1,0:T(8,128)(2,1)S(1)} collective-permute-done((bf16[1,256,1024]{2,1,0:T(8,128)(2,1)}, bf16[1,256,1024]{2,1,0:T(8,128)(2,1)S(1)}, u32[]{:S(2)}, u32[]{:S(2)}) %collective-permute-start.5) | collective-permute-done | bytes 524320 | tf_op jit(solution)/shard_map/ppermute | solution.py:586
  51.0 2.3 constant_dynamic-update-slice_fusion.11
  53.3 11.2 %collective-permute-done.1 = bf16[1,256,1024]{2,1,0:T(8,128)(2,1)S(1)} collective-permute-done((bf16[1,256,1024]{2,1,0:T(8,128)(2,1)}, bf16[1,256,1024]{2,1,0:T(8,128)(2,1)S(1)}, u32[]{:S(2)}, u32[]{:S(2)}) %collective-permute-start.1) | collective-permute-done | bytes 524320 | tf_op jit(solution)/shard_map/ppermute | solution.py:586
  65.3 17.2 %collective-permute-done.2 = bf16[1,256,1024]{2,1,0:T(8,128)(2,1)S(1)} collective-permute-done((bf16[1,256,1024]{2,1,0:T(8,128)(2,1)}, bf16[1,256,1024]{2,1,0:T(8,128)(2,1)S(1)}, u32[]{:S(2)}, u32[]{:S(2)}) %collective-permute-start.2) | collective-permute-done | bytes 524320 | tf_op jit(solution)/shard_map/ppermute | solution.py:586
  83.3 15.5 %all-gather.4.cloned.1.call-done.w_ref = bf16[1024,3200]{1,0:T(8,128)(2,1)} async-done(((bf16[32,3200]{1,0:T(8,128)(2,1)}), bf16[1024,3200]{1,0:T(8,128)(2,1)}) %all-gather.4.cloned.1.call-update) | async-done | bytes 6553616 | tf_op jit(solution)/shard_map/all_gather | solution.py:604
  102.0 1.9 convert_reduce_fusion
  103.9 11.4 %qkv_fwd.1 = (bf16[1024,1024]{1,0:T(8,128)(2,1)}, bf16[1024,1024]{1,0:T(8,128)(2,1)}, bf16[1024,1024]{1,0:T(8,128)(2,1)}, bf16[1024,1024]{1,0:T(8,128)(2,1)}) custom-call(bf16[1024,1024]{1,0:T(8,128)(2,1)} %bitcast.1.x_ref, f32[1,1024]{1,0:T(1,128)} %bitcast.26, bf16[1024,3200]{1,0:T(8,128)(2,1)} %all-gather.4.cloned.1.call-done.w_ref), custom_call_target="tpu_custom_call" | custom-call | flops 6442450944 | bytes 16777216 | tf_op jit(solution)/shard_map/qkv_fwd/pallas_call | solution.py:450
  115.4 43.5 %attn_fwd.1 = (bf16[1024,1024]{1,0:T(8,128)(2,1)}, f32[8,1024,128]{2,1,0:T(8,128)}) custom-call(s32[1]{0:T(128)} %dynamic_slice.53.len_ref, bf16[1024,1024]{1,0:T(8,128)(2,1)} %get-tuple-element.27.q_ref, bf16[1024,1024]{1,0:T(8,128)(2,1)} %get-tuple-element.28.k_ref, bf16[1024,1024]{1,0:T(8,128)(2,1)} %get-tuple-element.29.v_ref, f32[8,2,2048]{2,1,0:T(2,128)} %reshape.103.t_ref), custom_call_target="tpu_custom_call" | custom-call | flops 17179869184 | bytes 12582912 | tf_op jit(solution)/shard_map/attn_fwd/pallas_call | solution.py:344
  158.8 29.2 %all-gather.6.cloned.1.call-done = bf16[1024,5120]{1,0:T(8,128)(2,1)} async-done(((bf16[32,5120]{1,0:T(8,128)(2,1)}), bf16[1024,5120]{1,0:T(8,128)(2,1)}) %all-gather.6.cloned.1.call-update) | async-done | bytes 10485776 | tf_op jit(solution)/shard_map/all_gather | solution.py:606
  188.1 7.8 slice.64.win_ref
  195.8 3.1 slice.63.wo_ref
  198.9 68.0 %all-gather.8.cloned.1.call-done.wback_ref = bf16[4096,1024]{1,0:T(8,128)(2,1)} async-done(((bf16[128,1024]{1,0:T(8,128)(2,1)}), bf16[4096,1024]{1,0:T(8,128)(2,1)}) %all-gather.8.cloned.1.call-update) | async-done | bytes 8388624 | tf_op jit(solution)/shard_map/all_gather | solution.py:607
  266.9 76.4 %mid.1 = (bf16[1024,1024]{1,0:T(8,128)(2,1)}, bf16[1024,1024]{1,0:T(8,128)(2,1)}, bf16[1024,1024]{1,0:T(8,128)(2,1)}, bf16[1024,1024]{1,0:T(8,128)(2,1)}, bf16[1...) custom-call(s32[1]{0:T(128)} %dynamic_slice.53.len_ref, bf16[1024,1024]{1,0:T(8,128)(2,1)} %bitcast.1.x_ref, ...), custom_call_target="tpu_custom_call" | custom-call | flops 57982058496 | bytes 50331648 | tf_op jit(solution)/shard_map/mid/pallas_call | solution.py:524
  343.3 81.1 %attn_bwd.1 = (bf16[1024,1024]{1,0:T(8,128)(2,1)}, bf16[1024,1024]{1,0:T(8,128)(2,1)}, bf16[1024,1024]{1,0:T(8,128)(2,1)}, f32[8,2,2048]{2,1,0:T(2,128)}) custom-call(s32[1]{0:T(128)} %dynamic_slice.53.len_ref, bf16[1024,1024]{1,0:T(8,128)(2,1)} %get-tuple-element.27.q_ref, bf16[1024,1024]{1,0:T(8,128)(2,1)} %get-tuple-element.28.k_ref, ...), custom_call_target="tpu_custom_call" | custom-call | flops 42949672960 | bytes 20971520 | tf_op jit(solution)/shard_map/attn_bwd/pallas_call | solution.py:421
  426.3 12.8 %qkv_gw.1 = bf16[1024,3072]{1,0:T(8,128)(2,1)} custom-call(bf16[1024,1024]{1,0:T(8,128)(2,1)} %get-tuple-element.38.h_ref, bf16[1024,1024]{1,0:T(8,128)(2,1)} %get-tuple-element.35.dq_ref, bf16[1024,1024]{1,0:T(8,128)(2,1)} %get-tuple-element.36.dk_ref, bf16[1024,1024]{1,0:T(8,128)(2,1)} %get-tuple-element.37.dv_ref), custom_call_target="tpu_custom_call" | custom-call | flops 6442450944 | bytes 14680064 | tf_op jit(solution)/shard_map/qkv_gw/pallas_call | solution.py:549
  439.1 6.0 fusion.1
  446.8 9.8 %pad_maximum_fusion = bf16[1024,5120]{1,0:T(8,128)(2,1)} fusion(bf16[1024,4096]{1,0:T(8,128)(2,1)} %get-tuple-element.41, bf16[1024,1024]{1,0:T(8,128)(2,1)S(1)} %copy-done), kind=kLoop, calls=%fused_computation.2 | loop fusion | flops 20971520 | bytes 20971520 | tf_op jit(solution)/shard_map/concatenate | solution.py:629
  456.6 14.0 %qkv_gx.1 = bf16[1024,1024]{1,0:T(8,128)(2,1)} custom-call(bf16[1024,1024]{1,0:T(8,128)(2,1)} %bitcast.1.x_ref, bf16[1024,1024]{1,0:T(8,128)(2,1)} %get-tuple-element.32.gb_ref, bf16[1024,1024]{1,0:T(8,128)(2,1)} %get-tuple-element.35.dq_ref, bf16[1024,1024]{1,0:T(8,128)(2,1)} %get-tuple-element.36.dk_ref, bf16[1024,1024]{1,0:T(8,128)(2,1)} %get-tuple-element.37.dv_ref, ...), custom_call_target="tpu_custom_call" | custom-call | flops 6442450944 | bytes 18874368 | tf_op jit(solution)/shard_map/qkv_gx/pallas_call | solution.py:571
  477.0 22.1 %collective-permute-done.10 = bf16[1,256,1024]{2,1,0:T(8,128)(2,1)S(1)} collective-permute-done((bf16[1,256,1024]{2,1,0:T(8,128)(2,1)S(1)}, bf16[1,256,1024]{2,1,0:T(8,128)(2,1)S(1)}, u32[]{:S(2)}, u32[]{:S(2)}) %collective-permute-start.10) | collective-permute-done | bytes 524320 | tf_op jit(solution)/shard_map/ppermute | solution.py:586
  499.2 22.5 %collective-permute-done.11 = bf16[1,256,1024]{2,1,0:T(8,128)(2,1)S(1)} collective-permute-done((bf16[1,256,1024]{2,1,0:T(8,128)(2,1)S(1)}, bf16[1,256,1024]{2,1,0:T(8,128)(2,1)S(1)}, u32[]{:S(2)}, u32[]{:S(2)}) %collective-permute-start.11) | collective-permute-done | bytes 524320 | tf_op jit(solution)/shard_map/ppermute | solution.py:586
  521.9 22.2 %collective-permute-done.7 = bf16[1,256,1024]{2,1,0:T(8,128)(2,1)S(1)} collective-permute-done((bf16[1,256,1024]{2,1,0:T(8,128)(2,1)S(1)}, bf16[1,256,1024]{2,1,0:T(8,128)(2,1)S(1)}, u32[]{:S(2)}, u32[]{:S(2)}) %collective-permute-start.7) | collective-permute-done | bytes 524320 | tf_op jit(solution)/shard_map/ppermute | solution.py:586
  544.2 21.4 %collective-permute-done.8 = bf16[1,256,1024]{2,1,0:T(8,128)(2,1)S(1)} collective-permute-done((bf16[1,256,1024]{2,1,0:T(8,128)(2,1)S(1)}, bf16[1,256,1024]{2,1,0:T(8,128)(2,1)S(1)}, u32[]{:S(2)}, u32[]{:S(2)}) %collective-permute-start.8) | collective-permute-done | bytes 524320 | tf_op jit(solution)/shard_map/ppermute | solution.py:586
  565.7 24.3 %reduce-scatter.4.cloned.1.call-done = bf16[32,3200]{1,0:T(8,128)(2,1)} async-done(((bf16[1024,3200]{1,0:T(8,128)(2,1)}), bf16[32,3200]{1,0:T(8,128)(2,1)}) %reduce-scatter.4.cloned.1.call-update) | async-done | bytes 204816 | tf_op jit(solution)/shard_map/reduce_scatter | solution.py:627
  592.3 1.7 fusion.12
  594.0 143.1 %reduce-scatter.8.cloned.1.call-done = bf16[128,1024]{1,0:T(8,128)(2,1)} async-done(((bf16[4096,1024]{1,0:T(8,128)(2,1)}), bf16[128,1024]{1,0:T(8,128)(2,1)}) %reduce-scatter.8.cloned.1.call-update) | async-done | bytes 262160 | tf_op jit(solution)/shard_map/reduce_scatter | solution.py:627
  737.0 1.8 convert_element_type.108
  738.8 149.3 %reduce-scatter.6.cloned.1.call-done = bf16[32,5120]{1,0:T(8,128)(2,1)} async-done(((bf16[1024,5120]{1,0:T(8,128)(2,1)}), bf16[32,5120]{1,0:T(8,128)(2,1)}) %reduce-scatter.6.cloned.1.call-update) | async-done | bytes 327696 | tf_op jit(solution)/shard_map/reduce_scatter | solution.py:627
  888.1 1.9 multiply_reduce_fusion
  (120 shorter events, 34.7 us)
Async XLA Ops:
  7.2 6.9 copy-start.15
  7.2 7.7 copy-start.14
  7.2 91.7 %all-gather.4.cloned.1.call-start = ((), (), s32[]{:S(2)}) async-start(), calls=%async_computation.3 | async-start | bytes 6758400 | tf_op jit(solution)/shard_map/all_gather | solution.py:604
  12.9 175.1 %all-gather.6.cloned.1.call-start = ((), (), s32[]{:S(2)}) async-start(), calls=%async_computation.4 | async-start | bytes 10813440 | tf_op jit(solution)/shard_map/all_gather | solution.py:606
  14.9 252.0 %all-gather.8.cloned.1.call-start = ((), (), s32[]{:S(2)}) async-start(), calls=%async_computation.5 | async-start | bytes 8650752 | tf_op jit(solution)/shard_map/all_gather | solution.py:607
  15.7 574.3 %reduce-scatter.4.cloned.1.call-start = ((), (), s32[]{:S(2)}) async-start(), calls=%async_computation.6 | async-start | bytes 6758400 | tf_op jit(solution)/shard_map/reduce_scatter | solution.py:627
  18.8 4.7 copy-start.5
  18.8 8.9 collective-permute-start.3
  19.2 17.1 %collective-permute-start.4 = (bf16[1,256,1024]{2,1,0:T(8,128)(2,1)}, bf16[1,256,1024]{2,1,0:T(8,128)(2,1)}, u32[]{:S(2)}, u32[]{:S(2)}) collective-permute-start(bf16[1,256,1024]{2,1,0:T(8,128)(2,1)} %get-tuple-element.56), channel_id=1, source_target_pairs={{0,2},{1,3},{2,0},{3,1},{4,6},{5,7},{6,4},{7,5},{8,10},{9,11},{10,... | collective-permute-start | bytes 1572872 | tf_op jit(solution)/shard_map/ppermute | solution.py:586
  21.7 29.2 %collective-permute-start.5 = (bf16[1,256,1024]{2,1,0:T(8,128)(2,1)}, bf16[1,256,1024]{2,1,0:T(8,128)(2,1)S(1)}, u32[]{:S(2)}, u32[]{:S(2)}) collective-permute-start(bf16[1,256,1024]{2,1,0:T(8,128)(2,1)} %get-tuple-element.55), channel_id=1, source_target_pairs={{0,3},{1,2},{2,1},{3,0},{4,7},{5,6},{6,5},{7,4},{8,11},{9,10},{10,... | collective-permute-start | bytes 1572872 | tf_op jit(solution)/shard_map/ppermute | solution.py:586
  23.5 3.4 copy-start.19
  23.5 4.0 copy-start.16
  24.8 26.2 %collective-permute-start = (bf16[1,256,1024]{2,1,0:T(8,128)(2,1)}, bf16[1,256,1024]{2,1,0:T(8,128)(2,1)}, u32[]{:S(2)}, u32[]{:S(2)}) collective-permute-start(bf16[1,256,1024]{2,1,0:T(8,128)(2,1)} %get-tuple-element.61), channel_id=1, source_target_pairs={{0,1},{1,0},{2,3},{3,2},{4,5},{5,4},{6,7},{7,6},{8,9},{9,8},{10,11... | collective-permute-start | bytes 1572872 | tf_op jit(solution)/shard_map/ppermute | solution.py:586
  24.9 39.6 %collective-permute-start.1 = (bf16[1,256,1024]{2,1,0:T(8,128)(2,1)}, bf16[1,256,1024]{2,1,0:T(8,128)(2,1)S(1)}, u32[]{:S(2)}, u32[]{:S(2)}) collective-permute-start(bf16[1,256,1024]{2,1,0:T(8,128)(2,1)} %get-tuple-element.60), channel_id=1, source_target_pairs={{0,2},{1,3},{2,0},{3,1},{4,6},{5,7},{6,4},{7,5},{8,10},{9,11},{10,... | collective-permute-start | bytes 1572872 | tf_op jit(solution)/shard_map/ppermute | solution.py:586
  27.7 54.8 %collective-permute-start.2 = (bf16[1,256,1024]{2,1,0:T(8,128)(2,1)}, bf16[1,256,1024]{2,1,0:T(8,128)(2,1)S(1)}, u32[]{:S(2)}, u32[]{:S(2)}) collective-permute-start(bf16[1,256,1024]{2,1,0:T(8,128)(2,1)} %get-tuple-element.59), channel_id=1, source_target_pairs={{0,3},{1,2},{2,1},{3,0},{4,7},{5,6},{6,5},{7,4},{8,11},{9,10},{10,... | collective-permute-start | bytes 1572872 | tf_op jit(solution)/shard_map/ppermute | solution.py:586
  51.0 51.0 %copy-start.3 = (bf16[4,256,1024]{2,1,0:T(8,128)(2,1)}, bf16[4,256,1024]{2,1,0:T(8,128)(2,1)S(1)}, u32[]{:S(2)}) copy-start(bf16[4,256,1024]{2,1,0:T(8,128)(2,1)S(1)} %constant_dynamic-update-slice_fusion.5) | copy-start | bytes 6291460
  445.1 291.9 %reduce-scatter.8.cloned.1.call-start = ((), (), s32[]{:S(2)}) async-start(), calls=%async_computation.8 | async-start | bytes 8650752 | tf_op jit(solution)/shard_map/reduce_scatter | solution.py:627
  445.7 442.4 %reduce-scatter.6.cloned.1.call-start = ((), (), s32[]{:S(2)}) async-start(), calls=%async_computation.7 | async-start | bytes 10813440 | tf_op jit(solution)/shard_map/reduce_scatter | solution.py:627
  472.5 4.5 collective-permute-start.9
  472.8 26.3 %collective-permute-start.10 = (bf16[1,256,1024]{2,1,0:T(8,128)(2,1)S(1)}, bf16[1,256,1024]{2,1,0:T(8,128)(2,1)S(1)}, u32[]{:S(2)}, u32[]{:S(2)}) collective-permute-start(bf16[1,256,1024]{2,1,0:T(8,128)(2,1)S(1)} %get-tuple-element.48), channel_id=1, source_target_pairs={{0,2},{1,3},{2,0},{3,1},{4,6},{5,7},{6,4},{7,5},{8,10},{9,11},{10,... | collective-permute-start | bytes 1572872 | tf_op jit(solution)/shard_map/ppermute | solution.py:586
  474.2 47.6 %collective-permute-start.11 = (bf16[1,256,1024]{2,1,0:T(8,128)(2,1)S(1)}, bf16[1,256,1024]{2,1,0:T(8,128)(2,1)S(1)}, u32[]{:S(2)}, u32[]{:S(2)}) collective-permute-start(bf16[1,256,1024]{2,1,0:T(8,128)(2,1)S(1)} %get-tuple-element.47), channel_id=1, source_target_pairs={{0,3},{1,2},{2,1},{3,0},{4,7},{5,6},{6,5},{7,4},{8,11},{9,10},{10,... | collective-permute-start | bytes 1572872 | tf_op jit(solution)/shard_map/ppermute | solution.py:586
  474.9 46.9 %collective-permute-start.6 = (bf16[1,256,1024]{2,1,0:T(8,128)(2,1)S(1)}, bf16[1,256,1024]{2,1,0:T(8,128)(2,1)S(1)}, u32[]{:S(2)}, u32[]{:S(2)}) collective-permute-start(bf16[1,256,1024]{2,1,0:T(8,128)(2,1)S(1)} %get-tuple-element.53), channel_id=1, source_target_pairs={{0,1},{1,0},{2,3},{3,2},{4,5},{5,4},{6,7},{7,6},{8,9},{9,8},{10,11... | collective-permute-start | bytes 1572872 | tf_op jit(solution)/shard_map/ppermute | solution.py:586
  475.6 68.6 %collective-permute-start.7 = (bf16[1,256,1024]{2,1,0:T(8,128)(2,1)S(1)}, bf16[1,256,1024]{2,1,0:T(8,128)(2,1)S(1)}, u32[]{:S(2)}, u32[]{:S(2)}) collective-permute-start(bf16[1,256,1024]{2,1,0:T(8,128)(2,1)S(1)} %get-tuple-element.52), channel_id=1, source_target_pairs={{0,2},{1,3},{2,0},{3,1},{4,6},{5,7},{6,4},{7,5},{8,10},{9,11},{10,... | collective-permute-start | bytes 1572872 | tf_op jit(solution)/shard_map/ppermute | solution.py:586
  476.9 88.7 %collective-permute-start.8 = (bf16[1,256,1024]{2,1,0:T(8,128)(2,1)S(1)}, bf16[1,256,1024]{2,1,0:T(8,128)(2,1)S(1)}, u32[]{:S(2)}, u32[]{:S(2)}) collective-permute-start(bf16[1,256,1024]{2,1,0:T(8,128)(2,1)S(1)} %get-tuple-element.51), channel_id=1, source_target_pairs={{0,3},{1,2},{2,1},{3,0},{4,7},{5,6},{6,5},{7,4},{8,11},{9,10},{10,... | collective-permute-start | bytes 1572872 | tf_op jit(solution)/shard_map/ppermute | solution.py:586
  521.8 22.4 %copy-start.2 = (bf16[4,256,1024]{2,1,0:T(8,128)(2,1)}, bf16[4,256,1024]{2,1,0:T(8,128)(2,1)S(1)}, u32[]{:S(2)}) copy-start(bf16[4,256,1024]{2,1,0:T(8,128)(2,1)S(1)} %constant_dynamic-update-slice_fusion.1) | copy-start | bytes 6291460
  521.8 69.8 %copy-start.9 = (bf16[32,1024]{1,0:T(8,128)(2,1)S(1)}, bf16[32,1024]{1,0:T(8,128)(2,1)}, u32[]{:S(2)}) copy-start(bf16[32,1024]{1,0:T(8,128)(2,1)} %copy-done.8) | copy-start | bytes 196612
  521.8 69.8 %copy-start.11 = (bf16[32,1024]{1,0:T(8,128)(2,1)S(1)}, bf16[32,1024]{1,0:T(8,128)(2,1)}, u32[]{:S(2)}) copy-start(bf16[32,1024]{1,0:T(8,128)(2,1)} %copy-done.10) | copy-start | bytes 196612
  521.8 69.8 %copy-start.13 = (bf16[32,1024]{1,0:T(8,128)(2,1)S(1)}, bf16[32,1024]{1,0:T(8,128)(2,1)}, u32[]{:S(2)}) copy-start(bf16[32,1024]{1,0:T(8,128)(2,1)} %copy-done.12) | copy-start | bytes 196612
  521.8 70.0 %copy-start.17 = (f32[32]{0:T(128)S(1)}, f32[32]{0:T(128)}, u32[]{:S(2)}) copy-start(f32[32]{0:T(128)} %param.17) | copy-start | bytes 388
  544.2 344.0 %copy-start.4 = (f32[32,4096]{1,0:T(8,128)S(1)}, f32[32,4096]{1,0:T(8,128)}, u32[]{:S(2)}) copy-start(f32[32,4096]{1,0:T(8,128)} %param.24) | copy-start | bytes 1572868
  565.7 324.4 %copy-start.1 = (bf16[4,256,1024]{2,1,0:T(8,128)(2,1)}, bf16[4,256,1024]{2,1,0:T(8,128)(2,1)S(1)}, u32[]{:S(2)}) copy-start(bf16[4,256,1024]{2,1,0:T(8,128)(2,1)S(1)} %constant_dynamic-update-slice_fusion.2) | copy-start | bytes 6291460
  565.7 324.4 %copy-start.18 = (f32[32]{0:T(128)S(1)}, f32[32]{0:T(128)}, u32[]{:S(2)}) copy-start(f32[32]{0:T(128)} %param.23) | copy-start | bytes 388
  (6 other events, 8.9 us)
Sparse Core Ops, SparseCore 0:
  13.1 85.7 all-gather.3
  101.7 86.3 all-gather.5
  190.9 75.9 all-gather.7
  445.2 144.7 reduce-scatter.3
  592.2 144.8 reduce-scatter.7
  739.2 148.8 reduce-scatter.5

commit v2 on v1

--- a/solution.py
+++ b/solution.py
@@ -287,6 +287,7 @@
 NT = (((1,), (1,)), ((), ()))
 TN = (((0,), (0,)), ((), ()))
 STRIP = 128
+LIMIT = 58 << 20
 
 def _dot(a, b, dims=(((1,), (0,)), ((), ()))):
     return lax.dot_general(a, b, dims, preferred_element_type=jnp.float32)
@@ -303,6 +304,7 @@
 def fwd_kernel(len_ref, q_ref, k_ref, v_ref, t_ref, o_ref, lse_ref, strip, *, rows, seq_len):
     wide = t_ref.shape[-1]
     length = len_ref[0]
+    pair = pl.program_id(0)
     blocks = seq_len // rows
     per = rows // STRIP
     col_ok = lax.broadcasted_iota(jnp.int32, (1, seq_len), 1) < length
@@ -310,7 +312,7 @@
     k2 = k_ref[...]
     v2 = v_ref[...]
     for a in range(2):
-        strip[a] = skew(t_ref[0, a:a + 1, :], wide)
+        strip[a] = skew(t_ref[pl.ds(2 * pair + a, 1), :], wide)
 
     def step(b, carry):
         base = pl.multiple_of(b * rows, rows)
@@ -347,18 +349,20 @@
                    jax.ShapeDtypeStruct((pairs, seq_len, 128), jnp.float32)),
         grid_spec=pltpu.PrefetchScalarGridSpec(
             num_scalar_prefetch=1, grid=(pairs,),
-            in_specs=[blk, blk, blk, pl.BlockSpec((1, 2, wide), lambda p, n: (p, 0, 0))],
+            in_specs=[blk, blk, blk, pl.BlockSpec(t.shape, lambda p, n: (0, 0))],
             out_specs=[blk, pl.BlockSpec((1, seq_len, 128), lambda p, n: (p, 0, 0))],
             scratch_shapes=[pltpu.VMEM((2, STRIP, wide), jnp.float32)]),
-        compiler_params=pltpu.CompilerParams(vmem_limit_bytes=56 << 20),
-        cost_estimate=pl.CostEstimate(flops=4 * seq_len * seq_len * width * 4, bytes_accessed=seq_len * width * 12, transcendentals=seq_len * seq_len * 16),
+        compiler_params=pltpu.CompilerParams(vmem_limit_bytes=40 << 20),
+        cost_estimate=pl.CostEstimate(flops=8 * seq_len * seq_len * width, bytes_accessed=seq_len * width * 12, transcendentals=seq_len * seq_len * pairs * 2),
         name="attn_fwd",
     )(length, q, k, v, t)
 
-def bwd_kernel(len_ref, q_ref, k_ref, v_ref, do_ref, o_ref, lse_ref, t_ref,
-               dq_ref, dk_ref, dv_ref, g_ref, strip, acc, dq_acc, *, rows, seq_len):
+def bwd_kernel(len_ref, q_ref, k_ref, v_ref, do_ref, o_ref, lse_ref, t_ref, *refs, rows, seq_len, first):
+    dq_ref, dk_ref, dv_ref, g_ref, strip, acc, dq_acc = refs[-7:]
     wide = t_ref.shape[-1]
     length = len_ref[0]
+    local_pair = pl.program_id(0)
+    pair = first + local_pair
     blocks = seq_len // rows
     per = rows // STRIP
     lane = lax.broadcasted_iota(jnp.int32, (1, 128), 1)
@@ -369,7 +373,7 @@
     lse_rows = [stat[0:1, :], stat[64:65, :]]
     delta_rows = [jnp.sum(prod[0:64], axis=0, keepdims=True), jnp.sum(prod[64:128], axis=0, keepdims=True)]
     for a in range(2):
-        strip[a] = skew(t_ref[0, a:a + 1, :], wide)
+        strip[a] = skew(t_ref[pl.ds(2 * pair + a, 1), :], wide)
     acc[...] = jnp.zeros_like(acc)
     dq_acc[...] = jnp.zeros_like(dq_acc)
 
@@ -409,53 +413,110 @@
         while half > 1:
             half //= 2
             sums = sums + pltpu.roll(pltpu.roll(sums, 8 - half, 0), wide - half, 1)
-        g_ref[0, a:a + 1, :] = pltpu.roll(sums, STRIP - 1, 1)[0:1]
-
-def attn_bwd(length, q, k, v, do, o, lse, trev, rows=256):
+        g_ref[pl.ds(2 * local_pair + a, 1), :] = pltpu.roll(sums, STRIP - 1, 1)[0:1]
+
+def attn_bwd(length, q, k, v, do, o, lse, trev, first, count, prev=None, rows=256):
     seq_len, width = q.shape
-    pairs = width // 128
     wide = trev.shape[-1]
-    blk = pl.BlockSpec((seq_len, 128), lambda p, n: (0, p))
-    tb = pl.BlockSpec((1, 2, wide), lambda p, n: (p, 0, 0))
+    blk = pl.BlockSpec((seq_len, 128), lambda p, n: (0, first + p))
     mat = jax.ShapeDtypeStruct((seq_len, width), jnp.bfloat16)
+    prev = tuple(prev) if prev is not None else ()
     return pl.pallas_call(
-        functools.partial(bwd_kernel, rows=rows, seq_len=seq_len),
-        out_shape=(mat, mat, mat, jax.ShapeDtypeStruct((pairs, 2, wide), jnp.float32)),
+        functools.partial(bwd_kernel, rows=rows, seq_len=seq_len, first=first),
+        out_shape=(mat, mat, mat, jax.ShapeDtypeStruct((2 * count, wide), jnp.float32)),
         grid_spec=pltpu.PrefetchScalarGridSpec(
-            num_scalar_prefetch=1, grid=(pairs,),
-            in_specs=[blk, blk, blk, blk, blk, pl.BlockSpec((1, seq_len, 128), lambda p, n: (p, 0, 0)), tb],
-            out_specs=[blk, blk, blk, tb],
+            num_scalar_prefetch=1, grid=(count,),
+            in_specs=[blk, blk, blk, blk, blk, pl.BlockSpec((1, seq_len, 128), lambda p, n: (first + p, 0, 0)),
+                      pl.BlockSpec(trev.shape, lambda p, n: (0, 0))] + [pl.BlockSpec(memory_space=pl.ANY)] * len(prev),
+            out_specs=[blk, blk, blk, pl.BlockSpec((2 * count, wide), lambda p, n: (0, 0))],
             scratch_shapes=[pltpu.VMEM((2, STRIP, wide), jnp.float32), pltpu.VMEM((2, STRIP, wide), jnp.float32),
                             pltpu.VMEM((2, seq_len, 128), jnp.float32)]),
-        compiler_params=pltpu.CompilerParams(vmem_limit_bytes=56 << 20),
-        cost_estimate=pl.CostEstimate(flops=10 * seq_len * seq_len * width * 4, bytes_accessed=seq_len * width * 20, transcendentals=seq_len * seq_len * 16),
+        input_output_aliases={8 + i: i for i in range(len(prev))},
+        compiler_params=pltpu.CompilerParams(vmem_limit_bytes=40 << 20),
+        cost_estimate=pl.CostEstimate(flops=20 * seq_len * seq_len * 128 * count, bytes_accessed=seq_len * 128 * count * 20, transcendentals=seq_len * seq_len * count * 2),
         name="attn_bwd",
-    )(length, q, k, v, do, o, lse, trev)
-
-LIMIT = 58 << 20
-
-def qkv_kernel(x_ref, gain_ref, w_ref, h_ref, q_ref, k_ref, v_ref):
-    x = x_ref[...].astype(jnp.float32)
-    inverse = lax.rsqrt(jnp.mean(x * x, axis=1, keepdims=True) + epsilon)
-    hidden = (x * inverse * gain_ref[...]).astype(jnp.bfloat16)
-    h_ref[...] = hidden
-    width = x.shape[1]
-    for i, ref in enumerate((q_ref, k_ref, v_ref)):
-        ref[...] = _dot(hidden, w_ref[:, i * width:(i + 1) * width]).astype(jnp.bfloat16)
-
-def qkv_fwd(x, gain, w, rows=512):
-    total, width = x.shape
-    blk = pl.BlockSpec((rows, width), lambda i: (i, 0))
+    )(length, q, k, v, do, o, lse, trev, *prev)
+
+ANY = pl.BlockSpec(memory_space=pl.ANY)
+VM = pl.BlockSpec(memory_space=pltpu.VMEM)
+SM = pl.BlockSpec(memory_space=pltpu.SMEM)
+
+def rms_inverse(value):
+    return lax.rsqrt(jnp.mean(value * value, axis=1, keepdims=True) + epsilon)
+
+def pull_sequence(me, whole_ref, came, dst, sem):
+    rows = whole_ref.shape[1]
+    for mask, ref in enumerate((whole_ref,) + tuple(came)):
+        src = ref.at[me] if mask == 0 else ref.at[0]
+        at = pl.multiple_of((me ^ mask) * rows, rows)
+        pltpu.make_async_copy(src, dst.at[pl.ds(at, rows), :], sem).start()
+
+def qkv_kernel(ids_ref, x4_ref, c1_ref, c2_ref, c3_ref, *refs, masks):
+    gathered = refs[:len(masks)]
+    bucket_ref = refs[len(masks)]
+    x_out, h_out, q_out, k_out, v_out, w_out, gain_ref, t_ref, trev_ref, xs, hs, ps, ws, es, sems = refs[len(masks) + 1:]
+    me, flat = ids_ref[0], ids_ref[1]
+    width = xs.shape[1]
+    own = width // es.shape[0]
+    pull_sequence(me, x4_ref, (c1_ref, c2_ref, c3_ref), xs, sems.at[0])
+    for ref, ids in zip(gathered, masks):
+        for j, mask in enumerate(ids):
+            shard = flat ^ mask
+            pltpu.make_async_copy(ref.at[j, 3 * own:3 * own + 16, :], es.at[shard], sems.at[1]).start()
+    for ref, ids in zip(gathered, masks):
+        for j, mask in enumerate(ids):
+            at = pl.multiple_of((flat ^ mask) * own, own)
+            for i in range(3):
+                pltpu.make_async_copy(ref.at[j, i * own:(i + 1) * own, :], ws.at[pl.ds(at, own), i * width:(i + 1) * width], sems.at[2]).start()
+    pltpu.make_async_copy(es, es, sems.at[1]).wait()
+    extras = es[...].astype(jnp.float32)
+    gains = jnp.sum(extras, axis=0)
+    gain_ref[...] = gains[0:8]
+    table = extras[:, 8, 0:128].astype(jnp.bfloat16)
+    ids = lax.broadcasted_iota(jnp.int32, (es.shape[0], 1), 0)
+    heads = t_ref.shape[0]
+    for i, ref in enumerate((t_ref, trev_ref)):
+        hot = jnp.where(bucket_ref[i:i + 1, :] == ids, 1.0, 0.0).astype(jnp.bfloat16)
+        ref[...] = _dot(table, hot, TN)[0:heads]
+    pltpu.make_async_copy(xs, xs, sems.at[0]).wait()
+    part = 256
+    def norm(i, carry):
+        at = pl.ds(pl.multiple_of(i * part, part), part)
+        x = xs[at, :].astype(jnp.float32)
+        hs[at, :] = (x * rms_inverse(x) * gains[0:1]).astype(jnp.bfloat16)
+        return carry
+    lax.fori_loop(0, xs.shape[0] // part, norm, 0)
+    copies = [pltpu.make_async_copy(xs, x_out, sems.at[0]), pltpu.make_async_copy(hs, h_out, sems.at[1])]
+    for copy in copies:
+        copy.start()
+    pltpu.make_async_copy(ws, ws, sems.at[2]).wait()
+    copies.append(pltpu.make_async_copy(ws, w_out, sems.at[2]))
+    copies[-1].start()
+    for i, ref in enumerate((q_out, k_out, v_out)):
+        ps[i] = _dot(hs[...], ws[:, i * width:(i + 1) * width]).astype(jnp.bfloat16)
+        copies.append(pltpu.make_async_copy(ps.at[i], ref, sems.at[3 + i]))
+        copies[-1].start()
+    for copy in copies:
+        copy.wait()
+
+def qkv_fwd(ids, x4, came, gathered, masks, bucket_rows, heads):
+    parts, rows, width = x4.shape
+    total = parts * rows
+    shards = sum(len(m) for m in masks)
     mat = jax.ShapeDtypeStruct((total, width), jnp.bfloat16)
+    wide = bucket_rows.shape[1]
+    vm = lambda *s: pltpu.VMEM(s, jnp.bfloat16)
     return pl.pallas_call(
-        qkv_kernel, out_shape=(mat,) * 4, grid=(total // rows,),
-        in_specs=[blk, pl.BlockSpec((1, width), lambda i: (0, 0)),
-                  pl.BlockSpec((width, 3 * width), lambda i: (0, 0), pipeline_mode=pl.Buffered(1))],
-        out_specs=[blk] * 4,
+        functools.partial(qkv_kernel, masks=masks),
+        out_shape=(mat,) * 5 + (jax.ShapeDtypeStruct((width, 3 * width), jnp.bfloat16), jax.ShapeDtypeStruct((8, width), jnp.float32),
+                                jax.ShapeDtypeStruct((heads, wide), jnp.float32), jax.ShapeDtypeStruct((heads, wide), jnp.float32)),
+        in_specs=[SM] + [ANY] * (4 + len(gathered)) + [VM],
+        out_specs=[ANY] * 6 + [VM] * 3,
+        scratch_shapes=[vm(total, width), vm(total, width), vm(3, total, width), vm(width, 3 * width), vm(shards, 16, width), pltpu.SemaphoreType.DMA((6,))],
         compiler_params=pltpu.CompilerParams(vmem_limit_bytes=LIMIT),
-        cost_estimate=pl.CostEstimate(flops=6 * total * width * width, bytes_accessed=total * width * 10 + width * width * 6, transcendentals=0),
+        cost_estimate=pl.CostEstimate(flops=6 * total * width * width, bytes_accessed=total * width * 12 + width * width * 12, transcendentals=0),
         name="qkv_fwd",
-    )(x, gain, w)
+    )(ids, x4, *came, *gathered, bucket_rows)
 
 def gelu_both(v):
     t = jnp.tanh(root_coef * (v + cubic_coef * v * v * v))
@@ -463,95 +524,124 @@
     slope = half + 0.5 * v * (1.0 - t * t) * (root_coef * (1.0 + 3.0 * cubic_coef * v * v))
     return v * half, slope
 
-def mid_kernel(len_ref, x_ref, o_ref, g_ref, gain_ref, wo_ref, win_ref, wback_ref,
-               out_ref, gb_ref, do_ref, gwo_ref, gwin_ref, gwback_ref,
-               mixed, h2, h2t, acc, gh2, gm):
+def mid_kernel(ids_ref, x_ref, o_ref, g4_ref, c1_ref, c2_ref, c3_ref, gain_ref, wback_ref, wo_ref, win_ref,
+               out_ref, gb_ref, do_ref, gw_ref, gwback_ref,
+               mixed, h2, h2t, acc, gh2, gm, sem, *, ff_steps):
     step = pl.program_id(0)
-    rows = x_ref.shape[0]
-
+    rows, width = x_ref.shape
     part = 256
+    flat = lambda ref: ref[...].reshape(-1, ref.shape[-1])
 
     @pl.when(step == 0)
     def _():
+        pull_sequence(ids_ref[0], g4_ref, (c1_ref, c2_ref, c3_ref), gm, sem)
+        wo = flat(wo_ref)
         def load(i, carry):
             at = pl.ds(pl.multiple_of(i * part, part), part)
-            row_ok = i * part + lax.broadcasted_iota(jnp.int32, (part, 1), 0) < len_ref[0]
-            gm[at, :] = jnp.where(row_ok, g_ref[at, :], jnp.zeros((part, g_ref.shape[1]), jnp.bfloat16))
-            value = x_ref[at, :].astype(jnp.float32) + _dot(o_ref[at, :], wo_ref[...])
+            value = x_ref[at, :].astype(jnp.float32) + _dot(o_ref[at, :], wo)
             mixed[at, :] = value
             acc[at, :] = value
-            inverse = lax.rsqrt(jnp.mean(value * value, axis=1, keepdims=True) + epsilon)
-            hidden = (value * inverse * gain_ref[...]).astype(jnp.bfloat16)
+            hidden = (value * rms_inverse(value) * gain_ref[1:2, :]).astype(jnp.bfloat16)
             h2[at, :] = hidden
             h2t[:, at] = hidden.T
             gh2[at, :] = jnp.zeros_like(value)
             return carry
         lax.fori_loop(0, rows // part, load, 0)
-
-    pre = _dot(h2[...], win_ref[...])
-    grad_active = _dot(gm[...], wback_ref[...], NT)
-    act, slope = gelu_both(pre)
-    active = act.astype(jnp.bfloat16)
-    gpre = (grad_active * slope).astype(jnp.bfloat16)
-    acc[...] += _dot(active, wback_ref[...])
-    gwback_ref[...] = _dot(active, gm[...], TN).astype(jnp.bfloat16)
-    gwin_ref[...] = _dot(h2t[...], gpre).astype(jnp.bfloat16)
-    gh2[...] += _dot(gpre, win_ref[...], NT)
-
-    @pl.when(step == pl.num_programs(0) - 1)
+        pltpu.make_async_copy(gm, gm, sem).wait()
+        row_ok = lax.broadcasted_iota(jnp.int32, (rows, 1), 0) < ids_ref[2]
+        gm[...] = jnp.where(row_ok, gm[...], jnp.zeros_like(gm[...]))
+
+    @pl.when(step < ff_steps)
     def _():
+        win = flat(win_ref)
+        wback = flat(wback_ref)
+        pre = _dot(h2[...], win)
+        grad_active = _dot(gm[...], wback, NT)
+        act, slope = gelu_both(pre)
+        active = act.astype(jnp.bfloat16)
+        gpre = (grad_active * slope).astype(jnp.bfloat16)
+        acc[...] += _dot(active, wback)
+        gwback_ref[...] = _dot(active, gm[...], TN).astype(jnp.bfloat16)
+        gw_ref[...] = _dot(h2t[...], gpre).astype(jnp.bfloat16).reshape(gw_ref.shape)
+        gh2[...] += _dot(gpre, win, NT)
+
+    @pl.when(step == ff_steps)
+    def _():
+        wo = flat(wo_ref)
         def finish(i, carry):
             at = pl.ds(pl.multiple_of(i * part, part), part)
             out_ref[at, :] = acc[at, :].astype(jnp.bfloat16)
             value = mixed[at, :]
-            inverse = lax.rsqrt(jnp.mean(value * value, axis=1, keepdims=True) + epsilon)
+            inverse = rms_inverse(value)
             normed = value * inverse
-            scaled = gh2[at, :] * gain_ref[...]
+            scaled = gh2[at, :] * gain_ref[1:2, :]
             grad = inverse * (scaled - normed * jnp.mean(scaled * normed, axis=1, keepdims=True)) + gm[at, :].astype(jnp.float32)
             gb = grad.astype(jnp.bfloat16)
             gb_ref[at, :] = gb
-            do_ref[at, :] = _dot(gb, wo_ref[...], NT).astype(jnp.bfloat16)
+            do_ref[at, :] = _dot(gb, wo, NT).astype(jnp.bfloat16)
             return carry
         lax.fori_loop(0, rows // part, finish, 0)
-        gwo_ref[...] = _dot(o_ref[...], gb_ref[...], TN).astype(jnp.bfloat16)
-
-def mid(length, x, o, g, gain, wo, win, wback, cols=512):
+
+    @pl.when(step >= ff_steps)
+    def _():
+        cols = gw_ref.shape[-1]
+        at = pl.ds(pl.multiple_of((step - ff_steps) * cols, cols), cols)
+        gw_ref[...] = _dot(o_ref[...], gb_ref[:, at], TN).astype(jnp.bfloat16).reshape(gw_ref.shape)
+
+def mid(ids, x, o, g4, came, gains, full, cols=512):
     rows, width = x.shape
-    ff = win.shape[1]
-    one = lambda shape: pl.BlockSpec(shape, lambda i, n: (0, 0), pipeline_mode=pl.Buffered(1))
-    res = one
+    shards, stack, _ = full.shape
+    own = width // shards
+    ff_own = (stack - own) // 2
+    ff = ff_own * shards
+    ff_steps = ff // cols
+    wide = width // cols
+    one = lambda shape: pl.BlockSpec(shape, lambda i, n: (0,) * len(shape), pipeline_mode=pl.Buffered(1))
+    last = lambda i: jnp.minimum(i, ff_steps - 1)
     mat = jax.ShapeDtypeStruct((rows, width), jnp.bfloat16)
+    first = ff_own // own + 1
+    gw_map = lambda i, n: (0, jnp.where(i < ff_steps, 1 + i // wide, 0), jnp.where(i < ff_steps, i % wide, i - ff_steps))
     return pl.pallas_call(
-        mid_kernel,
-        out_shape=(mat, mat, mat, jax.ShapeDtypeStruct((width, width), jnp.bfloat16),
-                   jax.ShapeDtypeStruct((width, ff), jnp.bfloat16), jax.ShapeDtypeStruct((ff, width), jnp.bfloat16)),
+        functools.partial(mid_kernel, ff_steps=ff_steps),
+        out_shape=(mat, mat, mat, jax.ShapeDtypeStruct((shards, own + ff_own, width), jnp.bfloat16), jax.ShapeDtypeStruct((ff, width), jnp.bfloat16)),
         grid_spec=pltpu.PrefetchScalarGridSpec(
-            num_scalar_prefetch=1, grid=(ff // cols,),
-            in_specs=[one((rows, width)), one((rows, width)), one((rows, width)), one((1, width)), one((width, width)),
-                      pl.BlockSpec((width, cols), lambda i, n: (0, i)), pl.BlockSpec((cols, width), lambda i, n: (i, 0))],
-            out_specs=[res((rows, width)), res((rows, width)), res((rows, width)), res((width, width)),
-                       pl.BlockSpec((width, cols), lambda i, n: (0, i)), pl.BlockSpec((cols, width), lambda i, n: (i, 0))],
+            num_scalar_prefetch=1, grid=(ff_steps + wide,),
+            in_specs=[one((rows, width)), one((rows, width)), ANY, ANY, ANY, ANY, one(gains.shape),
+                      pl.BlockSpec((cols // ff_own, ff_own, width), lambda i, n: (last(i), 0, 0)),
+                      pl.BlockSpec((shards, own, width), lambda i, n: (0, first - 1, 0), pipeline_mode=pl.Buffered(1)),
+                      pl.BlockSpec((shards, own, cols), lambda i, n: (0, first + last(i) // wide, last(i) % wide))],
+            out_specs=[one((rows, width)), one((rows, width)), one((rows, width)),
+                       pl.BlockSpec((shards, own, cols), gw_map), pl.BlockSpec((cols, width), lambda i, n: (last(i), 0))],
             scratch_shapes=[pltpu.VMEM((rows, width), jnp.float32), pltpu.VMEM((rows, width), jnp.bfloat16),
                             pltpu.VMEM((width, rows), jnp.bfloat16), pltpu.VMEM((rows, width), jnp.float32),
-                            pltpu.VMEM((rows, width), jnp.float32), pltpu.VMEM((rows, width), jnp.bfloat16)]),
+                            pltpu.VMEM((rows, width), jnp.float32), pltpu.VMEM((rows, width), jnp.bfloat16), pltpu.SemaphoreType.DMA]),
         compiler_params=pltpu.CompilerParams(vmem_limit_bytes=LIMIT),
         cost_estimate=pl.CostEstimate(flops=12 * rows * width * ff + 6 * rows * width * width, bytes_accessed=rows * width * 12 + width * width * 4 + width * ff * 8, transcendentals=rows * ff),
         name="mid",
-    )(length, x, o, g, gain, wo, win, wback)
-
-def gw_kernel(h_ref, dq_ref, dk_ref, dv_ref, out_ref):
+    )(ids, x, o, g4, *came, gains, full, full, full)
+
+def gw_kernel(h_ref, dq_ref, dk_ref, dv_ref, bucket_ref, *refs):
+    out_ref = refs[-1]
+    shards, _, width = out_ref.shape
+    own = width // shards
     for i, ref in enumerate((dq_ref, dk_ref, dv_ref)):
-        w = ref.shape[1]
-        out_ref[:, i * w:(i + 1) * w] = _dot(h_ref[...], ref[...], TN).astype(jnp.bfloat16)
-
-def qkv_gw(h, dq, dk, dv):
+        out_ref[:, i * own:(i + 1) * own, :] = _dot(h_ref[...], ref[...], TN).astype(jnp.bfloat16).reshape(shards, own, width)
+    offs = jnp.concatenate([ref[...] for ref in refs[:-1]], 0)
+    ids = lax.broadcasted_iota(jnp.int32, (shards, 1), 0)
+    hot = jnp.where(bucket_ref[1:2, :] == ids, 1.0, 0.0)
+    table = lax.dot_general(hot, offs, NT, precision=lax.Precision.HIGHEST, preferred_element_type=jnp.float32)
+    out_ref[:, 3 * own:, :] = jnp.zeros((shards, 16, width), jnp.bfloat16)
+    out_ref[:, 3 * own:3 * own + 1, 0:offs.shape[0]] = table.astype(jnp.bfloat16).reshape(shards, 1, offs.shape[0])
+
+def qkv_gw(h, dq, dk, dv, bucket_rows, offs, shards):
     rows, width = h.shape
     return pl.pallas_call(
-        gw_kernel, out_shape=jax.ShapeDtypeStruct((width, 3 * width), jnp.bfloat16),
+        gw_kernel, out_shape=jax.ShapeDtypeStruct((shards, 3 * width // shards + 16, width), jnp.bfloat16),
+        in_specs=[VM] * (5 + len(offs)), out_specs=VM,
         compiler_params=pltpu.CompilerParams(vmem_limit_bytes=LIMIT),
         cost_estimate=pl.CostEstimate(flops=6 * rows * width * width, bytes_accessed=rows * width * 8 + width * width * 6, transcendentals=0),
         name="qkv_gw",
-    )(h, dq, dk, dv)
+    )(h, dq, dk, dv, bucket_rows, *offs)
 
 def gx_kernel(x_ref, gb_ref, dq_ref, dk_ref, dv_ref, gain_ref, w_ref, out_ref):
     width = x_ref.shape[1]
@@ -559,88 +649,167 @@
     grad += _dot(dk_ref[...], w_ref[:, width:2 * width], NT)
     grad += _dot(dv_ref[...], w_ref[:, 2 * width:3 * width], NT)
     x = x_ref[...].astype(jnp.float32)
-    inverse = lax.rsqrt(jnp.mean(x * x, axis=1, keepdims=True) + epsilon)
+    inverse = rms_inverse(x)
     normed = x * inverse
-    scaled = grad * gain_ref[...]
+    scaled = grad * gain_ref[0:1, :]
     out = inverse * (scaled - normed * jnp.mean(scaled * normed, axis=1, keepdims=True)) + gb_ref[...].astype(jnp.float32)
     out_ref[...] = out.astype(jnp.bfloat16)
 
-def qkv_gx(x, gb, dq, dk, dv, gain, w, rows=512):
+def qkv_gx(x, gb, dq, dk, dv, gains, w, rows=512):
     total, width = x.shape
     blk = pl.BlockSpec((rows, width), lambda i: (i, 0))
     return pl.pallas_call(
         gx_kernel, out_shape=jax.ShapeDtypeStruct((total, width), jnp.bfloat16), grid=(total // rows,),
-        in_specs=[blk] * 5 + [pl.BlockSpec((1, width), lambda i: (0, 0)),
+        in_specs=[blk] * 5 + [pl.BlockSpec(gains.shape, lambda i: (0, 0)),
                               pl.BlockSpec((width, 3 * width), lambda i: (0, 0), pipeline_mode=pl.Buffered(1))],
         out_specs=blk,
         compiler_params=pltpu.CompilerParams(vmem_limit_bytes=LIMIT),
         cost_estimate=pl.CostEstimate(flops=6 * total * width * width, bytes_accessed=total * width * 12 + width * width * 6, transcendentals=0),
         name="qkv_gx",
-    )(x, gb, dq, dk, dv, gain, w)
-def exchange(blocks):
-    parts = blocks.shape[0]
-    me = lax.axis_index("seq")
-    pick = lambda at: lax.dynamic_index_in_dim(blocks, at, 0, keepdims=True)
-    out = lax.dynamic_update_slice_in_dim(jnp.zeros_like(blocks), pick(me), me, 0)
-    for mask in range(1, parts):
-        came = lax.ppermute(pick(me ^ mask), "seq", [(i, i ^ mask) for i in range(parts)])
-        out = lax.dynamic_update_slice_in_dim(out, came, me ^ mask, 0)
-    return out
+    )(x, gb, dq, dk, dv, gains, w)
+
+def place_kernel(ids_ref, own_ref, c1_ref, c2_ref, c3_ref, out_ref, sem):
+    me = ids_ref[0]
+    copies = []
+    for mask, ref in enumerate((own_ref, c1_ref, c2_ref, c3_ref)):
+        src = ref.at[me] if mask == 0 else ref.at[0]
+        copies.append(pltpu.make_async_copy(src, out_ref.at[me ^ mask], sem.at[mask]))
+        copies[-1].start()
+    for copy in copies:
+        copy.wait()
+
+def place(ids, own, came):
+    return pl.pallas_call(
+        place_kernel, out_shape=jax.ShapeDtypeStruct(own.shape, own.dtype),
+        in_specs=[SM] + [ANY] * 4, out_specs=ANY, scratch_shapes=[pltpu.SemaphoreType.DMA((4,))],
+        cost_estimate=pl.CostEstimate(flops=0, bytes_accessed=own.size * 4, transcendentals=0),
+        name="place",
+    )(ids, own, *came)
+def swap(value, axis, mask):
+    return lax.ppermute(value, axis, [(i, i ^ mask) for i in range(lax.axis_size(axis))])
+
+
+def send_blocks(blocks, me):
+    return tuple(swap(lax.dynamic_index_in_dim(blocks, me ^ mask, 0), "seq", mask) for mask in range(1, blocks.shape[0]))
+
+
+MASKS = ((0, 8, 16, 24), (2, 10, 18, 26), (4, 12, 20, 28), (6, 14), (22, 30))
+
+
+def gather_staged(shard):
+    shard = shard[None]
+    column = jnp.concatenate([shard] + [swap(shard, "dp", 2 * z) for z in (1, 2, 3)], 0)
+    from_x, from_y = swap(column, "seq", 2), swap(column, "dp", 1)
+    corner_x, corner_y = swap(from_y[:2], "seq", 2), swap(from_x[2:], "dp", 1)
+    pieces = (column, from_x, from_y, corner_x, corner_y)
+    masks = MASKS + tuple(tuple(m | 1 for m in row) for row in MASKS)
+    return pieces + tuple(swap(p, "seq", 1) for p in pieces), masks
+
+
+class Scatter:
+    def __init__(self, grads, pos):
+        self.z, self.y, self.x, self.c = pos
+        self.grads = grads.reshape((4, 2, 2, 2) + grads.shape[1:])
+        self.other = swap(lax.dynamic_index_in_dim(self.grads, 1 - self.c, 3, keepdims=False), "seq", 1)
+
+    def fold(self):
+        pick = lambda v, at, axis: lax.dynamic_index_in_dim(v, at, axis, keepdims=False)
+        mine = pick(self.grads, self.c, 3)
+        def quarter(dy, dx):
+            cut = lambda v: pick(pick(v, self.y ^ dy, 1), self.x ^ dx, 1).astype(jnp.float32)
+            return (cut(mine) + cut(self.other)).astype(jnp.bfloat16)
+        far = quarter(1, 1)
+        self.to_x, self.to_y, self.own = quarter(0, 1), quarter(1, 0), quarter(0, 0)
+        self.came_x, self.came_y = swap(far[:2], "seq", 2), swap(far[2:], "dp", 1)
+
+    def turn(self):
+        add = lambda a, b: (a.astype(jnp.float32) + b.astype(jnp.float32)).astype(jnp.bfloat16)
+        to_x = lax.dynamic_update_slice_in_dim(self.to_x, add(self.to_x[2:], self.came_y), 2, 0)
+        to_y = lax.dynamic_update_slice_in_dim(self.to_y, add(self.to_y[:2], self.came_x), 0, 0)
+        self.came_x, self.came_y = swap(to_x, "seq", 2), swap(to_y, "dp", 1)
+
+    def column(self):
+        total = self.own.astype(jnp.float32) + self.came_x.astype(jnp.float32) + self.came_y.astype(jnp.float32)
+        total = total.astype(jnp.bfloat16)
+        block = lambda k: lax.dynamic_index_in_dim(total, self.z ^ k, 0, keepdims=False)
+        self.mine = block(0)
+        self.came = [swap(block(k), "dp", 2 * k) for k in (1, 2, 3)]
+
+    def result(self):
+        return sum((c.astype(jnp.float32) for c in self.came), self.mine.astype(jnp.float32))
+
+
+def tie(first, *later):
+    return lax.optimization_barrier((first,) + later)[1:]
 
 
 def local_whole(tokens, cotangent, lengths, buckets, norm1_gain, w_query, w_key, w_value, w_out, rel_table, norm2_gain, w_in, w_back):
-    micro_count, seq_count, row_count, width = tokens.shape
+    micro_count, seq_count, rows, width = tokens.shape
     parts = micro_count * seq_count
-    seq_len = parts * row_count
     both = ("dp", "seq")
-    me = lax.axis_index("seq")
+    me, dp = lax.axis_index("seq"), lax.axis_index("dp")
+    shards = lax.axis_size("seq") * lax.axis_size("dp")
+    flat = dp * parts + me
+    pos = (dp // 2, dp % 2, me // 2, me % 2)
     low = lambda v: v.astype(jnp.bfloat16)
-    own = norm1_gain.shape[0]
-    few = rel_table.shape[0]
-    small = jnp.stack([norm1_gain, norm2_gain, jnp.pad(rel_table, (0, own - few))], 1)
-    small = jnp.pad(low(small), ((0, 0), (0, 125)))
-    shard1 = jnp.concatenate([low(w_query), low(w_key), low(w_value), small], 1)
-    shard2 = jnp.concatenate([low(w_out), low(w_in)], 1)
-    full1 = lax.all_gather(shard1, both, axis=0, tiled=True)
-    x = exchange(tokens.reshape(parts, row_count, width)).reshape(seq_len, width)
-    full2 = lax.all_gather(shard2, both, axis=0, tiled=True)
-    full3 = lax.all_gather(low(w_back), both, axis=0, tiled=True)
-    g = exchange(cotangent.reshape(parts, row_count, width)).reshape(seq_len, width)
-    length = lax.dynamic_index_in_dim(lengths.reshape(parts), me, 0)
-
-    extra = full1[:, 3 * width:]
-    gain1 = extra[:, 0].astype(jnp.float32).reshape(1, width)
-    gain2 = extra[:, 1].astype(jnp.float32).reshape(1, width)
-    table = extra[:, 2].reshape(-1, own)[:, :few].reshape(BUCKETS, HEADS)
-    ids = jnp.arange(BUCKETS, dtype=jnp.int32)[:, None]
-    hot = low(jnp.pad(buckets, (0, 1), constant_values=-1)[None, :] == ids)
-    hot_back = low(jnp.pad(buckets[::-1], (0, 1), constant_values=-1)[None, :] == ids)
-    spread = lambda h: jnp.einsum("bh,bo->ho", table, h, preferred_element_type=jnp.float32).reshape(HEADS // 2, 2, -1)
-
-    hidden, q, k, v = qkv_fwd(x, gain1, full1)
-    attended, lse = attn_fwd(length, q, k, v, spread(hot))
-    out, gb, grad_attended, gwo, gwin, gwback = mid(length, x, attended, g, gain2, full2[:, :width], full2[:, width:], full3)
-    dq, dk, dv, g_off = attn_bwd(length, q, k, v, grad_attended, attended, lse, spread(hot_back))
-    g_table = jnp.dot(hot_back.astype(jnp.float32), g_off.reshape(HEADS, -1).T, precision=highest)
-    gw = qkv_gw(hidden, dq, dk, dv)
-    gx = qkv_gx(x, gb, dq, dk, dv, gain1, full1)
-    scatter = lambda v: lax.psum_scatter(v, both, scatter_dimension=0, tiled=True)
-    column = jnp.pad(g_table.reshape(-1, few), ((0, 0), (0, own - few))).reshape(-1, 1)
-    r2 = scatter(jnp.concatenate([gwo, gwin], 1)).astype(jnp.float32)
-    r3 = scatter(gwback).astype(jnp.float32)
-    r1 = scatter(jnp.concatenate([gw, jnp.pad(low(column), ((0, 0), (0, 127)))], 1)).astype(jnp.float32)
-    layer_out = exchange(out.reshape(parts, row_count, width)).reshape(tokens.shape)
-    input_grad = exchange(gx.reshape(parts, row_count, width)).reshape(tokens.shape)
     up = lambda v: v.astype(jnp.float32)
-    g_gain1 = jnp.sum(up(shard1[:, :3 * width]) * r1[:, :3 * width], axis=1) / up(low(norm1_gain))
-    g_gain2 = jnp.sum(up(shard2[:, width:]) * r2[:, width:], axis=1) / up(low(norm2_gain))
-    return (layer_out, input_grad, g_gain1, r1[:, :width], r1[:, width:2 * width], r1[:, 2 * width:3 * width],
-            r2[:, :width], r1[:few, 3 * width], g_gain2, r2[:, width:], r3)
+    own, ff_own = w_query.shape[0], w_back.shape[0]
+    ids = jnp.stack([me, flat, lax.dynamic_index_in_dim(lengths.reshape(parts), me, 0, keepdims=False)])
+    length = ids[2:3]
+
+    place_row = lambda v: lax.dynamic_update_slice(jnp.zeros((1, width), jnp.bfloat16), low(v)[None], (0, flat * own))
+    small = jnp.concatenate([place_row(norm1_gain), place_row(norm2_gain), jnp.zeros((6, width), jnp.bfloat16),
+                             jnp.pad(low(rel_table)[None], ((0, 7), (0, width - HEADS)))], 0)
+    shard1 = jnp.concatenate([low(w_query), low(w_key), low(w_value), small], 0)
+    shard2 = jnp.concatenate([low(w_back), low(w_out)] + [low(w_in[:, i * width:(i + 1) * width]) for i in range(ff_own // own)], 0)
+    x4, g4 = tokens.reshape(parts, rows, width), cotangent.reshape(parts, rows, width)
+    gathered, masks = gather_staged(shard1)
+    x_came = send_blocks(x4, me)
+    g_came = send_blocks(g4, me)
+    full2 = lax.all_gather(shard2, both, axis=0, tiled=False)
+    bucket_rows = jnp.stack([jnp.pad(buckets, (0, 1), constant_values=-1), jnp.pad(buckets[::-1], (0, 1), constant_values=-1)])
+
+    x, hidden, q, k, v, w_qkv, gains, t, t_back = qkv_fwd(ids, x4, x_came, gathered, masks, bucket_rows, HEADS)
+    attended, lse = attn_fwd(length, q, k, v, t)
+    out, gb, g_att, gw2, gw_back = mid(ids, x, attended, g4, g_came, gains, full2)
+    sc2 = Scatter(gw2, pos)
+    r_back = lax.psum_scatter(gw_back, both, scatter_dimension=0, tiled=True)
+    out4 = out.reshape(parts, rows, width)
+    out_came = send_blocks(out4, me)
+    pairs = HEADS // 2
+    count = pairs // 4
+    back = lambda first, g, prev: attn_bwd(length, q, k, v, g, attended, lse, t_back, first, count, prev)
+    dq, dk, dv, off0 = back(0, g_att, None)
+    sc2.fold()
+    g_att, = tie(sc2.own, g_att)
+    dq, dk, dv, off1 = back(count, g_att, (dq, dk, dv))
+    sc2.turn()
+    g_att, = tie(sc2.own, g_att)
+    layer_out = place(ids, out4, out_came)
+    dq, dk, dv, off2 = back(2 * count, g_att, (dq, dk, dv))
+    dq, dk, dv, off3 = back(3 * count, g_att, (dq, dk, dv))
+    sc2.column()
+    gw1 = qkv_gw(hidden, dq, dk, dv, bucket_rows, (off0, off1, off2, off3), shards)
+    sc1 = Scatter(gw1, pos)
+    gx = qkv_gx(x, gb, dq, dk, dv, gains, w_qkv)
+    gx4 = gx.reshape(parts, rows, width)
+    gx_came = send_blocks(gx4, me)
+    sc1.fold()
+    sc1.turn()
+    sc1.column()
+    input_grad = place(ids, gx4, gx_came)
+    r1, r2, r_back = sc1.result(), sc2.result(), up(r_back)
+    g_in = jnp.concatenate([r2[own * (1 + i):own * (2 + i)] for i in range(ff_own // own)], 1)
+    prod = up(shard1[:3 * own]) * r1[:3 * own]
+    g_gain1 = jnp.sum(prod[:own] + prod[own:2 * own] + prod[2 * own:], axis=1) / up(low(norm1_gain))
+    g_gain2 = jnp.sum(up(low(w_in)) * g_in, axis=1) / up(low(norm2_gain))
+    return (layer_out.reshape(tokens.shape), input_grad.reshape(tokens.shape), g_gain1, r1[:own], r1[own:2 * own], r1[2 * own:3 * own],
+            r2[:own], r1[3 * own, :HEADS], g_gain2, g_in, r_back)
 
 
 def local_any(shape, tokens, *rest):
-    whole = tokens.shape[0] * tokens.shape[1] == shape[1] and tokens.shape[3] % 128 == 0
-    return (local_whole if whole else local)(tokens, *rest)
+    fits = tuple(shape) == (8, 4) and tokens.shape[0] * tokens.shape[1] == 4 and tokens.shape[3] == HEADS * DH == 1024
+    return (local_whole if fits else local)(tokens, *rest)
 
 
 def solution(mesh):

time: 900 us -> 712 us (0.79)
  waiting for transfers between devices: 568 us -> 180 us
  Pallas kernels: 239 us -> 380 us
  starting transfers between devices: 9.42 us -> 61.4 us
    reduce_scatter x3 -> x1, waiting for transfers between devices: 317 us -> 0.01 us  [local_whole(): r_back = lax.psum_scatter(gw_back, both, scatter_dimension=0, tiled=True)]
    pallas_call x4 -> x9, Pallas kernels: 182 us -> 323 us  [the longest x2 131 us: place(): pl.pallas_call(place_kernel, out_shape=jax.ShapeDtypeStruct(own.shape, ow...]
    all_gather x3 -> x1, waiting for transfers between devices: 113 us -> 8.67 us  [local_whole(): full2 = lax.all_gather(shard2, both, axis=0, tiled=False)]
    ppermute x12 -> x40, starting transfers between devices: 9.17 us -> 61.3 us  [swap(): lax.ppermute(value, axis, [(i, i ^ mask) for i in range(lax.axis_size(axi...]
    ppermute x12 -> x40, waiting for transfers between devices: 138 us -> 172 us  [swap(): lax.ppermute(value, axis, [(i, i ^ mask) for i in range(lax.axis_size(axi...]
    concatenate x4 -> x1, other arithmetic: 17.2 us -> 0.12 us  [gather_staged(): jnp.concatenate([shard] + [swap(shard, 'dp', 2 * z) for z in (1, 2, 3)], 0)]
    unnamed x43 -> x87, local copies, waits for them, and re-layouts: 3.33 us -> 16.3 us
    convert_element_type x3 -> x5, other arithmetic: 4.69 us -> 16.8 us  [the longest x2 9.82 us: quarter(): return (cut(mine) + cut(self.other)).astype(jnp.bfloat16)]
  transfers between devices with their start and end apart: 18 -> 42, of which waited for: 14 -> 19; matrix products, arithmetic and copies ran while one was open for 5% -> 5% of each run, Pallas kernels for 8% -> 43%
where the time goes in v2:
time: 712 us; the launch traced here: 702 us
  Pallas kernels  380 us (53%)
  waiting for transfers between devices  180 us (25%)
  starting transfers between devices  61.4 us (9%)
  local copies, waits for them, and re-layouts  36.2 us (5%)
  other arithmetic  28.6 us (4%)
  between operations  15.3 us (2%)
    ppermute x40, waiting for transfers between devices, swap(): lax.ppermute(value, axis, [(i, i ^ mask) for i in range(lax.axis_size(axi...  172 us
    pallas_call x2, Pallas kernels, place(): pl.pallas_call(place_kernel, out_shape=jax.ShapeDtypeStruct(own.shape, ow...  131 us
    pallas_call x4, Pallas kernels, attn_bwd(): pl.pallas_call(functools.partial(bwd_kernel, rows=rows, seq_len=seq_len,...  88.4 us
    pallas_call x1, Pallas kernels, mid(): pl.pallas_call(functools.partial(mid_kernel, ff_steps=ff_steps), out_shap...  77.2 us
    ppermute x40, starting transfers between devices, swap(): lax.ppermute(value, axis, [(i, i ^ mask) for i in range(lax.axis_size(axi...  61.3 us
    pallas_call x1, Pallas kernels, attn_fwd(): pl.pallas_call(functools.partial(fwd_kernel, rows=rows, seq_len=seq_len),...  43 us
    unnamed x87, local copies, waits for them, and re-layouts  16.3 us
  transfers between devices with their start and end apart: 42, of which 19 were waited for; matrix products, arithmetic and copies ran while one was open for 5% of the time, Pallas kernels for 43%

profile of v2, /device:TPU:0, one launch (start us, length us, event | category | flops | bytes accessed | tf_op | source)
XLA Modules:
  0.0 702.0 jit_solution(8485094189780160266)
XLA Ops:
  12.1 3.1 collective-permute-start.3
  17.7 7.4 %collective-permute-done.3 = bf16[1,112,1024]{2,1,0:T(8,128)(2,1)S(1)} collective-permute-done((bf16[1,112,1024]{2,1,0:T(8,128)(2,1)S(1)}, bf16[1,112,1024]{2,1,0:T(8,128)(2,1)S(1)}, u32[]{:S(2)}, u32[]{:S(2)}) %collective-permute-start.3) | collective-permute-done | bytes 229408 | tf_op jit(solution)/shard_map/ppermute | solution.py:689
  25.2 12.7 %collective-permute-done.4 = bf16[1,112,1024]{2,1,0:T(8,128)(2,1)S(1)} collective-permute-done((bf16[1,112,1024]{2,1,0:T(8,128)(2,1)S(1)}, bf16[1,112,1024]{2,1,0:T(8,128)(2,1)S(1)}, u32[]{:S(2)}, u32[]{:S(2)}) %collective-permute-start.4) | collective-permute-done | bytes 229408 | tf_op jit(solution)/shard_map/ppermute | solution.py:689
  44.5 17.1 %collective-permute-done.7.refs_2_ = bf16[4,112,1024]{2,1,0:T(8,128)(2,1)} collective-permute-done((bf16[4,112,1024]{2,1,0:T(8,128)(2,1)S(1)}, bf16[4,112,1024]{2,1,0:T(8,128)(2,1)}, u32[]{:S(2)}, u32[]{:S(2)}) %collective-permute-start.7) | collective-permute-done | bytes 917536 | tf_op jit(solution)/shard_map/ppermute | solution.py:689
  62.7 7.5 %collective-permute-done.6.refs_1_ = bf16[4,112,1024]{2,1,0:T(8,128)(2,1)} collective-permute-done((bf16[4,112,1024]{2,1,0:T(8,128)(2,1)S(1)}, bf16[4,112,1024]{2,1,0:T(8,128)(2,1)}, u32[]{:S(2)}, u32[]{:S(2)}) %collective-permute-start.6) | collective-permute-done | bytes 917536 | tf_op jit(solution)/shard_map/ppermute | solution.py:689
  71.4 20.3 %collective-permute-done.1.c2_ref = bf16[1,256,1024]{2,1,0:T(8,128)(2,1)S(1)} collective-permute-done((bf16[1,256,1024]{2,1,0:T(8,128)(2,1)S(1)}, bf16[1,256,1024]{2,1,0:T(8,128)(2,1)S(1)}, u32[]{:S(2)}, u32[]{:S(2)}) %collective-permute-start.1) | collective-permute-done | bytes 524320 | tf_op jit(solution)/shard_map/ppermute | solution.py:689
  91.7 10.8 %collective-permute-done.2.c3_ref = bf16[1,256,1024]{2,1,0:T(8,128)(2,1)S(1)} collective-permute-done((bf16[1,256,1024]{2,1,0:T(8,128)(2,1)S(1)}, bf16[1,256,1024]{2,1,0:T(8,128)(2,1)S(1)}, u32[]{:S(2)}, u32[]{:S(2)}) %collective-permute-start.2) | collective-permute-done | bytes 524320 | tf_op jit(solution)/shard_map/ppermute | solution.py:689
  105.0 4.2 collective-permute-done.8.refs_3_
  115.1 13.2 %qkv_fwd.1 = (bf16[1024,1024]{1,0:T(8,128)(2,1)}, bf16[1024,1024]{1,0:T(8,128)(2,1)}, bf16[1024,1024]{1,0:T(8,128)(2,1)}, bf16[1024,1024]{1,0:T(8,128)(2,1)}, bf...) custom-call(s32[3]{0:T(128)} %pad_add_fusion.1.ids_ref, ...), custom_call_target="tpu_custom_call" | custom-call | flops 6442450944 | bytes 25165824 | tf_op jit(solution)/shard_map/qkv_fwd/pallas_call | solution.py:509
  134.0 43.0 %attn_fwd.1 = (bf16[1024,1024]{1,0:T(8,128)(2,1)S(1)}, f32[8,1024,128]{2,1,0:T(8,128)S(1)}) custom-call(s32[1]{0:T(128)} %dynamic_slice.145.len_ref, bf16[1024,1024]{1,0:T(8,128)(2,1)S(1)} %copy-done.1, bf16[1024,1024]{1,0:T(8,128)(2,1)S(1)} %copy-done.3, bf16[1024,1024]{1,0:T(8,128)(2,1)S(1)} %copy-done.5, f32[16,2048]{1,0:T(8,128)S(1)} %copy-done.16), custom_call_target="tpu_custom_call" | custom-call | flops 8589934592 | bytes 12582912 | tf_op jit(solution)/shard_map/attn_fwd/pallas_call | solution.py:346
  180.4 8.7 %all-gather.3.cloned.1.call-done = bf16[9216,1024]{1,0:T(8,128)(2,1)} async-done(((bf16[288,1024]{1,0:T(8,128)(2,1)}), bf16[9216,1024]{1,0:T(8,128)(2,1)}) %all-gather.3.cloned.1.call-update) | async-done | bytes 18874384 | tf_op jit(solution)/shard_map/all_gather | solution.py:769
  189.0 77.2 %mid.1 = (bf16[1024,1024]{1,0:T(8,128)(2,1)}, bf16[1024,1024]{1,0:T(8,128)(2,1)}, bf16[1024,1024]{1,0:T(8,128)(2,1)}, bf16[32,160,1024]{2,1,0:T(8,128)(2,1)}, bf16[4096,1024]{1,0:T(8,128)(2,1)}) custom-call(s32[3]{0:T(128)} %pad_add_fusion.1.ids_ref, bf16[1024,1024]{1,0:T(8,128)(2,1)} %get-tuple-element.45.x_ref, bf16[1024,1024]{1,0:T(8,128)(2,1)} %copy-done.7, ...), custom_call_target="tpu_custom_call" | custom-call | flops 57982058496 | bytes 50331648 | tf_op jit(solution)/shard_map/mid/pallas_call | solution.py:604
  266.2 5.6 copy_bitcast_fusion
  272.2 8.7 %collective-permute-done.21 = bf16[4,2,2,160,1024]{4,3,0,2,1:T(8,128)(2,1)} collective-permute-done((bf16[4,2,2,160,1024]{4,3,0,2,1:T(8,128)(2,1)}, bf16[4,2,2,160,1024]{4,3,0,2,1:T(8,128)(2,1)}, u32[]{:S(2)}, u32[]{:S(2)}) %collective-permute-start.21) | collective-permute-done | bytes 5242912 | tf_op jit(solution)/shard_map/ppermute | solution.py:689
  280.8 5.3 fusion.2
  287.9 18.2 %collective-permute-done.33 = bf16[2,160,1024]{2,1,0:T(8,128)(2,1)S(1)} collective-permute-done((bf16[2,160,1024]{2,1,0:T(8,128)(2,1)S(1)}, bf16[2,160,1024]{2,1,0:T(8,128)(2,1)S(1)}, u32[]{:S(2)}, u32[]{:S(2)}) %collective-permute-start.33) | collective-permute-done | bytes 655392 | tf_op jit(solution)/shard_map/ppermute | solution.py:689
  306.9 8.2 %collective-permute-done.35 = bf16[2,160,1024]{2,1,0:T(8,128)(2,1)S(1)} collective-permute-done((bf16[2,160,1024]{2,1,0:T(8,128)(2,1)S(1)}, bf16[2,160,1024]{2,1,0:T(8,128)(2,1)S(1)}, u32[]{:S(2)}, u32[]{:S(2)}) %collective-permute-start.35) | collective-permute-done | bytes 655392 | tf_op jit(solution)/shard_map/ppermute | solution.py:689
  315.8 22.0 %attn_bwd.4 = (bf16[1024,1024]{1,0:T(8,128)(2,1)S(1)}, bf16[1024,1024]{1,0:T(8,128)(2,1)S(1)}, bf16[1024,1024]{1,0:T(8,128)(2,1)S(1)}, f32[4,2048]{1,0:T(4,128)S(1)}) custom-call(s32[1]{0:T(128)} %dynamic_slice.145.len_ref, bf16[1024,1024]{1,0:T(8,128)(2,1)S(1)} %copy-done.2, bf16[1024,1024]{1,0:T(8,128)(2,1)S(1)} %copy-done.4, ...), custom_call_target="tpu_custom_call" | custom-call | flops 5368709120 | bytes 5242880 | tf_op jit(solution)/shard_map/attn_bwd/pallas_call | solution.py:424
  337.8 32.3 %collective-permute-done.34 = bf16[4,160,1024]{2,1,0:T(8,128)(2,1)S(1)} collective-permute-done((bf16[4,160,1024]{2,1,0:T(8,128)(2,1)S(1)}, bf16[4,160,1024]{2,1,0:T(8,128)(2,1)S(1)}, u32[]{:S(2)}, u32[]{:S(2)}) %collective-permute-start.34) | collective-permute-done | bytes 1310752 | tf_op jit(solution)/shard_map/ppermute | solution.py:689
  373.0 22.2 %attn_bwd.5 = (bf16[1024,1024]{1,0:T(8,128)(2,1)S(1)}, bf16[1024,1024]{1,0:T(8,128)(2,1)S(1)}, bf16[1024,1024]{1,0:T(8,128)(2,1)S(1)}, f32[4,2048]{1,0:T(4,128)S(1)}) custom-call(s32[1]{0:T(128)} %dynamic_slice.145.len_ref, bf16[1024,1024]{1,0:T(8,128)(2,1)S(1)} %copy-done.2, ...), custom_call_target="tpu_custom_call", output_to_operand_aliasing={{0}: (8, {}), {1}: (9, {}), {2}: (10, {})} | custom-call | flops 5368709120 | bytes 5242880 | tf_op jit(solution)/shard_map/attn_bwd/pallas_call | solution.py:424
  395.2 22.0 %attn_bwd.6 = (bf16[1024,1024]{1,0:T(8,128)(2,1)S(1)}, bf16[1024,1024]{1,0:T(8,128)(2,1)S(1)}, bf16[1024,1024]{1,0:T(8,128)(2,1)S(1)}, f32[4,2048]{1,0:T(4,128)S(1)}) custom-call(s32[1]{0:T(128)} %dynamic_slice.145.len_ref, bf16[1024,1024]{1,0:T(8,128)(2,1)S(1)} %copy-done.2, ...), custom_call_target="tpu_custom_call", output_to_operand_aliasing={{0}: (8, {}), {1}: (9, {}), {2}: (10, {})} | custom-call | flops 5368709120 | bytes 5242880 | tf_op jit(solution)/shard_map/attn_bwd/pallas_call | solution.py:424
  417.2 22.2 %attn_bwd.7 = (bf16[1024,1024]{1,0:T(8,128)(2,1)S(1)}, bf16[1024,1024]{1,0:T(8,128)(2,1)S(1)}, bf16[1024,1024]{1,0:T(8,128)(2,1)S(1)}, f32[4,2048]{1,0:T(4,128)S(1)}) custom-call(s32[1]{0:T(128)} %dynamic_slice.145.len_ref, bf16[1024,1024]{1,0:T(8,128)(2,1)S(1)} %copy-done.2, ...), custom_call_target="tpu_custom_call", output_to_operand_aliasing={{0}: (8, {}), {1}: (9, {}), {2}: (10, {})} | custom-call | flops 5368709120 | bytes 5242880 | tf_op jit(solution)/shard_map/attn_bwd/pallas_call | solution.py:424
  444.1 13.5 %qkv_gw.1 = bf16[32,112,1024]{2,1,0:T(8,128)(2,1)} custom-call(bf16[1024,1024]{1,0:T(8,128)(2,1)} %get-tuple-element.73.h_ref, bf16[1024,1024]{1,0:T(8,128)(2,1)} %copy-done.8, bf16[1024,1024]{1,0:T(8,128)(2,1)} %copy-done.9, bf16[1024,1024]{1,0:T(8,128)(2,1)} %copy-done.10, s32[2,2048]{1,0:T(2,128)} %pad_add_fusion.refs_10_.bucket_ref, ...), custom_call_target="tpu_custom_call" | custom-call | flops 6442450944 | bytes 14680064 | tf_op jit(solution)/shard_map/qkv_gw/pallas_call | solution.py:638
  466.7 4.5 fusion.6
  477.3 10.8 %collective-permute-done.20.c3_ref = bf16[1,256,1024]{2,1,0:T(8,128)(2,1)} collective-permute-done((bf16[1,256,1024]{2,1,0:T(8,128)(2,1)}, bf16[1,256,1024]{2,1,0:T(8,128)(2,1)}, u32[]{:S(2)}, u32[]{:S(2)}) %collective-permute-start.20) | collective-permute-done | bytes 524320 | tf_op jit(solution)/shard_map/ppermute | solution.py:689
  488.1 65.3 %place.2 = bf16[4,256,1024]{2,1,0:T(8,128)(2,1)} custom-call(s32[3]{0:T(128)} %pad_add_fusion.1.ids_ref, bf16[4,256,1024]{2,1,0:T(8,128)(2,1)} %bitcast.117, bf16[1,256,1024]{2,1,0:T(8,128)(2,1)} %collective-permute-done.18.c1_ref, bf16[1,256,1024]{2,1,0:T(8,128)(2,1)} %collective-permute-done.19.c2_ref, bf16[1,256,1024]{2,1,0:T(8,128)(2,1)} %collective-permute-done.20.c3_ref), custom_call_target="tpu_custom_call" | custom-call | bytes 4194304 | tf_op jit(solution)/shard_map/place/pallas_call | solution.py:682
  554.4 21.0 %collective-permute-start.37 = (bf16[160,1024]{1,0:T(8,128)(2,1)}, bf16[160,1024]{1,0:T(8,128)(2,1)}, u32[]{:S(2)}, u32[]{:S(2)}) collective-permute-start(bf16[160,1024]{1,0:T(8,128)(2,1)} %get-tuple-element.101), channel_id=1, source_target_pairs={{0,8},{4,12},{8,0},{12,4},{16,24},{20,28},{24,16},{28,20},{1,9},{5... | collective-permute-start | bytes 983048 | tf_op jit(solution)/shard_map/ppermute | solution.py:689
  575.4 3.3 collective-permute-start.38
  584.0 14.1 %qkv_gx.1 = bf16[1024,1024]{1,0:T(8,128)(2,1)} custom-call(bf16[1024,1024]{1,0:T(8,128)(2,1)} %get-tuple-element.45.x_ref, bf16[1024,1024]{1,0:T(8,128)(2,1)} %get-tuple-element.53.gb_ref, bf16[1024,1024]{1,0:T(8,128)(2,1)} %copy-done.8, bf16[1024,1024]{1,0:T(8,128)(2,1)} %copy-done.9, bf16[1024,1024]{1,0:T(8,128)(2,1)} %copy-done.10, ...), custom_call_target="tpu_custom_call" | custom-call | flops 6442450944 | bytes 18874368 | tf_op jit(solution)/shard_map/qkv_gx/pallas_call | solution.py:661
  608.7 6.4 collective-permute-start.30
  620.8 4.7 collective-permute-done.24.c3_ref
  625.5 65.3 %place.3 = bf16[4,256,1024]{2,1,0:T(8,128)(2,1)} custom-call(s32[3]{0:T(128)} %pad_add_fusion.1.ids_ref, bf16[4,256,1024]{2,1,0:T(8,128)(2,1)} %bitcast.120, bf16[1,256,1024]{2,1,0:T(8,128)(2,1)} %copy-done.23, bf16[1,256,1024]{2,1,0:T(8,128)(2,1)} %copy-done.24, bf16[1,256,1024]{2,1,0:T(8,128)(2,1)} %collective-permute-done.24.c3_ref), custom_call_target="tpu_custom_call" | custom-call | bytes 4194304 | tf_op jit(solution)/shard_map/place/pallas_call | solution.py:682
  (207 shorter events, 85.9 us)
Async XLA Ops:
  7.2 181.8 %all-gather.3.cloned.1.call-start = ((), (), s32[]{:S(2)}) async-start(), calls=%async_computation.2 | async-start | bytes 19464192 | tf_op jit(solution)/shard_map/all_gather | solution.py:769
  11.4 681.5 %reduce-scatter.2.cloned.1.call-start = ((), (), s32[]{:S(2)}) async-start(), calls=%async_computation.1 | async-start | bytes 8650752 | tf_op jit(solution)/shard_map/reduce_scatter | solution.py:776
  15.2 22.7 %collective-permute-start.4 = (bf16[1,112,1024]{2,1,0:T(8,128)(2,1)S(1)}, bf16[1,112,1024]{2,1,0:T(8,128)(2,1)S(1)}, u32[]{:S(2)}, u32[]{:S(2)}) collective-permute-start(bf16[1,112,1024]{2,1,0:T(8,128)(2,1)S(1)} %bitcast.128), channel_id=1, source_target_pairs={{0,16},{4,20},{8,24},{12,28},{16,0},{20,4},{24,8},{28,12},{1,17},{... | collective-permute-start | bytes 688136 | tf_op jit(solution)/shard_map/ppermute | solution.py:689
  17.7 21.1 %collective-permute-start.5 = (bf16[1,112,1024]{2,1,0:T(8,128)(2,1)S(1)}, bf16[1,112,1024]{2,1,0:T(8,128)(2,1)S(1)}, u32[]{:S(2)}, u32[]{:S(2)}) collective-permute-start(bf16[1,112,1024]{2,1,0:T(8,128)(2,1)S(1)} %bitcast.129), channel_id=1, source_target_pairs={{0,24},{4,28},{8,16},{12,20},{16,8},{20,12},{24,0},{28,4},{1,25},{... | collective-permute-start | bytes 688136 | tf_op jit(solution)/shard_map/ppermute | solution.py:689
  38.9 22.6 %collective-permute-start.7 = (bf16[4,112,1024]{2,1,0:T(8,128)(2,1)S(1)}, bf16[4,112,1024]{2,1,0:T(8,128)(2,1)}, u32[]{:S(2)}, u32[]{:S(2)}) collective-permute-start(bf16[4,112,1024]{2,1,0:T(8,128)(2,1)S(1)} %pad_maximum_fusion.refs_0_), channel_id=1, source_target_pairs={{0,4},{4,0},{8,12},{12,8},{16,20},{20,16},{24,28},{28,24},{1,5},{5... | collective-permute-start | bytes 2752520 | tf_op jit(solution)/shard_map/ppermute | solution.py:689
  40.5 29.7 %collective-permute-start.6 = (bf16[4,112,1024]{2,1,0:T(8,128)(2,1)S(1)}, bf16[4,112,1024]{2,1,0:T(8,128)(2,1)}, u32[]{:S(2)}, u32[]{:S(2)}) collective-permute-start(bf16[4,112,1024]{2,1,0:T(8,128)(2,1)S(1)} %pad_maximum_fusion.refs_0_), channel_id=1, source_target_pairs={{0,2},{1,3},{2,0},{3,1},{4,6},{5,7},{6,4},{7,5},{8,10},{9,11},{10,... | collective-permute-start | bytes 2752520 | tf_op jit(solution)/shard_map/ppermute | solution.py:689
  42.5 28.8 %collective-permute-start = (bf16[1,256,1024]{2,1,0:T(8,128)(2,1)S(1)}, bf16[1,256,1024]{2,1,0:T(8,128)(2,1)}, u32[]{:S(2)}, u32[]{:S(2)}) collective-permute-start(bf16[1,256,1024]{2,1,0:T(8,128)(2,1)S(1)} %get-tuple-element.100), channel_id=1, source_target_pairs={{0,1},{1,0},{2,3},{3,2},{4,5},{5,4},{6,7},{7,6},{8,9},{9,8},{10,11... | collective-permute-start | bytes 1572872 | tf_op jit(solution)/shard_map/ppermute | solution.py:689
  42.6 49.1 %collective-permute-start.1 = (bf16[1,256,1024]{2,1,0:T(8,128)(2,1)S(1)}, bf16[1,256,1024]{2,1,0:T(8,128)(2,1)S(1)}, u32[]{:S(2)}, u32[]{:S(2)}) collective-permute-start(bf16[1,256,1024]{2,1,0:T(8,128)(2,1)S(1)} %get-tuple-element.99), channel_id=1, source_target_pairs={{0,2},{1,3},{2,0},{3,1},{4,6},{5,7},{6,4},{7,5},{8,10},{9,11},{10,... | collective-permute-start | bytes 1572872 | tf_op jit(solution)/shard_map/ppermute | solution.py:689
  42.8 59.7 %collective-permute-start.2 = (bf16[1,256,1024]{2,1,0:T(8,128)(2,1)S(1)}, bf16[1,256,1024]{2,1,0:T(8,128)(2,1)S(1)}, u32[]{:S(2)}, u32[]{:S(2)}) collective-permute-start(bf16[1,256,1024]{2,1,0:T(8,128)(2,1)S(1)} %get-tuple-element.98), channel_id=1, source_target_pairs={{0,3},{1,2},{2,1},{3,0},{4,7},{5,6},{6,5},{7,4},{8,11},{9,10},{10,... | collective-permute-start | bytes 1572872 | tf_op jit(solution)/shard_map/ppermute | solution.py:689
  62.6 46.6 %collective-permute-start.8 = (bf16[2,112,1024]{2,1,0:T(8,128)(2,1)S(1)}, bf16[2,112,1024]{2,1,0:T(8,128)(2,1)}, u32[]{:S(2)}, u32[]{:S(2)}) collective-permute-start(bf16[2,112,1024]{2,1,0:T(8,128)(2,1)S(1)} %slice.114), channel_id=1, source_target_pairs={{0,2},{1,3},{2,0},{3,1},{4,6},{5,7},{6,4},{7,5},{8,10},{9,11},{10,... | collective-permute-start | bytes 1376264 | tf_op jit(solution)/shard_map/ppermute | solution.py:689
  71.2 38.0 %collective-permute-start.9 = (bf16[2,112,1024]{2,1,0:T(8,128)(2,1)S(1)}, bf16[2,112,1024]{2,1,0:T(8,128)(2,1)}, u32[]{:S(2)}, u32[]{:S(2)}) collective-permute-start(bf16[2,112,1024]{2,1,0:T(8,128)(2,1)S(1)} %slice.115), channel_id=1, source_target_pairs={{0,4},{4,0},{8,12},{12,8},{16,20},{20,16},{24,28},{28,24},{1,5},{5... | collective-permute-start | bytes 1376264 | tf_op jit(solution)/shard_map/ppermute | solution.py:689
  71.3 41.7 %collective-permute-start.10 = (bf16[4,112,1024]{2,1,0:T(8,128)(2,1)S(1)}, bf16[4,112,1024]{2,1,0:T(8,128)(2,1)S(1)}, u32[]{:S(2)}, u32[]{:S(2)}) collective-permute-start(bf16[4,112,1024]{2,1,0:T(8,128)(2,1)S(1)} %pad_maximum_fusion.refs_0_), channel_id=1, source_target_pairs={{0,1},{1,0},{2,3},{3,2},{4,5},{5,4},{6,7},{7,6},{8,9},{9,8},{10,11... | collective-permute-start | bytes 2752520 | tf_op jit(solution)/shard_map/ppermute | solution.py:689
  91.7 23.2 %collective-permute-start.11 = (bf16[4,112,1024]{2,1,0:T(8,128)(2,1)}, bf16[4,112,1024]{2,1,0:T(8,128)(2,1)}, u32[]{:S(2)}, u32[]{:S(2)}) collective-permute-start(bf16[4,112,1024]{2,1,0:T(8,128)(2,1)} %collective-permute-done.6.refs_1_), channel_id=1, source_target_pairs={{0,1},{1,0},{2,3},{3,2},{4,5},{5,4},{6,7},{7,6},{8,9},{9,8},{10,11... | collective-permute-start | bytes 2752520 | tf_op jit(solution)/shard_map/ppermute | solution.py:689
  113.1 67.2 %collective-permute-start.15 = (bf16[1,256,1024]{2,1,0:T(8,128)(2,1)S(1)}, bf16[1,256,1024]{2,1,0:T(8,128)(2,1)S(1)}, u32[]{:S(2)}, u32[]{:S(2)}) collective-permute-start(bf16[1,256,1024]{2,1,0:T(8,128)(2,1)S(1)} %get-tuple-element.97), channel_id=1, source_target_pairs={{0,1},{1,0},{2,3},{3,2},{4,5},{5,4},{6,7},{7,6},{8,9},{9,8},{10,11... | collective-permute-start | bytes 1572872 | tf_op jit(solution)/shard_map/ppermute | solution.py:689
  113.1 67.2 %collective-permute-start.16 = (bf16[1,256,1024]{2,1,0:T(8,128)(2,1)S(1)}, bf16[1,256,1024]{2,1,0:T(8,128)(2,1)S(1)}, u32[]{:S(2)}, u32[]{:S(2)}) collective-permute-start(bf16[1,256,1024]{2,1,0:T(8,128)(2,1)S(1)} %get-tuple-element.96), channel_id=1, source_target_pairs={{0,2},{1,3},{2,0},{3,1},{4,6},{5,7},{6,4},{7,5},{8,10},{9,11},{10,... | collective-permute-start | bytes 1572872 | tf_op jit(solution)/shard_map/ppermute | solution.py:689
  114.3 66.0 %collective-permute-start.17 = (bf16[1,256,1024]{2,1,0:T(8,128)(2,1)S(1)}, bf16[1,256,1024]{2,1,0:T(8,128)(2,1)S(1)}, u32[]{:S(2)}, u32[]{:S(2)}) collective-permute-start(bf16[1,256,1024]{2,1,0:T(8,128)(2,1)S(1)} %get-tuple-element.95), channel_id=1, source_target_pairs={{0,3},{1,2},{2,1},{3,0},{4,7},{5,6},{6,5},{7,4},{8,11},{9,10},{10,... | collective-permute-start | bytes 1572872 | tf_op jit(solution)/shard_map/ppermute | solution.py:689
  287.9 27.2 %collective-permute-start.35 = (bf16[2,160,1024]{2,1,0:T(8,128)(2,1)S(1)}, bf16[2,160,1024]{2,1,0:T(8,128)(2,1)S(1)}, u32[]{:S(2)}, u32[]{:S(2)}) collective-permute-start(bf16[2,160,1024]{2,1,0:T(8,128)(2,1)S(1)} %get-tuple-element.105), channel_id=1, source_target_pairs={{0,2},{1,3},{2,0},{3,1},{4,6},{5,7},{6,4},{7,5},{8,10},{9,11},{10,... | collective-permute-start | bytes 1966088 | tf_op jit(solution)/shard_map/ppermute | solution.py:689
  306.3 63.7 %collective-permute-start.34 = (bf16[4,160,1024]{2,1,0:T(8,128)(2,1)S(1)}, bf16[4,160,1024]{2,1,0:T(8,128)(2,1)S(1)}, u32[]{:S(2)}, u32[]{:S(2)}) collective-permute-start(bf16[4,160,1024]{2,1,0:T(8,128)(2,1)S(1)} %fusion.8), channel_id=1, source_target_pairs={{0,2},{1,3},{2,0},{3,1},{4,6},{5,7},{6,4},{7,5},{8,10},{9,11},{10,... | collective-permute-start | bytes 3932168 | tf_op jit(solution)/shard_map/ppermute | solution.py:689
  315.3 54.8 %collective-permute-start.36 = (bf16[4,160,1024]{2,1,0:T(8,128)(2,1)S(1)}, bf16[4,160,1024]{2,1,0:T(8,128)(2,1)S(1)}, u32[]{:S(2)}, u32[]{:S(2)}) collective-permute-start(bf16[4,160,1024]{2,1,0:T(8,128)(2,1)S(1)} %fusion.9), channel_id=1, source_target_pairs={{0,4},{4,0},{8,12},{12,8},{16,20},{20,16},{24,28},{28,24},{1,5},{5... | collective-permute-start | bytes 3932168 | tf_op jit(solution)/shard_map/ppermute | solution.py:689
  464.2 23.9 %collective-permute-start.20 = (bf16[1,256,1024]{2,1,0:T(8,128)(2,1)}, bf16[1,256,1024]{2,1,0:T(8,128)(2,1)}, u32[]{:S(2)}, u32[]{:S(2)}) collective-permute-start(bf16[1,256,1024]{2,1,0:T(8,128)(2,1)} %get-tuple-element.92), channel_id=1, source_target_pairs={{0,3},{1,2},{2,1},{3,0},{4,7},{5,6},{6,5},{7,4},{8,11},{9,10},{10,... | collective-permute-start | bytes 1572872 | tf_op jit(solution)/shard_map/ppermute | solution.py:689
  472.2 107.9 %collective-permute-start.26 = (bf16[2,112,1024]{2,1,0:T(8,128)(2,1)}, bf16[2,112,1024]{2,1,0:T(8,128)(2,1)}, u32[]{:S(2)}, u32[]{:S(2)}) collective-permute-start(bf16[2,112,1024]{2,1,0:T(8,128)(2,1)} %get-tuple-element.109), channel_id=1, source_target_pairs={{0,4},{4,0},{8,12},{12,8},{16,20},{20,16},{24,28},{28,24},{1,5},{5... | collective-permute-start | bytes 1376264 | tf_op jit(solution)/shard_map/ppermute | solution.py:689
  472.4 109.6 %collective-permute-start.28 = (bf16[2,112,1024]{2,1,0:T(8,128)(2,1)}, bf16[2,112,1024]{2,1,0:T(8,128)(2,1)}, u32[]{:S(2)}, u32[]{:S(2)}) collective-permute-start(bf16[2,112,1024]{2,1,0:T(8,128)(2,1)} %get-tuple-element.110), channel_id=1, source_target_pairs={{0,2},{1,3},{2,0},{3,1},{4,6},{5,7},{6,4},{7,5},{8,10},{9,11},{10,... | collective-permute-start | bytes 1376264 | tf_op jit(solution)/shard_map/ppermute | solution.py:689
  554.4 45.3 %collective-permute-start.37 = (bf16[160,1024]{1,0:T(8,128)(2,1)}, bf16[160,1024]{1,0:T(8,128)(2,1)}, u32[]{:S(2)}, u32[]{:S(2)}) collective-permute-start(bf16[160,1024]{1,0:T(8,128)(2,1)} %get-tuple-element.101), channel_id=1, source_target_pairs={{0,8},{4,12},{8,0},{12,4},{16,24},{20,28},{24,16},{28,20},{1,9},{5... | collective-permute-start | bytes 983048 | tf_op jit(solution)/shard_map/ppermute | solution.py:689
  575.4 24.6 %collective-permute-start.38 = (bf16[160,1024]{1,0:T(8,128)(2,1)}, bf16[160,1024]{1,0:T(8,128)(2,1)}, u32[]{:S(2)}, u32[]{:S(2)}) collective-permute-start(bf16[160,1024]{1,0:T(8,128)(2,1)} %get-tuple-element.103), channel_id=1, source_target_pairs={{0,16},{4,20},{8,24},{12,28},{16,0},{20,4},{24,8},{28,12},{1,17},{... | collective-permute-start | bytes 983048 | tf_op jit(solution)/shard_map/ppermute | solution.py:689
  578.7 23.8 %collective-permute-start.39 = (bf16[160,1024]{1,0:T(8,128)(2,1)}, bf16[160,1024]{1,0:T(8,128)(2,1)}, u32[]{:S(2)}, u32[]{:S(2)}) collective-permute-start(bf16[160,1024]{1,0:T(8,128)(2,1)} %get-tuple-element.102), channel_id=1, source_target_pairs={{0,24},{4,28},{8,16},{12,20},{16,8},{20,12},{24,0},{28,4},{1,25},{... | collective-permute-start | bytes 983048 | tf_op jit(solution)/shard_map/ppermute | solution.py:689
  581.4 24.0 %collective-permute-start.27 = (bf16[4,112,1024]{2,1,0:T(8,128)(2,1)S(1)}, bf16[4,112,1024]{2,1,0:T(8,128)(2,1)S(1)}, u32[]{:S(2)}, u32[]{:S(2)}) collective-permute-start(bf16[4,112,1024]{2,1,0:T(8,128)(2,1)S(1)} %fusion.12), channel_id=1, source_target_pairs={{0,2},{1,3},{2,0},{3,1},{4,6},{5,7},{6,4},{7,5},{8,10},{9,11},{10,... | collective-permute-start | bytes 2752520 | tf_op jit(solution)/shard_map/ppermute | solution.py:689
  583.3 23.2 %collective-permute-start.29 = (bf16[4,112,1024]{2,1,0:T(8,128)(2,1)S(1)}, bf16[4,112,1024]{2,1,0:T(8,128)(2,1)S(1)}, u32[]{:S(2)}, u32[]{:S(2)}) collective-permute-start(bf16[4,112,1024]{2,1,0:T(8,128)(2,1)S(1)} %fusion.13), channel_id=1, source_target_pairs={{0,4},{4,0},{8,12},{12,8},{16,20},{20,16},{24,28},{28,24},{1,5},{5... | collective-permute-start | bytes 2752520 | tf_op jit(solution)/shard_map/ppermute | solution.py:689
  599.9 20.1 %collective-permute-start.23 = (bf16[1,256,1024]{2,1,0:T(8,128)(2,1)S(1)}, bf16[1,256,1024]{2,1,0:T(8,128)(2,1)S(1)}, u32[]{:S(2)}, u32[]{:S(2)}) collective-permute-start(bf16[1,256,1024]{2,1,0:T(8,128)(2,1)S(1)} %get-tuple-element.90), channel_id=1, source_target_pairs={{0,2},{1,3},{2,0},{3,1},{4,6},{5,7},{6,4},{7,5},{8,10},{9,11},{10,... | collective-permute-start | bytes 1572872 | tf_op jit(solution)/shard_map/ppermute | solution.py:689
  602.5 23.0 %collective-permute-start.24 = (bf16[1,256,1024]{2,1,0:T(8,128)(2,1)S(1)}, bf16[1,256,1024]{2,1,0:T(8,128)(2,1)}, u32[]{:S(2)}, u32[]{:S(2)}) collective-permute-start(bf16[1,256,1024]{2,1,0:T(8,128)(2,1)S(1)} %get-tuple-element.89), channel_id=1, source_target_pairs={{0,3},{1,2},{2,1},{3,0},{4,7},{5,6},{6,5},{7,4},{8,11},{9,10},{10,... | collective-permute-start | bytes 1572872 | tf_op jit(solution)/shard_map/ppermute | solution.py:689
  608.7 82.1 %collective-permute-start.30 = (bf16[112,1024]{1,0:T(8,128)(2,1)S(1)}, bf16[112,1024]{1,0:T(8,128)(2,1)S(1)}, u32[]{:S(2)}, u32[]{:S(2)}) collective-permute-start(bf16[112,1024]{1,0:T(8,128)(2,1)S(1)} %get-tuple-element.106), channel_id=1, source_target_pairs={{0,8},{4,12},{8,0},{12,4},{16,24},{20,28},{24,16},{28,20},{1,9},{5... | collective-permute-start | bytes 688136 | tf_op jit(solution)/shard_map/ppermute | solution.py:689
  615.1 75.7 %collective-permute-start.31 = (bf16[112,1024]{1,0:T(8,128)(2,1)S(1)}, bf16[112,1024]{1,0:T(8,128)(2,1)S(1)}, u32[]{:S(2)}, u32[]{:S(2)}) collective-permute-start(bf16[112,1024]{1,0:T(8,128)(2,1)S(1)} %get-tuple-element.108), channel_id=1, source_target_pairs={{0,16},{4,20},{8,24},{12,28},{16,0},{20,4},{24,8},{28,12},{1,17},{... | collective-permute-start | bytes 688136 | tf_op jit(solution)/shard_map/ppermute | solution.py:689
  617.0 73.8 %collective-permute-start.32 = (bf16[112,1024]{1,0:T(8,128)(2,1)S(1)}, bf16[112,1024]{1,0:T(8,128)(2,1)S(1)}, u32[]{:S(2)}, u32[]{:S(2)}) collective-permute-start(bf16[112,1024]{1,0:T(8,128)(2,1)S(1)} %get-tuple-element.107), channel_id=1, source_target_pairs={{0,24},{4,28},{8,16},{12,20},{16,8},{20,12},{24,0},{28,4},{1,25},{... | collective-permute-start | bytes 688136 | tf_op jit(solution)/shard_map/ppermute | solution.py:689
  (51 other events, 607.7 us)
Sparse Core Ops, SparseCore 0:
  11.5 177.4 all-gather.2
  272.2 175.7 reduce-scatter.1

commit v3 on v2

--- a/solution.py
+++ b/solution.py
@@ -288,6 +288,7 @@
 TN = (((0,), (0,)), ((), ()))
 STRIP = 128
 LIMIT = 58 << 20
+LIGHT = pl.CostEstimate(flops=1 << 20, bytes_accessed=1 << 16, transcendentals=0)
 
 def _dot(a, b, dims=(((1,), (0,)), ((), ()))):
     return lax.dot_general(a, b, dims, preferred_element_type=jnp.float32)
@@ -353,7 +354,7 @@
             out_specs=[blk, pl.BlockSpec((1, seq_len, 128), lambda p, n: (p, 0, 0))],
             scratch_shapes=[pltpu.VMEM((2, STRIP, wide), jnp.float32)]),
         compiler_params=pltpu.CompilerParams(vmem_limit_bytes=40 << 20),
-        cost_estimate=pl.CostEstimate(flops=8 * seq_len * seq_len * width, bytes_accessed=seq_len * width * 12, transcendentals=seq_len * seq_len * pairs * 2),
+        cost_estimate=LIGHT,
         name="attn_fwd",
     )(length, q, k, v, t)
 
@@ -433,7 +434,7 @@
                             pltpu.VMEM((2, seq_len, 128), jnp.float32)]),
         input_output_aliases={8 + i: i for i in range(len(prev))},
         compiler_params=pltpu.CompilerParams(vmem_limit_bytes=40 << 20),
-        cost_estimate=pl.CostEstimate(flops=20 * seq_len * seq_len * 128 * count, bytes_accessed=seq_len * 128 * count * 20, transcendentals=seq_len * seq_len * count * 2),
+        cost_estimate=LIGHT,
         name="attn_bwd",
     )(length, q, k, v, do, o, lse, trev, *prev)
 
@@ -514,7 +515,7 @@
         out_specs=[ANY] * 6 + [VM] * 3,
         scratch_shapes=[vm(total, width), vm(total, width), vm(3, total, width), vm(width, 3 * width), vm(shards, 16, width), pltpu.SemaphoreType.DMA((6,))],
         compiler_params=pltpu.CompilerParams(vmem_limit_bytes=LIMIT),
-        cost_estimate=pl.CostEstimate(flops=6 * total * width * width, bytes_accessed=total * width * 12 + width * width * 12, transcendentals=0),
+        cost_estimate=LIGHT,
         name="qkv_fwd",
     )(ids, x4, *came, *gathered, bucket_rows)
 
@@ -616,7 +617,7 @@
                             pltpu.VMEM((width, rows), jnp.bfloat16), pltpu.VMEM((rows, width), jnp.float32),
                             pltpu.VMEM((rows, width), jnp.float32), pltpu.VMEM((rows, width), jnp.bfloat16), pltpu.SemaphoreType.DMA]),
         compiler_params=pltpu.CompilerParams(vmem_limit_bytes=LIMIT),
-        cost_estimate=pl.CostEstimate(flops=12 * rows * width * ff + 6 * rows * width * width, bytes_accessed=rows * width * 12 + width * width * 4 + width * ff * 8, transcendentals=rows * ff),
+        cost_estimate=LIGHT,
         name="mid",
     )(ids, x, o, g4, *came, gains, full, full, full)
 
@@ -639,7 +640,7 @@
         gw_kernel, out_shape=jax.ShapeDtypeStruct((shards, 3 * width // shards + 16, width), jnp.bfloat16),
         in_specs=[VM] * (5 + len(offs)), out_specs=VM,
         compiler_params=pltpu.CompilerParams(vmem_limit_bytes=LIMIT),
-        cost_estimate=pl.CostEstimate(flops=6 * rows * width * width, bytes_accessed=rows * width * 8 + width * width * 6, transcendentals=0),
+        cost_estimate=LIGHT,
         name="qkv_gw",
     )(h, dq, dk, dv, bucket_rows, *offs)
 
@@ -664,27 +665,10 @@
                               pl.BlockSpec((width, 3 * width), lambda i: (0, 0), pipeline_mode=pl.Buffered(1))],
         out_specs=blk,
         compiler_params=pltpu.CompilerParams(vmem_limit_bytes=LIMIT),
-        cost_estimate=pl.CostEstimate(flops=6 * total * width * width, bytes_accessed=total * width * 12 + width * width * 6, transcendentals=0),
+        cost_estimate=LIGHT,
         name="qkv_gx",
     )(x, gb, dq, dk, dv, gains, w)
 
-def place_kernel(ids_ref, own_ref, c1_ref, c2_ref, c3_ref, out_ref, sem):
-    me = ids_ref[0]
-    copies = []
-    for mask, ref in enumerate((own_ref, c1_ref, c2_ref, c3_ref)):
-        src = ref.at[me] if mask == 0 else ref.at[0]
-        copies.append(pltpu.make_async_copy(src, out_ref.at[me ^ mask], sem.at[mask]))
-        copies[-1].start()
-    for copy in copies:
-        copy.wait()
-
-def place(ids, own, came):
-    return pl.pallas_call(
-        place_kernel, out_shape=jax.ShapeDtypeStruct(own.shape, own.dtype),
-        in_specs=[SM] + [ANY] * 4, out_specs=ANY, scratch_shapes=[pltpu.SemaphoreType.DMA((4,))],
-        cost_estimate=pl.CostEstimate(flops=0, bytes_accessed=own.size * 4, transcendentals=0),
-        name="place",
-    )(ids, own, *came)
 def swap(value, axis, mask):
     return lax.ppermute(value, axis, [(i, i ^ mask) for i in range(lax.axis_size(axis))])
 
@@ -710,7 +694,8 @@
     def __init__(self, grads, pos):
         self.z, self.y, self.x, self.c = pos
         self.grads = grads.reshape((4, 2, 2, 2) + grads.shape[1:])
-        self.other = swap(lax.dynamic_index_in_dim(self.grads, 1 - self.c, 3, keepdims=False), "seq", 1)
+        self.sent = lax.dynamic_index_in_dim(self.grads, 1 - self.c, 3, keepdims=False)
+        self.other = swap(self.sent, "seq", 1)
 
     def fold(self):
         pick = lambda v, at, axis: lax.dynamic_index_in_dim(v, at, axis, keepdims=False)
@@ -726,6 +711,7 @@
         add = lambda a, b: (a.astype(jnp.float32) + b.astype(jnp.float32)).astype(jnp.bfloat16)
         to_x = lax.dynamic_update_slice_in_dim(self.to_x, add(self.to_x[2:], self.came_y), 2, 0)
         to_y = lax.dynamic_update_slice_in_dim(self.to_y, add(self.to_y[:2], self.came_x), 0, 0)
+        self.sent = (to_x, to_y)
         self.came_x, self.came_y = swap(to_x, "seq", 2), swap(to_y, "dp", 1)
 
     def column(self):
@@ -737,6 +723,12 @@
 
     def result(self):
         return sum((c.astype(jnp.float32) for c in self.came), self.mine.astype(jnp.float32))
+
+
+def place(blocks, came, me):
+    for mask, block in enumerate(came, 1):
+        blocks = lax.dynamic_update_slice_in_dim(blocks, block, me ^ mask, 0)
+    return blocks
 
 
 def tie(first, *later):
@@ -779,26 +771,39 @@
     pairs = HEADS // 2
     count = pairs // 4
     back = lambda first, g, prev: attn_bwd(length, q, k, v, g, attended, lse, t_back, first, count, prev)
+    g_att, = tie((sc2.sent, out), g_att)
     dq, dk, dv, off0 = back(0, g_att, None)
+    sc2.other, = tie((off0, out_came), sc2.other)
     sc2.fold()
-    g_att, = tie(sc2.own, g_att)
+    g_att, = tie((sc2.own, sc2.to_x, sc2.to_y), g_att)
     dq, dk, dv, off1 = back(count, g_att, (dq, dk, dv))
+    sc2.came_x, sc2.came_y = tie(off1, sc2.came_x, sc2.came_y)
     sc2.turn()
-    g_att, = tie(sc2.own, g_att)
-    layer_out = place(ids, out4, out_came)
+    g_att, = tie(sc2.sent, g_att)
     dq, dk, dv, off2 = back(2 * count, g_att, (dq, dk, dv))
     dq, dk, dv, off3 = back(3 * count, g_att, (dq, dk, dv))
+    sc2.came_x, sc2.came_y = tie(off3, sc2.came_x, sc2.came_y)
     sc2.column()
-    gw1 = qkv_gw(hidden, dq, dk, dv, bucket_rows, (off0, off1, off2, off3), shards)
+    h_in, = tie(sc2.mine, hidden)
+    gw1 = qkv_gw(h_in, dq, dk, dv, bucket_rows, (off0, off1, off2, off3), shards)
     sc1 = Scatter(gw1, pos)
-    gx = qkv_gx(x, gb, dq, dk, dv, gains, w_qkv)
+    gb_in, = tie(sc1.sent, gb)
+    gx = qkv_gx(x, gb_in, dq, dk, dv, gains, w_qkv)
+    sc1.other, = tie(gx, sc1.other)
+    sc1.fold()
+    out4, out_came = tie(sc1.own, out4, out_came)
+    layer_out = place(out4, out_came, me)
+    sc1.turn()
+    sc2.came = list(tie((sc1.sent, layer_out), *sc2.came))
+    r2 = sc2.result()
+    sc1.came_x, sc1.came_y = tie(r2, sc1.came_x, sc1.came_y)
+    sc1.column()
+    gx, = tie(sc1.mine, gx)
     gx4 = gx.reshape(parts, rows, width)
     gx_came = send_blocks(gx4, me)
-    sc1.fold()
-    sc1.turn()
-    sc1.column()
-    input_grad = place(ids, gx4, gx_came)
-    r1, r2, r_back = sc1.result(), sc2.result(), up(r_back)
+    input_grad = place(gx4, gx_came, me)
+    sc1.came = list(tie(input_grad, *sc1.came))
+    r1, r_back = sc1.result(), up(r_back)
     g_in = jnp.concatenate([r2[own * (1 + i):own * (2 + i)] for i in range(ff_own // own)], 1)
     prod = up(shard1[:3 * own]) * r1[:3 * own]
     g_gain1 = jnp.sum(prod[:own] + prod[own:2 * own] + prod[2 * own:], axis=1) / up(low(norm1_gain))

time: 712 us -> 585 us (0.82)
  the two profiles are of different devices: /device:TPU:0 before, /device:TPU:20 now
where the time goes in v3:
time: 585 us; the launch traced here: 576 us
  Pallas kernels  250 us (43%)
  waiting for transfers between devices  183 us (31%)
  local copies, waits for them, and re-layouts  55.4 us (9%)
  starting transfers between devices  44.7 us (8%)
  other arithmetic  28 us (5%)
  between operations  15.2 us (3%)
    ppermute x40, waiting for transfers between devices, swap(): lax.ppermute(value, axis, [(i, i ^ mask) for i in range(lax.axis_size(axi...  183 us
    pallas_call x4, Pallas kernels, attn_bwd(): pl.pallas_call(functools.partial(bwd_kernel, rows=rows, seq_len=seq_len,...  89.3 us
    pallas_call x1, Pallas kernels, mid(): pl.pallas_call(functools.partial(mid_kernel, ff_steps=ff_steps), out_shap...  76.8 us
    ppermute x40, starting transfers between devices, swap(): lax.ppermute(value, axis, [(i, i ^ mask) for i in range(lax.axis_size(axi...  44.6 us
    pallas_call x1, Pallas kernels, attn_fwd(): pl.pallas_call(functools.partial(fwd_kernel, rows=rows, seq_len=seq_len),...  43 us
    unnamed x127, local copies, waits for them, and re-layouts  32.8 us
    pallas_call x1, Pallas kernels, qkv_gx(): pl.pallas_call(gx_kernel, out_shape=jax.ShapeDtypeStruct((total, width),...  14.1 us
    pallas_call x1, Pallas kernels, qkv_gw(): pl.pallas_call(gw_kernel, out_shape=jax.ShapeDtypeStruct((shards, 3 * wid...  13.5 us
  transfers between devices with their start and end apart: 42, of which 17 were waited for; matrix products, arithmetic and copies ran while one was open for 7% of the time, Pallas kernels for 30%

profile of v3, /device:TPU:20, one launch (start us, length us, event | category | flops | bytes accessed | tf_op | source)
XLA Modules:
  0.0 575.7 jit_solution(10074453386968363561)
XLA Ops:
  15.6 6.8 %collective-permute-done.3 = bf16[1,112,1024]{2,1,0:T(8,128)(2,1)S(1)} collective-permute-done((bf16[1,112,1024]{2,1,0:T(8,128)(2,1)S(1)}, bf16[1,112,1024]{2,1,0:T(8,128)(2,1)S(1)}, u32[]{:S(2)}, u32[]{:S(2)}) %collective-permute-start.3) | collective-permute-done | bytes 229408 | tf_op jit(solution)/shard_map/ppermute | solution.py:673
  22.4 9.2 %collective-permute-done.4 = bf16[1,112,1024]{2,1,0:T(8,128)(2,1)S(1)} collective-permute-done((bf16[1,112,1024]{2,1,0:T(8,128)(2,1)S(1)}, bf16[1,112,1024]{2,1,0:T(8,128)(2,1)S(1)}, u32[]{:S(2)}, u32[]{:S(2)}) %collective-permute-start.4) | collective-permute-done | bytes 229408 | tf_op jit(solution)/shard_map/ppermute | solution.py:673
  31.6 16.6 %collective-permute-done.5 = bf16[1,112,1024]{2,1,0:T(8,128)(2,1)S(1)} collective-permute-done((bf16[1,112,1024]{2,1,0:T(8,128)(2,1)S(1)}, bf16[1,112,1024]{2,1,0:T(8,128)(2,1)S(1)}, u32[]{:S(2)}, u32[]{:S(2)}) %collective-permute-start.5) | collective-permute-done | bytes 229408 | tf_op jit(solution)/shard_map/ppermute | solution.py:673
  52.5 23.0 %collective-permute-done.7.refs_2_ = bf16[4,112,1024]{2,1,0:T(8,128)(2,1)} collective-permute-done((bf16[4,112,1024]{2,1,0:T(8,128)(2,1)S(1)}, bf16[4,112,1024]{2,1,0:T(8,128)(2,1)}, u32[]{:S(2)}, u32[]{:S(2)}) %collective-permute-start.7) | collective-permute-done | bytes 917536 | tf_op jit(solution)/shard_map/ppermute | solution.py:673
  76.7 11.3 %collective-permute-done.6.refs_1_ = bf16[4,112,1024]{2,1,0:T(8,128)(2,1)} collective-permute-done((bf16[4,112,1024]{2,1,0:T(8,128)(2,1)S(1)}, bf16[4,112,1024]{2,1,0:T(8,128)(2,1)}, u32[]{:S(2)}, u32[]{:S(2)}) %collective-permute-start.6) | collective-permute-done | bytes 917536 | tf_op jit(solution)/shard_map/ppermute | solution.py:673
  93.4 35.5 %collective-permute-done.8.refs_3_ = bf16[2,112,1024]{2,1,0:T(8,128)(2,1)S(1)} collective-permute-done((bf16[2,112,1024]{2,1,0:T(8,128)(2,1)S(1)}, bf16[2,112,1024]{2,1,0:T(8,128)(2,1)S(1)}, u32[]{:S(2)}, u32[]{:S(2)}) %collective-permute-start.8) | collective-permute-done | bytes 458784 | tf_op jit(solution)/shard_map/ppermute | solution.py:673
  139.0 13.2 %qkv_fwd.1 = (bf16[1024,1024]{1,0:T(8,128)(2,1)}, bf16[1024,1024]{1,0:T(8,128)(2,1)}, bf16[1024,1024]{1,0:T(8,128)(2,1)}, bf16[1024,1024]{1,0:T(8,128)(2,1)}, bf...) custom-call(s32[3]{0:T(128)} %pad_add_fusion.1.ids_ref, ...), custom_call_target="tpu_custom_call" | custom-call | flops 1048576 | bytes 65536 | tf_op jit(solution)/shard_map/qkv_fwd/pallas_call | solution.py:510
  157.8 43.0 %attn_fwd.1 = (bf16[1024,1024]{1,0:T(8,128)(2,1)S(1)}, f32[8,1024,128]{2,1,0:T(8,128)S(1)}) custom-call(s32[1]{0:T(128)} %dynamic_slice.145.len_ref, bf16[1024,1024]{1,0:T(8,128)(2,1)S(1)} %copy-done.8, bf16[1024,1024]{1,0:T(8,128)(2,1)S(1)} %copy-done.12, bf16[1024,1024]{1,0:T(8,128)(2,1)S(1)} %copy-done.16, f32[16,2048]{1,0:T(8,128)S(1)} %copy-done.21), custom_call_target="tpu_custom_call" | custom-call | flops 1048576 | bytes 65536 | tf_op jit(solution)/shard_map/attn_fwd/pallas_call | solution.py:347
  205.2 76.8 %mid.1 = (bf16[1024,1024]{1,0:T(8,128)(2,1)}, bf16[1024,1024]{1,0:T(8,128)(2,1)}, bf16[1024,1024]{1,0:T(8,128)(2,1)}, bf16[32,160,1024]{2,1,0:T(8,128)(2,1)}, bf16[4096,1024]{1,0:T(8,128)(2,1)}) custom-call(s32[3]{0:T(128)} %pad_add_fusion.1.ids_ref, bf16[1024,1024]{1,0:T(8,128)(2,1)} %get-tuple-element.67.x_ref, bf16[1024,1024]{1,0:T(8,128)(2,1)} %copy-done.19, ...), custom_call_target="tpu_custom_call" | custom-call | flops 1048576 | bytes 65536 | tf_op jit(solution)/shard_map/mid/pallas_call | solution.py:605
  282.0 5.6 copy_bitcast_fusion
  297.2 22.7 %attn_bwd.4 = (bf16[1024,1024]{1,0:T(8,128)(2,1)S(1)}, bf16[1024,1024]{1,0:T(8,128)(2,1)S(1)}, bf16[1024,1024]{1,0:T(8,128)(2,1)S(1)}, f32[4,2048]{1,0:T(4,128)S(1)}) custom-call(s32[1]{0:T(128)} %dynamic_slice.145.len_ref, bf16[1024,1024]{1,0:T(8,128)(2,1)S(1)} %copy-done.9, bf16[1024,1024]{1,0:T(8,128)(2,1)S(1)} %copy-done.13, ...), custom_call_target="tpu_custom_call" | custom-call | flops 1048576 | bytes 65536 | tf_op jit(solution)/shard_map/attn_bwd/pallas_call | solution.py:425
  319.9 16.8 %collective-permute-done.20 = bf16[1,256,1024]{2,1,0:T(8,128)(2,1)} collective-permute-done((bf16[1,256,1024]{2,1,0:T(8,128)(2,1)S(1)}, bf16[1,256,1024]{2,1,0:T(8,128)(2,1)}, u32[]{:S(2)}, u32[]{:S(2)}) %collective-permute-start.20) | collective-permute-done | bytes 524320 | tf_op jit(solution)/shard_map/ppermute | solution.py:673
  336.7 6.8 %fusion = (bf16[4,160,1024]{2,1,0:T(8,128)(2,1)}, bf16[4,160,1024]{2,1,0:T(8,128)(2,1)}, bf16[4,160,1024]{2,1,0:T(8,128)(2,1)}, bf16[4,160,1024]{2,1,0:T(8,128)(2,1)S(1)}) fusion(bf16[4,2,2,160,1024]{4,3,0,2,1:T(8,128)(2,1)} %collective-permute-done.21, s32[]{:T(128)S(6)} %select_n.151, s32[]{:T(128)S(6)} %select_n.149, ...), kind=kLoop, calls=%fused_computation.3 | loop fusion | flops 10485760 | bytes 15728660 | tf_op jit(solution)/shard_map/convert_element_type | solution.py:705
  346.1 4.3 collective-permute-start.23
  350.4 22.0 %attn_bwd.5 = (bf16[1024,1024]{1,0:T(8,128)(2,1)S(1)}, bf16[1024,1024]{1,0:T(8,128)(2,1)S(1)}, bf16[1024,1024]{1,0:T(8,128)(2,1)S(1)}, f32[4,2048]{1,0:T(4,128)S(1)}) custom-call(s32[1]{0:T(128)} %dynamic_slice.145.len_ref, bf16[1024,1024]{1,0:T(8,128)(2,1)S(1)} %copy-done.10, ...), custom_call_target="tpu_custom_call", output_to_operand_aliasing={{0}: (8, {}), {1}: (9, {}), {2}: (10, {})} | custom-call | flops 1048576 | bytes 65536 | tf_op jit(solution)/shard_map/attn_bwd/pallas_call | solution.py:425
  375.6 2.8 collective-permute-done.22
  395.2 22.4 %attn_bwd.6 = (bf16[1024,1024]{1,0:T(8,128)(2,1)S(1)}, bf16[1024,1024]{1,0:T(8,128)(2,1)S(1)}, bf16[1024,1024]{1,0:T(8,128)(2,1)S(1)}, f32[4,2048]{1,0:T(4,128)S(1)}) custom-call(s32[1]{0:T(128)} %dynamic_slice.145.len_ref, bf16[1024,1024]{1,0:T(8,128)(2,1)S(1)} %copy-done.11, ...), custom_call_target="tpu_custom_call", output_to_operand_aliasing={{0}: (8, {}), {1}: (9, {}), {2}: (10, {})} | custom-call | flops 1048576 | bytes 65536 | tf_op jit(solution)/shard_map/attn_bwd/pallas_call | solution.py:425
  417.7 22.2 %attn_bwd.7 = (bf16[1024,1024]{1,0:T(8,128)(2,1)S(1)}, bf16[1024,1024]{1,0:T(8,128)(2,1)S(1)}, bf16[1024,1024]{1,0:T(8,128)(2,1)S(1)}, f32[4,2048]{1,0:T(4,128)S(1)}) custom-call(s32[1]{0:T(128)} %dynamic_slice.145.len_ref, bf16[1024,1024]{1,0:T(8,128)(2,1)S(1)} %copy-done.11, ...), custom_call_target="tpu_custom_call", output_to_operand_aliasing={{0}: (8, {}), {1}: (9, {}), {2}: (10, {})} | custom-call | flops 1048576 | bytes 65536 | tf_op jit(solution)/shard_map/attn_bwd/pallas_call | solution.py:425
  441.2 4.7 collective-permute-done.24
  448.6 13.5 %qkv_gw.1 = bf16[32,112,1024]{2,1,0:T(8,128)(2,1)} custom-call(bf16[1024,1024]{1,0:T(8,128)(2,1)} %get-tuple-element.100.h_ref, bf16[1024,1024]{1,0:T(8,128)(2,1)} %copy-done.1, bf16[1024,1024]{1,0:T(8,128)(2,1)} %copy-done.4, bf16[1024,1024]{1,0:T(8,128)(2,1)} %copy-done.7, s32[2,2048]{1,0:T(2,128)} %pad_add_fusion.refs_10_.bucket_ref, ...), custom_call_target="tpu_custom_call" | custom-call | flops 1048576 | bytes 65536 | tf_op jit(solution)/shard_map/qkv_gw/pallas_call | solution.py:639
  462.1 4.4 copy_bitcast_fusion.1
  466.5 14.1 %qkv_gx.1 = bf16[1024,1024]{1,0:T(8,128)(2,1)} custom-call(bf16[1024,1024]{1,0:T(8,128)(2,1)} %get-tuple-element.67.x_ref, bf16[1024,1024]{1,0:T(8,128)(2,1)} %get-tuple-element.106.gb_ref, bf16[1024,1024]{1,0:T(8,128)(2,1)} %copy-done.1, bf16[1024,1024]{1,0:T(8,128)(2,1)} %copy-done.4, bf16[1024,1024]{1,0:T(8,128)(2,1)} %copy-done.7, ...), custom_call_target="tpu_custom_call" | custom-call | flops 1048576 | bytes 65536 | tf_op jit(solution)/shard_map/qkv_gx/pallas_call | solution.py:662
  480.6 3.9 fusion.4
  484.8 3.6 collective-permute-start.27
  488.4 9.2 %collective-permute-done.28 = bf16[2,112,1024]{2,1,0:T(8,128)(2,1)S(1)} collective-permute-done((bf16[2,112,1024]{2,1,0:T(8,128)(2,1)S(1)}, bf16[2,112,1024]{2,1,0:T(8,128)(2,1)S(1)}, u32[]{:S(2)}, u32[]{:S(2)}) %collective-permute-start.28) | collective-permute-done | bytes 458784 | tf_op jit(solution)/shard_map/ppermute | solution.py:673
  501.8 3.5 collective-permute-start.31
  508.6 3.9 collective-permute-done.29
  512.5 3.5 collective-permute-done.30
  516.0 16.9 %collective-permute-done.31 = bf16[160,1024]{1,0:T(8,128)(2,1)S(1)} collective-permute-done((bf16[160,1024]{1,0:T(8,128)(2,1)S(1)}, bf16[160,1024]{1,0:T(8,128)(2,1)S(1)}, u32[]{:S(2)}, u32[]{:S(2)}) %collective-permute-start.31) | collective-permute-done | bytes 327712 | tf_op jit(solution)/shard_map/ppermute | solution.py:673
  544.1 7.6 %collective-permute-done.35 = bf16[1,256,1024]{2,1,0:T(8,128)(2,1)S(1)} collective-permute-done((bf16[1,256,1024]{2,1,0:T(8,128)(2,1)S(1)}, bf16[1,256,1024]{2,1,0:T(8,128)(2,1)S(1)}, u32[]{:S(2)}, u32[]{:S(2)}) %collective-permute-start.35) | collective-permute-done | bytes 524320 | tf_op jit(solution)/shard_map/ppermute | solution.py:673
  551.7 9.6 %collective-permute-done.36 = bf16[1,256,1024]{2,1,0:T(8,128)(2,1)S(1)} collective-permute-done((bf16[1,256,1024]{2,1,0:T(8,128)(2,1)S(1)}, bf16[1,256,1024]{2,1,0:T(8,128)(2,1)S(1)}, u32[]{:S(2)}, u32[]{:S(2)}) %collective-permute-start.36) | collective-permute-done | bytes 524320 | tf_op jit(solution)/shard_map/ppermute | solution.py:673
  561.4 3.4 collective-permute-done.39
  (251 shorter events, 98.1 us)
Async XLA Ops:
  7.2 196.9 %all-gather.3.cloned.1.call-start = ((), (), s32[]{:S(2)}) async-start(), calls=%async_computation.2 | async-start | bytes 19464192 | tf_op jit(solution)/shard_map/all_gather | solution.py:761
  11.4 555.5 %reduce-scatter.2.cloned.1.call-start = ((), (), s32[]{:S(2)}) async-start(), calls=%async_computation.1 | async-start | bytes 8650752 | tf_op jit(solution)/shard_map/reduce_scatter | solution.py:768
  13.7 17.9 %collective-permute-start.4 = (bf16[1,112,1024]{2,1,0:T(8,128)(2,1)S(1)}, bf16[1,112,1024]{2,1,0:T(8,128)(2,1)S(1)}, u32[]{:S(2)}, u32[]{:S(2)}) collective-permute-start(bf16[1,112,1024]{2,1,0:T(8,128)(2,1)S(1)} %bitcast.121), channel_id=1, source_target_pairs={{0,16},{4,20},{8,24},{12,28},{16,0},{20,4},{24,8},{28,12},{1,17},{... | collective-permute-start | bytes 688136 | tf_op jit(solution)/shard_map/ppermute | solution.py:673
  14.0 34.2 %collective-permute-start.5 = (bf16[1,112,1024]{2,1,0:T(8,128)(2,1)S(1)}, bf16[1,112,1024]{2,1,0:T(8,128)(2,1)S(1)}, u32[]{:S(2)}, u32[]{:S(2)}) collective-permute-start(bf16[1,112,1024]{2,1,0:T(8,128)(2,1)S(1)} %bitcast.122), channel_id=1, source_target_pairs={{0,24},{4,28},{8,16},{12,20},{16,8},{20,12},{24,0},{28,4},{1,25},{... | collective-permute-start | bytes 688136 | tf_op jit(solution)/shard_map/ppermute | solution.py:673
  48.4 27.2 %collective-permute-start.7 = (bf16[4,112,1024]{2,1,0:T(8,128)(2,1)S(1)}, bf16[4,112,1024]{2,1,0:T(8,128)(2,1)}, u32[]{:S(2)}, u32[]{:S(2)}) collective-permute-start(bf16[4,112,1024]{2,1,0:T(8,128)(2,1)S(1)} %pad_maximum_fusion.refs_0_), channel_id=1, source_target_pairs={{0,4},{4,0},{8,12},{12,8},{16,20},{20,16},{24,28},{28,24},{1,5},{5... | collective-permute-start | bytes 2752520 | tf_op jit(solution)/shard_map/ppermute | solution.py:673
  49.0 39.0 %collective-permute-start.6 = (bf16[4,112,1024]{2,1,0:T(8,128)(2,1)S(1)}, bf16[4,112,1024]{2,1,0:T(8,128)(2,1)}, u32[]{:S(2)}, u32[]{:S(2)}) collective-permute-start(bf16[4,112,1024]{2,1,0:T(8,128)(2,1)S(1)} %pad_maximum_fusion.refs_0_), channel_id=1, source_target_pairs={{0,2},{1,3},{2,0},{3,1},{4,6},{5,7},{6,4},{7,5},{8,10},{9,11},{10,... | collective-permute-start | bytes 2752520 | tf_op jit(solution)/shard_map/ppermute | solution.py:673
  50.6 40.8 %collective-permute-start = (bf16[1,256,1024]{2,1,0:T(8,128)(2,1)S(1)}, bf16[1,256,1024]{2,1,0:T(8,128)(2,1)S(1)}, u32[]{:S(2)}, u32[]{:S(2)}) collective-permute-start(bf16[1,256,1024]{2,1,0:T(8,128)(2,1)S(1)} %get-tuple-element.144), channel_id=1, source_target_pairs={{0,1},{1,0},{2,3},{3,2},{4,5},{5,4},{6,7},{7,6},{8,9},{9,8},{10,11... | collective-permute-start | bytes 1572872 | tf_op jit(solution)/shard_map/ppermute | solution.py:673
  50.7 78.8 %collective-permute-start.1 = (bf16[1,256,1024]{2,1,0:T(8,128)(2,1)S(1)}, bf16[1,256,1024]{2,1,0:T(8,128)(2,1)}, u32[]{:S(2)}, u32[]{:S(2)}) collective-permute-start(bf16[1,256,1024]{2,1,0:T(8,128)(2,1)S(1)} %get-tuple-element.143), channel_id=1, source_target_pairs={{0,2},{1,3},{2,0},{3,1},{4,6},{5,7},{6,4},{7,5},{8,10},{9,11},{10,... | collective-permute-start | bytes 1572872 | tf_op jit(solution)/shard_map/ppermute | solution.py:673
  51.3 78.3 %collective-permute-start.2 = (bf16[1,256,1024]{2,1,0:T(8,128)(2,1)S(1)}, bf16[1,256,1024]{2,1,0:T(8,128)(2,1)}, u32[]{:S(2)}, u32[]{:S(2)}) collective-permute-start(bf16[1,256,1024]{2,1,0:T(8,128)(2,1)S(1)} %get-tuple-element.142), channel_id=1, source_target_pairs={{0,3},{1,2},{2,1},{3,0},{4,7},{5,6},{6,5},{7,4},{8,11},{9,10},{10,... | collective-permute-start | bytes 1572872 | tf_op jit(solution)/shard_map/ppermute | solution.py:673
  75.6 55.6 %collective-permute-start.10 = (bf16[4,112,1024]{2,1,0:T(8,128)(2,1)S(1)}, bf16[4,112,1024]{2,1,0:T(8,128)(2,1)S(1)}, u32[]{:S(2)}, u32[]{:S(2)}) collective-permute-start(bf16[4,112,1024]{2,1,0:T(8,128)(2,1)S(1)} %pad_maximum_fusion.refs_0_), channel_id=1, source_target_pairs={{0,1},{1,0},{2,3},{3,2},{4,5},{5,4},{6,7},{7,6},{8,9},{9,8},{10,11... | collective-permute-start | bytes 2752520 | tf_op jit(solution)/shard_map/ppermute | solution.py:673
  87.9 41.0 %collective-permute-start.8 = (bf16[2,112,1024]{2,1,0:T(8,128)(2,1)S(1)}, bf16[2,112,1024]{2,1,0:T(8,128)(2,1)S(1)}, u32[]{:S(2)}, u32[]{:S(2)}) collective-permute-start(bf16[2,112,1024]{2,1,0:T(8,128)(2,1)S(1)} %slice.114), channel_id=1, source_target_pairs={{0,2},{1,3},{2,0},{3,1},{4,6},{5,7},{6,4},{7,5},{8,10},{9,11},{10,... | collective-permute-start | bytes 1376264 | tf_op jit(solution)/shard_map/ppermute | solution.py:673
  91.4 37.5 %collective-permute-start.9 = (bf16[2,112,1024]{2,1,0:T(8,128)(2,1)S(1)}, bf16[2,112,1024]{2,1,0:T(8,128)(2,1)S(1)}, u32[]{:S(2)}, u32[]{:S(2)}) collective-permute-start(bf16[2,112,1024]{2,1,0:T(8,128)(2,1)S(1)} %slice.115), channel_id=1, source_target_pairs={{0,4},{4,0},{8,12},{12,8},{16,20},{20,16},{24,28},{28,24},{1,5},{5... | collective-permute-start | bytes 1376264 | tf_op jit(solution)/shard_map/ppermute | solution.py:673
  131.1 73.0 %collective-permute-start.15 = (bf16[1,256,1024]{2,1,0:T(8,128)(2,1)}, bf16[1,256,1024]{2,1,0:T(8,128)(2,1)S(1)}, u32[]{:S(2)}, u32[]{:S(2)}) collective-permute-start(bf16[1,256,1024]{2,1,0:T(8,128)(2,1)} %get-tuple-element.141), channel_id=1, source_target_pairs={{0,1},{1,0},{2,3},{3,2},{4,5},{5,4},{6,7},{7,6},{8,9},{9,8},{10,11... | collective-permute-start | bytes 1572872 | tf_op jit(solution)/shard_map/ppermute | solution.py:673
  131.3 72.9 %collective-permute-start.16 = (bf16[1,256,1024]{2,1,0:T(8,128)(2,1)}, bf16[1,256,1024]{2,1,0:T(8,128)(2,1)S(1)}, u32[]{:S(2)}, u32[]{:S(2)}) collective-permute-start(bf16[1,256,1024]{2,1,0:T(8,128)(2,1)} %get-tuple-element.140), channel_id=1, source_target_pairs={{0,2},{1,3},{2,0},{3,1},{4,6},{5,7},{6,4},{7,5},{8,10},{9,11},{10,... | collective-permute-start | bytes 1572872 | tf_op jit(solution)/shard_map/ppermute | solution.py:673
  134.0 70.1 %collective-permute-start.17 = (bf16[1,256,1024]{2,1,0:T(8,128)(2,1)}, bf16[1,256,1024]{2,1,0:T(8,128)(2,1)S(1)}, u32[]{:S(2)}, u32[]{:S(2)}) collective-permute-start(bf16[1,256,1024]{2,1,0:T(8,128)(2,1)} %get-tuple-element.139), channel_id=1, source_target_pairs={{0,3},{1,2},{2,1},{3,0},{4,7},{5,6},{6,5},{7,4},{8,11},{9,10},{10,... | collective-permute-start | bytes 1572872 | tf_op jit(solution)/shard_map/ppermute | solution.py:673
  287.6 49.1 %collective-permute-start.21 = (bf16[4,2,2,160,1024]{4,3,0,2,1:T(8,128)(2,1)}, bf16[4,2,2,160,1024]{4,3,0,2,1:T(8,128)(2,1)}, u32[]{:S(2)}, u32[]{:S(2)}) collective-permute-start(bf16[4,2,2,160,1024]{4,3,0,2,1:T(8,128)(2,1)} %copy_bitcast_fusion), channel_id=1, source_target_pairs={{0,1},{1,0},{2,3},{3,2},{4,5},{5,4},{6,7},{7,6},{8,9},{9,8},{10,11... | collective-permute-start | bytes 15728648 | tf_op jit(solution)/shard_map/ppermute | solution.py:673
  290.5 29.4 %collective-permute-start.18 = (bf16[1,256,1024]{2,1,0:T(8,128)(2,1)}, bf16[1,256,1024]{2,1,0:T(8,128)(2,1)}, u32[]{:S(2)}, u32[]{:S(2)}) collective-permute-start(bf16[1,256,1024]{2,1,0:T(8,128)(2,1)} %get-tuple-element.138), channel_id=1, source_target_pairs={{0,1},{1,0},{2,3},{3,2},{4,5},{5,4},{6,7},{7,6},{8,9},{9,8},{10,11... | collective-permute-start | bytes 1572872 | tf_op jit(solution)/shard_map/ppermute | solution.py:673
  290.6 29.3 %collective-permute-start.19 = (bf16[1,256,1024]{2,1,0:T(8,128)(2,1)S(1)}, bf16[1,256,1024]{2,1,0:T(8,128)(2,1)}, u32[]{:S(2)}, u32[]{:S(2)}) collective-permute-start(bf16[1,256,1024]{2,1,0:T(8,128)(2,1)S(1)} %get-tuple-element.137), channel_id=1, source_target_pairs={{0,2},{1,3},{2,0},{3,1},{4,6},{5,7},{6,4},{7,5},{8,10},{9,11},{10,... | collective-permute-start | bytes 1572872 | tf_op jit(solution)/shard_map/ppermute | solution.py:673
  291.2 45.5 %collective-permute-start.20 = (bf16[1,256,1024]{2,1,0:T(8,128)(2,1)S(1)}, bf16[1,256,1024]{2,1,0:T(8,128)(2,1)}, u32[]{:S(2)}, u32[]{:S(2)}) collective-permute-start(bf16[1,256,1024]{2,1,0:T(8,128)(2,1)S(1)} %get-tuple-element.136), channel_id=1, source_target_pairs={{0,3},{1,2},{2,1},{3,0},{4,7},{5,6},{6,5},{7,4},{8,11},{9,10},{10,... | collective-permute-start | bytes 1572872 | tf_op jit(solution)/shard_map/ppermute | solution.py:673
  345.1 33.3 %collective-permute-start.22 = (bf16[2,160,1024]{2,1,0:T(8,128)(2,1)S(1)}, bf16[2,160,1024]{2,1,0:T(8,128)(2,1)S(1)}, u32[]{:S(2)}, u32[]{:S(2)}) collective-permute-start(bf16[2,160,1024]{2,1,0:T(8,128)(2,1)S(1)} %get-tuple-element.150), channel_id=1, source_target_pairs={{0,2},{1,3},{2,0},{3,1},{4,6},{5,7},{6,4},{7,5},{8,10},{9,11},{10,... | collective-permute-start | bytes 1966088 | tf_op jit(solution)/shard_map/ppermute | solution.py:673
  346.1 32.3 %collective-permute-start.23 = (bf16[2,160,1024]{2,1,0:T(8,128)(2,1)S(1)}, bf16[2,160,1024]{2,1,0:T(8,128)(2,1)S(1)}, u32[]{:S(2)}, u32[]{:S(2)}) collective-permute-start(bf16[2,160,1024]{2,1,0:T(8,128)(2,1)S(1)} %get-tuple-element.149), channel_id=1, source_target_pairs={{0,4},{4,0},{8,12},{12,8},{16,20},{20,16},{24,28},{28,24},{1,5},{5... | collective-permute-start | bytes 1966088 | tf_op jit(solution)/shard_map/ppermute | solution.py:673
  382.7 58.4 %collective-permute-start.25 = (bf16[4,160,1024]{2,1,0:T(8,128)(2,1)}, bf16[4,160,1024]{2,1,0:T(8,128)(2,1)}, u32[]{:S(2)}, u32[]{:S(2)}) collective-permute-start(bf16[4,160,1024]{2,1,0:T(8,128)(2,1)} %fusion.9), channel_id=1, source_target_pairs={{0,4},{4,0},{8,12},{12,8},{16,20},{20,16},{24,28},{28,24},{1,5},{5... | collective-permute-start | bytes 3932168 | tf_op jit(solution)/shard_map/ppermute | solution.py:673
  384.8 61.1 %collective-permute-start.24 = (bf16[4,160,1024]{2,1,0:T(8,128)(2,1)}, bf16[4,160,1024]{2,1,0:T(8,128)(2,1)}, u32[]{:S(2)}, u32[]{:S(2)}) collective-permute-start(bf16[4,160,1024]{2,1,0:T(8,128)(2,1)} %fusion.8), channel_id=1, source_target_pairs={{0,2},{1,3},{2,0},{3,1},{4,6},{5,7},{6,4},{7,5},{8,10},{9,11},{10,... | collective-permute-start | bytes 3932168 | tf_op jit(solution)/shard_map/ppermute | solution.py:673
  484.8 15.0 %collective-permute-start.27 = (bf16[2,112,1024]{2,1,0:T(8,128)(2,1)S(1)}, bf16[2,112,1024]{2,1,0:T(8,128)(2,1)S(1)}, u32[]{:S(2)}, u32[]{:S(2)}) collective-permute-start(bf16[2,112,1024]{2,1,0:T(8,128)(2,1)S(1)} %get-tuple-element.156), channel_id=1, source_target_pairs={{0,4},{4,0},{8,12},{12,8},{16,20},{20,16},{24,28},{28,24},{1,5},{5... | collective-permute-start | bytes 1376264 | tf_op jit(solution)/shard_map/ppermute | solution.py:673
  497.7 35.3 %collective-permute-start.33 = (bf16[4,112,1024]{2,1,0:T(8,128)(2,1)S(1)}, bf16[4,112,1024]{2,1,0:T(8,128)(2,1)S(1)}, u32[]{:S(2)}, u32[]{:S(2)}) collective-permute-start(bf16[4,112,1024]{2,1,0:T(8,128)(2,1)S(1)} %fusion.11), channel_id=1, source_target_pairs={{0,4},{4,0},{8,12},{12,8},{16,20},{20,16},{24,28},{28,24},{1,5},{5... | collective-permute-start | bytes 2752520 | tf_op jit(solution)/shard_map/ppermute | solution.py:673
  500.0 33.1 %collective-permute-start.32 = (bf16[4,112,1024]{2,1,0:T(8,128)(2,1)S(1)}, bf16[4,112,1024]{2,1,0:T(8,128)(2,1)S(1)}, u32[]{:S(2)}, u32[]{:S(2)}) collective-permute-start(bf16[4,112,1024]{2,1,0:T(8,128)(2,1)S(1)} %fusion.10), channel_id=1, source_target_pairs={{0,2},{1,3},{2,0},{3,1},{4,6},{5,7},{6,4},{7,5},{8,10},{9,11},{10,... | collective-permute-start | bytes 2752520 | tf_op jit(solution)/shard_map/ppermute | solution.py:673
  501.8 31.0 %collective-permute-start.31 = (bf16[160,1024]{1,0:T(8,128)(2,1)S(1)}, bf16[160,1024]{1,0:T(8,128)(2,1)S(1)}, u32[]{:S(2)}, u32[]{:S(2)}) collective-permute-start(bf16[160,1024]{1,0:T(8,128)(2,1)S(1)} %get-tuple-element.145), channel_id=1, source_target_pairs={{0,24},{4,28},{8,16},{12,20},{16,8},{20,12},{24,0},{28,4},{1,25},{... | collective-permute-start | bytes 983048 | tf_op jit(solution)/shard_map/ppermute | solution.py:673
  536.8 14.8 %collective-permute-start.35 = (bf16[1,256,1024]{2,1,0:T(8,128)(2,1)S(1)}, bf16[1,256,1024]{2,1,0:T(8,128)(2,1)S(1)}, u32[]{:S(2)}, u32[]{:S(2)}) collective-permute-start(bf16[1,256,1024]{2,1,0:T(8,128)(2,1)S(1)} %get-tuple-element.134), channel_id=1, source_target_pairs={{0,2},{1,3},{2,0},{3,1},{4,6},{5,7},{6,4},{7,5},{8,10},{9,11},{10,... | collective-permute-start | bytes 1572872 | tf_op jit(solution)/shard_map/ppermute | solution.py:673
  538.1 23.2 %collective-permute-start.36 = (bf16[1,256,1024]{2,1,0:T(8,128)(2,1)S(1)}, bf16[1,256,1024]{2,1,0:T(8,128)(2,1)S(1)}, u32[]{:S(2)}, u32[]{:S(2)}) collective-permute-start(bf16[1,256,1024]{2,1,0:T(8,128)(2,1)S(1)} %get-tuple-element.133), channel_id=1, source_target_pairs={{0,3},{1,2},{2,1},{3,0},{4,7},{5,6},{6,5},{7,4},{8,11},{9,10},{10,... | collective-permute-start | bytes 1572872 | tf_op jit(solution)/shard_map/ppermute | solution.py:673
  540.6 20.8 %collective-permute-start.37 = (bf16[112,1024]{1,0:T(8,128)(2,1)S(1)}, bf16[112,1024]{1,0:T(8,128)(2,1)S(1)}, u32[]{:S(2)}, u32[]{:S(2)}) collective-permute-start(bf16[112,1024]{1,0:T(8,128)(2,1)S(1)} %get-tuple-element.153), channel_id=1, source_target_pairs={{0,8},{4,12},{8,0},{12,4},{16,24},{20,28},{24,16},{28,20},{1,9},{5... | collective-permute-start | bytes 688136 | tf_op jit(solution)/shard_map/ppermute | solution.py:673
  540.6 20.8 %collective-permute-start.38 = (bf16[112,1024]{1,0:T(8,128)(2,1)S(1)}, bf16[112,1024]{1,0:T(8,128)(2,1)S(1)}, u32[]{:S(2)}, u32[]{:S(2)}) collective-permute-start(bf16[112,1024]{1,0:T(8,128)(2,1)S(1)} %get-tuple-element.152), channel_id=1, source_target_pairs={{0,16},{4,20},{8,24},{12,28},{16,0},{20,4},{24,8},{28,12},{1,17},{... | collective-permute-start | bytes 688136 | tf_op jit(solution)/shard_map/ppermute | solution.py:673
  541.6 23.1 %collective-permute-start.39 = (bf16[112,1024]{1,0:T(8,128)(2,1)S(1)}, bf16[112,1024]{1,0:T(8,128)(2,1)S(1)}, u32[]{:S(2)}, u32[]{:S(2)}) collective-permute-start(bf16[112,1024]{1,0:T(8,128)(2,1)S(1)} %get-tuple-element.151), channel_id=1, source_target_pairs={{0,24},{4,28},{8,16},{12,20},{16,8},{20,12},{24,0},{28,4},{1,25},{... | collective-permute-start | bytes 688136 | tf_op jit(solution)/shard_map/ppermute | solution.py:673
  (71 other events, 808.7 us)
Sparse Core Ops, SparseCore 0:
  11.5 175.8 all-gather.2
  288.1 163.3 reduce-scatter.1

commit v4 on v3

--- a/solution.py
+++ b/solution.py
@@ -287,124 +287,138 @@
 NT = (((1,), (1,)), ((), ()))
 TN = (((0,), (0,)), ((), ()))
 STRIP = 128
+LOG2E = 1.4426950408889634
+LN2 = 0.6931471805599453
 LIMIT = 58 << 20
 LIGHT = pl.CostEstimate(flops=1 << 20, bytes_accessed=1 << 16, transcendentals=0)
 
 def _dot(a, b, dims=(((1,), (0,)), ((), ()))):
     return lax.dot_general(a, b, dims, preferred_element_type=jnp.float32)
 
-def head_lanes(x, which, width=64):
+def with_extras(x, which, extras, width=64):
     lane = lax.broadcasted_iota(jnp.int32, (1, x.shape[1]), 1)
-    keep = (lane < width) if which == 0 else (lane >= width)
-    return jnp.where(keep, x, jnp.zeros_like(x))
+    spare = lane - width if which == 0 else lane
+    own = (lane < width) if which == 0 else (lane >= width)
+    fill = jnp.zeros_like(x)
+    for i, extra in enumerate(extras):
+        fill = jnp.where(spare == i, extra, fill)
+    return jnp.where(own, x, fill).astype(jnp.bfloat16)
+
+def three_parts(x):
+    low = lambda v: v.astype(jnp.bfloat16).astype(jnp.float32)
+    high = low(x)
+    middle = low(x - high)
+    return [high, middle, low(x - high - middle)]
+
+def slot_floor(size, length):
+    return jnp.where(lax.broadcasted_iota(jnp.int32, (size, 1), 0) < length, 0.0, floor_score)
 
 def skew(row, wide):
-    rows = jnp.broadcast_to(row, (STRIP, wide))
-    return pltpu.roll(rows, wide - (STRIP - 1), 1, stride=1, stride_axis=0)
-
-def fwd_kernel(len_ref, q_ref, k_ref, v_ref, t_ref, o_ref, lse_ref, strip, *, rows, seq_len):
+    return pltpu.roll(jnp.broadcast_to(row, (STRIP, wide)), wide - (STRIP - 1), 1, stride=1, stride_axis=0)
+
+def fwd_kernel(len_ref, q_ref, k_ref, v_ref, t_ref, *refs, rows, seq_len, first):
+    o_ref, lse_ref, strip, kx, vx = refs[-5:]
     wide = t_ref.shape[-1]
-    length = len_ref[0]
-    pair = pl.program_id(0)
-    blocks = seq_len // rows
+    pair = first + pl.program_id(0)
     per = rows // STRIP
-    col_ok = lax.broadcasted_iota(jnp.int32, (1, seq_len), 1) < length
     lane = lax.broadcasted_iota(jnp.int32, (1, 128), 1)
-    k2 = k_ref[...]
-    v2 = v_ref[...]
+    k2 = k_ref[...].astype(jnp.float32)
+    vx[:, 0:128] = v_ref[...]
+    vx[:, 128:256] = jnp.ones_like(v_ref[...])
     for a in range(2):
+        kx[a] = with_extras(k2, a, [slot_floor(seq_len, len_ref[0])])
         strip[a] = skew(t_ref[pl.ds(2 * pair + a, 1), :], wide)
 
     def step(b, carry):
-        base = pl.multiple_of(b * rows, rows)
-        q2 = q_ref[pl.ds(base, rows), :]
+        base = b * rows
+        q2 = q_ref[pl.ds(base, rows), :].astype(jnp.float32)
         outs, stats = [], []
         for a in range(2):
-            scores = _dot(head_lanes(q2, a), k2, NT)
+            scores = _dot(with_extras(q2, a, [1.0]), kx[a], NT)
             parts = []
             for i in range(per):
-                off = pl.multiple_of((seq_len - STRIP) - (b * per + i) * STRIP, STRIP)
+                off = (seq_len - STRIP) - (b * per + i) * STRIP
                 parts.append(strip[a, :, pl.ds(off, seq_len)])
-            bias = jnp.concatenate(parts, 0) if per > 1 else parts[0]
-            scores = jnp.where(col_ok, scores + bias, floor_score)
+            scores = scores + (jnp.concatenate(parts, 0) if per > 1 else parts[0])
             top = jnp.max(scores, axis=1, keepdims=True)
-            probs = jnp.exp(scores - top)
-            total = jnp.sum(probs, axis=1, keepdims=True)
-            out = _dot(probs.astype(jnp.bfloat16), v2)
-            outs.append(out * (1.0 / total))
-            stats.append(top + jnp.log(total))
+            probs = jnp.exp2(scores - top).astype(jnp.bfloat16)
+            out = _dot(probs, vx[...])
+            outs.append(out[:, 0:128] / out[:, 128:256])
+            stats.append(top + jnp.log2(out[:, 128:256]))
         o_ref[pl.ds(base, rows), :] = jnp.where(lane < 64, outs[0], outs[1]).astype(jnp.bfloat16)
         lse_ref[0, pl.ds(base, rows), :] = jnp.where(lane < 64, stats[0], stats[1])
         return carry
 
-    lax.fori_loop(0, blocks, step, 0, unroll=2)
-
-def attn_fwd(length, q, k, v, t, rows=256):
+    for b in range(seq_len // rows):
+        step(b, 0)
+
+def attn_fwd(length, q, k, v, t, first, count, prev=(), rows=256):
     seq_len, width = q.shape
     pairs = width // 128
     wide = t.shape[-1]
-    blk = pl.BlockSpec((seq_len, 128), lambda p, n: (0, p))
+    blk = pl.BlockSpec((seq_len, 128), lambda p, n: (0, first + p))
     return pl.pallas_call(
-        functools.partial(fwd_kernel, rows=rows, seq_len=seq_len),
+        functools.partial(fwd_kernel, rows=rows, seq_len=seq_len, first=first),
         out_shape=(jax.ShapeDtypeStruct((seq_len, width), jnp.bfloat16),
                    jax.ShapeDtypeStruct((pairs, seq_len, 128), jnp.float32)),
         grid_spec=pltpu.PrefetchScalarGridSpec(
-            num_scalar_prefetch=1, grid=(pairs,),
-            in_specs=[blk, blk, blk, pl.BlockSpec(t.shape, lambda p, n: (0, 0))],
-            out_specs=[blk, pl.BlockSpec((1, seq_len, 128), lambda p, n: (p, 0, 0))],
-            scratch_shapes=[pltpu.VMEM((2, STRIP, wide), jnp.float32)]),
-        compiler_params=pltpu.CompilerParams(vmem_limit_bytes=40 << 20),
+            num_scalar_prefetch=1, grid=(count,),
+            in_specs=[blk, blk, blk, pl.BlockSpec(t.shape, lambda p, n: (0, 0))] + [pl.BlockSpec(memory_space=pl.ANY)] * len(prev),
+            out_specs=[blk, pl.BlockSpec((1, seq_len, 128), lambda p, n: (first + p, 0, 0))],
+            scratch_shapes=[pltpu.VMEM((2, STRIP, wide), jnp.float32), pltpu.VMEM((2, seq_len, 128), jnp.bfloat16),
+                            pltpu.VMEM((seq_len, 256), jnp.bfloat16)]),
+        input_output_aliases={5 + i: i for i in range(len(prev))},
+        compiler_params=pltpu.CompilerParams(vmem_limit_bytes=LIMIT),
         cost_estimate=LIGHT,
         name="attn_fwd",
-    )(length, q, k, v, t)
+    )(length, q, k, v, t, *prev)
 
 def bwd_kernel(len_ref, q_ref, k_ref, v_ref, do_ref, o_ref, lse_ref, t_ref, *refs, rows, seq_len, first):
-    dq_ref, dk_ref, dv_ref, g_ref, strip, acc, dq_acc = refs[-7:]
+    dq_ref, dk_ref, dv_ref, g_ref, strip, acc, dq_acc, qx, kx, vx, dox = refs[-11:]
     wide = t_ref.shape[-1]
-    length = len_ref[0]
     local_pair = pl.program_id(0)
     pair = first + local_pair
-    blocks = seq_len // rows
     per = rows // STRIP
     lane = lax.broadcasted_iota(jnp.int32, (1, 128), 1)
-    q2 = q_ref[...]
-    do2 = do_ref[...]
-    prod = (do2.astype(jnp.float32) * o_ref[...].astype(jnp.float32)).T
-    stat = lse_ref[0].T
-    lse_rows = [stat[0:1, :], stat[64:65, :]]
-    delta_rows = [jnp.sum(prod[0:64], axis=0, keepdims=True), jnp.sum(prod[64:128], axis=0, keepdims=True)]
+    up = lambda ref: ref[...].astype(jnp.float32)
+    floor = slot_floor(seq_len, len_ref[0])
+    prod = up(do_ref) * up(o_ref)
     for a in range(2):
+        mine = (lane < 64) if a == 0 else (lane >= 64)
+        delta = jnp.sum(jnp.where(mine, prod, 0.0), axis=1, keepdims=True)
+        lse = lse_ref[0, :, 64 * a:64 * a + 1]
+        qx[a] = with_extras(up(q_ref), a, [1.0] + three_parts(-lse))
+        kx[a] = with_extras(up(k_ref), a, [floor, 1.0, 1.0, 1.0])
+        vx[a] = with_extras(up(v_ref), a, [1.0, 1.0, 1.0])
+        dox[a] = with_extras(up(do_ref), a, three_parts(-delta))
         strip[a] = skew(t_ref[pl.ds(2 * pair + a, 1), :], wide)
     acc[...] = jnp.zeros_like(acc)
+    k2t = k_ref[...].T
     dq_acc[...] = jnp.zeros_like(dq_acc)
 
     def step(b, carry):
-        base = pl.multiple_of(b * rows, rows)
-        k2 = k_ref[pl.ds(base, rows), :]
-        v2 = v_ref[pl.ds(base, rows), :]
-        row_ok = (base + lax.broadcasted_iota(jnp.int32, (rows, 1), 0)) < length
+        at = pl.ds(b * rows, rows)
         dks, dvs = [], []
         for a in range(2):
-            scores = _dot(head_lanes(k2, a), q2, NT)
-            offs = [pl.multiple_of((seq_len - STRIP) - (b * per + i) * STRIP, STRIP) for i in range(per)]
+            scores = _dot(kx[a, at, :], qx[a], NT)
+            offs = [(seq_len - STRIP) - (b * per + i) * STRIP for i in range(per)]
             bias = [strip[a, :, pl.ds(off, seq_len)] for off in offs]
-            bias = jnp.concatenate(bias, 0) if per > 1 else bias[0]
-            probs = jnp.where(row_ok, jnp.exp(scores + bias - lse_rows[a]), 0.0)
-            grad_probs = _dot(head_lanes(v2, a), do2, NT)
-            grad_scores = probs * (grad_probs - delta_rows[a])
+            probs = jnp.exp2(scores + (jnp.concatenate(bias, 0) if per > 1 else bias[0]))
+            grad_scores = probs * _dot(vx[a, at, :], dox[a], NT)
             for i, off in enumerate(offs):
                 acc[a, :, pl.ds(off, seq_len)] += grad_scores[i * STRIP:(i + 1) * STRIP]
             probs_b = probs.astype(jnp.bfloat16)
             gs_b = grad_scores.astype(jnp.bfloat16)
-            dvs.append(_dot(probs_b, do2))
-            dks.append(_dot(gs_b, q2))
-            dq_acc[a] += _dot(gs_b, k2, TN)
-        dk_ref[pl.ds(base, rows), :] = jnp.where(lane < 64, dks[0], dks[1]).astype(jnp.bfloat16)
-        dv_ref[pl.ds(base, rows), :] = jnp.where(lane < 64, dvs[0], dvs[1]).astype(jnp.bfloat16)
+            dvs.append(_dot(probs_b, do_ref[...]))
+            dks.append(_dot(gs_b, q_ref[...]))
+            dq_acc[a] += _dot(k2t[:, b * rows:(b + 1) * rows], gs_b)
+        dk_ref[at, :] = (jnp.where(lane < 64, dks[0], dks[1]) * LN2).astype(jnp.bfloat16)
+        dv_ref[at, :] = jnp.where(lane < 64, dvs[0], dvs[1]).astype(jnp.bfloat16)
         return carry
 
-    lax.fori_loop(0, blocks, step, 0)
-    dq_ref[...] = jnp.where(lane < 64, dq_acc[0], dq_acc[1]).astype(jnp.bfloat16)
+    for b in range(seq_len // rows):
+        step(b, 0)
+    dq_ref[...] = jnp.concatenate([dq_acc[0, 0:64], dq_acc[1, 64:128]], 0).T.astype(jnp.bfloat16)
     for a in range(2):
         sums = acc[a]
         half = STRIP
@@ -416,7 +430,7 @@
             sums = sums + pltpu.roll(pltpu.roll(sums, 8 - half, 0), wide - half, 1)
         g_ref[pl.ds(2 * local_pair + a, 1), :] = pltpu.roll(sums, STRIP - 1, 1)[0:1]
 
-def attn_bwd(length, q, k, v, do, o, lse, trev, first, count, prev=None, rows=256):
+def attn_bwd(length, q, k, v, do, o, lse, trev, first, count, prev=None, rows=512):
     seq_len, width = q.shape
     wide = trev.shape[-1]
     blk = pl.BlockSpec((seq_len, 128), lambda p, n: (0, first + p))
@@ -431,9 +445,9 @@
                       pl.BlockSpec(trev.shape, lambda p, n: (0, 0))] + [pl.BlockSpec(memory_space=pl.ANY)] * len(prev),
             out_specs=[blk, blk, blk, pl.BlockSpec((2 * count, wide), lambda p, n: (0, 0))],
             scratch_shapes=[pltpu.VMEM((2, STRIP, wide), jnp.float32), pltpu.VMEM((2, STRIP, wide), jnp.float32),
-                            pltpu.VMEM((2, seq_len, 128), jnp.float32)]),
+                            pltpu.VMEM((2, 128, seq_len), jnp.float32)] + [pltpu.VMEM((2, seq_len, 128), jnp.bfloat16)] * 4),
         input_output_aliases={8 + i: i for i in range(len(prev))},
-        compiler_params=pltpu.CompilerParams(vmem_limit_bytes=40 << 20),
+        compiler_params=pltpu.CompilerParams(vmem_limit_bytes=LIMIT),
         cost_estimate=LIGHT,
         name="attn_bwd",
     )(length, q, k, v, do, o, lse, trev, *prev)
@@ -478,7 +492,7 @@
     heads = t_ref.shape[0]
     for i, ref in enumerate((t_ref, trev_ref)):
         hot = jnp.where(bucket_ref[i:i + 1, :] == ids, 1.0, 0.0).astype(jnp.bfloat16)
-        ref[...] = _dot(table, hot, TN)[0:heads]
+        ref[...] = _dot(table, hot, TN)[0:heads] * LOG2E
     pltpu.make_async_copy(xs, xs, sems.at[0]).wait()
     part = 256
     def norm(i, carry):
@@ -494,7 +508,8 @@
     copies.append(pltpu.make_async_copy(ws, w_out, sems.at[2]))
     copies[-1].start()
     for i, ref in enumerate((q_out, k_out, v_out)):
-        ps[i] = _dot(hs[...], ws[:, i * width:(i + 1) * width]).astype(jnp.bfloat16)
+        full = _dot(hs[...], ws[:, i * width:(i + 1) * width])
+        ps[i] = (full * LOG2E if i == 0 else full).astype(jnp.bfloat16)
         copies.append(pltpu.make_async_copy(ps.at[i], ref, sems.at[3 + i]))
         copies[-1].start()
     for copy in copies:
@@ -525,101 +540,189 @@
     slope = half + 0.5 * v * (1.0 - t * t) * (root_coef * (1.0 + 3.0 * cubic_coef * v * v))
     return v * half, slope
 
-def mid_kernel(ids_ref, x_ref, o_ref, g4_ref, c1_ref, c2_ref, c3_ref, gain_ref, wback_ref, wo_ref, win_ref,
-               out_ref, gb_ref, do_ref, gw_ref, gwback_ref,
-               mixed, h2, h2t, acc, gh2, gm, sem, *, ff_steps):
-    step = pl.program_id(0)
-    rows, width = x_ref.shape
-    part = 256
-    flat = lambda ref: ref[...].reshape(-1, ref.shape[-1])
-
-    @pl.when(step == 0)
-    def _():
-        pull_sequence(ids_ref[0], g4_ref, (c1_ref, c2_ref, c3_ref), gm, sem)
-        wo = flat(wo_ref)
-        def load(i, carry):
-            at = pl.ds(pl.multiple_of(i * part, part), part)
-            value = x_ref[at, :].astype(jnp.float32) + _dot(o_ref[at, :], wo)
-            mixed[at, :] = value
-            acc[at, :] = value
-            hidden = (value * rms_inverse(value) * gain_ref[1:2, :]).astype(jnp.bfloat16)
-            h2[at, :] = hidden
-            h2t[:, at] = hidden.T
-            gh2[at, :] = jnp.zeros_like(value)
-            return carry
-        lax.fori_loop(0, rows // part, load, 0)
-        pltpu.make_async_copy(gm, gm, sem).wait()
-        row_ok = lax.broadcasted_iota(jnp.int32, (rows, 1), 0) < ids_ref[2]
-        gm[...] = jnp.where(row_ok, gm[...], jnp.zeros_like(gm[...]))
-
-    @pl.when(step < ff_steps)
-    def _():
-        win = flat(win_ref)
-        wback = flat(wback_ref)
+def ff_chunks(h2, h2t, gm, acc, gh2, ws_in, ws_back, st_in, st_back, gw_out, row_in, sems, before_add, cols=512):
+    steps = ws_in.shape[1] // cols
+    half = st_back.shape[1]
+    shards, own = st_in.shape[0], h2.shape[1] // st_in.shape[0]
+    wide = h2.shape[1] // cols
+    group = cols // half
+
+    def step(c, carry):
+        at = pl.ds(pl.multiple_of(c * cols, cols), cols)
+        win, wback = ws_in[:, at], ws_back[at, :]
         pre = _dot(h2[...], win)
         grad_active = _dot(gm[...], wback, NT)
         act, slope = gelu_both(pre)
         active = act.astype(jnp.bfloat16)
         gpre = (grad_active * slope).astype(jnp.bfloat16)
+        @pl.when(c == 0)
+        def _():
+            before_add()
         acc[...] += _dot(active, wback)
-        gwback_ref[...] = _dot(active, gm[...], TN).astype(jnp.bfloat16)
-        gw_ref[...] = _dot(h2t[...], gpre).astype(jnp.bfloat16).reshape(gw_ref.shape)
         gh2[...] += _dot(gpre, win, NT)
-
-    @pl.when(step == ff_steps)
-    def _():
-        wo = flat(wo_ref)
-        def finish(i, carry):
-            at = pl.ds(pl.multiple_of(i * part, part), part)
-            out_ref[at, :] = acc[at, :].astype(jnp.bfloat16)
-            value = mixed[at, :]
-            inverse = rms_inverse(value)
-            normed = value * inverse
-            scaled = gh2[at, :] * gain_ref[1:2, :]
-            grad = inverse * (scaled - normed * jnp.mean(scaled * normed, axis=1, keepdims=True)) + gm[at, :].astype(jnp.float32)
-            gb = grad.astype(jnp.bfloat16)
-            gb_ref[at, :] = gb
-            do_ref[at, :] = _dot(gb, wo, NT).astype(jnp.bfloat16)
-            return carry
-        lax.fori_loop(0, rows // part, finish, 0)
-
-    @pl.when(step >= ff_steps)
-    def _():
-        cols = gw_ref.shape[-1]
-        at = pl.ds(pl.multiple_of((step - ff_steps) * cols, cols), cols)
-        gw_ref[...] = _dot(o_ref[...], gb_ref[:, at], TN).astype(jnp.bfloat16).reshape(gw_ref.shape)
-
-def mid(ids, x, o, g4, came, gains, full, cols=512):
+        rows_b = pl.ds(c * group, group)
+        st_back[rows_b, :, :] = _dot(active, gm[...], TN).astype(jnp.bfloat16).reshape(group, half, h2.shape[1])
+        pltpu.make_async_copy(st_back.at[rows_b, :, :], gw_out.at[rows_b, 0:half, :], sems.at[0]).start()
+        up = pl.multiple_of((c // wide) * own, own)
+        lanes = pl.ds(pl.multiple_of((c % wide) * cols, cols), cols)
+        st_in[:, pl.ds(up, own), lanes] = _dot(h2t[...], gpre).astype(jnp.bfloat16).reshape(shards, own, cols)
+        pltpu.make_async_copy(st_in.at[:, pl.ds(up, own), lanes], gw_out.at[:, pl.ds(row_in + up, own), lanes], sems.at[1]).start()
+        return carry
+    lax.fori_loop(0, steps, step, 0)
+
+def finish_chunks(st_in, st_back, sems):
+    pltpu.make_async_copy(st_back, st_back, sems.at[0]).wait()
+    pltpu.make_async_copy(st_in, st_in, sems.at[1]).wait()
+
+def aligned(at, size):
+    return at if isinstance(at, int) else pl.multiple_of(at, size)
+
+def pull_ff(flat, gathered, masks, ws_in, ws_back, row_in, sems):
+    width = ws_in.shape[0]
+    shards = sum(len(m) for m in masks)
+    own, half = width // shards, ws_back.shape[0] // shards
+    for ref, ids in zip(gathered, masks):
+        for j, mask in enumerate(ids):
+            shard = flat ^ mask
+            pltpu.make_async_copy(ref.at[j, 0:half, :], ws_back.at[pl.ds(aligned(shard * half, half), half), :], sems.at[1]).start()
+            at = pl.ds(aligned(shard * own, own), own)
+            for i in range(ws_in.shape[1] // width):
+                pltpu.make_async_copy(ref.at[j, row_in + i * own:row_in + (i + 1) * own, :], ws_in.at[at, i * width:(i + 1) * width], sems.at[0]).start()
+
+def mid_a_kernel(ids_ref, x_hbm, o_hbm, g4_ref, c1_ref, c2_ref, c3_ref, gain_ref, *refs, masks):
+    gathered = refs[:len(masks)]
+    (mixed_out, acc_out, gh2_out, h2_out, h2t_out, gm_out, wo_out, gw_out,
+     xs, os, wo, ws_in, ws_back, mixed, h2, h2t, acc, gh2, gm, st_in, st_back, sems) = refs[len(masks):]
+    flat = ids_ref[1]
+    rows, width = xs.shape
+    half, own = st_back.shape[1], width // st_in.shape[0]
+    loads = [pltpu.make_async_copy(x_hbm, xs, sems.at[0]), pltpu.make_async_copy(o_hbm, os, sems.at[1])]
+    for load in loads:
+        load.start()
+    for ref, ids in zip(gathered, masks):
+        for j, mask in enumerate(ids):
+            at = pl.ds(pl.multiple_of((flat ^ mask) * own, own), own)
+            pltpu.make_async_copy(ref.at[j, half:half + own, :], wo.at[at, :], sems.at[2]).start()
+    pull_ff(flat, gathered, masks, ws_in, ws_back, half + own, sems.at[3:5])
+    pull_sequence(ids_ref[0], g4_ref, (c1_ref, c2_ref, c3_ref), gm, sems.at[5])
+    for load in loads:
+        load.wait()
+    pltpu.make_async_copy(wo, wo, sems.at[2]).wait()
+    stores = [pltpu.make_async_copy(wo, wo_out, sems.at[2])]
+    stores[0].start()
+    part = 256
+    def load_rows(i, carry):
+        at = pl.ds(pl.multiple_of(i * part, part), part)
+        value = xs[at, :].astype(jnp.float32) + _dot(os[at, :], wo[...])
+        mixed[at, :] = value
+        acc[at, :] = value
+        hidden = (value * rms_inverse(value) * gain_ref[1:2, :]).astype(jnp.bfloat16)
+        h2[at, :] = hidden
+        h2t[:, at] = hidden.T
+        gh2[at, :] = jnp.zeros_like(value)
+        return carry
+    lax.fori_loop(0, rows // part, load_rows, 0)
+    pltpu.make_async_copy(gm, gm, sems.at[5]).wait()
+    row_ok = lax.broadcasted_iota(jnp.int32, (rows, 1), 0) < ids_ref[2]
+    gm[...] = jnp.where(row_ok, gm[...], jnp.zeros_like(gm[...]))
+    pltpu.make_async_copy(ws_in, ws_in, sems.at[3]).wait()
+    pltpu.make_async_copy(ws_back, ws_back, sems.at[4]).wait()
+    for i, (src, dst) in enumerate(((mixed, mixed_out), (h2, h2_out), (h2t, h2t_out), (gm, gm_out))):
+        stores.append(pltpu.make_async_copy(src, dst, sems.at[6 + i]))
+        stores[-1].start()
+    ff_chunks(h2, h2t, gm, acc, gh2, ws_in, ws_back, st_in, st_back, gw_out, half, sems.at[0:2], lambda: None)
+    for i, (src, dst) in enumerate(((acc, acc_out), (gh2, gh2_out))):
+        stores.append(pltpu.make_async_copy(src, dst, sems.at[3 + i]))
+        stores[-1].start()
+    finish_chunks(st_in, st_back, sems.at[0:2])
+    for store in stores:
+        store.wait()
+
+def mid_a(ids, x, o, g4, came, gains, gathered, masks, ff):
     rows, width = x.shape
-    shards, stack, _ = full.shape
-    own = width // shards
-    ff_own = (stack - own) // 2
-    ff = ff_own * shards
-    ff_steps = ff // cols
-    wide = width // cols
-    one = lambda shape: pl.BlockSpec(shape, lambda i, n: (0,) * len(shape), pipeline_mode=pl.Buffered(1))
-    last = lambda i: jnp.minimum(i, ff_steps - 1)
-    mat = jax.ShapeDtypeStruct((rows, width), jnp.bfloat16)
-    first = ff_own // own + 1
-    gw_map = lambda i, n: (0, jnp.where(i < ff_steps, 1 + i // wide, 0), jnp.where(i < ff_steps, i % wide, i - ff_steps))
+    shards = sum(len(m) for m in masks)
+    half = ff // shards
+    low = lambda *s: jax.ShapeDtypeStruct(s, jnp.bfloat16)
+    full = lambda *s: jax.ShapeDtypeStruct(s, jnp.float32)
+    vm = lambda *s: pltpu.VMEM(s, jnp.bfloat16)
+    vf = lambda *s: pltpu.VMEM(s, jnp.float32)
+    stack = half + ff // width * (width // shards)
     return pl.pallas_call(
-        functools.partial(mid_kernel, ff_steps=ff_steps),
-        out_shape=(mat, mat, mat, jax.ShapeDtypeStruct((shards, own + ff_own, width), jnp.bfloat16), jax.ShapeDtypeStruct((ff, width), jnp.bfloat16)),
-        grid_spec=pltpu.PrefetchScalarGridSpec(
-            num_scalar_prefetch=1, grid=(ff_steps + wide,),
-            in_specs=[one((rows, width)), one((rows, width)), ANY, ANY, ANY, ANY, one(gains.shape),
-                      pl.BlockSpec((cols // ff_own, ff_own, width), lambda i, n: (last(i), 0, 0)),
-                      pl.BlockSpec((shards, own, width), lambda i, n: (0, first - 1, 0), pipeline_mode=pl.Buffered(1)),
-                      pl.BlockSpec((shards, own, cols), lambda i, n: (0, first + last(i) // wide, last(i) % wide))],
-            out_specs=[one((rows, width)), one((rows, width)), one((rows, width)),
-                       pl.BlockSpec((shards, own, cols), gw_map), pl.BlockSpec((cols, width), lambda i, n: (last(i), 0))],
-            scratch_shapes=[pltpu.VMEM((rows, width), jnp.float32), pltpu.VMEM((rows, width), jnp.bfloat16),
-                            pltpu.VMEM((width, rows), jnp.bfloat16), pltpu.VMEM((rows, width), jnp.float32),
-                            pltpu.VMEM((rows, width), jnp.float32), pltpu.VMEM((rows, width), jnp.bfloat16), pltpu.SemaphoreType.DMA]),
+        functools.partial(mid_a_kernel, masks=masks),
+        out_shape=(full(rows, width), full(rows, width), full(rows, width), low(rows, width), low(width, rows), low(rows, width), low(width, width), low(shards, stack, width)),
+        in_specs=[SM] + [ANY] * 6 + [VM] + [ANY] * len(gathered), out_specs=[ANY] * 8,
+        scratch_shapes=[vm(rows, width), vm(rows, width), vm(width, width), vm(width, ff), vm(ff, width), vf(rows, width), vm(rows, width), vm(width, rows),
+                        vf(rows, width), vf(rows, width), vm(rows, width), vm(shards, stack - half, width), vm(shards, half, width), pltpu.SemaphoreType.DMA((10,))],
         compiler_params=pltpu.CompilerParams(vmem_limit_bytes=LIMIT),
         cost_estimate=LIGHT,
-        name="mid",
-    )(ids, x, o, g4, *came, gains, full, full, full)
+        name="mid_a",
+    )(ids, x, o, g4, *came, gains, *gathered)
+
+def mid_b_kernel( gain_ref, mixed_hbm, acc_hbm, gh2_hbm, h2_hbm, h2t_hbm, gm_hbm, wo_hbm, o_hbm, full_ref, *refs):
+    (out_ref, gb_out, do_ref, gw_out,
+     os, wo, ws_in, ws_back, mixed, h2, h2t, acc, gh2, gm, gb, st_in, st_back, st_o, sems) = refs
+    rows, width = os.shape
+    shards, half, own = st_in.shape[0], st_back.shape[1], width // st_in.shape[0]
+    early = [(h2_hbm, h2), (gm_hbm, gm), (h2t_hbm, h2t)]
+    late = [(acc_hbm, acc), (gh2_hbm, gh2), (mixed_hbm, mixed), (wo_hbm, wo), (o_hbm, os)]
+    early = [pltpu.make_async_copy(a, b, sems.at[4 + i]) for i, (a, b) in enumerate(early)]
+    late = [pltpu.make_async_copy(a, b, sems.at[7 + i]) for i, (a, b) in enumerate(late)]
+    for load in early:
+        load.start()
+    pull_ff(0, (full_ref,), (range(shards),), ws_in, ws_back, half, sems.at[2:4])
+    for load in late:
+        load.start()
+    for load in early:
+        load.wait()
+    pltpu.make_async_copy(ws_in, ws_in, sems.at[2]).wait()
+    pltpu.make_async_copy(ws_back, ws_back, sems.at[3]).wait()
+    def before_add():
+        late[0].wait()
+        late[1].wait()
+    ff_chunks(h2, h2t, gm, acc, gh2, ws_in, ws_back, st_in, st_back, gw_out, half + own, sems.at[0:2], before_add)
+    for load in late[2:]:
+        load.wait()
+    part = 256
+    def finish(i, carry):
+        at = pl.ds(pl.multiple_of(i * part, part), part)
+        out_ref[at, :] = acc[at, :].astype(jnp.bfloat16)
+        value = mixed[at, :]
+        inverse = rms_inverse(value)
+        normed = value * inverse
+        scaled = gh2[at, :] * gain_ref[1:2, :]
+        grad = inverse * (scaled - normed * jnp.mean(scaled * normed, axis=1, keepdims=True)) + gm[at, :].astype(jnp.float32)
+        low = grad.astype(jnp.bfloat16)
+        gb[at, :] = low
+        do_ref[at, :] = _dot(low, wo[...], NT).astype(jnp.bfloat16)
+        return carry
+    lax.fori_loop(0, rows // part, finish, 0)
+    st_o[...] = _dot(os[...], gb[...], TN).astype(jnp.bfloat16).reshape(st_o.shape)
+    stores = [pltpu.make_async_copy(st_o, gw_out.at[:, half:half + own, :], sems.at[2]), pltpu.make_async_copy(gb, gb_out, sems.at[3])]
+    for store in stores:
+        store.start()
+    finish_chunks(st_in, st_back, sems.at[0:2])
+    for store in stores:
+        store.wait()
+
+def mid_b(gains, state, o, full, ff):
+    rows, width = o.shape
+    shards = full.shape[0]
+    half, own = ff // shards, width // shards
+    low = lambda *s: jax.ShapeDtypeStruct(s, jnp.bfloat16)
+    vm = lambda *s: pltpu.VMEM(s, jnp.bfloat16)
+    vf = lambda *s: pltpu.VMEM(s, jnp.float32)
+    rest = ff // width * own
+    return pl.pallas_call(
+        mid_b_kernel,
+        out_shape=(low(rows, width), low(rows, width), low(rows, width), low(shards, half + own + rest, width)),
+        in_specs=[VM] + [ANY] * 9, out_specs=[VM, ANY, VM, ANY],
+        scratch_shapes=[vm(rows, width), vm(width, width), vm(width, ff), vm(ff, width), vf(rows, width), vm(rows, width), vm(width, rows),
+                        vf(rows, width), vf(rows, width), vm(rows, width), vm(rows, width), vm(shards, rest, width), vm(shards, half, width), vm(shards, own, width),
+                        pltpu.SemaphoreType.DMA((12,))],
+        compiler_params=pltpu.CompilerParams(vmem_limit_bytes=LIMIT),
+        cost_estimate=LIGHT,
+        name="mid_b",
+    )(gains, *state, o, full)
 
 def gw_kernel(h_ref, dq_ref, dk_ref, dv_ref, bucket_ref, *refs):
     out_ref = refs[-1]
@@ -673,21 +776,35 @@
     return lax.ppermute(value, axis, [(i, i ^ mask) for i in range(lax.axis_size(axis))])
 
 
-def send_blocks(blocks, me):
-    return tuple(swap(lax.dynamic_index_in_dim(blocks, me ^ mask, 0), "seq", mask) for mask in range(1, blocks.shape[0]))
-
-
-MASKS = ((0, 8, 16, 24), (2, 10, 18, 26), (4, 12, 20, 28), (6, 14), (22, 30))
-
-
-def gather_staged(shard):
-    shard = shard[None]
-    column = jnp.concatenate([shard] + [swap(shard, "dp", 2 * z) for z in (1, 2, 3)], 0)
-    from_x, from_y = swap(column, "seq", 2), swap(column, "dp", 1)
-    corner_x, corner_y = swap(from_y[:2], "seq", 2), swap(from_x[2:], "dp", 1)
-    pieces = (column, from_x, from_y, corner_x, corner_y)
-    masks = MASKS + tuple(tuple(m | 1 for m in row) for row in MASKS)
-    return pieces + tuple(swap(p, "seq", 1) for p in pieces), masks
+def send_blocks(blocks, me, masks=(1, 2, 3)):
+    return tuple(swap(lax.dynamic_index_in_dim(blocks, me ^ mask, 0), "seq", mask) for mask in masks)
+
+
+class Gather:
+    def __init__(self, shard):
+        shard = shard[None]
+        self.sent = [shard] + [swap(shard, "dp", 2 * z) for z in (1, 2, 3)]
+        self.pieces, self.masks = [], []
+
+    def take(self, piece, mask, rows=(0, 1, 2, 3)):
+        ids = tuple(8 * z | mask for z in rows)
+        self.pieces += [piece, swap(piece, "seq", 1)]
+        self.masks += [ids, tuple(m | 1 for m in ids)]
+
+    def fill(self):
+        self.own = jnp.concatenate(self.sent, 0)
+
+    def sides(self):
+        self.x, self.y = swap(self.own, "seq", 2), swap(self.own, "dp", 1)
+
+    def corner_halves(self):
+        self.near, self.far = swap(self.y[:2], "seq", 2), swap(self.x[2:], "dp", 1)
+
+    def corner_y(self):
+        self.corner = swap(self.x, "dp", 1)
+
+    def all_pieces(self):
+        return tuple(self.pieces), tuple(self.masks)
 
 
 class Scatter:
@@ -753,22 +870,55 @@
     small = jnp.concatenate([place_row(norm1_gain), place_row(norm2_gain), jnp.zeros((6, width), jnp.bfloat16),
                              jnp.pad(low(rel_table)[None], ((0, 7), (0, width - HEADS)))], 0)
     shard1 = jnp.concatenate([low(w_query), low(w_key), low(w_value), small], 0)
-    shard2 = jnp.concatenate([low(w_back), low(w_out)] + [low(w_in[:, i * width:(i + 1) * width]) for i in range(ff_own // own)], 0)
+    ff = w_in.shape[1] // 2
+    half = ff_own // 2
+    halves = low(w_in).reshape(own, shards, 2, half)
+    in_half = lambda i: [halves[:, :, i].reshape(own, ff)[:, j:j + width] for j in range(0, ff, width)]
+    shard2 = jnp.concatenate([low(w_back[:half]), low(w_out)] + in_half(0), 0)
+    shard3 = jnp.concatenate([low(w_back[half:])] + in_half(1), 0)
     x4, g4 = tokens.reshape(parts, rows, width), cotangent.reshape(parts, rows, width)
-    gathered, masks = gather_staged(shard1)
+    bucket_rows = jnp.stack([jnp.pad(buckets, (0, 1), constant_values=-1), jnp.pad(buckets[::-1], (0, 1), constant_values=-1)])
+
+    g1 = Gather(shard1)
     x_came = send_blocks(x4, me)
-    g_came = send_blocks(g4, me)
-    full2 = lax.all_gather(shard2, both, axis=0, tiled=False)
-    bucket_rows = jnp.stack([jnp.pad(buckets, (0, 1), constant_values=-1), jnp.pad(buckets[::-1], (0, 1), constant_values=-1)])
-
-    x, hidden, q, k, v, w_qkv, gains, t, t_back = qkv_fwd(ids, x4, x_came, gathered, masks, bucket_rows, HEADS)
-    attended, lse = attn_fwd(length, q, k, v, t)
-    out, gb, g_att, gw2, gw_back = mid(ids, x, attended, g4, g_came, gains, full2)
+    g1.fill()
+    g1.own, = tie(x_came, g1.own)
+    g1.sides()
+    g1.take(g1.own, 0)
+    shard2, = tie(g1.own, shard2)
+    g2 = Gather(shard2)
+    g1.x, g1.y = tie((g2.sent[1], g1.pieces[1]), g1.x, g1.y)
+    g1.corner_halves()
+    g1.take(g1.x, 2)
+    g1.take(g1.y, 4)
+    g2.fill()
+    g1.near, g1.far, g2.own = tie((g1.pieces[3], g1.pieces[5]), g1.near, g1.far, g2.own)
+    g2.sides()
+    g1.take(g1.near, 6, (0, 1))
+    g1.take(g1.far, 6, (2, 3))
+    shard3, = tie((g1.near, g1.far), shard3)
+    full3 = lax.all_gather(shard3, both, axis=0, tiled=False)
+    x, hidden, q, k, v, w_qkv, gains, t, t_back = qkv_fwd(ids, x4, x_came, *g1.all_pieces(), bucket_rows, HEADS)
+    pairs = HEADS // 2
+    att = attn_fwd(length, q, k, v, t, 0, pairs // 2)
+    g2.take(g2.own, 0)
+    g_core = send_blocks(g4, me, (1,))
+    g2.x, g2.y = tie((att[0], g2.pieces[1], g_core), g2.x, g2.y)
+    g2.corner_y()
+    g4_in, = tie(g2.x, g4)
+    g_came = g_core + send_blocks(g4_in, me, (2, 3))
+    g2.take(g2.x, 2)
+    g2.take(g2.y, 4)
+    q_in, = tie((g2.x, g2.y), q)
+    attended, lse = attn_fwd(length, q_in, k, v, t, pairs // 2, pairs // 2, att)
+    g2.corner, = tie((attended, g_came, g2.pieces[3], g2.pieces[5]), g2.corner)
+    g2.take(g2.corner, 6)
+    *state, gw_a = mid_a(ids, x, attended, g4, g_came, gains, *g2.all_pieces(), ff)
+    r_a = lax.psum_scatter(gw_a.reshape(-1, width), both, scatter_dimension=0, tiled=True)
+    out, gb, g_att, gw2 = mid_b(gains, state, attended, full3, ff)
     sc2 = Scatter(gw2, pos)
-    r_back = lax.psum_scatter(gw_back, both, scatter_dimension=0, tiled=True)
     out4 = out.reshape(parts, rows, width)
     out_came = send_blocks(out4, me)
-    pairs = HEADS // 2
     count = pairs // 4
     back = lambda first, g, prev: attn_bwd(length, q, k, v, g, attended, lse, t_back, first, count, prev)
     g_att, = tie((sc2.sent, out), g_att)
@@ -784,12 +934,12 @@
     dq, dk, dv, off3 = back(3 * count, g_att, (dq, dk, dv))
     sc2.came_x, sc2.came_y = tie(off3, sc2.came_x, sc2.came_y)
     sc2.column()
-    h_in, = tie(sc2.mine, hidden)
+    h_in, = tie((sc2.mine, r_a), hidden)
     gw1 = qkv_gw(h_in, dq, dk, dv, bucket_rows, (off0, off1, off2, off3), shards)
     sc1 = Scatter(gw1, pos)
     gb_in, = tie(sc1.sent, gb)
     gx = qkv_gx(x, gb_in, dq, dk, dv, gains, w_qkv)
-    sc1.other, = tie(gx, sc1.other)
+    sc1.other, = tie((gx, sc2.came), sc1.other)
     sc1.fold()
     out4, out_came = tie(sc1.own, out4, out_came)
     layer_out = place(out4, out_came, me)
@@ -803,13 +953,15 @@
     gx_came = send_blocks(gx4, me)
     input_grad = place(gx4, gx_came, me)
     sc1.came = list(tie(input_grad, *sc1.came))
-    r1, r_back = sc1.result(), up(r_back)
-    g_in = jnp.concatenate([r2[own * (1 + i):own * (2 + i)] for i in range(ff_own // own)], 1)
+    r1, r_a = sc1.result(), up(r_a)
+    join = lambda v: jnp.concatenate([v[i:i + own] for i in range(0, v.shape[0], own)], 1).reshape(own, shards, 1, half)
+    g_in = jnp.concatenate([join(r_a[half:]), join(r2[half + own:])], 2).reshape(w_in.shape)
+    g_back = jnp.concatenate([r_a[:half], r2[:half]], 0)
     prod = up(shard1[:3 * own]) * r1[:3 * own]
     g_gain1 = jnp.sum(prod[:own] + prod[own:2 * own] + prod[2 * own:], axis=1) / up(low(norm1_gain))
     g_gain2 = jnp.sum(up(low(w_in)) * g_in, axis=1) / up(low(norm2_gain))
     return (layer_out.reshape(tokens.shape), input_grad.reshape(tokens.shape), g_gain1, r1[:own], r1[own:2 * own], r1[2 * own:3 * own],
-            r2[:own], r1[3 * own, :HEADS], g_gain2, g_in, r_back)
+            r2[half:half + own], r1[3 * own, :HEADS], g_gain2, g_in, g_back)
 
 
 def local_any(shape, tokens, *rest):

time: 585 us -> 560 us (0.957)
  the two profiles are of different devices: /device:TPU:20 before, /device:TPU:0 now
where the time goes in v4:
time: 560 us; the launch traced here: 551 us
  Pallas kernels  225 us (40%)
  waiting for transfers between devices  169 us (30%)
  starting transfers between devices  65.6 us (12%)
  local copies, waits for them, and re-layouts  41.3 us (7%)
  other arithmetic  35.4 us (6%)
  between operations  15.3 us (3%)
    ppermute x50, waiting for transfers between devices, swap(): lax.ppermute(value, axis, [(i, i ^ mask) for i in range(lax.axis_size(axi...  169 us
    ppermute x50, starting transfers between devices, swap(): lax.ppermute(value, axis, [(i, i ^ mask) for i in range(lax.axis_size(axi...  65.5 us
    pallas_call x4, Pallas kernels, attn_bwd(): pl.pallas_call(functools.partial(bwd_kernel, rows=rows, seq_len=seq_len,...  65.5 us
    pallas_call x1, Pallas kernels, mid_b(): pl.pallas_call(mid_b_kernel, out_shape=(low(rows, width), low(rows, width...  45.4 us
    pallas_call x1, Pallas kernels, mid_a(): pl.pallas_call(functools.partial(mid_a_kernel, masks=masks), out_shape=(f...  39.8 us
    pallas_call x2, Pallas kernels, attn_fwd(): pl.pallas_call(functools.partial(fwd_kernel, rows=rows, seq_len=seq_len,...  33.2 us
    pallas_call x1, Pallas kernels, qkv_gx(): pl.pallas_call(gx_kernel, out_shape=jax.ShapeDtypeStruct((total, width),...  14.1 us
    pallas_call x1, Pallas kernels, qkv_gw(): pl.pallas_call(gw_kernel, out_shape=jax.ShapeDtypeStruct((shards, 3 * wid...  13.4 us
  transfers between devices with their start and end apart: 52, of which 23 were waited for; matrix products, arithmetic and copies ran while one was open for 10% of the time, Pallas kernels for 38%

profile of v4, /device:TPU:0, one launch (start us, length us, event | category | flops | bytes accessed | tf_op | source)
XLA Modules:
  0.0 551.3 jit_solution(2286802494898786260)
XLA Ops:
  25.8 12.7 %collective-permute-done.4 = bf16[1,112,1024]{2,1,0:T(8,128)(2,1)} collective-permute-done((bf16[1,112,1024]{2,1,0:T(8,128)(2,1)S(1)}, bf16[1,112,1024]{2,1,0:T(8,128)(2,1)}, u32[]{:S(2)}, u32[]{:S(2)}) %collective-permute-start.4) | collective-permute-done | bytes 229408 | tf_op jit(solution)/shard_map/ppermute | solution.py:776
  55.3 7.8 %collective-permute-done.7 = bf16[1,160,1024]{2,1,0:T(8,128)(2,1)S(1)} collective-permute-done((bf16[1,160,1024]{2,1,0:T(8,128)(2,1)S(1)}, bf16[1,160,1024]{2,1,0:T(8,128)(2,1)S(1)}, u32[]{:S(2)}, u32[]{:S(2)}) %collective-permute-start.7) | collective-permute-done | bytes 327712 | tf_op jit(solution)/shard_map/ppermute | solution.py:776
  77.6 16.9 %collective-permute-done.14 = bf16[1,160,1024]{2,1,0:T(8,128)(2,1)} collective-permute-done((bf16[1,160,1024]{2,1,0:T(8,128)(2,1)S(1)}, bf16[1,160,1024]{2,1,0:T(8,128)(2,1)}, u32[]{:S(2)}, u32[]{:S(2)}) %collective-permute-start.14) | collective-permute-done | bytes 327712 | tf_op jit(solution)/shard_map/ppermute | solution.py:776
  98.3 7.8 %collective-permute-done.13.refs_8_ = bf16[2,112,1024]{2,1,0:T(8,128)(2,1)} collective-permute-done((bf16[2,112,1024]{2,1,0:T(8,128)(2,1)}, bf16[2,112,1024]{2,1,0:T(8,128)(2,1)}, u32[]{:S(2)}, u32[]{:S(2)}) %collective-permute-start.13) | collective-permute-done | bytes 458784 | tf_op jit(solution)/shard_map/ppermute | solution.py:776
  113.3 13.1 %qkv_fwd.1 = (bf16[1024,1024]{1,0:T(8,128)(2,1)}, bf16[1024,1024]{1,0:T(8,128)(2,1)}, bf16[1024,1024]{1,0:T(8,128)(2,1)}, bf16[1024,1024]{1,0:T(8,128)(2,1)}, bf...) custom-call(s32[3]{0:T(128)} %pad_add_fusion.1.ids_ref, ...), custom_call_target="tpu_custom_call" | custom-call | flops 1048576 | bytes 65536 | tf_op jit(solution)/shard_map/qkv_fwd/pallas_call | solution.py:525
  126.4 16.5 %attn_fwd.2 = (bf16[1024,1024]{1,0:T(8,128)(2,1)}, f32[8,1024,128]{2,1,0:T(8,128)}) custom-call(s32[1]{0:T(128)} %dynamic_slice.145.len_ref, bf16[1024,1024]{1,0:T(8,128)(2,1)} %get-tuple-element.105.q_ref, bf16[1024,1024]{1,0:T(8,128)(2,1)} %get-tuple-element.98.k_ref, bf16[1024,1024]{1,0:T(8,128)(2,1)} %get-tuple-element.99.v_ref, ...), custom_call_target="tpu_custom_call" | custom-call | flops 1048576 | bytes 65536 | tf_op jit(solution)/shard_map/attn_fwd/pallas_call | solution.py:360
  149.0 16.7 %attn_fwd.3 = (bf16[1024,1024]{1,0:T(8,128)(2,1)}, f32[8,1024,128]{2,1,0:T(8,128)}) custom-call(s32[1]{0:T(128)} %dynamic_slice.145.len_ref, bf16[1024,1024]{1,0:T(8,128)(2,1)} %get-tuple-element.105.q_ref, bf16[1024,1024]{1,0:T(8,128)(2,1)} %get-tuple-element.98.k_ref, ...), custom_call_target="tpu_custom_call", output_to_operand_aliasing={{0}: (5, {}), {1}: (6, {})} | custom-call | flops 1048576 | bytes 65536 | tf_op jit(solution)/shard_map/attn_fwd/pallas_call | solution.py:360
  166.4 18.9 %collective-permute-done.23.c3_ref = bf16[1,256,1024]{2,1,0:T(8,128)(2,1)S(1)} collective-permute-done((bf16[1,256,1024]{2,1,0:T(8,128)(2,1)}, bf16[1,256,1024]{2,1,0:T(8,128)(2,1)S(1)}, u32[]{:S(2)}, u32[]{:S(2)}) %collective-permute-start.23) | collective-permute-done | bytes 524320 | tf_op jit(solution)/shard_map/ppermute | solution.py:776
  185.4 5.8 %collective-permute-done.26.refs_6_ = bf16[4,160,1024]{2,1,0:T(8,128)(2,1)S(1)} collective-permute-done((bf16[4,160,1024]{2,1,0:T(8,128)(2,1)}, bf16[4,160,1024]{2,1,0:T(8,128)(2,1)S(1)}, u32[]{:S(2)}, u32[]{:S(2)}) %collective-permute-start.26) | collective-permute-done | bytes 1310752 | tf_op jit(solution)/shard_map/ppermute | solution.py:776
  191.1 3.6 collective-permute-done.27.refs_7_
  195.8 39.8 %mid_a.1 = (f32[1024,1024]{1,0:T(8,128)}, f32[1024,1024]{1,0:T(8,128)}, f32[1024,1024]{1,0:T(8,128)}, bf16[1024,1024]{1,0:T(8,128)(2,1)}, bf16[1024,1024]{1,0:T(...) custom-call(s32[3]{0:T(128)} %pad_add_fusion.1.ids_ref, ...), custom_call_target="tpu_custom_call" | custom-call | flops 1048576 | bytes 65536 | tf_op jit(solution)/shard_map/mid_a/pallas_call | solution.py:650
  235.8 45.4 %mid_b.1 = (bf16[1024,1024]{1,0:T(8,128)(2,1)}, bf16[1024,1024]{1,0:T(8,128)(2,1)}, bf16[1024,1024]{1,0:T(8,128)(2,1)}, bf16[32,160,1024]{2,1,0:T(8,128)(2,1)}) custom-call(f32[8,1024]{1,0:T(8,128)} %get-tuple-element.95.gain_ref, f32[1024,1024]{1,0:T(8,128)} %get-tuple-element.110.mixed_hbm, f32[1024,1024]{1,0:T(8,128)} %get-tuple-element.111.acc_hbm, ...), custom_call_target="tpu_custom_call" | custom-call | flops 1048576 | bytes 65536 | tf_op jit(solution)/shard_map/mid_b/pallas_call | solution.py:715
  281.2 5.8 %copy_bitcast_fusion = bf16[4,2,2,160,1024]{4,3,0,2,1:T(8,128)(2,1)} fusion(bf16[4,2,2,2,160,1024]{5,4,3,2,1,0:T(8,128)(2,1)} %bitcast.107, s32[]{:T(128)S(6)} %select_n.147), kind=kLoop, calls=%fused_computation | loop fusion | bytes 10485764 | tf_op jit(solution)/shard_map/jit(dynamic_index_in_dim)/squeeze | solution.py:814
  289.1 16.6 %attn_bwd.4 = (bf16[1024,1024]{1,0:T(8,128)(2,1)}, bf16[1024,1024]{1,0:T(8,128)(2,1)}, bf16[1024,1024]{1,0:T(8,128)(2,1)}, f32[4,2048]{1,0:T(4,128)}) custom-call(s32[1]{0:T(128)} %dynamic_slice.145.len_ref, bf16[1024,1024]{1,0:T(8,128)(2,1)} %get-tuple-element.105.q_ref, bf16[1024,1024]{1,0:T(8,128)(2,1)} %get-tuple-element.98.k_ref, ...), custom_call_target="tpu_custom_call" | custom-call | flops 1048576 | bytes 65536 | tf_op jit(solution)/shard_map/attn_bwd/pallas_call | solution.py:439
  308.3 21.7 %collective-permute-done.30 = bf16[1,256,1024]{2,1,0:T(8,128)(2,1)S(1)} collective-permute-done((bf16[1,256,1024]{2,1,0:T(8,128)(2,1)S(1)}, bf16[1,256,1024]{2,1,0:T(8,128)(2,1)S(1)}, u32[]{:S(2)}, u32[]{:S(2)}) %collective-permute-start.30) | collective-permute-done | bytes 524320 | tf_op jit(solution)/shard_map/ppermute | solution.py:776
  330.8 8.0 %fusion = (bf16[4,160,1024]{2,1,0:T(8,128)(2,1)S(1)}, bf16[4,160,1024]{2,1,0:T(8,128)(2,1)}, bf16[4,160,1024]{2,1,0:T(8,128)(2,1)S(1)}, bf16[4,160,1024]{2,1,0:T(8,128)(2,1)S(1)}) fusion(bf16[4,2,2,160,1024]{4,3,0,2,1:T(8,128)(2,1)} %collective-permute-done.31, s32[]{:T(128)S(6)} %select_n.151, s32[]{:T(128)S(6)} %select_n.149, ...), kind=kLoop, calls=%fused_computation.3 | loop fusion | flops 10485760 | bytes 15728660 | tf_op jit(solution)/shard_map/convert_element_type | solution.py:822
  340.6 5.1 collective-permute-start.33
  345.7 16.2 %attn_bwd.5 = (bf16[1024,1024]{1,0:T(8,128)(2,1)}, bf16[1024,1024]{1,0:T(8,128)(2,1)}, bf16[1024,1024]{1,0:T(8,128)(2,1)}, f32[4,2048]{1,0:T(4,128)}) custom-call(s32[1]{0:T(128)} %dynamic_slice.145.len_ref, bf16[1024,1024]{1,0:T(8,128)(2,1)} %get-tuple-element.105.q_ref, ...), custom_call_target="tpu_custom_call", output_to_operand_aliasing={{0}: (8, {}), {1}: (9, {}), {2}: (10, {})} | custom-call | flops 1048576 | bytes 65536 | tf_op jit(solution)/shard_map/attn_bwd/pallas_call | solution.py:439
  361.9 9.3 %collective-permute-done.32 = bf16[2,160,1024]{2,1,0:T(8,128)(2,1)S(1)} collective-permute-done((bf16[2,160,1024]{2,1,0:T(8,128)(2,1)S(1)}, bf16[2,160,1024]{2,1,0:T(8,128)(2,1)S(1)}, u32[]{:S(2)}, u32[]{:S(2)}) %collective-permute-start.32) | collective-permute-done | bytes 655392 | tf_op jit(solution)/shard_map/ppermute | solution.py:776
  373.7 8.1 %collective-permute-start.35 = (bf16[4,160,1024]{2,1,0:T(8,128)(2,1)}, bf16[4,160,1024]{2,1,0:T(8,128)(2,1)}, u32[]{:S(2)}, u32[]{:S(2)}) collective-permute-start(bf16[4,160,1024]{2,1,0:T(8,128)(2,1)} %fusion.9), channel_id=1, source_target_pairs={{0,4},{4,0},{8,12},{12,8},{16,20},{20,16},{24,28},{28,24},{1,5},{5... | collective-permute-start | bytes 3932168 | tf_op jit(solution)/shard_map/ppermute | solution.py:776
  381.8 16.4 %attn_bwd.6 = (bf16[1024,1024]{1,0:T(8,128)(2,1)}, bf16[1024,1024]{1,0:T(8,128)(2,1)}, bf16[1024,1024]{1,0:T(8,128)(2,1)}, f32[4,2048]{1,0:T(4,128)}) custom-call(s32[1]{0:T(128)} %dynamic_slice.145.len_ref, bf16[1024,1024]{1,0:T(8,128)(2,1)} %get-tuple-element.105.q_ref, ...), custom_call_target="tpu_custom_call", output_to_operand_aliasing={{0}: (8, {}), {1}: (9, {}), {2}: (10, {})} | custom-call | flops 1048576 | bytes 65536 | tf_op jit(solution)/shard_map/attn_bwd/pallas_call | solution.py:439
  398.1 16.3 %attn_bwd.7 = (bf16[1024,1024]{1,0:T(8,128)(2,1)}, bf16[1024,1024]{1,0:T(8,128)(2,1)}, bf16[1024,1024]{1,0:T(8,128)(2,1)}, f32[4,2048]{1,0:T(4,128)}) custom-call(s32[1]{0:T(128)} %dynamic_slice.145.len_ref, bf16[1024,1024]{1,0:T(8,128)(2,1)} %get-tuple-element.105.q_ref, ...), custom_call_target="tpu_custom_call", output_to_operand_aliasing={{0}: (8, {}), {1}: (9, {}), {2}: (10, {})} | custom-call | flops 1048576 | bytes 65536 | tf_op jit(solution)/shard_map/attn_bwd/pallas_call | solution.py:439
  417.2 13.4 %qkv_gw.1 = bf16[32,112,1024]{2,1,0:T(8,128)(2,1)} custom-call(bf16[1024,1024]{1,0:T(8,128)(2,1)} %get-tuple-element.145.h_ref, bf16[1024,1024]{1,0:T(8,128)(2,1)} %get-tuple-element.146.dq_ref, bf16[1024,1024]{1,0:T(8,128)(2,1)} %get-tuple-element.147.dk_ref, bf16[1024,1024]{1,0:T(8,128)(2,1)} %get-tuple-element.148.dv_ref, ...), custom_call_target="tpu_custom_call" | custom-call | flops 1048576 | bytes 65536 | tf_op jit(solution)/shard_map/qkv_gw/pallas_call | solution.py:742
  430.6 4.4 copy_bitcast_fusion.1
  439.4 14.1 %qkv_gx.1 = bf16[1024,1024]{1,0:T(8,128)(2,1)} custom-call(bf16[1024,1024]{1,0:T(8,128)(2,1)} %get-tuple-element.96.x_hbm.x_ref, bf16[1024,1024]{1,0:T(8,128)(2,1)} %get-tuple-element.151.gb_ref, bf16[1024,1024]{1,0:T(8,128)(2,1)} %get-tuple-element.146.dq_ref, bf16[1024,1024]{1,0:T(8,128)(2,1)} %get-tuple-element.147.dk_ref, ...), custom_call_target="tpu_custom_call" | custom-call | flops 1048576 | bytes 65536 | tf_op jit(solution)/shard_map/qkv_gx/pallas_call | solution.py:765
  453.5 7.1 %collective-permute-done.37 = bf16[160,1024]{1,0:T(8,128)(2,1)} collective-permute-done((bf16[160,1024]{1,0:T(8,128)(2,1)S(1)}, bf16[160,1024]{1,0:T(8,128)(2,1)}, u32[]{:S(2)}, u32[]{:S(2)}) %collective-permute-start.37) | collective-permute-done | bytes 327712 | tf_op jit(solution)/shard_map/ppermute | solution.py:776
  460.6 3.9 fusion.4
  466.8 9.9 %collective-permute-done.41 = bf16[2,112,1024]{2,1,0:T(8,128)(2,1)S(1)} collective-permute-done((bf16[2,112,1024]{2,1,0:T(8,128)(2,1)S(1)}, bf16[2,112,1024]{2,1,0:T(8,128)(2,1)S(1)}, u32[]{:S(2)}, u32[]{:S(2)}) %collective-permute-start.41) | collective-permute-done | bytes 458784 | tf_op jit(solution)/shard_map/ppermute | solution.py:776
  481.1 16.9 %collective-permute-done.43 = bf16[4,112,1024]{2,1,0:T(8,128)(2,1)S(1)} collective-permute-done((bf16[4,112,1024]{2,1,0:T(8,128)(2,1)S(1)}, bf16[4,112,1024]{2,1,0:T(8,128)(2,1)S(1)}, u32[]{:S(2)}, u32[]{:S(2)}) %collective-permute-start.43) | collective-permute-done | bytes 917536 | tf_op jit(solution)/shard_map/ppermute | solution.py:776
  514.5 8.0 %collective-permute-start.47 = (bf16[112,1024]{1,0:T(8,128)(2,1)}, bf16[112,1024]{1,0:T(8,128)(2,1)S(1)}, u32[]{:S(2)}, u32[]{:S(2)}) collective-permute-start(bf16[112,1024]{1,0:T(8,128)(2,1)} %get-tuple-element.196), channel_id=1, source_target_pairs={{0,8},{4,12},{8,0},{12,4},{16,24},{20,28},{24,16},{28,20},{1,9},{5... | collective-permute-start | bytes 688136 | tf_op jit(solution)/shard_map/ppermute | solution.py:776
  525.9 6.6 %collective-permute-done.46 = bf16[1,256,1024]{2,1,0:T(8,128)(2,1)} collective-permute-done((bf16[1,256,1024]{2,1,0:T(8,128)(2,1)}, bf16[1,256,1024]{2,1,0:T(8,128)(2,1)}, u32[]{:S(2)}, u32[]{:S(2)}) %collective-permute-start.46) | collective-permute-done | bytes 524320 | tf_op jit(solution)/shard_map/ppermute | solution.py:776
  533.6 8.3 %collective-permute-done.48 = bf16[112,1024]{1,0:T(8,128)(2,1)S(1)} collective-permute-done((bf16[112,1024]{1,0:T(8,128)(2,1)}, bf16[112,1024]{1,0:T(8,128)(2,1)S(1)}, u32[]{:S(2)}, u32[]{:S(2)}) %collective-permute-start.48) | collective-permute-done | bytes 229408 | tf_op jit(solution)/shard_map/ppermute | solution.py:776
  (250 shorter events, 114.9 us)
Async XLA Ops:
  7.2 228.6 %all-gather.3.cloned.1.call-start = ((), (), s32[]{:S(2)}) async-start(), calls=%async_computation.2 | async-start | bytes 8650752 | tf_op jit(solution)/shard_map/all_gather | solution.py:900
  18.0 21.6 %collective-permute-start = (bf16[1,256,1024]{2,1,0:T(8,128)(2,1)}, bf16[1,256,1024]{2,1,0:T(8,128)(2,1)S(1)}, u32[]{:S(2)}, u32[]{:S(2)}) collective-permute-start(bf16[1,256,1024]{2,1,0:T(8,128)(2,1)} %get-tuple-element.187), channel_id=1, source_target_pairs={{0,1},{1,0},{2,3},{3,2},{4,5},{5,4},{6,7},{7,6},{8,9},{9,8},{10,11... | collective-permute-start | bytes 1572872 | tf_op jit(solution)/shard_map/ppermute | solution.py:776
  18.0 21.6 %collective-permute-start.1 = (bf16[1,256,1024]{2,1,0:T(8,128)(2,1)}, bf16[1,256,1024]{2,1,0:T(8,128)(2,1)S(1)}, u32[]{:S(2)}, u32[]{:S(2)}) collective-permute-start(bf16[1,256,1024]{2,1,0:T(8,128)(2,1)} %get-tuple-element.186), channel_id=1, source_target_pairs={{0,2},{1,3},{2,0},{3,1},{4,6},{5,7},{6,4},{7,5},{8,10},{9,11},{10,... | collective-permute-start | bytes 1572872 | tf_op jit(solution)/shard_map/ppermute | solution.py:776
  19.7 23.8 %collective-permute-start.2 = (bf16[1,256,1024]{2,1,0:T(8,128)(2,1)S(1)}, bf16[1,256,1024]{2,1,0:T(8,128)(2,1)}, u32[]{:S(2)}, u32[]{:S(2)}) collective-permute-start(bf16[1,256,1024]{2,1,0:T(8,128)(2,1)S(1)} %get-tuple-element.185), channel_id=1, source_target_pairs={{0,3},{1,2},{2,1},{3,0},{4,7},{5,6},{6,5},{7,4},{8,11},{9,10},{10,... | collective-permute-start | bytes 1572872 | tf_op jit(solution)/shard_map/ppermute | solution.py:776
  43.7 22.7 %collective-permute-start.8 = (bf16[4,112,1024]{2,1,0:T(8,128)(2,1)S(1)}, bf16[4,112,1024]{2,1,0:T(8,128)(2,1)}, u32[]{:S(2)}, u32[]{:S(2)}) collective-permute-start(bf16[4,112,1024]{2,1,0:T(8,128)(2,1)S(1)} %pad_maximum_fusion.2.refs_0_), channel_id=1, source_target_pairs={{0,2},{1,3},{2,0},{3,1},{4,6},{5,7},{6,4},{7,5},{8,10},{9,11},{10,... | collective-permute-start | bytes 2752520 | tf_op jit(solution)/shard_map/ppermute | solution.py:776
  45.4 22.4 %collective-permute-start.9 = (bf16[4,112,1024]{2,1,0:T(8,128)(2,1)S(1)}, bf16[4,112,1024]{2,1,0:T(8,128)(2,1)}, u32[]{:S(2)}, u32[]{:S(2)}) collective-permute-start(bf16[4,112,1024]{2,1,0:T(8,128)(2,1)S(1)} %pad_maximum_fusion.2.refs_0_), channel_id=1, source_target_pairs={{0,4},{4,0},{8,12},{12,8},{16,20},{20,16},{24,28},{28,24},{1,5},{5... | collective-permute-start | bytes 2752520 | tf_op jit(solution)/shard_map/ppermute | solution.py:776
  67.8 38.3 %collective-permute-start.10 = (bf16[4,112,1024]{2,1,0:T(8,128)(2,1)}, bf16[4,112,1024]{2,1,0:T(8,128)(2,1)}, u32[]{:S(2)}, u32[]{:S(2)}) collective-permute-start(bf16[4,112,1024]{2,1,0:T(8,128)(2,1)} %collective-permute-done.8.refs_2_), channel_id=1, source_target_pairs={{0,1},{1,0},{2,3},{3,2},{4,5},{5,4},{6,7},{7,6},{8,9},{9,8},{10,11... | collective-permute-start | bytes 2752520 | tf_op jit(solution)/shard_map/ppermute | solution.py:776
  67.8 38.3 %collective-permute-start.11 = (bf16[4,112,1024]{2,1,0:T(8,128)(2,1)}, bf16[4,112,1024]{2,1,0:T(8,128)(2,1)}, u32[]{:S(2)}, u32[]{:S(2)}) collective-permute-start(bf16[4,112,1024]{2,1,0:T(8,128)(2,1)} %collective-permute-done.9.refs_4_), channel_id=1, source_target_pairs={{0,1},{1,0},{2,3},{3,2},{4,5},{5,4},{6,7},{7,6},{8,9},{9,8},{10,11... | collective-permute-start | bytes 2752520 | tf_op jit(solution)/shard_map/ppermute | solution.py:776
  68.3 26.2 %collective-permute-start.14 = (bf16[1,160,1024]{2,1,0:T(8,128)(2,1)S(1)}, bf16[1,160,1024]{2,1,0:T(8,128)(2,1)}, u32[]{:S(2)}, u32[]{:S(2)}) collective-permute-start(bf16[1,160,1024]{2,1,0:T(8,128)(2,1)S(1)} %bitcast.120), channel_id=1, source_target_pairs={{0,16},{4,20},{8,24},{12,28},{16,0},{20,4},{24,8},{28,12},{1,17},{... | collective-permute-start | bytes 983048 | tf_op jit(solution)/shard_map/ppermute | solution.py:776
  72.1 24.7 %collective-permute-start.15 = (bf16[1,160,1024]{2,1,0:T(8,128)(2,1)S(1)}, bf16[1,160,1024]{2,1,0:T(8,128)(2,1)}, u32[]{:S(2)}, u32[]{:S(2)}) collective-permute-start(bf16[1,160,1024]{2,1,0:T(8,128)(2,1)S(1)} %bitcast.121), channel_id=1, source_target_pairs={{0,24},{4,28},{8,16},{12,20},{16,8},{20,12},{24,0},{28,4},{1,25},{... | collective-permute-start | bytes 983048 | tf_op jit(solution)/shard_map/ppermute | solution.py:776
  77.2 21.1 %collective-permute-start.12 = (bf16[2,112,1024]{2,1,0:T(8,128)(2,1)}, bf16[2,112,1024]{2,1,0:T(8,128)(2,1)}, u32[]{:S(2)}, u32[]{:S(2)}) collective-permute-start(bf16[2,112,1024]{2,1,0:T(8,128)(2,1)} %slice.115), channel_id=1, source_target_pairs={{0,2},{1,3},{2,0},{3,1},{4,6},{5,7},{6,4},{7,5},{8,10},{9,11},{10,... | collective-permute-start | bytes 1376264 | tf_op jit(solution)/shard_map/ppermute | solution.py:776
  106.1 311.1 %reduce-scatter.2.cloned.1.call-start = ((), (), s32[]{:S(2)}) async-start(), calls=%async_computation.1 | async-start | bytes 8650752 | tf_op jit(solution)/shard_map/reduce_scatter | solution.py:917
  106.2 36.8 %collective-permute-start.18 = (bf16[4,160,1024]{2,1,0:T(8,128)(2,1)S(1)}, bf16[4,160,1024]{2,1,0:T(8,128)(2,1)}, u32[]{:S(2)}, u32[]{:S(2)}) collective-permute-start(bf16[4,160,1024]{2,1,0:T(8,128)(2,1)S(1)} %pad_maximum_fusion.refs_0_), channel_id=1, source_target_pairs={{0,1},{1,0},{2,3},{3,2},{4,5},{5,4},{6,7},{7,6},{8,9},{9,8},{10,11... | collective-permute-start | bytes 3932168 | tf_op jit(solution)/shard_map/ppermute | solution.py:776
  106.3 38.5 %collective-permute-start.20 = (bf16[4,160,1024]{2,1,0:T(8,128)(2,1)S(1)}, bf16[4,160,1024]{2,1,0:T(8,128)(2,1)}, u32[]{:S(2)}, u32[]{:S(2)}) collective-permute-start(bf16[4,160,1024]{2,1,0:T(8,128)(2,1)S(1)} %pad_maximum_fusion.refs_0_), channel_id=1, source_target_pairs={{0,2},{1,3},{2,0},{3,1},{4,6},{5,7},{6,4},{7,5},{8,10},{9,11},{10,... | collective-permute-start | bytes 3932168 | tf_op jit(solution)/shard_map/ppermute | solution.py:776
  106.7 38.1 %collective-permute-start.21 = (bf16[4,160,1024]{2,1,0:T(8,128)(2,1)S(1)}, bf16[4,160,1024]{2,1,0:T(8,128)(2,1)}, u32[]{:S(2)}, u32[]{:S(2)}) collective-permute-start(bf16[4,160,1024]{2,1,0:T(8,128)(2,1)S(1)} %pad_maximum_fusion.refs_0_), channel_id=1, source_target_pairs={{0,4},{4,0},{8,12},{12,8},{16,20},{20,16},{24,28},{28,24},{1,5},{5... | collective-permute-start | bytes 3932168 | tf_op jit(solution)/shard_map/ppermute | solution.py:776
  109.1 33.9 %collective-permute-start.19 = (bf16[1,256,1024]{2,1,0:T(8,128)(2,1)}, bf16[1,256,1024]{2,1,0:T(8,128)(2,1)}, u32[]{:S(2)}, u32[]{:S(2)}) collective-permute-start(bf16[1,256,1024]{2,1,0:T(8,128)(2,1)} %constant_dynamic-slice_fusion.10), channel_id=1, source_target_pairs={{0,1},{1,0},{2,3},{3,2},{4,5},{5,4},{6,7},{7,6},{8,9},{9,8},{10,11... | collective-permute-start | bytes 1572872 | tf_op jit(solution)/shard_map/ppermute | solution.py:776
  144.8 40.5 %collective-permute-start.24 = (bf16[4,160,1024]{2,1,0:T(8,128)(2,1)}, bf16[4,160,1024]{2,1,0:T(8,128)(2,1)S(1)}, u32[]{:S(2)}, u32[]{:S(2)}) collective-permute-start(bf16[4,160,1024]{2,1,0:T(8,128)(2,1)} %collective-permute-done.20.refs_2_), channel_id=1, source_target_pairs={{0,1},{1,0},{2,3},{3,2},{4,5},{5,4},{6,7},{7,6},{8,9},{9,8},{10,11... | collective-permute-start | bytes 3932168 | tf_op jit(solution)/shard_map/ppermute | solution.py:776
  144.8 40.5 %collective-permute-start.25 = (bf16[4,160,1024]{2,1,0:T(8,128)(2,1)}, bf16[4,160,1024]{2,1,0:T(8,128)(2,1)S(1)}, u32[]{:S(2)}, u32[]{:S(2)}) collective-permute-start(bf16[4,160,1024]{2,1,0:T(8,128)(2,1)} %collective-permute-done.21.refs_4_), channel_id=1, source_target_pairs={{0,1},{1,0},{2,3},{3,2},{4,5},{5,4},{6,7},{7,6},{8,9},{9,8},{10,11... | collective-permute-start | bytes 3932168 | tf_op jit(solution)/shard_map/ppermute | solution.py:776
  145.3 45.8 %collective-permute-start.26 = (bf16[4,160,1024]{2,1,0:T(8,128)(2,1)}, bf16[4,160,1024]{2,1,0:T(8,128)(2,1)S(1)}, u32[]{:S(2)}, u32[]{:S(2)}) collective-permute-start(bf16[4,160,1024]{2,1,0:T(8,128)(2,1)} %collective-permute-done.20.refs_2_), channel_id=1, source_target_pairs={{0,4},{4,0},{8,12},{12,8},{16,20},{20,16},{24,28},{28,24},{1,5},{5... | collective-permute-start | bytes 3932168 | tf_op jit(solution)/shard_map/ppermute | solution.py:776
  148.1 37.3 %collective-permute-start.23 = (bf16[1,256,1024]{2,1,0:T(8,128)(2,1)}, bf16[1,256,1024]{2,1,0:T(8,128)(2,1)S(1)}, u32[]{:S(2)}, u32[]{:S(2)}) collective-permute-start(bf16[1,256,1024]{2,1,0:T(8,128)(2,1)} %get-tuple-element.183), channel_id=1, source_target_pairs={{0,3},{1,2},{2,1},{3,0},{4,7},{5,6},{6,5},{7,4},{8,11},{9,10},{10,... | collective-permute-start | bytes 1572872 | tf_op jit(solution)/shard_map/ppermute | solution.py:776
  287.0 43.1 %collective-permute-start.31 = (bf16[4,2,2,160,1024]{4,3,0,2,1:T(8,128)(2,1)}, bf16[4,2,2,160,1024]{4,3,0,2,1:T(8,128)(2,1)}, u32[]{:S(2)}, u32[]{:S(2)}) collective-permute-start(bf16[4,2,2,160,1024]{4,3,0,2,1:T(8,128)(2,1)} %copy_bitcast_fusion), channel_id=1, source_target_pairs={{0,1},{1,0},{2,3},{3,2},{4,5},{5,4},{6,7},{7,6},{8,9},{9,8},{10,11... | collective-permute-start | bytes 15728648 | tf_op jit(solution)/shard_map/ppermute | solution.py:776
  287.7 20.6 %collective-permute-start.29 = (bf16[1,256,1024]{2,1,0:T(8,128)(2,1)S(1)}, bf16[1,256,1024]{2,1,0:T(8,128)(2,1)S(1)}, u32[]{:S(2)}, u32[]{:S(2)}) collective-permute-start(bf16[1,256,1024]{2,1,0:T(8,128)(2,1)S(1)} %get-tuple-element.181), channel_id=1, source_target_pairs={{0,2},{1,3},{2,0},{3,1},{4,6},{5,7},{6,4},{7,5},{8,10},{9,11},{10,... | collective-permute-start | bytes 1572872 | tf_op jit(solution)/shard_map/ppermute | solution.py:776
  287.7 42.3 %collective-permute-start.30 = (bf16[1,256,1024]{2,1,0:T(8,128)(2,1)S(1)}, bf16[1,256,1024]{2,1,0:T(8,128)(2,1)S(1)}, u32[]{:S(2)}, u32[]{:S(2)}) collective-permute-start(bf16[1,256,1024]{2,1,0:T(8,128)(2,1)S(1)} %get-tuple-element.180), channel_id=1, source_target_pairs={{0,3},{1,2},{2,1},{3,0},{4,7},{5,6},{6,5},{7,4},{8,11},{9,10},{10,... | collective-permute-start | bytes 1572872 | tf_op jit(solution)/shard_map/ppermute | solution.py:776
  339.0 32.3 %collective-permute-start.32 = (bf16[2,160,1024]{2,1,0:T(8,128)(2,1)S(1)}, bf16[2,160,1024]{2,1,0:T(8,128)(2,1)S(1)}, u32[]{:S(2)}, u32[]{:S(2)}) collective-permute-start(bf16[2,160,1024]{2,1,0:T(8,128)(2,1)S(1)} %get-tuple-element.193), channel_id=1, source_target_pairs={{0,2},{1,3},{2,0},{3,1},{4,6},{5,7},{6,4},{7,5},{8,10},{9,11},{10,... | collective-permute-start | bytes 1966088 | tf_op jit(solution)/shard_map/ppermute | solution.py:776
  340.6 30.6 %collective-permute-start.33 = (bf16[2,160,1024]{2,1,0:T(8,128)(2,1)S(1)}, bf16[2,160,1024]{2,1,0:T(8,128)(2,1)S(1)}, u32[]{:S(2)}, u32[]{:S(2)}) collective-permute-start(bf16[2,160,1024]{2,1,0:T(8,128)(2,1)S(1)} %get-tuple-element.192), channel_id=1, source_target_pairs={{0,4},{4,0},{8,12},{12,8},{16,20},{20,16},{24,28},{28,24},{1,5},{5... | collective-permute-start | bytes 1966088 | tf_op jit(solution)/shard_map/ppermute | solution.py:776
  373.7 40.8 %collective-permute-start.35 = (bf16[4,160,1024]{2,1,0:T(8,128)(2,1)}, bf16[4,160,1024]{2,1,0:T(8,128)(2,1)}, u32[]{:S(2)}, u32[]{:S(2)}) collective-permute-start(bf16[4,160,1024]{2,1,0:T(8,128)(2,1)} %fusion.9), channel_id=1, source_target_pairs={{0,4},{4,0},{8,12},{12,8},{16,20},{20,16},{24,28},{28,24},{1,5},{5... | collective-permute-start | bytes 3932168 | tf_op jit(solution)/shard_map/ppermute | solution.py:776
  381.8 32.7 %collective-permute-start.34 = (bf16[4,160,1024]{2,1,0:T(8,128)(2,1)S(1)}, bf16[4,160,1024]{2,1,0:T(8,128)(2,1)}, u32[]{:S(2)}, u32[]{:S(2)}) collective-permute-start(bf16[4,160,1024]{2,1,0:T(8,128)(2,1)S(1)} %fusion.8), channel_id=1, source_target_pairs={{0,2},{1,3},{2,0},{3,1},{4,6},{5,7},{6,4},{7,5},{8,10},{9,11},{10,... | collective-permute-start | bytes 3932168 | tf_op jit(solution)/shard_map/ppermute | solution.py:776
  435.0 25.6 %collective-permute-start.39 = (bf16[4,2,2,112,1024]{4,3,0,2,1:T(8,128)(2,1)}, bf16[4,2,2,112,1024]{4,3,0,2,1:T(8,128)(2,1)S(1)}, u32[]{:S(2)}, u32[]{:S(2)}) collective-permute-start(bf16[4,2,2,112,1024]{4,3,0,2,1:T(8,128)(2,1)} %copy_bitcast_fusion.1), channel_id=1, source_target_pairs={{0,1},{1,0},{2,3},{3,2},{4,5},{5,4},{6,7},{7,6},{8,9},{9,8},{10,11... | collective-permute-start | bytes 11010056 | tf_op jit(solution)/shard_map/ppermute | solution.py:776
  435.0 25.6 %collective-permute-start.37 = (bf16[160,1024]{1,0:T(8,128)(2,1)S(1)}, bf16[160,1024]{1,0:T(8,128)(2,1)}, u32[]{:S(2)}, u32[]{:S(2)}) collective-permute-start(bf16[160,1024]{1,0:T(8,128)(2,1)S(1)} %get-tuple-element.189), channel_id=1, source_target_pairs={{0,16},{4,20},{8,24},{12,28},{16,0},{20,4},{24,8},{28,12},{1,17},{... | collective-permute-start | bytes 983048 | tf_op jit(solution)/shard_map/ppermute | solution.py:776
  436.0 24.6 %collective-permute-start.38 = (bf16[160,1024]{1,0:T(8,128)(2,1)S(1)}, bf16[160,1024]{1,0:T(8,128)(2,1)}, u32[]{:S(2)}, u32[]{:S(2)}) collective-permute-start(bf16[160,1024]{1,0:T(8,128)(2,1)S(1)} %get-tuple-element.188), channel_id=1, source_target_pairs={{0,24},{4,28},{8,16},{12,20},{16,8},{20,12},{24,0},{28,4},{1,25},{... | collective-permute-start | bytes 983048 | tf_op jit(solution)/shard_map/ppermute | solution.py:776
  476.9 21.0 %collective-permute-start.43 = (bf16[4,112,1024]{2,1,0:T(8,128)(2,1)S(1)}, bf16[4,112,1024]{2,1,0:T(8,128)(2,1)S(1)}, u32[]{:S(2)}, u32[]{:S(2)}) collective-permute-start(bf16[4,112,1024]{2,1,0:T(8,128)(2,1)S(1)} %fusion.11), channel_id=1, source_target_pairs={{0,4},{4,0},{8,12},{12,8},{16,20},{20,16},{24,28},{28,24},{1,5},{5... | collective-permute-start | bytes 2752520 | tf_op jit(solution)/shard_map/ppermute | solution.py:776
  508.0 24.5 %collective-permute-start.46 = (bf16[1,256,1024]{2,1,0:T(8,128)(2,1)}, bf16[1,256,1024]{2,1,0:T(8,128)(2,1)}, u32[]{:S(2)}, u32[]{:S(2)}) collective-permute-start(bf16[1,256,1024]{2,1,0:T(8,128)(2,1)} %get-tuple-element.177), channel_id=1, source_target_pairs={{0,3},{1,2},{2,1},{3,0},{4,7},{5,6},{6,5},{7,4},{8,11},{9,10},{10,... | collective-permute-start | bytes 1572872 | tf_op jit(solution)/shard_map/ppermute | solution.py:776
  (61 other events, 873.3 us)
Sparse Core Ops, SparseCore 0:
  106.3 93.1 all-gather.2
  235.8 151.8 reduce-scatter.1

commit v5 on v4

--- a/solution.py
+++ b/solution.py
@@ -459,21 +459,20 @@
 def rms_inverse(value):
     return lax.rsqrt(jnp.mean(value * value, axis=1, keepdims=True) + epsilon)
 
-def pull_sequence(me, whole_ref, came, dst, sem):
+def pull_sequence(me, whole_ref, chip_ref, core_ref, dst, sem):
     rows = whole_ref.shape[1]
-    for mask, ref in enumerate((whole_ref,) + tuple(came)):
-        src = ref.at[me] if mask == 0 else ref.at[0]
+    for mask, src in enumerate((whole_ref.at[me], core_ref.at[0], chip_ref.at[me & 1], core_ref.at[1])):
         at = pl.multiple_of((me ^ mask) * rows, rows)
         pltpu.make_async_copy(src, dst.at[pl.ds(at, rows), :], sem).start()
 
-def qkv_kernel(ids_ref, x4_ref, c1_ref, c2_ref, c3_ref, *refs, masks):
+def qkv_kernel(ids_ref, x4_ref, chip_ref, core_ref, *refs, masks):
     gathered = refs[:len(masks)]
     bucket_ref = refs[len(masks)]
     x_out, h_out, q_out, k_out, v_out, w_out, gain_ref, t_ref, trev_ref, xs, hs, ps, ws, es, sems = refs[len(masks) + 1:]
     me, flat = ids_ref[0], ids_ref[1]
     width = xs.shape[1]
     own = width // es.shape[0]
-    pull_sequence(me, x4_ref, (c1_ref, c2_ref, c3_ref), xs, sems.at[0])
+    pull_sequence(me, x4_ref, chip_ref, core_ref, xs, sems.at[0])
     for ref, ids in zip(gathered, masks):
         for j, mask in enumerate(ids):
             shard = flat ^ mask
@@ -526,7 +525,7 @@
         functools.partial(qkv_kernel, masks=masks),
         out_shape=(mat,) * 5 + (jax.ShapeDtypeStruct((width, 3 * width), jnp.bfloat16), jax.ShapeDtypeStruct((8, width), jnp.float32),
                                 jax.ShapeDtypeStruct((heads, wide), jnp.float32), jax.ShapeDtypeStruct((heads, wide), jnp.float32)),
-        in_specs=[SM] + [ANY] * (4 + len(gathered)) + [VM],
+        in_specs=[SM] + [ANY] * (3 + len(gathered)) + [VM],
         out_specs=[ANY] * 6 + [VM] * 3,
         scratch_shapes=[vm(total, width), vm(total, width), vm(3, total, width), vm(width, 3 * width), vm(shards, 16, width), pltpu.SemaphoreType.DMA((6,))],
         compiler_params=pltpu.CompilerParams(vmem_limit_bytes=LIMIT),
@@ -540,12 +539,19 @@
     slope = half + 0.5 * v * (1.0 - t * t) * (root_coef * (1.0 + 3.0 * cubic_coef * v * v))
     return v * half, slope
 
-def ff_chunks(h2, h2t, gm, acc, gh2, ws_in, ws_back, st_in, st_back, gw_out, row_in, sems, before_add, cols=512):
+def by_core(core, keep, send, src, dst_rows, sem, lead=slice(None), src_rows=slice(None), lanes=slice(None)):
+    for parity in range(2):
+        @pl.when(core == parity)
+        def _():
+            for dst, at in ((keep, parity), (send, 1 - parity)):
+                pltpu.make_async_copy(src.at[lead, at, src_rows, lanes], dst.at[lead, dst_rows, lanes], sem).start()
+
+def ff_chunks(h2, h2t, gm, acc, gh2, ws_in, ws_back, st_in, st_back, row_in, emit, before_add, cols=512):
     steps = ws_in.shape[1] // cols
-    half = st_back.shape[1]
-    shards, own = st_in.shape[0], h2.shape[1] // st_in.shape[0]
-    wide = h2.shape[1] // cols
-    group = cols // half
+    half, width = st_back.shape[2:]
+    own = width // (2 * st_in.shape[0])
+    wide = width // cols
+    group = cols // (2 * half)
 
     def step(c, carry):
         at = pl.ds(pl.multiple_of(c * cols, cols), cols)
@@ -560,13 +566,13 @@
             before_add()
         acc[...] += _dot(active, wback)
         gh2[...] += _dot(gpre, win, NT)
-        rows_b = pl.ds(c * group, group)
-        st_back[rows_b, :, :] = _dot(active, gm[...], TN).astype(jnp.bfloat16).reshape(group, half, h2.shape[1])
-        pltpu.make_async_copy(st_back.at[rows_b, :, :], gw_out.at[rows_b, 0:half, :], sems.at[0]).start()
+        lead = pl.ds(c * group, group)
+        st_back[lead] = _dot(active, gm[...], TN).astype(jnp.bfloat16).reshape(group, 2, half, width)
+        emit(st_back, 0, lead=lead, dst_rows=slice(0, half))
         up = pl.multiple_of((c // wide) * own, own)
         lanes = pl.ds(pl.multiple_of((c % wide) * cols, cols), cols)
-        st_in[:, pl.ds(up, own), lanes] = _dot(h2t[...], gpre).astype(jnp.bfloat16).reshape(shards, own, cols)
-        pltpu.make_async_copy(st_in.at[:, pl.ds(up, own), lanes], gw_out.at[:, pl.ds(row_in + up, own), lanes], sems.at[1]).start()
+        st_in[:, :, pl.ds(up, own), lanes] = _dot(h2t[...], gpre).astype(jnp.bfloat16).reshape(-1, 2, own, cols)
+        emit(st_in, 1, src_rows=pl.ds(up, own), dst_rows=pl.ds(row_in + up, own), lanes=lanes)
         return carry
     lax.fori_loop(0, steps, step, 0)
 
@@ -589,13 +595,15 @@
             for i in range(ws_in.shape[1] // width):
                 pltpu.make_async_copy(ref.at[j, row_in + i * own:row_in + (i + 1) * own, :], ws_in.at[at, i * width:(i + 1) * width], sems.at[0]).start()
 
-def mid_a_kernel(ids_ref, x_hbm, o_hbm, g4_ref, c1_ref, c2_ref, c3_ref, gain_ref, *refs, masks):
+def mid_a_kernel(ids_ref, x_hbm, o_hbm, g4_ref, chip_ref, core_ref, gain_ref, *refs, masks):
     gathered = refs[:len(masks)]
     (mixed_out, acc_out, gh2_out, h2_out, h2t_out, gm_out, wo_out, gw_out,
      xs, os, wo, ws_in, ws_back, mixed, h2, h2t, acc, gh2, gm, st_in, st_back, sems) = refs[len(masks):]
     flat = ids_ref[1]
     rows, width = xs.shape
-    half, own = st_back.shape[1], width // st_in.shape[0]
+    half, own = st_back.shape[2], width // (2 * st_in.shape[0])
+    def emit(src, which, dst_rows, lead=slice(None), src_rows=slice(None), lanes=slice(None)):
+        pltpu.make_async_copy(src.at[lead, :, src_rows, lanes], gw_out.at[lead, :, dst_rows, lanes], sems.at[which]).start()
     loads = [pltpu.make_async_copy(x_hbm, xs, sems.at[0]), pltpu.make_async_copy(o_hbm, os, sems.at[1])]
     for load in loads:
         load.start()
@@ -604,7 +612,7 @@
             at = pl.ds(pl.multiple_of((flat ^ mask) * own, own), own)
             pltpu.make_async_copy(ref.at[j, half:half + own, :], wo.at[at, :], sems.at[2]).start()
     pull_ff(flat, gathered, masks, ws_in, ws_back, half + own, sems.at[3:5])
-    pull_sequence(ids_ref[0], g4_ref, (c1_ref, c2_ref, c3_ref), gm, sems.at[5])
+    pull_sequence(ids_ref[0], g4_ref, chip_ref, core_ref, gm, sems.at[5])
     for load in loads:
         load.wait()
     pltpu.make_async_copy(wo, wo, sems.at[2]).wait()
@@ -630,7 +638,7 @@
     for i, (src, dst) in enumerate(((mixed, mixed_out), (h2, h2_out), (h2t, h2t_out), (gm, gm_out))):
         stores.append(pltpu.make_async_copy(src, dst, sems.at[6 + i]))
         stores[-1].start()
-    ff_chunks(h2, h2t, gm, acc, gh2, ws_in, ws_back, st_in, st_back, gw_out, half, sems.at[0:2], lambda: None)
+    ff_chunks(h2, h2t, gm, acc, gh2, ws_in, ws_back, st_in, st_back, half, emit, lambda: None)
     for i, (src, dst) in enumerate(((acc, acc_out), (gh2, gh2_out))):
         stores.append(pltpu.make_async_copy(src, dst, sems.at[3 + i]))
         stores[-1].start()
@@ -649,20 +657,23 @@
     stack = half + ff // width * (width // shards)
     return pl.pallas_call(
         functools.partial(mid_a_kernel, masks=masks),
-        out_shape=(full(rows, width), full(rows, width), full(rows, width), low(rows, width), low(width, rows), low(rows, width), low(width, width), low(shards, stack, width)),
-        in_specs=[SM] + [ANY] * 6 + [VM] + [ANY] * len(gathered), out_specs=[ANY] * 8,
+        out_shape=(full(rows, width), full(rows, width), full(rows, width), low(rows, width), low(width, rows), low(rows, width), low(width, width), low(shards // 2, 2, stack, width)),
+        in_specs=[SM] + [ANY] * 5 + [VM] + [ANY] * len(gathered), out_specs=[ANY] * 8,
         scratch_shapes=[vm(rows, width), vm(rows, width), vm(width, width), vm(width, ff), vm(ff, width), vf(rows, width), vm(rows, width), vm(width, rows),
-                        vf(rows, width), vf(rows, width), vm(rows, width), vm(shards, stack - half, width), vm(shards, half, width), pltpu.SemaphoreType.DMA((10,))],
+                        vf(rows, width), vf(rows, width), vm(rows, width), vm(shards // 2, 2, stack - half, width), vm(shards // 2, 2, half, width), pltpu.SemaphoreType.DMA((10,))],
         compiler_params=pltpu.CompilerParams(vmem_limit_bytes=LIMIT),
         cost_estimate=LIGHT,
         name="mid_a",
     )(ids, x, o, g4, *came, gains, *gathered)
 
-def mid_b_kernel( gain_ref, mixed_hbm, acc_hbm, gh2_hbm, h2_hbm, h2t_hbm, gm_hbm, wo_hbm, o_hbm, full_ref, *refs):
-    (out_ref, gb_out, do_ref, gw_out,
+def mid_b_kernel(ids_ref, gain_ref, mixed_hbm, acc_hbm, gh2_hbm, h2_hbm, h2t_hbm, gm_hbm, wo_hbm, o_hbm, full_ref, *refs):
+    (out_ref, gb_out, do_ref, keep_out, send_out,
      os, wo, ws_in, ws_back, mixed, h2, h2t, acc, gh2, gm, gb, st_in, st_back, st_o, sems) = refs
     rows, width = os.shape
-    shards, half, own = st_in.shape[0], st_back.shape[1], width // st_in.shape[0]
+    shards, half, own = 2 * st_in.shape[0], st_back.shape[2], width // (2 * st_in.shape[0])
+    core = ids_ref[1] & 1
+    def emit(src, which, **at):
+        by_core(core, keep_out, send_out, src, sem=sems.at[which], **at)
     early = [(h2_hbm, h2), (gm_hbm, gm), (h2t_hbm, h2t)]
     late = [(acc_hbm, acc), (gh2_hbm, gh2), (mixed_hbm, mixed), (wo_hbm, wo), (o_hbm, os)]
     early = [pltpu.make_async_copy(a, b, sems.at[4 + i]) for i, (a, b) in enumerate(early)]
@@ -679,7 +690,7 @@
     def before_add():
         late[0].wait()
         late[1].wait()
-    ff_chunks(h2, h2t, gm, acc, gh2, ws_in, ws_back, st_in, st_back, gw_out, half + own, sems.at[0:2], before_add)
+    ff_chunks(h2, h2t, gm, acc, gh2, ws_in, ws_back, st_in, st_back, half + own, emit, before_add)
     for load in late[2:]:
         load.wait()
     part = 256
@@ -697,14 +708,14 @@
         return carry
     lax.fori_loop(0, rows // part, finish, 0)
     st_o[...] = _dot(os[...], gb[...], TN).astype(jnp.bfloat16).reshape(st_o.shape)
-    stores = [pltpu.make_async_copy(st_o, gw_out.at[:, half:half + own, :], sems.at[2]), pltpu.make_async_copy(gb, gb_out, sems.at[3])]
-    for store in stores:
-        store.start()
+    emit(st_o, 2, dst_rows=slice(half, half + own))
+    store = pltpu.make_async_copy(gb, gb_out, sems.at[3])
+    store.start()
     finish_chunks(st_in, st_back, sems.at[0:2])
-    for store in stores:
-        store.wait()
-
-def mid_b(gains, state, o, full, ff):
+    pltpu.make_async_copy(st_o, st_o, sems.at[2]).wait()
+    store.wait()
+
+def mid_b(ids, gains, state, o, full, ff):
     rows, width = o.shape
     shards = full.shape[0]
     half, own = ff // shards, width // shards
@@ -714,38 +725,46 @@
     rest = ff // width * own
     return pl.pallas_call(
         mid_b_kernel,
-        out_shape=(low(rows, width), low(rows, width), low(rows, width), low(shards, half + own + rest, width)),
-        in_specs=[VM] + [ANY] * 9, out_specs=[VM, ANY, VM, ANY],
+        out_shape=(low(rows, width), low(rows, width), low(rows, width), low(shards // 2, half + own + rest, width), low(shards // 2, half + own + rest, width)),
+        in_specs=[SM, VM] + [ANY] * 9, out_specs=[VM, ANY, VM, ANY, ANY],
         scratch_shapes=[vm(rows, width), vm(width, width), vm(width, ff), vm(ff, width), vf(rows, width), vm(rows, width), vm(width, rows),
-                        vf(rows, width), vf(rows, width), vm(rows, width), vm(rows, width), vm(shards, rest, width), vm(shards, half, width), vm(shards, own, width),
+                        vf(rows, width), vf(rows, width), vm(rows, width), vm(rows, width), vm(shards // 2, 2, rest, width), vm(shards // 2, 2, half, width), vm(shards // 2, 2, own, width),
                         pltpu.SemaphoreType.DMA((12,))],
         compiler_params=pltpu.CompilerParams(vmem_limit_bytes=LIMIT),
         cost_estimate=LIGHT,
         name="mid_b",
-    )(gains, *state, o, full)
-
-def gw_kernel(h_ref, dq_ref, dk_ref, dv_ref, bucket_ref, *refs):
-    out_ref = refs[-1]
-    shards, _, width = out_ref.shape
-    own = width // shards
-    for i, ref in enumerate((dq_ref, dk_ref, dv_ref)):
-        out_ref[:, i * own:(i + 1) * own, :] = _dot(h_ref[...], ref[...], TN).astype(jnp.bfloat16).reshape(shards, own, width)
-    offs = jnp.concatenate([ref[...] for ref in refs[:-1]], 0)
-    ids = lax.broadcasted_iota(jnp.int32, (shards, 1), 0)
+    )(ids, gains, *state, o, full)
+
+def gw_kernel(ids_ref, h_ref, dq_ref, dk_ref, dv_ref, bucket_ref, *refs):
+    keep_out, send_out, st, sems = refs[-4:]
+    offs = jnp.concatenate([ref[...] for ref in refs[:-4]], 0)
+    pairs, _, stack, width = st.shape
+    own = width // (2 * pairs)
+    core = ids_ref[1] & 1
+    ids = lax.broadcasted_iota(jnp.int32, (2 * pairs, 1), 0)
     hot = jnp.where(bucket_ref[1:2, :] == ids, 1.0, 0.0)
     table = lax.dot_general(hot, offs, NT, precision=lax.Precision.HIGHEST, preferred_element_type=jnp.float32)
-    out_ref[:, 3 * own:, :] = jnp.zeros((shards, 16, width), jnp.bfloat16)
-    out_ref[:, 3 * own:3 * own + 1, 0:offs.shape[0]] = table.astype(jnp.bfloat16).reshape(shards, 1, offs.shape[0])
-
-def qkv_gw(h, dq, dk, dv, bucket_rows, offs, shards):
+    heads = offs.shape[0]
+    st[:, :, 3 * own:, :] = jnp.zeros((pairs, 2, stack - 3 * own, width), jnp.bfloat16)
+    st[:, :, 3 * own:3 * own + 1, 0:heads] = table.astype(jnp.bfloat16).reshape(pairs, 2, 1, heads)
+    for i, ref in enumerate((dq_ref, dk_ref, dv_ref)):
+        at = slice(i * own, (i + 1) * own) if i < 2 else slice(i * own, stack)
+        st[:, :, i * own:(i + 1) * own, :] = _dot(h_ref[...], ref[...], TN).astype(jnp.bfloat16).reshape(pairs, 2, own, width)
+        by_core(core, keep_out, send_out, st, at, sems.at[0], src_rows=at)
+    pltpu.make_async_copy(st, st, sems.at[0]).wait()
+
+def qkv_gw(ids, h, dq, dk, dv, bucket_rows, offs, shards):
     rows, width = h.shape
+    stack = 3 * width // shards + 16
+    half = jax.ShapeDtypeStruct((shards // 2, stack, width), jnp.bfloat16)
     return pl.pallas_call(
-        gw_kernel, out_shape=jax.ShapeDtypeStruct((shards, 3 * width // shards + 16, width), jnp.bfloat16),
-        in_specs=[VM] * (5 + len(offs)), out_specs=VM,
+        gw_kernel, out_shape=(half, half),
+        in_specs=[SM] + [VM] * (5 + len(offs)), out_specs=[ANY, ANY],
+        scratch_shapes=[pltpu.VMEM((shards // 2, 2, stack, width), jnp.bfloat16), pltpu.SemaphoreType.DMA((1,))],
         compiler_params=pltpu.CompilerParams(vmem_limit_bytes=LIMIT),
         cost_estimate=LIGHT,
         name="qkv_gw",
-    )(h, dq, dk, dv, bucket_rows, *offs)
+    )(ids, h, dq, dk, dv, bucket_rows, *offs)
 
 def gx_kernel(x_ref, gb_ref, dq_ref, dk_ref, dv_ref, gain_ref, w_ref, out_ref):
     width = x_ref.shape[1]
@@ -776,8 +795,14 @@
     return lax.ppermute(value, axis, [(i, i ^ mask) for i in range(lax.axis_size(axis))])
 
 
-def send_blocks(blocks, me, masks=(1, 2, 3)):
-    return tuple(swap(lax.dynamic_index_in_dim(blocks, me ^ mask, 0), "seq", mask) for mask in masks)
+def send_chip(blocks, me):
+    return swap(lax.dynamic_slice_in_dim(blocks, 2 * (1 - me // 2), 2, 0), "seq", 2)
+
+
+def send_core(blocks, from_chip, me):
+    own = lax.dynamic_index_in_dim(blocks, me ^ 1, 0)
+    passed = lax.dynamic_index_in_dim(from_chip, 1 - me % 2, 0)
+    return swap(jnp.concatenate([own, passed], 0), "seq", 1)
 
 
 class Gather:
@@ -808,26 +833,31 @@
 
 
 class Scatter:
-    def __init__(self, grads, pos):
-        self.z, self.y, self.x, self.c = pos
-        self.grads = grads.reshape((4, 2, 2, 2) + grads.shape[1:])
-        self.sent = lax.dynamic_index_in_dim(self.grads, 1 - self.c, 3, keepdims=False)
+    def __init__(self, keep, send, pos, corner_y):
+        self.z, self.y, self.x = pos
+        cube = (4, 2, 2) + keep.shape[1:]
+        self.mine, self.sent, self.corner_y = keep.reshape(cube), send.reshape(cube), corner_y
         self.other = swap(self.sent, "seq", 1)
 
     def fold(self):
         pick = lambda v, at, axis: lax.dynamic_index_in_dim(v, at, axis, keepdims=False)
-        mine = pick(self.grads, self.c, 3)
         def quarter(dy, dx):
             cut = lambda v: pick(pick(v, self.y ^ dy, 1), self.x ^ dx, 1).astype(jnp.float32)
-            return (cut(mine) + cut(self.other)).astype(jnp.bfloat16)
+            return (cut(self.mine) + cut(self.other)).astype(jnp.bfloat16)
         far = quarter(1, 1)
         self.to_x, self.to_y, self.own = quarter(0, 1), quarter(1, 0), quarter(0, 0)
-        self.came_x, self.came_y = swap(far[:2], "seq", 2), swap(far[2:], "dp", 1)
+        if self.corner_y:
+            self.came_x, self.came_y = None, swap(far, "dp", 1)
+        else:
+            self.came_x, self.came_y = swap(far[:2], "seq", 2), swap(far[2:], "dp", 1)
 
     def turn(self):
         add = lambda a, b: (a.astype(jnp.float32) + b.astype(jnp.float32)).astype(jnp.bfloat16)
-        to_x = lax.dynamic_update_slice_in_dim(self.to_x, add(self.to_x[2:], self.came_y), 2, 0)
-        to_y = lax.dynamic_update_slice_in_dim(self.to_y, add(self.to_y[:2], self.came_x), 0, 0)
+        if self.corner_y:
+            to_x, to_y = add(self.to_x, self.came_y), self.to_y
+        else:
+            to_x = lax.dynamic_update_slice_in_dim(self.to_x, add(self.to_x[2:], self.came_y), 2, 0)
+            to_y = lax.dynamic_update_slice_in_dim(self.to_y, add(self.to_y[:2], self.came_x), 0, 0)
         self.sent = (to_x, to_y)
         self.came_x, self.came_y = swap(to_x, "seq", 2), swap(to_y, "dp", 1)
 
@@ -842,8 +872,8 @@
         return sum((c.astype(jnp.float32) for c in self.came), self.mine.astype(jnp.float32))
 
 
-def place(blocks, came, me):
-    for mask, block in enumerate(came, 1):
+def place(blocks, from_chip, from_core, me):
+    for mask, block in ((1, from_core[0:1]), (2, lax.dynamic_index_in_dim(from_chip, me % 2, 0)), (3, from_core[1:2])):
         blocks = lax.dynamic_update_slice_in_dim(blocks, block, me ^ mask, 0)
     return blocks
 
@@ -859,7 +889,7 @@
     me, dp = lax.axis_index("seq"), lax.axis_index("dp")
     shards = lax.axis_size("seq") * lax.axis_size("dp")
     flat = dp * parts + me
-    pos = (dp // 2, dp % 2, me // 2, me % 2)
+    pos = (dp // 2, dp % 2, me // 2)
     low = lambda v: v.astype(jnp.bfloat16)
     up = lambda v: v.astype(jnp.float32)
     own, ff_own = w_query.shape[0], w_back.shape[0]
@@ -880,78 +910,83 @@
     bucket_rows = jnp.stack([jnp.pad(buckets, (0, 1), constant_values=-1), jnp.pad(buckets[::-1], (0, 1), constant_values=-1)])
 
     g1 = Gather(shard1)
-    x_came = send_blocks(x4, me)
+    x_chip = send_chip(x4, me)
+    g2 = Gather(shard2)
     g1.fill()
-    g1.own, = tie(x_came, g1.own)
+    g1.own, = tie((x_chip, g2.sent[1], shard3), g1.own)
     g1.sides()
+    g1.x, g1.y = tie(g2.sent[2], g1.x, g1.y)
+    g1.corner_halves()
+    g2.fill()
     g1.take(g1.own, 0)
-    shard2, = tie(g1.own, shard2)
-    g2 = Gather(shard2)
-    g1.x, g1.y = tie((g2.sent[1], g1.pieces[1]), g1.x, g1.y)
-    g1.corner_halves()
+    g1.near, g1.far, g2.own = tie(g1.pieces[1], g1.near, g1.far, g2.own)
+    g2.sides()
+    g1.x, g1.y, x4_in = tie((g1.near, g1.far), g1.x, g1.y, x4)
     g1.take(g1.x, 2)
     g1.take(g1.y, 4)
-    g2.fill()
-    g1.near, g1.far, g2.own = tie((g1.pieces[3], g1.pieces[5]), g1.near, g1.far, g2.own)
-    g2.sides()
     g1.take(g1.near, 6, (0, 1))
     g1.take(g1.far, 6, (2, 3))
+    x_core = send_core(x4_in, x_chip, me)
     shard3, = tie((g1.near, g1.far), shard3)
     full3 = lax.all_gather(shard3, both, axis=0, tiled=False)
-    x, hidden, q, k, v, w_qkv, gains, t, t_back = qkv_fwd(ids, x4, x_came, *g1.all_pieces(), bucket_rows, HEADS)
+    x, hidden, q, k, v, w_qkv, gains, t, t_back = qkv_fwd(ids, x4, (x_chip, x_core), *g1.all_pieces(), bucket_rows, HEADS)
     pairs = HEADS // 2
     att = attn_fwd(length, q, k, v, t, 0, pairs // 2)
     g2.take(g2.own, 0)
-    g_core = send_blocks(g4, me, (1,))
-    g2.x, g2.y = tie((att[0], g2.pieces[1], g_core), g2.x, g2.y)
+    g2.x, g2.y = tie((att[0], g2.pieces[1]), g2.x, g2.y)
     g2.corner_y()
     g4_in, = tie(g2.x, g4)
-    g_came = g_core + send_blocks(g4_in, me, (2, 3))
+    g_chip = send_chip(g4_in, me)
     g2.take(g2.x, 2)
     g2.take(g2.y, 4)
     q_in, = tie((g2.x, g2.y), q)
     attended, lse = attn_fwd(length, q_in, k, v, t, pairs // 2, pairs // 2, att)
-    g2.corner, = tie((attended, g_came, g2.pieces[3], g2.pieces[5]), g2.corner)
+    g2.corner, g_chip = tie((attended, g2.pieces[3], g2.pieces[5]), g2.corner, g_chip)
     g2.take(g2.corner, 6)
-    *state, gw_a = mid_a(ids, x, attended, g4, g_came, gains, *g2.all_pieces(), ff)
+    g_core = send_core(g4, g_chip, me)
+    *state, gw_a = mid_a(ids, x, attended, g4, (g_chip, g_core), gains, *g2.all_pieces(), ff)
     r_a = lax.psum_scatter(gw_a.reshape(-1, width), both, scatter_dimension=0, tiled=True)
-    out, gb, g_att, gw2 = mid_b(gains, state, attended, full3, ff)
-    sc2 = Scatter(gw2, pos)
+    out, gb, g_att, keep2, send2 = mid_b(ids, gains, state, attended, full3, ff)
+    sc2 = Scatter(keep2, send2, pos, True)
     out4 = out.reshape(parts, rows, width)
-    out_came = send_blocks(out4, me)
+    out_chip = send_chip(out4, me)
     count = pairs // 4
     back = lambda first, g, prev: attn_bwd(length, q, k, v, g, attended, lse, t_back, first, count, prev)
-    g_att, = tie((sc2.sent, out), g_att)
     dq, dk, dv, off0 = back(0, g_att, None)
-    sc2.other, = tie((off0, out_came), sc2.other)
+    sc2.other, = tie(off0, sc2.other)
     sc2.fold()
     g_att, = tie((sc2.own, sc2.to_x, sc2.to_y), g_att)
     dq, dk, dv, off1 = back(count, g_att, (dq, dk, dv))
-    sc2.came_x, sc2.came_y = tie(off1, sc2.came_x, sc2.came_y)
+    sc2.came_y, sc2.to_x = tie((off1, out_chip), sc2.came_y, sc2.to_x)
     sc2.turn()
+    out4_in, out_chip = tie(sc2.sent, out4, out_chip)
+    out_core = send_core(out4_in, out_chip, me)
     g_att, = tie(sc2.sent, g_att)
     dq, dk, dv, off2 = back(2 * count, g_att, (dq, dk, dv))
     dq, dk, dv, off3 = back(3 * count, g_att, (dq, dk, dv))
-    sc2.came_x, sc2.came_y = tie(off3, sc2.came_x, sc2.came_y)
+    sc2.came_x, sc2.came_y = tie((off3, out_core), sc2.came_x, sc2.came_y)
     sc2.column()
     h_in, = tie((sc2.mine, r_a), hidden)
-    gw1 = qkv_gw(h_in, dq, dk, dv, bucket_rows, (off0, off1, off2, off3), shards)
-    sc1 = Scatter(gw1, pos)
-    gb_in, = tie(sc1.sent, gb)
+    keep1, send1 = qkv_gw(ids, h_in, dq, dk, dv, bucket_rows, (off0, off1, off2, off3), shards)
+    sc1 = Scatter(keep1, send1, pos, False)
+    gb_in, = tie(send1, gb)
     gx = qkv_gx(x, gb_in, dq, dk, dv, gains, w_qkv)
-    sc1.other, = tie((gx, sc2.came), sc1.other)
+    sc1.other, = tie(gx, sc1.other)
     sc1.fold()
-    out4, out_came = tie(sc1.own, out4, out_came)
-    layer_out = place(out4, out_came, me)
+    out4, out_chip, out_core = tie(sc1.own, out4, out_chip, out_core)
+    layer_out = place(out4, out_chip, out_core, me)
+    sc1.came_x, sc1.came_y = tie((layer_out, sc2.came), sc1.came_x, sc1.came_y)
     sc1.turn()
-    sc2.came = list(tie((sc1.sent, layer_out), *sc2.came))
+    sc2.came = list(tie(sc1.sent, *sc2.came))
     r2 = sc2.result()
     sc1.came_x, sc1.came_y = tie(r2, sc1.came_x, sc1.came_y)
     sc1.column()
     gx, = tie(sc1.mine, gx)
     gx4 = gx.reshape(parts, rows, width)
-    gx_came = send_blocks(gx4, me)
-    input_grad = place(gx4, gx_came, me)
+    gx_chip = send_chip(gx4, me)
+    gx_chip, = tie(sc1.came, gx_chip)
+    gx_core = send_core(gx4, gx_chip, me)
+    input_grad = place(gx4, gx_chip, gx_core, me)
     sc1.came = list(tie(input_grad, *sc1.came))
     r1, r_a = sc1.result(), up(r_a)
     join = lambda v: jnp.concatenate([v[i:i + own] for i in range(0, v.shape[0], own)], 1).reshape(own, shards, 1, half)

time: 560 us -> 519 us (0.927)
  starting transfers between devices: 65.6 us -> 42.1 us
  waiting for transfers between devices: 169 us -> 155 us
  local copies, waits for them, and re-layouts: 41.3 us -> 33.5 us
  other arithmetic: 35.4 us -> 41.6 us
    ppermute x50 -> x45, starting transfers between devices: 65.5 us -> 42.1 us  [swap(): lax.ppermute(value, axis, [(i, i ^ mask) for i in range(lax.axis_size(axi...]
    ppermute x50 -> x45, waiting for transfers between devices: 169 us -> 155 us  [swap(): lax.ppermute(value, axis, [(i, i ^ mask) for i in range(lax.axis_size(axi...]
    squeeze x2 -> x0, local copies, waits for them, and re-layouts: 10.2 us -> none  [__init__(): lax.dynamic_index_in_dim(self.grads, 1 - self.c, 3, keepdims=False)]
    convert_element_type x2 -> x5, other arithmetic: 11.9 us -> 17.6 us  [the longest x4 14.7 us: quarter(): return (cut(self.mine) + cut(self.other)).astype(jnp.bfloat16)]
  transfers between devices with their start and end apart: 52 -> 47, of which waited for: 23 -> 21; matrix products, arithmetic and copies ran while one was open for 10% -> 11% of each run, Pallas kernels for 38% -> 41%
where the time goes in v5:
time: 519 us; the launch traced here: 512 us
  Pallas kernels  224 us (43%)
  waiting for transfers between devices  155 us (30%)
  starting transfers between devices  42.1 us (8%)
  other arithmetic  41.6 us (8%)
  local copies, waits for them, and re-layouts  33.5 us (6%)
  between operations  15.5 us (3%)
    ppermute x45, waiting for transfers between devices, swap(): lax.ppermute(value, axis, [(i, i ^ mask) for i in range(lax.axis_size(axi...  155 us
    pallas_call x4, Pallas kernels, attn_bwd(): pl.pallas_call(functools.partial(bwd_kernel, rows=rows, seq_len=seq_len,...  65.8 us
    pallas_call x1, Pallas kernels, mid_b(): pl.pallas_call(mid_b_kernel, out_shape=(low(rows, width), low(rows, width...  45.3 us
    ppermute x45, starting transfers between devices, swap(): lax.ppermute(value, axis, [(i, i ^ mask) for i in range(lax.axis_size(axi...  42.1 us
    pallas_call x1, Pallas kernels, mid_a(): pl.pallas_call(functools.partial(mid_a_kernel, masks=masks), out_shape=(f...  39.7 us
    pallas_call x2, Pallas kernels, attn_fwd(): pl.pallas_call(functools.partial(fwd_kernel, rows=rows, seq_len=seq_len,...  33.2 us
    convert_element_type x4, other arithmetic, quarter(): return (cut(self.mine) + cut(self.other)).astype(jnp.bfloat16)  14.7 us
    pallas_call x1, Pallas kernels, qkv_gx(): pl.pallas_call(gx_kernel, out_shape=jax.ShapeDtypeStruct((total, width),...  14.3 us
  transfers between devices with their start and end apart: 47, of which 21 were waited for; matrix products, arithmetic and copies ran while one was open for 11% of the time, Pallas kernels for 41%

profile of v5, /device:TPU:0, one launch (start us, length us, event | category | flops | bytes accessed | tf_op | source)
XLA Modules:
  0.0 511.6 jit_solution(8736512726603271656)
XLA Ops:
  12.5 3.1 collective-permute-start.2
  23.0 3.0 slice_reduce_fusion
  28.2 6.7 %collective-permute-done.3 = bf16[1,112,1024]{2,1,0:T(8,128)(2,1)S(1)} collective-permute-done((bf16[1,112,1024]{2,1,0:T(8,128)(2,1)S(1)}, bf16[1,112,1024]{2,1,0:T(8,128)(2,1)S(1)}, u32[]{:S(2)}, u32[]{:S(2)}) %collective-permute-start.3) | collective-permute-done | bytes 229408 | tf_op jit(solution)/shard_map/ppermute | solution.py:795
  36.7 3.7 collective-permute-done.1
  40.5 4.8 collective-permute-done.chip_ref
  51.8 21.9 %collective-permute-done.6 = bf16[1,160,1024]{2,1,0:T(8,128)(2,1)S(1)} collective-permute-done((bf16[1,160,1024]{2,1,0:T(8,128)(2,1)S(1)}, bf16[1,160,1024]{2,1,0:T(8,128)(2,1)S(1)}, u32[]{:S(2)}, u32[]{:S(2)}) %collective-permute-start.6) | collective-permute-done | bytes 327712 | tf_op jit(solution)/shard_map/ppermute | solution.py:795
  78.3 7.3 %collective-permute-done.10.refs_8_ = bf16[2,112,1024]{2,1,0:T(8,128)(2,1)S(1)} collective-permute-done((bf16[2,112,1024]{2,1,0:T(8,128)(2,1)S(1)}, bf16[2,112,1024]{2,1,0:T(8,128)(2,1)S(1)}, u32[]{:S(2)}, u32[]{:S(2)}) %collective-permute-start.10) | collective-permute-done | bytes 458784 | tf_op jit(solution)/shard_map/ppermute | solution.py:795
  99.3 13.2 %qkv_fwd.1 = (bf16[1024,1024]{1,0:T(8,128)(2,1)}, bf16[1024,1024]{1,0:T(8,128)(2,1)}, bf16[1024,1024]{1,0:T(8,128)(2,1)}, bf16[1024,1024]{1,0:T(8,128)(2,1)}, bf...) custom-call(s32[3]{0:T(128)} %pad_add_fusion.1.ids_ref, ...), custom_call_target="tpu_custom_call" | custom-call | flops 1048576 | bytes 65536 | tf_op jit(solution)/shard_map/qkv_fwd/pallas_call | solution.py:524
  112.6 16.6 %attn_fwd.2 = (bf16[1024,1024]{1,0:T(8,128)(2,1)}, f32[8,1024,128]{2,1,0:T(8,128)}) custom-call(s32[1]{0:T(128)} %dynamic_slice.142.len_ref, bf16[1024,1024]{1,0:T(8,128)(2,1)} %get-tuple-element.116.q_ref, bf16[1024,1024]{1,0:T(8,128)(2,1)} %get-tuple-element.109.k_ref, bf16[1024,1024]{1,0:T(8,128)(2,1)} %get-tuple-element.110.v_ref, ...), custom_call_target="tpu_custom_call" | custom-call | flops 1048576 | bytes 65536 | tf_op jit(solution)/shard_map/attn_fwd/pallas_call | solution.py:360
  131.9 16.6 %attn_fwd.3 = (bf16[1024,1024]{1,0:T(8,128)(2,1)}, f32[8,1024,128]{2,1,0:T(8,128)}) custom-call(s32[1]{0:T(128)} %dynamic_slice.142.len_ref, bf16[1024,1024]{1,0:T(8,128)(2,1)} %get-tuple-element.116.q_ref, bf16[1024,1024]{1,0:T(8,128)(2,1)} %get-tuple-element.109.k_ref, ...), custom_call_target="tpu_custom_call", output_to_operand_aliasing={{0}: (5, {}), {1}: (6, {})} | custom-call | flops 1048576 | bytes 65536 | tf_op jit(solution)/shard_map/attn_fwd/pallas_call | solution.py:360
  148.6 22.8 %collective-permute-done.23.chip_ref = bf16[2,256,1024]{2,1,0:T(8,128)(2,1)S(1)} collective-permute-done((bf16[2,256,1024]{2,1,0:T(8,128)(2,1)}, bf16[2,256,1024]{2,1,0:T(8,128)(2,1)S(1)}, u32[]{:S(2)}, u32[]{:S(2)}) %collective-permute-start.23) | collective-permute-done | bytes 1048608 | tf_op jit(solution)/shard_map/ppermute | solution.py:795
  171.4 4.4 collective-permute-done.22.refs_6_
  176.5 4.4 collective-permute-done.24.core_ref
  182.4 39.7 %mid_a.1 = (f32[1024,1024]{1,0:T(8,128)}, f32[1024,1024]{1,0:T(8,128)}, f32[1024,1024]{1,0:T(8,128)}, bf16[1024,1024]{1,0:T(8,128)(2,1)}, bf16[1024,1024]{1,0:T(...) custom-call(s32[3]{0:T(128)} %pad_add_fusion.1.ids_ref, ...), custom_call_target="tpu_custom_call" | custom-call | flops 1048576 | bytes 65536 | tf_op jit(solution)/shard_map/mid_a/pallas_call | solution.py:658
  222.2 45.3 %mid_b.1 = (bf16[1024,1024]{1,0:T(8,128)(2,1)}, bf16[1024,1024]{1,0:T(8,128)(2,1)}, bf16[1024,1024]{1,0:T(8,128)(2,1)}, bf16[16,160,1024]{2,1,0:T(8,128)(2,1)}, bf16[16,160,1024]{2,1,0:T(8,128)(2,1)}) custom-call(s32[3]{0:T(128)} %pad_add_fusion.1.ids_ref, f32[8,1024]{1,0:T(8,128)} %get-tuple-element.106.gain_ref, ...), custom_call_target="tpu_custom_call" | custom-call | flops 1048576 | bytes 65536 | tf_op jit(solution)/shard_map/mid_b/pallas_call | solution.py:726
  267.6 16.2 %attn_bwd.4 = (bf16[1024,1024]{1,0:T(8,128)(2,1)}, bf16[1024,1024]{1,0:T(8,128)(2,1)}, bf16[1024,1024]{1,0:T(8,128)(2,1)}, f32[4,2048]{1,0:T(4,128)}) custom-call(s32[1]{0:T(128)} %dynamic_slice.142.len_ref, bf16[1024,1024]{1,0:T(8,128)(2,1)} %get-tuple-element.116.q_ref, bf16[1024,1024]{1,0:T(8,128)(2,1)} %get-tuple-element.109.k_ref, ...), custom_call_target="tpu_custom_call" | custom-call | flops 1048576 | bytes 65536 | tf_op jit(solution)/shard_map/attn_bwd/pallas_call | solution.py:439
  283.8 3.5 fusion.3
  290.1 6.4 %fusion.2 = (bf16[4,160,1024]{2,1,0:T(8,128)(2,1)}, bf16[4,160,1024]{2,1,0:T(8,128)(2,1)S(1)}, bf16[4,160,1024]{2,1,0:T(8,128)(2,1)S(1)}) fusion(s32[]{:T(128)S(6)} %select_n.159, s32[]{:T(128)S(6)} %select_n.155, bf16[4,2,2,160,1024]{4,3,2,1,0:T(8,128)(2,1)} %bitcast.97, s32[]{:T(128)S(6)} %select_n.153, s32[]{:T(128)S(6)} %select_n.157, ...), kind=kLoop, calls=%fused_computation.13 | loop fusion | flops 7864320 | bytes 11796496 | tf_op jit(solution)/shard_map/convert_element_type | solution.py:846
  298.1 16.6 %attn_bwd.5 = (bf16[1024,1024]{1,0:T(8,128)(2,1)}, bf16[1024,1024]{1,0:T(8,128)(2,1)}, bf16[1024,1024]{1,0:T(8,128)(2,1)}, f32[4,2048]{1,0:T(4,128)}) custom-call(s32[1]{0:T(128)} %dynamic_slice.142.len_ref, bf16[1024,1024]{1,0:T(8,128)(2,1)} %get-tuple-element.116.q_ref, ...), custom_call_target="tpu_custom_call", output_to_operand_aliasing={{0}: (8, {}), {1}: (9, {}), {2}: (10, {})} | custom-call | flops 1048576 | bytes 65536 | tf_op jit(solution)/shard_map/attn_bwd/pallas_call | solution.py:439
  314.6 23.1 %collective-permute-done.27 = bf16[2,256,1024]{2,1,0:T(8,128)(2,1)} collective-permute-done((bf16[2,256,1024]{2,1,0:T(8,128)(2,1)}, bf16[2,256,1024]{2,1,0:T(8,128)(2,1)}, u32[]{:S(2)}, u32[]{:S(2)}) %collective-permute-start.27) | collective-permute-done | bytes 1048608 | tf_op jit(solution)/shard_map/ppermute | solution.py:795
  337.8 2.9 add_convert_fusion.1
  343.1 16.4 %attn_bwd.6 = (bf16[1024,1024]{1,0:T(8,128)(2,1)}, bf16[1024,1024]{1,0:T(8,128)(2,1)}, bf16[1024,1024]{1,0:T(8,128)(2,1)}, f32[4,2048]{1,0:T(4,128)}) custom-call(s32[1]{0:T(128)} %dynamic_slice.142.len_ref, bf16[1024,1024]{1,0:T(8,128)(2,1)} %get-tuple-element.116.q_ref, ...), custom_call_target="tpu_custom_call", output_to_operand_aliasing={{0}: (8, {}), {1}: (9, {}), {2}: (10, {})} | custom-call | flops 1048576 | bytes 65536 | tf_op jit(solution)/shard_map/attn_bwd/pallas_call | solution.py:439
  359.5 16.7 %attn_bwd.7 = (bf16[1024,1024]{1,0:T(8,128)(2,1)}, bf16[1024,1024]{1,0:T(8,128)(2,1)}, bf16[1024,1024]{1,0:T(8,128)(2,1)}, f32[4,2048]{1,0:T(4,128)}) custom-call(s32[1]{0:T(128)} %dynamic_slice.142.len_ref, bf16[1024,1024]{1,0:T(8,128)(2,1)} %get-tuple-element.116.q_ref, ...), custom_call_target="tpu_custom_call", output_to_operand_aliasing={{0}: (8, {}), {1}: (9, {}), {2}: (10, {})} | custom-call | flops 1048576 | bytes 65536 | tf_op jit(solution)/shard_map/attn_bwd/pallas_call | solution.py:439
  376.2 13.2 %collective-permute-done.30 = bf16[4,160,1024]{2,1,0:T(8,128)(2,1)} collective-permute-done((bf16[4,160,1024]{2,1,0:T(8,128)(2,1)}, bf16[4,160,1024]{2,1,0:T(8,128)(2,1)}, u32[]{:S(2)}, u32[]{:S(2)}) %collective-permute-start.30) | collective-permute-done | bytes 1310752 | tf_op jit(solution)/shard_map/ppermute | solution.py:795
  391.7 12.1 %qkv_gw.1 = (bf16[16,112,1024]{2,1,0:T(8,128)(2,1)}, bf16[16,112,1024]{2,1,0:T(8,128)(2,1)}) custom-call(s32[3]{0:T(128)} %pad_add_fusion.1.ids_ref, bf16[1024,1024]{1,0:T(8,128)(2,1)} %get-tuple-element.159.h_ref, bf16[1024,1024]{1,0:T(8,128)(2,1)} %get-tuple-element.160.dq_ref, bf16[1024,1024]{1,0:T(8,128)(2,1)} %get-tuple-element.161.dk_ref, ...), custom_call_target="tpu_custom_call" | custom-call | flops 1048576 | bytes 65536 | tf_op jit(solution)/shard_map/qkv_gw/pallas_call | solution.py:760
  408.4 14.3 %qkv_gx.1 = bf16[1024,1024]{1,0:T(8,128)(2,1)} custom-call(bf16[1024,1024]{1,0:T(8,128)(2,1)} %get-tuple-element.107.x_hbm.x_ref, bf16[1024,1024]{1,0:T(8,128)(2,1)} %get-tuple-element.167.gb_ref, bf16[1024,1024]{1,0:T(8,128)(2,1)} %get-tuple-element.160.dq_ref, bf16[1024,1024]{1,0:T(8,128)(2,1)} %get-tuple-element.161.dk_ref, ...), custom_call_target="tpu_custom_call" | custom-call | flops 1048576 | bytes 65536 | tf_op jit(solution)/shard_map/qkv_gx/pallas_call | solution.py:784
  422.7 3.2 add_convert_fusion.8
  433.8 4.3 collective-permute-done.36
  444.1 16.4 %collective-permute-done.39 = bf16[4,112,1024]{2,1,0:T(8,128)(2,1)S(1)} collective-permute-done((bf16[4,112,1024]{2,1,0:T(8,128)(2,1)S(1)}, bf16[4,112,1024]{2,1,0:T(8,128)(2,1)S(1)}, u32[]{:S(2)}, u32[]{:S(2)}) %collective-permute-start.39) | collective-permute-done | bytes 917536 | tf_op jit(solution)/shard_map/ppermute | solution.py:795
  465.9 3.1 collective-permute-start.41
  474.9 9.4 %collective-permute-done.41 = bf16[112,1024]{1,0:T(8,128)(2,1)} collective-permute-done((bf16[112,1024]{1,0:T(8,128)(2,1)}, bf16[112,1024]{1,0:T(8,128)(2,1)}, u32[]{:S(2)}, u32[]{:S(2)}) %collective-permute-start.41) | collective-permute-done | bytes 229408 | tf_op jit(solution)/shard_map/ppermute | solution.py:795
  484.4 3.0 collective-permute-done.43
  (241 shorter events, 101.8 us)
Async XLA Ops:
  7.2 215.0 %all-gather.3.cloned.1.call-start = ((), (), s32[]{:S(2)}) async-start(), calls=%async_computation.2 | async-start | bytes 8650752 | tf_op jit(solution)/shard_map/all_gather | solution.py:931
  12.5 15.7 %collective-permute-start.2 = (bf16[1,112,1024]{2,1,0:T(8,128)(2,1)S(1)}, bf16[1,112,1024]{2,1,0:T(8,128)(2,1)S(1)}, u32[]{:S(2)}, u32[]{:S(2)}) collective-permute-start(bf16[1,112,1024]{2,1,0:T(8,128)(2,1)S(1)} %bitcast.104), channel_id=1, source_target_pairs={{0,8},{4,12},{8,0},{12,4},{16,24},{20,28},{24,16},{28,20},{1,9},{5... | collective-permute-start | bytes 688136 | tf_op jit(solution)/shard_map/ppermute | solution.py:795
  15.6 19.3 %collective-permute-start.3 = (bf16[1,112,1024]{2,1,0:T(8,128)(2,1)S(1)}, bf16[1,112,1024]{2,1,0:T(8,128)(2,1)S(1)}, u32[]{:S(2)}, u32[]{:S(2)}) collective-permute-start(bf16[1,112,1024]{2,1,0:T(8,128)(2,1)S(1)} %bitcast.105), channel_id=1, source_target_pairs={{0,16},{4,20},{8,24},{12,28},{16,0},{20,4},{24,8},{28,12},{1,17},{... | collective-permute-start | bytes 688136 | tf_op jit(solution)/shard_map/ppermute | solution.py:795
  18.2 17.4 %collective-permute-start.4 = (bf16[1,112,1024]{2,1,0:T(8,128)(2,1)S(1)}, bf16[1,112,1024]{2,1,0:T(8,128)(2,1)}, u32[]{:S(2)}, u32[]{:S(2)}) collective-permute-start(bf16[1,112,1024]{2,1,0:T(8,128)(2,1)S(1)} %bitcast.106), channel_id=1, source_target_pairs={{0,24},{4,28},{8,16},{12,20},{16,8},{20,12},{24,0},{28,4},{1,25},{... | collective-permute-start | bytes 688136 | tf_op jit(solution)/shard_map/ppermute | solution.py:795
  20.5 24.8 %collective-permute-start = (bf16[2,256,1024]{2,1,0:T(8,128)(2,1)}, bf16[2,256,1024]{2,1,0:T(8,128)(2,1)S(1)}, u32[]{:S(2)}, u32[]{:S(2)}) collective-permute-start(bf16[2,256,1024]{2,1,0:T(8,128)(2,1)} %constant_dynamic-slice_fusion.11), channel_id=1, source_target_pairs={{0,2},{1,3},{2,0},{3,1},{4,6},{5,7},{6,4},{7,5},{8,10},{9,11},{10,... | collective-permute-start | bytes 3145736 | tf_op jit(solution)/shard_map/ppermute | solution.py:795
  45.3 28.5 %collective-permute-start.7 = (bf16[4,112,1024]{2,1,0:T(8,128)(2,1)S(1)}, bf16[4,112,1024]{2,1,0:T(8,128)(2,1)S(1)}, u32[]{:S(2)}, u32[]{:S(2)}) collective-permute-start(bf16[4,112,1024]{2,1,0:T(8,128)(2,1)S(1)} %pad_maximum_fusion.6.refs_0_), channel_id=1, source_target_pairs={{0,2},{1,3},{2,0},{3,1},{4,6},{5,7},{6,4},{7,5},{8,10},{9,11},{10,... | collective-permute-start | bytes 2752520 | tf_op jit(solution)/shard_map/ppermute | solution.py:795
  46.8 27.0 %collective-permute-start.8 = (bf16[4,112,1024]{2,1,0:T(8,128)(2,1)S(1)}, bf16[4,112,1024]{2,1,0:T(8,128)(2,1)}, u32[]{:S(2)}, u32[]{:S(2)}) collective-permute-start(bf16[4,112,1024]{2,1,0:T(8,128)(2,1)S(1)} %pad_maximum_fusion.6.refs_0_), channel_id=1, source_target_pairs={{0,4},{4,0},{8,12},{12,8},{16,20},{20,16},{24,28},{28,24},{1,5},{5... | collective-permute-start | bytes 2752520 | tf_op jit(solution)/shard_map/ppermute | solution.py:795
  48.3 29.0 %collective-permute-start.5 = (bf16[4,112,1024]{2,1,0:T(8,128)(2,1)S(1)}, bf16[4,112,1024]{2,1,0:T(8,128)(2,1)S(1)}, u32[]{:S(2)}, u32[]{:S(2)}) collective-permute-start(bf16[4,112,1024]{2,1,0:T(8,128)(2,1)S(1)} %pad_maximum_fusion.6.refs_0_), channel_id=1, source_target_pairs={{0,1},{1,0},{2,3},{3,2},{4,5},{5,4},{6,7},{7,6},{8,9},{9,8},{10,11... | collective-permute-start | bytes 2752520 | tf_op jit(solution)/shard_map/ppermute | solution.py:795
  48.3 25.4 %collective-permute-start.6 = (bf16[1,160,1024]{2,1,0:T(8,128)(2,1)S(1)}, bf16[1,160,1024]{2,1,0:T(8,128)(2,1)S(1)}, u32[]{:S(2)}, u32[]{:S(2)}) collective-permute-start(bf16[1,160,1024]{2,1,0:T(8,128)(2,1)S(1)} %maximum_bitcast_fusion), channel_id=1, source_target_pairs={{0,16},{4,20},{8,24},{12,28},{16,0},{20,4},{24,8},{28,12},{1,17},{... | collective-permute-start | bytes 983048 | tf_op jit(solution)/shard_map/ppermute | solution.py:795
  49.9 26.1 %collective-permute-start.11 = (bf16[1,160,1024]{2,1,0:T(8,128)(2,1)S(1)}, bf16[1,160,1024]{2,1,0:T(8,128)(2,1)S(1)}, u32[]{:S(2)}, u32[]{:S(2)}) collective-permute-start(bf16[1,160,1024]{2,1,0:T(8,128)(2,1)S(1)} %maximum_bitcast_fusion), channel_id=1, source_target_pairs={{0,24},{4,28},{8,16},{12,20},{16,8},{20,12},{24,0},{28,4},{1,25},{... | collective-permute-start | bytes 983048 | tf_op jit(solution)/shard_map/ppermute | solution.py:795
  87.1 304.6 %reduce-scatter.2.cloned.1.call-start = ((), (), s32[]{:S(2)}) async-start(), calls=%async_computation.1 | async-start | bytes 8650752 | tf_op jit(solution)/shard_map/reduce_scatter | solution.py:948
  87.9 41.3 %collective-permute-start.17 = (bf16[4,160,1024]{2,1,0:T(8,128)(2,1)S(1)}, bf16[4,160,1024]{2,1,0:T(8,128)(2,1)S(1)}, u32[]{:S(2)}, u32[]{:S(2)}) collective-permute-start(bf16[4,160,1024]{2,1,0:T(8,128)(2,1)S(1)} %pad_maximum_fusion.refs_0_), channel_id=1, source_target_pairs={{0,1},{1,0},{2,3},{3,2},{4,5},{5,4},{6,7},{7,6},{8,9},{9,8},{10,11... | collective-permute-start | bytes 3932168 | tf_op jit(solution)/shard_map/ppermute | solution.py:795
  88.4 40.8 %collective-permute-start.18 = (bf16[4,160,1024]{2,1,0:T(8,128)(2,1)S(1)}, bf16[4,160,1024]{2,1,0:T(8,128)(2,1)}, u32[]{:S(2)}, u32[]{:S(2)}) collective-permute-start(bf16[4,160,1024]{2,1,0:T(8,128)(2,1)S(1)} %pad_maximum_fusion.refs_0_), channel_id=1, source_target_pairs={{0,2},{1,3},{2,0},{3,1},{4,6},{5,7},{6,4},{7,5},{8,10},{9,11},{10,... | collective-permute-start | bytes 3932168 | tf_op jit(solution)/shard_map/ppermute | solution.py:795
  91.3 37.8 %collective-permute-start.19 = (bf16[4,160,1024]{2,1,0:T(8,128)(2,1)S(1)}, bf16[4,160,1024]{2,1,0:T(8,128)(2,1)}, u32[]{:S(2)}, u32[]{:S(2)}) collective-permute-start(bf16[4,160,1024]{2,1,0:T(8,128)(2,1)S(1)} %pad_maximum_fusion.refs_0_), channel_id=1, source_target_pairs={{0,4},{4,0},{8,12},{12,8},{16,20},{20,16},{24,28},{28,24},{1,5},{5... | collective-permute-start | bytes 3932168 | tf_op jit(solution)/shard_map/ppermute | solution.py:795
  129.2 42.2 %collective-permute-start.20 = (bf16[4,160,1024]{2,1,0:T(8,128)(2,1)}, bf16[4,160,1024]{2,1,0:T(8,128)(2,1)}, u32[]{:S(2)}, u32[]{:S(2)}) collective-permute-start(bf16[4,160,1024]{2,1,0:T(8,128)(2,1)} %collective-permute-done.18.refs_2_), channel_id=1, source_target_pairs={{0,1},{1,0},{2,3},{3,2},{4,5},{5,4},{6,7},{7,6},{8,9},{9,8},{10,11... | collective-permute-start | bytes 3932168 | tf_op jit(solution)/shard_map/ppermute | solution.py:795
  129.4 42.0 %collective-permute-start.21 = (bf16[4,160,1024]{2,1,0:T(8,128)(2,1)}, bf16[4,160,1024]{2,1,0:T(8,128)(2,1)}, u32[]{:S(2)}, u32[]{:S(2)}) collective-permute-start(bf16[4,160,1024]{2,1,0:T(8,128)(2,1)} %collective-permute-done.19.refs_4_), channel_id=1, source_target_pairs={{0,1},{1,0},{2,3},{3,2},{4,5},{5,4},{6,7},{7,6},{8,9},{9,8},{10,11... | collective-permute-start | bytes 3932168 | tf_op jit(solution)/shard_map/ppermute | solution.py:795
  129.8 46.0 %collective-permute-start.22 = (bf16[4,160,1024]{2,1,0:T(8,128)(2,1)}, bf16[4,160,1024]{2,1,0:T(8,128)(2,1)}, u32[]{:S(2)}, u32[]{:S(2)}) collective-permute-start(bf16[4,160,1024]{2,1,0:T(8,128)(2,1)} %collective-permute-done.18.refs_2_), channel_id=1, source_target_pairs={{0,4},{4,0},{8,12},{12,8},{16,20},{20,16},{24,28},{28,24},{1,5},{5... | collective-permute-start | bytes 3932168 | tf_op jit(solution)/shard_map/ppermute | solution.py:795
  131.3 40.0 %collective-permute-start.23 = (bf16[2,256,1024]{2,1,0:T(8,128)(2,1)}, bf16[2,256,1024]{2,1,0:T(8,128)(2,1)S(1)}, u32[]{:S(2)}, u32[]{:S(2)}) collective-permute-start(bf16[2,256,1024]{2,1,0:T(8,128)(2,1)} %constant_dynamic-slice_fusion.8), channel_id=1, source_target_pairs={{0,2},{1,3},{2,0},{3,1},{4,6},{5,7},{6,4},{7,5},{8,10},{9,11},{10,... | collective-permute-start | bytes 3145736 | tf_op jit(solution)/shard_map/ppermute | solution.py:795
  267.5 16.3 %collective-permute-start.26 = (bf16[4,2,2,160,1024]{4,3,2,1,0:T(8,128)(2,1)}, bf16[4,2,2,160,1024]{4,3,2,1,0:T(8,128)(2,1)}, u32[]{:S(2)}, u32[]{:S(2)}) collective-permute-start(bf16[4,2,2,160,1024]{4,3,2,1,0:T(8,128)(2,1)} %bitcast.111), channel_id=1, source_target_pairs={{0,1},{1,0},{2,3},{3,2},{4,5},{5,4},{6,7},{7,6},{8,9},{9,8},{10,11... | collective-permute-start | bytes 15728648 | tf_op jit(solution)/shard_map/ppermute | solution.py:795
  287.3 50.5 %collective-permute-start.28 = (bf16[4,160,1024]{2,1,0:T(8,128)(2,1)}, bf16[4,160,1024]{2,1,0:T(8,128)(2,1)}, u32[]{:S(2)}, u32[]{:S(2)}) collective-permute-start(bf16[4,160,1024]{2,1,0:T(8,128)(2,1)} %fusion.3), channel_id=1, source_target_pairs={{0,4},{4,0},{8,12},{12,8},{16,20},{20,16},{24,28},{28,24},{1,5},{5... | collective-permute-start | bytes 3932168 | tf_op jit(solution)/shard_map/ppermute | solution.py:795
  289.8 48.0 %collective-permute-start.27 = (bf16[2,256,1024]{2,1,0:T(8,128)(2,1)}, bf16[2,256,1024]{2,1,0:T(8,128)(2,1)}, u32[]{:S(2)}, u32[]{:S(2)}) collective-permute-start(bf16[2,256,1024]{2,1,0:T(8,128)(2,1)} %constant_dynamic-slice_fusion.5), channel_id=1, source_target_pairs={{0,2},{1,3},{2,0},{3,1},{4,6},{5,7},{6,4},{7,5},{8,10},{9,11},{10,... | collective-permute-start | bytes 3145736 | tf_op jit(solution)/shard_map/ppermute | solution.py:795
  296.5 79.7 %collective-permute-start.31 = (bf16[4,160,1024]{2,1,0:T(8,128)(2,1)}, bf16[4,160,1024]{2,1,0:T(8,128)(2,1)S(1)}, u32[]{:S(2)}, u32[]{:S(2)}) collective-permute-start(bf16[4,160,1024]{2,1,0:T(8,128)(2,1)} %get-tuple-element.187), channel_id=1, source_target_pairs={{0,4},{4,0},{8,12},{12,8},{16,20},{20,16},{24,28},{28,24},{1,5},{5... | collective-permute-start | bytes 3932168 | tf_op jit(solution)/shard_map/ppermute | solution.py:795
  340.7 48.7 %collective-permute-start.30 = (bf16[4,160,1024]{2,1,0:T(8,128)(2,1)}, bf16[4,160,1024]{2,1,0:T(8,128)(2,1)}, u32[]{:S(2)}, u32[]{:S(2)}) collective-permute-start(bf16[4,160,1024]{2,1,0:T(8,128)(2,1)} %add_convert_fusion.1), channel_id=1, source_target_pairs={{0,2},{1,3},{2,0},{3,1},{4,6},{5,7},{6,4},{7,5},{8,10},{9,11},{10,... | collective-permute-start | bytes 3932168 | tf_op jit(solution)/shard_map/ppermute | solution.py:795
  343.1 33.1 %collective-permute-start.29 = (bf16[2,256,1024]{2,1,0:T(8,128)(2,1)}, bf16[2,256,1024]{2,1,0:T(8,128)(2,1)}, u32[]{:S(2)}, u32[]{:S(2)}) collective-permute-start(bf16[2,256,1024]{2,1,0:T(8,128)(2,1)} %pad_maximum_fusion.3), channel_id=1, source_target_pairs={{0,1},{1,0},{2,3},{3,2},{4,5},{5,4},{6,7},{7,6},{8,9},{9,8},{10,11... | collective-permute-start | bytes 3145736 | tf_op jit(solution)/shard_map/ppermute | solution.py:795
  403.8 18.8 %collective-permute-start.32 = (bf16[4,2,2,112,1024]{4,3,2,1,0:T(8,128)(2,1)}, bf16[4,2,2,112,1024]{4,3,2,1,0:T(8,128)(2,1)}, u32[]{:S(2)}, u32[]{:S(2)}) collective-permute-start(bf16[4,2,2,112,1024]{4,3,2,1,0:T(8,128)(2,1)} %bitcast.112), channel_id=1, source_target_pairs={{0,1},{1,0},{2,3},{3,2},{4,5},{5,4},{6,7},{7,6},{8,9},{9,8},{10,11... | collective-permute-start | bytes 11010056 | tf_op jit(solution)/shard_map/ppermute | solution.py:795
  403.9 29.8 %collective-permute-start.33 = (bf16[160,1024]{1,0:T(8,128)(2,1)S(1)}, bf16[160,1024]{1,0:T(8,128)(2,1)S(1)}, u32[]{:S(2)}, u32[]{:S(2)}) collective-permute-start(bf16[160,1024]{1,0:T(8,128)(2,1)S(1)} %get-tuple-element.195), channel_id=1, source_target_pairs={{0,8},{4,12},{8,0},{12,4},{16,24},{20,28},{24,16},{28,20},{1,9},{5... | collective-permute-start | bytes 983048 | tf_op jit(solution)/shard_map/ppermute | solution.py:795
  404.0 29.8 %collective-permute-start.34 = (bf16[160,1024]{1,0:T(8,128)(2,1)S(1)}, bf16[160,1024]{1,0:T(8,128)(2,1)S(1)}, u32[]{:S(2)}, u32[]{:S(2)}) collective-permute-start(bf16[160,1024]{1,0:T(8,128)(2,1)S(1)} %get-tuple-element.194), channel_id=1, source_target_pairs={{0,16},{4,20},{8,24},{12,28},{16,0},{20,4},{24,8},{28,12},{1,17},{... | collective-permute-start | bytes 983048 | tf_op jit(solution)/shard_map/ppermute | solution.py:795
  406.9 26.9 %collective-permute-start.35 = (bf16[160,1024]{1,0:T(8,128)(2,1)S(1)}, bf16[160,1024]{1,0:T(8,128)(2,1)S(1)}, u32[]{:S(2)}, u32[]{:S(2)}) collective-permute-start(bf16[160,1024]{1,0:T(8,128)(2,1)S(1)} %get-tuple-element.193), channel_id=1, source_target_pairs={{0,24},{4,28},{8,16},{12,20},{16,8},{20,12},{24,0},{28,4},{1,25},{... | collective-permute-start | bytes 983048 | tf_op jit(solution)/shard_map/ppermute | solution.py:795
  439.3 21.3 %collective-permute-start.39 = (bf16[4,112,1024]{2,1,0:T(8,128)(2,1)S(1)}, bf16[4,112,1024]{2,1,0:T(8,128)(2,1)S(1)}, u32[]{:S(2)}, u32[]{:S(2)}) collective-permute-start(bf16[4,112,1024]{2,1,0:T(8,128)(2,1)S(1)} %fusion.8), channel_id=1, source_target_pairs={{0,4},{4,0},{8,12},{12,8},{16,20},{20,16},{24,28},{28,24},{1,5},{5... | collective-permute-start | bytes 2752520 | tf_op jit(solution)/shard_map/ppermute | solution.py:795
  441.2 20.7 %collective-permute-start.38 = (bf16[4,112,1024]{2,1,0:T(8,128)(2,1)S(1)}, bf16[4,112,1024]{2,1,0:T(8,128)(2,1)S(1)}, u32[]{:S(2)}, u32[]{:S(2)}) collective-permute-start(bf16[4,112,1024]{2,1,0:T(8,128)(2,1)S(1)} %fusion.7), channel_id=1, source_target_pairs={{0,2},{1,3},{2,0},{3,1},{4,6},{5,7},{6,4},{7,5},{8,10},{9,11},{10,... | collective-permute-start | bytes 2752520 | tf_op jit(solution)/shard_map/ppermute | solution.py:795
  464.5 22.9 %collective-permute-start.43 = (bf16[2,256,1024]{2,1,0:T(8,128)(2,1)}, bf16[2,256,1024]{2,1,0:T(8,128)(2,1)}, u32[]{:S(2)}, u32[]{:S(2)}) collective-permute-start(bf16[2,256,1024]{2,1,0:T(8,128)(2,1)} %constant_dynamic-slice_fusion.1), channel_id=1, source_target_pairs={{0,2},{1,3},{2,0},{3,1},{4,6},{5,7},{6,4},{7,5},{8,10},{9,11},{10,... | collective-permute-start | bytes 3145736 | tf_op jit(solution)/shard_map/ppermute | solution.py:795
  465.9 18.5 %collective-permute-start.41 = (bf16[112,1024]{1,0:T(8,128)(2,1)}, bf16[112,1024]{1,0:T(8,128)(2,1)}, u32[]{:S(2)}, u32[]{:S(2)}) collective-permute-start(bf16[112,1024]{1,0:T(8,128)(2,1)} %get-tuple-element.198), channel_id=1, source_target_pairs={{0,16},{4,20},{8,24},{12,28},{16,0},{20,4},{24,8},{28,12},{1,17},{... | collective-permute-start | bytes 688136 | tf_op jit(solution)/shard_map/ppermute | solution.py:795
  (52 other events, 557.8 us)
Sparse Core Ops, SparseCore 0:
  87.2 97.5 all-gather.2
  222.2 155.8 reduce-scatter.1

commit v6 on v5

--- a/solution.py
+++ b/solution.py
@@ -737,30 +737,33 @@
 
 def gw_kernel(ids_ref, h_ref, dq_ref, dk_ref, dv_ref, bucket_ref, *refs):
     keep_out, send_out, st, sems = refs[-4:]
-    offs = jnp.concatenate([ref[...] for ref in refs[:-4]], 0)
-    pairs, _, stack, width = st.shape
-    own = width // (2 * pairs)
+    pairs, _, stack, cols = st.shape
+    own = h_ref.shape[1] // (2 * pairs)
     core = ids_ref[1] & 1
-    ids = lax.broadcasted_iota(jnp.int32, (2 * pairs, 1), 0)
-    hot = jnp.where(bucket_ref[1:2, :] == ids, 1.0, 0.0)
-    table = lax.dot_general(hot, offs, NT, precision=lax.Precision.HIGHEST, preferred_element_type=jnp.float32)
-    heads = offs.shape[0]
-    st[:, :, 3 * own:, :] = jnp.zeros((pairs, 2, stack - 3 * own, width), jnp.bfloat16)
-    st[:, :, 3 * own:3 * own + 1, 0:heads] = table.astype(jnp.bfloat16).reshape(pairs, 2, 1, heads)
+    if refs[:-4]:
+        offs = jnp.concatenate([ref[...] for ref in refs[:-4]], 0)
+        ids = lax.broadcasted_iota(jnp.int32, (2 * pairs, 1), 0)
+        hot = jnp.where(bucket_ref[1:2, :] == ids, 1.0, 0.0)
+        table = lax.dot_general(hot, offs, NT, precision=lax.Precision.HIGHEST, preferred_element_type=jnp.float32)
+        heads = offs.shape[0]
+        st[:, :, 3 * own:, :] = jnp.zeros((pairs, 2, stack - 3 * own, cols), jnp.bfloat16)
+        st[:, :, 3 * own:3 * own + 1, 0:heads] = table.astype(jnp.bfloat16).reshape(pairs, 2, 1, heads)
     for i, ref in enumerate((dq_ref, dk_ref, dv_ref)):
         at = slice(i * own, (i + 1) * own) if i < 2 else slice(i * own, stack)
-        st[:, :, i * own:(i + 1) * own, :] = _dot(h_ref[...], ref[...], TN).astype(jnp.bfloat16).reshape(pairs, 2, own, width)
+        st[:, :, i * own:(i + 1) * own, :] = _dot(h_ref[...], ref[...], TN).astype(jnp.bfloat16).reshape(pairs, 2, own, cols)
         by_core(core, keep_out, send_out, st, at, sems.at[0], src_rows=at)
     pltpu.make_async_copy(st, st, sems.at[0]).wait()
 
-def qkv_gw(ids, h, dq, dk, dv, bucket_rows, offs, shards):
+def qkv_gw(ids, h, dq, dk, dv, bucket_rows, offs, shards, first, cols):
     rows, width = h.shape
-    stack = 3 * width // shards + 16
-    half = jax.ShapeDtypeStruct((shards // 2, stack, width), jnp.bfloat16)
+    stack = 3 * width // shards + (16 if offs else 0)
+    half = jax.ShapeDtypeStruct((shards // 2, stack, cols), jnp.bfloat16)
+    part = pl.BlockSpec((rows, cols), lambda i: (0, first // cols))
+    whole = lambda a: pl.BlockSpec(a.shape, lambda i: (0, 0))
     return pl.pallas_call(
-        gw_kernel, out_shape=(half, half),
-        in_specs=[SM] + [VM] * (5 + len(offs)), out_specs=[ANY, ANY],
-        scratch_shapes=[pltpu.VMEM((shards // 2, 2, stack, width), jnp.bfloat16), pltpu.SemaphoreType.DMA((1,))],
+        gw_kernel, out_shape=(half, half), grid=(1,),
+        in_specs=[SM, whole(h), part, part, part, whole(bucket_rows)] + [whole(o) for o in offs], out_specs=[ANY, ANY],
+        scratch_shapes=[pltpu.VMEM((shards // 2, 2, stack, cols), jnp.bfloat16), pltpu.SemaphoreType.DMA((1,))],
         compiler_params=pltpu.CompilerParams(vmem_limit_bytes=LIMIT),
         cost_estimate=LIGHT,
         name="qkv_gw",
@@ -854,10 +857,11 @@
     def turn(self):
         add = lambda a, b: (a.astype(jnp.float32) + b.astype(jnp.float32)).astype(jnp.bfloat16)
         if self.corner_y:
-            to_x, to_y = add(self.to_x, self.came_y), self.to_y
+            to_y, = tie(self.came_y, self.to_y)
+            to_x = add(self.to_x, self.came_y)
         else:
-            to_x = lax.dynamic_update_slice_in_dim(self.to_x, add(self.to_x[2:], self.came_y), 2, 0)
-            to_y = lax.dynamic_update_slice_in_dim(self.to_y, add(self.to_y[:2], self.came_x), 0, 0)
+            to_x = jnp.concatenate([self.to_x[:2], add(self.to_x[2:], self.came_y)], 0)
+            to_y = jnp.concatenate([add(self.to_y[:2], self.came_x), self.to_y[2:]], 0)
         self.sent = (to_x, to_y)
         self.came_x, self.came_y = swap(to_x, "seq", 2), swap(to_y, "dp", 1)
 
@@ -957,46 +961,58 @@
     sc2.fold()
     g_att, = tie((sc2.own, sc2.to_x, sc2.to_y), g_att)
     dq, dk, dv, off1 = back(count, g_att, (dq, dk, dv))
-    sc2.came_y, sc2.to_x = tie((off1, out_chip), sc2.came_y, sc2.to_x)
+    sc2.came_y, = tie(off1, sc2.came_y)
     sc2.turn()
-    out4_in, out_chip = tie(sc2.sent, out4, out_chip)
-    out_core = send_core(out4_in, out_chip, me)
     g_att, = tie(sc2.sent, g_att)
     dq, dk, dv, off2 = back(2 * count, g_att, (dq, dk, dv))
+    cols = 128 * count
+    keep, send = qkv_gw(ids, hidden, dq, dk, dv, bucket_rows, (), shards, 0, 3 * cols)
+    sc1 = Scatter(keep, send, pos, False)
+    sc2.came_x, sc2.came_y = tie(keep, sc2.came_x, sc2.came_y)
+    sc2.column()
+    g_att, = tie((sc2.mine, out_chip), g_att)
+    out4_in, out_chip = tie(sc2.mine, out4, out_chip)
+    out_core = send_core(out4_in, out_chip, me)
     dq, dk, dv, off3 = back(3 * count, g_att, (dq, dk, dv))
-    sc2.came_x, sc2.came_y = tie((off3, out_core), sc2.came_x, sc2.came_y)
-    sc2.column()
-    h_in, = tie((sc2.mine, r_a), hidden)
-    keep1, send1 = qkv_gw(ids, h_in, dq, dk, dv, bucket_rows, (off0, off1, off2, off3), shards)
-    sc1 = Scatter(keep1, send1, pos, False)
-    gb_in, = tie(send1, gb)
+    sc1.other, = tie((off3, out_core), sc1.other)
+    sc1.fold()
+    h_in, = tie(sc1.own, hidden)
+    keep, send = qkv_gw(ids, h_in, dq, dk, dv, bucket_rows, (off0, off1, off2, off3), shards, 3 * cols, cols)
+    sc0 = Scatter(keep, send, pos, False)
+    gb_in, = tie(keep, gb)
     gx = qkv_gx(x, gb_in, dq, dk, dv, gains, w_qkv)
-    sc1.other, = tie(gx, sc1.other)
-    sc1.fold()
-    out4, out_chip, out_core = tie(sc1.own, out4, out_chip, out_core)
-    layer_out = place(out4, out_chip, out_core, me)
-    sc1.came_x, sc1.came_y = tie((layer_out, sc2.came), sc1.came_x, sc1.came_y)
-    sc1.turn()
-    sc2.came = list(tie(sc1.sent, *sc2.came))
-    r2 = sc2.result()
-    sc1.came_x, sc1.came_y = tie(r2, sc1.came_x, sc1.came_y)
-    sc1.column()
-    gx, = tie(sc1.mine, gx)
     gx4 = gx.reshape(parts, rows, width)
     gx_chip = send_chip(gx4, me)
-    gx_chip, = tie(sc1.came, gx_chip)
+    sc1.came_x, sc1.came_y = tie((gx, sc2.came), sc1.came_x, sc1.came_y)
+    sc1.turn()
+    sc0.other, r_a = tie(sc1.sent, sc0.other, r_a)
+    sc0.fold()
+    out4, out_chip, out_core = tie(sc0.own, out4, out_chip, out_core)
+    layer_out = place(out4, out_chip, out_core, me)
+    sc0.came_x, sc0.came_y = tie(layer_out, sc0.came_x, sc0.came_y)
+    sc0.turn()
+    sc2.came = list(tie(sc0.sent, *sc2.came))
+    r2, r_a = sc2.result(), up(r_a)
+    sc1.came_x, sc1.came_y = tie((r2, sc0.sent), sc1.came_x, sc1.came_y)
+    sc1.column()
+    sc0.came_x, sc0.came_y = tie(sc1.came[0], sc0.came_x, sc0.came_y)
+    sc0.column()
+    gx4, gx_chip = tie((sc0.came[0], sc1.came), gx4, gx_chip)
     gx_core = send_core(gx4, gx_chip, me)
     input_grad = place(gx4, gx_chip, gx_core, me)
-    sc1.came = list(tie(input_grad, *sc1.came))
-    r1, r_a = sc1.result(), up(r_a)
+    sc1.came = list(tie(sc0.came[0], *sc1.came))
+    sc0.came = list(tie(input_grad, *sc0.came))
+    r1, r0 = sc1.result(), sc0.result()
     join = lambda v: jnp.concatenate([v[i:i + own] for i in range(0, v.shape[0], own)], 1).reshape(own, shards, 1, half)
     g_in = jnp.concatenate([join(r_a[half:]), join(r2[half + own:])], 2).reshape(w_in.shape)
     g_back = jnp.concatenate([r_a[:half], r2[:half]], 0)
-    prod = up(shard1[:3 * own]) * r1[:3 * own]
+    table_row = r0[3 * own, :HEADS]
+    r1 = jnp.concatenate([r1, r0[:3 * own]], 1)
+    prod = up(shard1[:3 * own]) * r1
     g_gain1 = jnp.sum(prod[:own] + prod[own:2 * own] + prod[2 * own:], axis=1) / up(low(norm1_gain))
     g_gain2 = jnp.sum(up(low(w_in)) * g_in, axis=1) / up(low(norm2_gain))
     return (layer_out.reshape(tokens.shape), input_grad.reshape(tokens.shape), g_gain1, r1[:own], r1[own:2 * own], r1[2 * own:3 * own],
-            r2[half:half + own], r1[3 * own, :HEADS], g_gain2, g_in, g_back)
+            r2[half:half + own], table_row, g_gain2, g_in, g_back)
 
 
 def local_any(shape, tokens, *rest):

time: 519 us -> 556 us (1.071)
  waiting for transfers between devices: 155 us -> 171 us
  local copies, waits for them, and re-layouts: 33.5 us -> 41.9 us
  starting transfers between devices: 42.1 us -> 49.5 us
    ppermute x45 -> x53, waiting for transfers between devices: 155 us -> 171 us  [swap(): lax.ppermute(value, axis, [(i, i ^ mask) for i in range(lax.axis_size(axi...]
    ppermute x45 -> x53, starting transfers between devices: 42.1 us -> 49.4 us  [swap(): lax.ppermute(value, axis, [(i, i ^ mask) for i in range(lax.axis_size(axi...]
    pallas_call x1 -> x2, Pallas kernels: 12.1 us -> 14.5 us  [qkv_gw(): pl.pallas_call(gw_kernel, out_shape=(half, half), grid=(1,), in_specs=[SM...]
  transfers between devices with their start and end apart: 47 -> 55, of which waited for: 21 -> 21; matrix products, arithmetic and copies ran while one was open for 11% -> 13% of each run, Pallas kernels for 41% -> 41%
where the time goes in v6:
time: 556 us; the launch traced here: 549 us
  Pallas kernels  226 us (41%)
  waiting for transfers between devices  171 us (31%)
  starting transfers between devices  49.5 us (9%)
  other arithmetic  44.8 us (8%)
  local copies, waits for them, and re-layouts  41.9 us (8%)
  between operations  15.5 us (3%)
    ppermute x53, waiting for transfers between devices, swap(): lax.ppermute(value, axis, [(i, i ^ mask) for i in range(lax.axis_size(axi...  171 us
    pallas_call x4, Pallas kernels, attn_bwd(): pl.pallas_call(functools.partial(bwd_kernel, rows=rows, seq_len=seq_len,...  65.9 us
    ppermute x53, starting transfers between devices, swap(): lax.ppermute(value, axis, [(i, i ^ mask) for i in range(lax.axis_size(axi...  49.4 us
    pallas_call x1, Pallas kernels, mid_b(): pl.pallas_call(mid_b_kernel, out_shape=(low(rows, width), low(rows, width...  45.4 us
    pallas_call x1, Pallas kernels, mid_a(): pl.pallas_call(functools.partial(mid_a_kernel, masks=masks), out_shape=(f...  39.6 us
    pallas_call x2, Pallas kernels, attn_fwd(): pl.pallas_call(functools.partial(fwd_kernel, rows=rows, seq_len=seq_len,...  33.3 us
    pallas_call x2, Pallas kernels, qkv_gw(): pl.pallas_call(gw_kernel, out_shape=(half, half), grid=(1,), in_specs=[SM...  14.5 us
    pallas_call x1, Pallas kernels, qkv_gx(): pl.pallas_call(gx_kernel, out_shape=jax.ShapeDtypeStruct((total, width),...  14.2 us
  transfers between devices with their start and end apart: 55, of which 21 were waited for; matrix products, arithmetic and copies ran while one was open for 13% of the time, Pallas kernels for 41%

profile of v6, /device:TPU:0, one launch (start us, length us, event | category | flops | bytes accessed | tf_op | source)
XLA Modules:
  0.0 548.7 jit_solution(2035774404695945061)
XLA Ops:
  12.5 3.1 collective-permute-start.2
  23.0 3.0 slice_reduce_fusion
  28.2 6.7 %collective-permute-done.3 = bf16[1,112,1024]{2,1,0:T(8,128)(2,1)S(1)} collective-permute-done((bf16[1,112,1024]{2,1,0:T(8,128)(2,1)S(1)}, bf16[1,112,1024]{2,1,0:T(8,128)(2,1)S(1)}, u32[]{:S(2)}, u32[]{:S(2)}) %collective-permute-start.3) | collective-permute-done | bytes 229408 | tf_op jit(solution)/shard_map/ppermute | solution.py:798
  36.7 3.7 collective-permute-done.1
  40.5 4.8 collective-permute-done.chip_ref
  51.8 21.9 %collective-permute-done.6 = bf16[1,160,1024]{2,1,0:T(8,128)(2,1)S(1)} collective-permute-done((bf16[1,160,1024]{2,1,0:T(8,128)(2,1)S(1)}, bf16[1,160,1024]{2,1,0:T(8,128)(2,1)S(1)}, u32[]{:S(2)}, u32[]{:S(2)}) %collective-permute-start.6) | collective-permute-done | bytes 327712 | tf_op jit(solution)/shard_map/ppermute | solution.py:798
  78.3 7.3 %collective-permute-done.10.refs_8_ = bf16[2,112,1024]{2,1,0:T(8,128)(2,1)S(1)} collective-permute-done((bf16[2,112,1024]{2,1,0:T(8,128)(2,1)S(1)}, bf16[2,112,1024]{2,1,0:T(8,128)(2,1)S(1)}, u32[]{:S(2)}, u32[]{:S(2)}) %collective-permute-start.10) | collective-permute-done | bytes 458784 | tf_op jit(solution)/shard_map/ppermute | solution.py:798
  99.3 13.3 %qkv_fwd.1 = (bf16[1024,1024]{1,0:T(8,128)(2,1)}, bf16[1024,1024]{1,0:T(8,128)(2,1)}, bf16[1024,1024]{1,0:T(8,128)(2,1)}, bf16[1024,1024]{1,0:T(8,128)(2,1)}, bf...) custom-call(s32[3]{0:T(128)} %pad_add_fusion.1.ids_ref, ...), custom_call_target="tpu_custom_call" | custom-call | flops 1048576 | bytes 65536 | tf_op jit(solution)/shard_map/qkv_fwd/pallas_call | solution.py:524
  112.6 16.7 %attn_fwd.2 = (bf16[1024,1024]{1,0:T(8,128)(2,1)}, f32[8,1024,128]{2,1,0:T(8,128)}) custom-call(s32[1]{0:T(128)} %dynamic_slice.189.len_ref, bf16[1024,1024]{1,0:T(8,128)(2,1)} %get-tuple-element.129.q_ref, bf16[1024,1024]{1,0:T(8,128)(2,1)} %get-tuple-element.120.k_ref, bf16[1024,1024]{1,0:T(8,128)(2,1)} %get-tuple-element.121.v_ref, ...), custom_call_target="tpu_custom_call" | custom-call | flops 1048576 | bytes 65536 | tf_op jit(solution)/shard_map/attn_fwd/pallas_call | solution.py:360
  132.1 16.7 %attn_fwd.3 = (bf16[1024,1024]{1,0:T(8,128)(2,1)}, f32[8,1024,128]{2,1,0:T(8,128)}) custom-call(s32[1]{0:T(128)} %dynamic_slice.189.len_ref, bf16[1024,1024]{1,0:T(8,128)(2,1)} %get-tuple-element.129.q_ref, bf16[1024,1024]{1,0:T(8,128)(2,1)} %get-tuple-element.120.k_ref, ...), custom_call_target="tpu_custom_call", output_to_operand_aliasing={{0}: (5, {}), {1}: (6, {})} | custom-call | flops 1048576 | bytes 65536 | tf_op jit(solution)/shard_map/attn_fwd/pallas_call | solution.py:360
  148.8 22.8 %collective-permute-done.23.chip_ref = bf16[2,256,1024]{2,1,0:T(8,128)(2,1)S(1)} collective-permute-done((bf16[2,256,1024]{2,1,0:T(8,128)(2,1)}, bf16[2,256,1024]{2,1,0:T(8,128)(2,1)S(1)}, u32[]{:S(2)}, u32[]{:S(2)}) %collective-permute-start.23) | collective-permute-done | bytes 1048608 | tf_op jit(solution)/shard_map/ppermute | solution.py:798
  171.6 4.4 collective-permute-done.22.refs_6_
  176.7 4.1 collective-permute-done.24.core_ref
  182.6 39.6 %mid_a.1 = (f32[1024,1024]{1,0:T(8,128)}, f32[1024,1024]{1,0:T(8,128)}, f32[1024,1024]{1,0:T(8,128)}, bf16[1024,1024]{1,0:T(8,128)(2,1)}, bf16[1024,1024]{1,0:T(...) custom-call(s32[3]{0:T(128)} %pad_add_fusion.1.ids_ref, ...), custom_call_target="tpu_custom_call" | custom-call | flops 1048576 | bytes 65536 | tf_op jit(solution)/shard_map/mid_a/pallas_call | solution.py:658
  222.3 45.4 %mid_b.1 = (bf16[1024,1024]{1,0:T(8,128)(2,1)}, bf16[1024,1024]{1,0:T(8,128)(2,1)}, bf16[1024,1024]{1,0:T(8,128)(2,1)}, bf16[16,160,1024]{2,1,0:T(8,128)(2,1)}, bf16[16,160,1024]{2,1,0:T(8,128)(2,1)}) custom-call(s32[3]{0:T(128)} %pad_add_fusion.1.ids_ref, f32[8,1024]{1,0:T(8,128)} %get-tuple-element.122.gain_ref, ...), custom_call_target="tpu_custom_call" | custom-call | flops 1048576 | bytes 65536 | tf_op jit(solution)/shard_map/mid_b/pallas_call | solution.py:726
  267.8 16.2 %attn_bwd.4 = (bf16[1024,1024]{1,0:T(8,128)(2,1)}, bf16[1024,1024]{1,0:T(8,128)(2,1)}, bf16[1024,1024]{1,0:T(8,128)(2,1)}, f32[4,2048]{1,0:T(4,128)}) custom-call(s32[1]{0:T(128)} %dynamic_slice.189.len_ref, bf16[1024,1024]{1,0:T(8,128)(2,1)} %get-tuple-element.129.q_ref, bf16[1024,1024]{1,0:T(8,128)(2,1)} %get-tuple-element.120.k_ref, ...), custom_call_target="tpu_custom_call" | custom-call | flops 1048576 | bytes 65536 | tf_op jit(solution)/shard_map/attn_bwd/pallas_call | solution.py:439
  284.0 3.3 fusion.3
  287.9 5.6 %fusion.2 = (bf16[4,160,1024]{2,1,0:T(8,128)(2,1)S(1)}, bf16[4,160,1024]{2,1,0:T(8,128)(2,1)S(1)}, bf16[4,160,1024]{2,1,0:T(8,128)(2,1)S(1)}) fusion(s32[]{:T(128)S(6)} %select_n.182, s32[]{:T(128)S(6)} %select_n.180, bf16[4,2,2,160,1024]{4,3,2,1,0:T(8,128)(2,1)} %bitcast.139, s32[]{:T(128)S(6)} %select_n.176, s32[]{:T(128)S(6)} %select_n.178, ...), kind=kLoop, calls=%fused_computation.8 | loop fusion | flops 7864320 | bytes 11796496 | tf_op jit(solution)/shard_map/convert_element_type | solution.py:849
  293.5 16.7 %attn_bwd.5 = (bf16[1024,1024]{1,0:T(8,128)(2,1)}, bf16[1024,1024]{1,0:T(8,128)(2,1)}, bf16[1024,1024]{1,0:T(8,128)(2,1)}, f32[4,2048]{1,0:T(4,128)}) custom-call(s32[1]{0:T(128)} %dynamic_slice.189.len_ref, bf16[1024,1024]{1,0:T(8,128)(2,1)} %get-tuple-element.129.q_ref, ...), custom_call_target="tpu_custom_call", output_to_operand_aliasing={{0}: (8, {}), {1}: (9, {}), {2}: (10, {})} | custom-call | flops 1048576 | bytes 65536 | tf_op jit(solution)/shard_map/attn_bwd/pallas_call | solution.py:439
  310.2 19.9 %collective-permute-done.27 = bf16[4,160,1024]{2,1,0:T(8,128)(2,1)} collective-permute-done((bf16[4,160,1024]{2,1,0:T(8,128)(2,1)}, bf16[4,160,1024]{2,1,0:T(8,128)(2,1)}, u32[]{:S(2)}, u32[]{:S(2)}) %collective-permute-start.27) | collective-permute-done | bytes 1310752 | tf_op jit(solution)/shard_map/ppermute | solution.py:798
  338.6 16.6 %attn_bwd.6 = (bf16[1024,1024]{1,0:T(8,128)(2,1)}, bf16[1024,1024]{1,0:T(8,128)(2,1)}, bf16[1024,1024]{1,0:T(8,128)(2,1)}, f32[4,2048]{1,0:T(4,128)}) custom-call(s32[1]{0:T(128)} %dynamic_slice.189.len_ref, bf16[1024,1024]{1,0:T(8,128)(2,1)} %get-tuple-element.129.q_ref, ...), custom_call_target="tpu_custom_call", output_to_operand_aliasing={{0}: (8, {}), {1}: (9, {}), {2}: (10, {})} | custom-call | flops 1048576 | bytes 65536 | tf_op jit(solution)/shard_map/attn_bwd/pallas_call | solution.py:439
  355.2 9.3 %qkv_gw.2 = (bf16[16,96,768]{2,1,0:T(8,128)(2,1)}, bf16[16,96,768]{2,1,0:T(8,128)(2,1)}) custom-call(s32[3]{0:T(128)} %pad_add_fusion.1.ids_ref, bf16[1024,1024]{1,0:T(8,128)(2,1)} %get-tuple-element.174.h_ref, bf16[1024,1024]{1,0:T(8,128)(2,1)} %get-tuple-element.161.dq_ref.refs_0_, bf16[1024,1024]{1,0:T(8,128)(2,1)} %get-tuple-element.162.dk_ref.refs_1_, ...), custom_call_target="tpu_custom_call" | custom-call | flops 1048576 | bytes 65536 | tf_op jit(solution)/shard_map/qkv_gw/pallas_call | solution.py:763
  364.5 3.3 copy.44
  367.8 6.9 %collective-permute-done.29 = bf16[4,160,1024]{2,1,0:T(8,128)(2,1)} collective-permute-done((bf16[4,160,1024]{2,1,0:T(8,128)(2,1)S(1)}, bf16[4,160,1024]{2,1,0:T(8,128)(2,1)}, u32[]{:S(2)}, u32[]{:S(2)}) %collective-permute-start.29) | collective-permute-done | bytes 1310752 | tf_op jit(solution)/shard_map/ppermute | solution.py:798
  374.7 9.9 %collective-permute-done.28 = bf16[4,160,1024]{2,1,0:T(8,128)(2,1)} collective-permute-done((bf16[4,160,1024]{2,1,0:T(8,128)(2,1)}, bf16[4,160,1024]{2,1,0:T(8,128)(2,1)}, u32[]{:S(2)}, u32[]{:S(2)}) %collective-permute-start.28) | collective-permute-done | bytes 1310752 | tf_op jit(solution)/shard_map/ppermute | solution.py:798
  388.0 18.6 %collective-permute-done.30 = bf16[2,256,1024]{2,1,0:T(8,128)(2,1)} collective-permute-done((bf16[2,256,1024]{2,1,0:T(8,128)(2,1)}, bf16[2,256,1024]{2,1,0:T(8,128)(2,1)}, u32[]{:S(2)}, u32[]{:S(2)}) %collective-permute-start.30) | collective-permute-done | bytes 1048608 | tf_op jit(solution)/shard_map/ppermute | solution.py:798
  409.5 3.0 collective-permute-start.35
  412.5 16.5 %attn_bwd.7 = (bf16[1024,1024]{1,0:T(8,128)(2,1)}, bf16[1024,1024]{1,0:T(8,128)(2,1)}, bf16[1024,1024]{1,0:T(8,128)(2,1)}, f32[4,2048]{1,0:T(4,128)}) custom-call(s32[1]{0:T(128)} %dynamic_slice.189.len_ref, bf16[1024,1024]{1,0:T(8,128)(2,1)} %get-tuple-element.129.q_ref, ...), custom_call_target="tpu_custom_call", output_to_operand_aliasing={{0}: (8, {}), {1}: (9, {}), {2}: (10, {})} | custom-call | flops 1048576 | bytes 65536 | tf_op jit(solution)/shard_map/attn_bwd/pallas_call | solution.py:439
  433.1 5.2 qkv_gw.3
  439.6 14.2 %qkv_gx.1 = bf16[1024,1024]{1,0:T(8,128)(2,1)} custom-call(bf16[1024,1024]{1,0:T(8,128)(2,1)} %get-tuple-element.123.x_hbm.x_ref, bf16[1024,1024]{1,0:T(8,128)(2,1)} %get-tuple-element.181.gb_ref, bf16[1024,1024]{1,0:T(8,128)(2,1)} %get-tuple-element.175.dq_ref, bf16[1024,1024]{1,0:T(8,128)(2,1)} %get-tuple-element.176.dk_ref, ...), custom_call_target="tpu_custom_call" | custom-call | flops 1048576 | bytes 65536 | tf_op jit(solution)/shard_map/qkv_gx/pallas_call | solution.py:787
  470.9 26.1 %collective-permute-done.39 = bf16[2,112,256]{2,1,0:T(8,128)(2,1)S(1)} collective-permute-done((bf16[2,112,256]{2,1,0:T(8,128)(2,1)S(1)}, bf16[2,112,256]{2,1,0:T(8,128)(2,1)S(1)}, u32[]{:S(2)}, u32[]{:S(2)}) %collective-permute-start.39) | collective-permute-done | bytes 114720 | tf_op jit(solution)/shard_map/ppermute | solution.py:798
  508.0 5.0 collective-permute-done.43
  (281 shorter events, 123.6 us)
Async XLA Ops:
  7.2 215.1 %all-gather.3.cloned.1.call-start = ((), (), s32[]{:S(2)}) async-start(), calls=%async_computation.2 | async-start | bytes 8650752 | tf_op jit(solution)/shard_map/all_gather | solution.py:935
  20.5 24.8 %collective-permute-start = (bf16[2,256,1024]{2,1,0:T(8,128)(2,1)}, bf16[2,256,1024]{2,1,0:T(8,128)(2,1)S(1)}, u32[]{:S(2)}, u32[]{:S(2)}) collective-permute-start(bf16[2,256,1024]{2,1,0:T(8,128)(2,1)} %constant_dynamic-slice_fusion.11), channel_id=1, source_target_pairs={{0,2},{1,3},{2,0},{3,1},{4,6},{5,7},{6,4},{7,5},{8,10},{9,11},{10,... | collective-permute-start | bytes 3145736 | tf_op jit(solution)/shard_map/ppermute | solution.py:798
  45.3 28.5 %collective-permute-start.7 = (bf16[4,112,1024]{2,1,0:T(8,128)(2,1)S(1)}, bf16[4,112,1024]{2,1,0:T(8,128)(2,1)S(1)}, u32[]{:S(2)}, u32[]{:S(2)}) collective-permute-start(bf16[4,112,1024]{2,1,0:T(8,128)(2,1)S(1)} %pad_maximum_fusion.6.refs_0_), channel_id=1, source_target_pairs={{0,2},{1,3},{2,0},{3,1},{4,6},{5,7},{6,4},{7,5},{8,10},{9,11},{10,... | collective-permute-start | bytes 2752520 | tf_op jit(solution)/shard_map/ppermute | solution.py:798
  46.8 27.0 %collective-permute-start.8 = (bf16[4,112,1024]{2,1,0:T(8,128)(2,1)S(1)}, bf16[4,112,1024]{2,1,0:T(8,128)(2,1)}, u32[]{:S(2)}, u32[]{:S(2)}) collective-permute-start(bf16[4,112,1024]{2,1,0:T(8,128)(2,1)S(1)} %pad_maximum_fusion.6.refs_0_), channel_id=1, source_target_pairs={{0,4},{4,0},{8,12},{12,8},{16,20},{20,16},{24,28},{28,24},{1,5},{5... | collective-permute-start | bytes 2752520 | tf_op jit(solution)/shard_map/ppermute | solution.py:798
  48.3 29.0 %collective-permute-start.5 = (bf16[4,112,1024]{2,1,0:T(8,128)(2,1)S(1)}, bf16[4,112,1024]{2,1,0:T(8,128)(2,1)S(1)}, u32[]{:S(2)}, u32[]{:S(2)}) collective-permute-start(bf16[4,112,1024]{2,1,0:T(8,128)(2,1)S(1)} %pad_maximum_fusion.6.refs_0_), channel_id=1, source_target_pairs={{0,1},{1,0},{2,3},{3,2},{4,5},{5,4},{6,7},{7,6},{8,9},{9,8},{10,11... | collective-permute-start | bytes 2752520 | tf_op jit(solution)/shard_map/ppermute | solution.py:798
  48.3 25.4 %collective-permute-start.6 = (bf16[1,160,1024]{2,1,0:T(8,128)(2,1)S(1)}, bf16[1,160,1024]{2,1,0:T(8,128)(2,1)S(1)}, u32[]{:S(2)}, u32[]{:S(2)}) collective-permute-start(bf16[1,160,1024]{2,1,0:T(8,128)(2,1)S(1)} %maximum_bitcast_fusion), channel_id=1, source_target_pairs={{0,16},{4,20},{8,24},{12,28},{16,0},{20,4},{24,8},{28,12},{1,17},{... | collective-permute-start | bytes 983048 | tf_op jit(solution)/shard_map/ppermute | solution.py:798
  49.9 26.1 %collective-permute-start.11 = (bf16[1,160,1024]{2,1,0:T(8,128)(2,1)S(1)}, bf16[1,160,1024]{2,1,0:T(8,128)(2,1)S(1)}, u32[]{:S(2)}, u32[]{:S(2)}) collective-permute-start(bf16[1,160,1024]{2,1,0:T(8,128)(2,1)S(1)} %maximum_bitcast_fusion), channel_id=1, source_target_pairs={{0,24},{4,28},{8,16},{12,20},{16,8},{20,12},{24,0},{28,4},{1,25},{... | collective-permute-start | bytes 983048 | tf_op jit(solution)/shard_map/ppermute | solution.py:798
  87.1 371.9 %reduce-scatter.2.cloned.1.call-start = ((), (), s32[]{:S(2)}) async-start(), calls=%async_computation.1 | async-start | bytes 8650752 | tf_op jit(solution)/shard_map/reduce_scatter | solution.py:952
  87.8 41.4 %collective-permute-start.17 = (bf16[4,160,1024]{2,1,0:T(8,128)(2,1)S(1)}, bf16[4,160,1024]{2,1,0:T(8,128)(2,1)S(1)}, u32[]{:S(2)}, u32[]{:S(2)}) collective-permute-start(bf16[4,160,1024]{2,1,0:T(8,128)(2,1)S(1)} %pad_maximum_fusion.refs_0_), channel_id=1, source_target_pairs={{0,1},{1,0},{2,3},{3,2},{4,5},{5,4},{6,7},{7,6},{8,9},{9,8},{10,11... | collective-permute-start | bytes 3932168 | tf_op jit(solution)/shard_map/ppermute | solution.py:798
  88.3 40.9 %collective-permute-start.18 = (bf16[4,160,1024]{2,1,0:T(8,128)(2,1)S(1)}, bf16[4,160,1024]{2,1,0:T(8,128)(2,1)}, u32[]{:S(2)}, u32[]{:S(2)}) collective-permute-start(bf16[4,160,1024]{2,1,0:T(8,128)(2,1)S(1)} %pad_maximum_fusion.refs_0_), channel_id=1, source_target_pairs={{0,2},{1,3},{2,0},{3,1},{4,6},{5,7},{6,4},{7,5},{8,10},{9,11},{10,... | collective-permute-start | bytes 3932168 | tf_op jit(solution)/shard_map/ppermute | solution.py:798
  91.3 37.9 %collective-permute-start.19 = (bf16[4,160,1024]{2,1,0:T(8,128)(2,1)S(1)}, bf16[4,160,1024]{2,1,0:T(8,128)(2,1)}, u32[]{:S(2)}, u32[]{:S(2)}) collective-permute-start(bf16[4,160,1024]{2,1,0:T(8,128)(2,1)S(1)} %pad_maximum_fusion.refs_0_), channel_id=1, source_target_pairs={{0,4},{4,0},{8,12},{12,8},{16,20},{20,16},{24,28},{28,24},{1,5},{5... | collective-permute-start | bytes 3932168 | tf_op jit(solution)/shard_map/ppermute | solution.py:798
  129.3 42.2 %collective-permute-start.20 = (bf16[4,160,1024]{2,1,0:T(8,128)(2,1)}, bf16[4,160,1024]{2,1,0:T(8,128)(2,1)}, u32[]{:S(2)}, u32[]{:S(2)}) collective-permute-start(bf16[4,160,1024]{2,1,0:T(8,128)(2,1)} %collective-permute-done.18.refs_2_), channel_id=1, source_target_pairs={{0,1},{1,0},{2,3},{3,2},{4,5},{5,4},{6,7},{7,6},{8,9},{9,8},{10,11... | collective-permute-start | bytes 3932168 | tf_op jit(solution)/shard_map/ppermute | solution.py:798
  129.5 42.0 %collective-permute-start.21 = (bf16[4,160,1024]{2,1,0:T(8,128)(2,1)}, bf16[4,160,1024]{2,1,0:T(8,128)(2,1)}, u32[]{:S(2)}, u32[]{:S(2)}) collective-permute-start(bf16[4,160,1024]{2,1,0:T(8,128)(2,1)} %collective-permute-done.19.refs_4_), channel_id=1, source_target_pairs={{0,1},{1,0},{2,3},{3,2},{4,5},{5,4},{6,7},{7,6},{8,9},{9,8},{10,11... | collective-permute-start | bytes 3932168 | tf_op jit(solution)/shard_map/ppermute | solution.py:798
  129.9 46.1 %collective-permute-start.22 = (bf16[4,160,1024]{2,1,0:T(8,128)(2,1)}, bf16[4,160,1024]{2,1,0:T(8,128)(2,1)}, u32[]{:S(2)}, u32[]{:S(2)}) collective-permute-start(bf16[4,160,1024]{2,1,0:T(8,128)(2,1)} %collective-permute-done.18.refs_2_), channel_id=1, source_target_pairs={{0,4},{4,0},{8,12},{12,8},{16,20},{20,16},{24,28},{28,24},{1,5},{5... | collective-permute-start | bytes 3932168 | tf_op jit(solution)/shard_map/ppermute | solution.py:798
  131.4 40.1 %collective-permute-start.23 = (bf16[2,256,1024]{2,1,0:T(8,128)(2,1)}, bf16[2,256,1024]{2,1,0:T(8,128)(2,1)S(1)}, u32[]{:S(2)}, u32[]{:S(2)}) collective-permute-start(bf16[2,256,1024]{2,1,0:T(8,128)(2,1)} %constant_dynamic-slice_fusion.8), channel_id=1, source_target_pairs={{0,2},{1,3},{2,0},{3,1},{4,6},{5,7},{6,4},{7,5},{8,10},{9,11},{10,... | collective-permute-start | bytes 3145736 | tf_op jit(solution)/shard_map/ppermute | solution.py:798
  287.4 42.7 %collective-permute-start.27 = (bf16[4,160,1024]{2,1,0:T(8,128)(2,1)}, bf16[4,160,1024]{2,1,0:T(8,128)(2,1)}, u32[]{:S(2)}, u32[]{:S(2)}) collective-permute-start(bf16[4,160,1024]{2,1,0:T(8,128)(2,1)} %fusion.3), channel_id=1, source_target_pairs={{0,4},{4,0},{8,12},{12,8},{16,20},{20,16},{24,28},{28,24},{1,5},{5... | collective-permute-start | bytes 3932168 | tf_op jit(solution)/shard_map/ppermute | solution.py:798
  333.0 41.7 %collective-permute-start.29 = (bf16[4,160,1024]{2,1,0:T(8,128)(2,1)S(1)}, bf16[4,160,1024]{2,1,0:T(8,128)(2,1)}, u32[]{:S(2)}, u32[]{:S(2)}) collective-permute-start(bf16[4,160,1024]{2,1,0:T(8,128)(2,1)S(1)} %get-tuple-element.156), channel_id=1, source_target_pairs={{0,4},{4,0},{8,12},{12,8},{16,20},{20,16},{24,28},{28,24},{1,5},{5... | collective-permute-start | bytes 3932168 | tf_op jit(solution)/shard_map/ppermute | solution.py:798
  335.5 49.0 %collective-permute-start.28 = (bf16[4,160,1024]{2,1,0:T(8,128)(2,1)}, bf16[4,160,1024]{2,1,0:T(8,128)(2,1)}, u32[]{:S(2)}, u32[]{:S(2)}) collective-permute-start(bf16[4,160,1024]{2,1,0:T(8,128)(2,1)} %add_convert_fusion.1), channel_id=1, source_target_pairs={{0,2},{1,3},{2,0},{3,1},{4,6},{5,7},{6,4},{7,5},{8,10},{9,11},{10,... | collective-permute-start | bytes 3932168 | tf_op jit(solution)/shard_map/ppermute | solution.py:798
  338.5 68.1 %collective-permute-start.30 = (bf16[2,256,1024]{2,1,0:T(8,128)(2,1)}, bf16[2,256,1024]{2,1,0:T(8,128)(2,1)}, u32[]{:S(2)}, u32[]{:S(2)}) collective-permute-start(bf16[2,256,1024]{2,1,0:T(8,128)(2,1)} %constant_dynamic-slice_fusion.5), channel_id=1, source_target_pairs={{0,2},{1,3},{2,0},{3,1},{4,6},{5,7},{6,4},{7,5},{8,10},{9,11},{10,... | collective-permute-start | bytes 3145736 | tf_op jit(solution)/shard_map/ppermute | solution.py:798
  367.8 61.3 %collective-permute-start.32 = (bf16[4,2,2,96,768]{4,3,0,2,1:T(8,128)(2,1)}, bf16[4,2,2,96,768]{4,3,0,2,1:T(8,128)(2,1)}, u32[]{:S(2)}, u32[]{:S(2)}) collective-permute-start(bf16[4,2,2,96,768]{4,3,0,2,1:T(8,128)(2,1)} %copy.44), channel_id=1, source_target_pairs={{0,1},{1,0},{2,3},{3,2},{4,5},{5,4},{6,7},{7,6},{8,9},{9,8},{10,11... | collective-permute-start | bytes 7077896 | tf_op jit(solution)/shard_map/ppermute | solution.py:798
  408.0 21.1 %collective-permute-start.31 = (bf16[2,256,1024]{2,1,0:T(8,128)(2,1)S(1)}, bf16[2,256,1024]{2,1,0:T(8,128)(2,1)}, u32[]{:S(2)}, u32[]{:S(2)}) collective-permute-start(bf16[2,256,1024]{2,1,0:T(8,128)(2,1)S(1)} %pad_maximum_fusion.3), channel_id=1, source_target_pairs={{0,1},{1,0},{2,3},{3,2},{4,5},{5,4},{6,7},{7,6},{8,9},{9,8},{10,11... | collective-permute-start | bytes 3145736 | tf_op jit(solution)/shard_map/ppermute | solution.py:798
  408.1 31.5 %collective-permute-start.33 = (bf16[160,1024]{1,0:T(8,128)(2,1)}, bf16[160,1024]{1,0:T(8,128)(2,1)}, u32[]{:S(2)}, u32[]{:S(2)}) collective-permute-start(bf16[160,1024]{1,0:T(8,128)(2,1)} %get-tuple-element.224), channel_id=1, source_target_pairs={{0,8},{4,12},{8,0},{12,4},{16,24},{20,28},{24,16},{28,20},{1,9},{5... | collective-permute-start | bytes 983048 | tf_op jit(solution)/shard_map/ppermute | solution.py:798
  408.2 48.0 %collective-permute-start.34 = (bf16[160,1024]{1,0:T(8,128)(2,1)S(1)}, bf16[160,1024]{1,0:T(8,128)(2,1)}, u32[]{:S(2)}, u32[]{:S(2)}) collective-permute-start(bf16[160,1024]{1,0:T(8,128)(2,1)S(1)} %get-tuple-element.223), channel_id=1, source_target_pairs={{0,16},{4,20},{8,24},{12,28},{16,0},{20,4},{24,8},{28,12},{1,17},{... | collective-permute-start | bytes 983048 | tf_op jit(solution)/shard_map/ppermute | solution.py:798
  409.5 47.9 %collective-permute-start.35 = (bf16[160,1024]{1,0:T(8,128)(2,1)S(1)}, bf16[160,1024]{1,0:T(8,128)(2,1)}, u32[]{:S(2)}, u32[]{:S(2)}) collective-permute-start(bf16[160,1024]{1,0:T(8,128)(2,1)S(1)} %get-tuple-element.222), channel_id=1, source_target_pairs={{0,24},{4,28},{8,16},{12,20},{16,8},{20,12},{24,0},{28,4},{1,25},{... | collective-permute-start | bytes 983048 | tf_op jit(solution)/shard_map/ppermute | solution.py:798
  431.3 26.1 %collective-permute-start.36 = (bf16[2,96,768]{2,1,0:T(8,128)(2,1)S(1)}, bf16[2,96,768]{2,1,0:T(8,128)(2,1)S(1)}, u32[]{:S(2)}, u32[]{:S(2)}) collective-permute-start(bf16[2,96,768]{2,1,0:T(8,128)(2,1)S(1)} %get-tuple-element.233), channel_id=1, source_target_pairs={{0,2},{1,3},{2,0},{3,1},{4,6},{5,7},{6,4},{7,5},{8,10},{9,11},{10,... | collective-permute-start | bytes 884744 | tf_op jit(solution)/shard_map/ppermute | solution.py:798
  431.4 26.0 %collective-permute-start.37 = (bf16[2,96,768]{2,1,0:T(8,128)(2,1)S(1)}, bf16[2,96,768]{2,1,0:T(8,128)(2,1)S(1)}, u32[]{:S(2)}, u32[]{:S(2)}) collective-permute-start(bf16[2,96,768]{2,1,0:T(8,128)(2,1)S(1)} %get-tuple-element.232), channel_id=1, source_target_pairs={{0,4},{4,0},{8,12},{12,8},{16,20},{20,16},{24,28},{28,24},{1,5},{5... | collective-permute-start | bytes 884744 | tf_op jit(solution)/shard_map/ppermute | solution.py:798
  439.5 19.5 %collective-permute-start.38 = (bf16[4,2,2,112,256]{4,3,0,2,1:T(8,128)(2,1)S(1)}, bf16[4,2,2,112,256]{4,3,0,2,1:T(8,128)(2,1)}, u32[]{:S(2)}, u32[]{:S(2)}) collective-permute-start(bf16[4,2,2,112,256]{4,3,0,2,1:T(8,128)(2,1)S(1)} %copy.49), channel_id=1, source_target_pairs={{0,1},{1,0},{2,3},{3,2},{4,5},{5,4},{6,7},{7,6},{8,9},{9,8},{10,11... | collective-permute-start | bytes 2752520 | tf_op jit(solution)/shard_map/ppermute | solution.py:798
  456.1 61.3 %collective-permute-start.49 = (bf16[2,256,1024]{2,1,0:T(8,128)(2,1)}, bf16[2,256,1024]{2,1,0:T(8,128)(2,1)}, u32[]{:S(2)}, u32[]{:S(2)}) collective-permute-start(bf16[2,256,1024]{2,1,0:T(8,128)(2,1)} %constant_dynamic-slice_fusion), channel_id=1, source_target_pairs={{0,2},{1,3},{2,0},{3,1},{4,6},{5,7},{6,4},{7,5},{8,10},{9,11},{10,... | collective-permute-start | bytes 3145736 | tf_op jit(solution)/shard_map/ppermute | solution.py:798
  457.6 44.7 %collective-permute-start.42 = (bf16[4,96,768]{2,1,0:T(8,128)(2,1)S(1)}, bf16[4,96,768]{2,1,0:T(8,128)(2,1)}, u32[]{:S(2)}, u32[]{:S(2)}) collective-permute-start(bf16[4,96,768]{2,1,0:T(8,128)(2,1)S(1)} %pad_maximum_fusion.9), channel_id=1, source_target_pairs={{0,4},{4,0},{8,12},{12,8},{16,20},{20,16},{24,28},{28,24},{1,5},{5... | collective-permute-start | bytes 1769480 | tf_op jit(solution)/shard_map/ppermute | solution.py:798
  458.9 43.4 %collective-permute-start.41 = (bf16[4,96,768]{2,1,0:T(8,128)(2,1)S(1)}, bf16[4,96,768]{2,1,0:T(8,128)(2,1)}, u32[]{:S(2)}, u32[]{:S(2)}) collective-permute-start(bf16[4,96,768]{2,1,0:T(8,128)(2,1)S(1)} %pad_maximum_fusion.8), channel_id=1, source_target_pairs={{0,2},{1,3},{2,0},{3,1},{4,6},{5,7},{6,4},{7,5},{8,10},{9,11},{10,... | collective-permute-start | bytes 1769480 | tf_op jit(solution)/shard_map/ppermute | solution.py:798
  461.6 35.4 %collective-permute-start.39 = (bf16[2,112,256]{2,1,0:T(8,128)(2,1)S(1)}, bf16[2,112,256]{2,1,0:T(8,128)(2,1)S(1)}, u32[]{:S(2)}, u32[]{:S(2)}) collective-permute-start(bf16[2,112,256]{2,1,0:T(8,128)(2,1)S(1)} %get-tuple-element.245), channel_id=1, source_target_pairs={{0,2},{1,3},{2,0},{3,1},{4,6},{5,7},{6,4},{7,5},{8,10},{9,11},{10,... | collective-permute-start | bytes 344072 | tf_op jit(solution)/shard_map/ppermute | solution.py:798
  463.6 33.4 %collective-permute-start.40 = (bf16[2,112,256]{2,1,0:T(8,128)(2,1)S(1)}, bf16[2,112,256]{2,1,0:T(8,128)(2,1)S(1)}, u32[]{:S(2)}, u32[]{:S(2)}) collective-permute-start(bf16[2,112,256]{2,1,0:T(8,128)(2,1)S(1)} %get-tuple-element.244), channel_id=1, source_target_pairs={{0,4},{4,0},{8,12},{12,8},{16,20},{20,16},{24,28},{28,24},{1,5},{5... | collective-permute-start | bytes 344072 | tf_op jit(solution)/shard_map/ppermute | solution.py:798
  (64 other events, 658.0 us)
Sparse Core Ops, SparseCore 0:
  87.2 97.5 all-gather.2
  222.4 151.2 reduce-scatter.1

commit v7 on v5

--- a/solution.py
+++ b/solution.py
@@ -597,13 +597,14 @@
 
 def mid_a_kernel(ids_ref, x_hbm, o_hbm, g4_ref, chip_ref, core_ref, gain_ref, *refs, masks):
     gathered = refs[:len(masks)]
-    (mixed_out, acc_out, gh2_out, h2_out, h2t_out, gm_out, wo_out, gw_out,
+    (mixed_out, acc_out, gh2_out, h2_out, h2t_out, gm_out, wo_out, keep_out, send_out,
      xs, os, wo, ws_in, ws_back, mixed, h2, h2t, acc, gh2, gm, st_in, st_back, sems) = refs[len(masks):]
     flat = ids_ref[1]
     rows, width = xs.shape
     half, own = st_back.shape[2], width // (2 * st_in.shape[0])
-    def emit(src, which, dst_rows, lead=slice(None), src_rows=slice(None), lanes=slice(None)):
-        pltpu.make_async_copy(src.at[lead, :, src_rows, lanes], gw_out.at[lead, :, dst_rows, lanes], sems.at[which]).start()
+    core = flat & 1
+    def emit(src, which, **at):
+        by_core(core, keep_out, send_out, src, sem=sems.at[which], **at)
     loads = [pltpu.make_async_copy(x_hbm, xs, sems.at[0]), pltpu.make_async_copy(o_hbm, os, sems.at[1])]
     for load in loads:
         load.start()
@@ -657,8 +658,8 @@
     stack = half + ff // width * (width // shards)
     return pl.pallas_call(
         functools.partial(mid_a_kernel, masks=masks),
-        out_shape=(full(rows, width), full(rows, width), full(rows, width), low(rows, width), low(width, rows), low(rows, width), low(width, width), low(shards // 2, 2, stack, width)),
-        in_specs=[SM] + [ANY] * 5 + [VM] + [ANY] * len(gathered), out_specs=[ANY] * 8,
+        out_shape=(full(rows, width), full(rows, width), full(rows, width), low(rows, width), low(width, rows), low(rows, width), low(width, width), low(shards // 2, stack, width), low(shards // 2, stack, width)),
+        in_specs=[SM] + [ANY] * 5 + [VM] + [ANY] * len(gathered), out_specs=[ANY] * 9,
         scratch_shapes=[vm(rows, width), vm(rows, width), vm(width, width), vm(width, ff), vm(ff, width), vf(rows, width), vm(rows, width), vm(width, rows),
                         vf(rows, width), vf(rows, width), vm(rows, width), vm(shards // 2, 2, stack - half, width), vm(shards // 2, 2, half, width), pltpu.SemaphoreType.DMA((10,))],
         compiler_params=pltpu.CompilerParams(vmem_limit_bytes=LIMIT),
@@ -854,7 +855,8 @@
     def turn(self):
         add = lambda a, b: (a.astype(jnp.float32) + b.astype(jnp.float32)).astype(jnp.bfloat16)
         if self.corner_y:
-            to_x, to_y = add(self.to_x, self.came_y), self.to_y
+            to_y, = tie(self.came_y, self.to_y)
+            to_x = add(self.to_x, self.came_y)
         else:
             to_x = lax.dynamic_update_slice_in_dim(self.to_x, add(self.to_x[2:], self.came_y), 2, 0)
             to_y = lax.dynamic_update_slice_in_dim(self.to_y, add(self.to_y[:2], self.came_x), 0, 0)
@@ -944,29 +946,39 @@
     g2.corner, g_chip = tie((attended, g2.pieces[3], g2.pieces[5]), g2.corner, g_chip)
     g2.take(g2.corner, 6)
     g_core = send_core(g4, g_chip, me)
-    *state, gw_a = mid_a(ids, x, attended, g4, (g_chip, g_core), gains, *g2.all_pieces(), ff)
-    r_a = lax.psum_scatter(gw_a.reshape(-1, width), both, scatter_dimension=0, tiled=True)
+    *state, keep3, send3 = mid_a(ids, x, attended, g4, (g_chip, g_core), gains, *g2.all_pieces(), ff)
+    sc3 = Scatter(keep3, send3, pos, True)
     out, gb, g_att, keep2, send2 = mid_b(ids, gains, state, attended, full3, ff)
-    sc2 = Scatter(keep2, send2, pos, True)
+    sc3.other, = tie(gb, sc3.other)
+    sc3.fold()
+    send2, = tie(sc3.own, send2)
+    sc2 = Scatter(keep2, send2, pos, False)
     out4 = out.reshape(parts, rows, width)
+    out4, = tie(sc3.own, out4)
     out_chip = send_chip(out4, me)
     count = pairs // 4
     back = lambda first, g, prev: attn_bwd(length, q, k, v, g, attended, lse, t_back, first, count, prev)
+    g_att, = tie(sc3.own, g_att)
     dq, dk, dv, off0 = back(0, g_att, None)
     sc2.other, = tie(off0, sc2.other)
     sc2.fold()
-    g_att, = tie((sc2.own, sc2.to_x, sc2.to_y), g_att)
+    sc3.came_y, = tie(sc2.own, sc3.came_y)
+    sc3.turn()
+    g_att, = tie(sc3.sent, g_att)
     dq, dk, dv, off1 = back(count, g_att, (dq, dk, dv))
-    sc2.came_y, sc2.to_x = tie((off1, out_chip), sc2.came_y, sc2.to_x)
+    sc2.came_x, sc2.came_y = tie((off1, out_chip), sc2.came_x, sc2.came_y)
     sc2.turn()
     out4_in, out_chip = tie(sc2.sent, out4, out_chip)
     out_core = send_core(out4_in, out_chip, me)
     g_att, = tie(sc2.sent, g_att)
     dq, dk, dv, off2 = back(2 * count, g_att, (dq, dk, dv))
+    sc3.came_x, sc3.came_y = tie((off2, out_core), sc3.came_x, sc3.came_y)
+    sc3.column()
+    g_att, = tie(sc3.mine, g_att)
     dq, dk, dv, off3 = back(3 * count, g_att, (dq, dk, dv))
-    sc2.came_x, sc2.came_y = tie((off3, out_core), sc2.came_x, sc2.came_y)
+    sc2.came_x, sc2.came_y = tie(off3, sc2.came_x, sc2.came_y)
     sc2.column()
-    h_in, = tie((sc2.mine, r_a), hidden)
+    h_in, = tie((sc2.mine, sc3.came), hidden)
     keep1, send1 = qkv_gw(ids, h_in, dq, dk, dv, bucket_rows, (off0, off1, off2, off3), shards)
     sc1 = Scatter(keep1, send1, pos, False)
     gb_in, = tie(send1, gb)
@@ -978,7 +990,8 @@
     sc1.came_x, sc1.came_y = tie((layer_out, sc2.came), sc1.came_x, sc1.came_y)
     sc1.turn()
     sc2.came = list(tie(sc1.sent, *sc2.came))
-    r2 = sc2.result()
+    sc3.came = list(tie(sc1.sent, *sc3.came))
+    r2, r_a = sc2.result(), sc3.result()
     sc1.came_x, sc1.came_y = tie(r2, sc1.came_x, sc1.came_y)
     sc1.column()
     gx, = tie(sc1.mine, gx)
@@ -988,7 +1001,7 @@
     gx_core = send_core(gx4, gx_chip, me)
     input_grad = place(gx4, gx_chip, gx_core, me)
     sc1.came = list(tie(input_grad, *sc1.came))
-    r1, r_a = sc1.result(), up(r_a)
+    r1 = sc1.result()
     join = lambda v: jnp.concatenate([v[i:i + own] for i in range(0, v.shape[0], own)], 1).reshape(own, shards, 1, half)
     g_in = jnp.concatenate([join(r_a[half:]), join(r2[half + own:])], 2).reshape(w_in.shape)
     g_back = jnp.concatenate([r_a[:half], r2[:half]], 0)

time: 519 us -> 510 us (0.983)
  waiting for transfers between devices: 155 us -> 121 us
  other arithmetic: 41.6 us -> 52.3 us
  starting transfers between devices: 42.1 us -> 50.2 us
    ppermute x45 -> x53, waiting for transfers between devices: 155 us -> 121 us  [swap(): lax.ppermute(value, axis, [(i, i ^ mask) for i in range(lax.axis_size(axi...]
    ppermute x45 -> x53, starting transfers between devices: 42.1 us -> 50.2 us  [swap(): lax.ppermute(value, axis, [(i, i ^ mask) for i in range(lax.axis_size(axi...]
    convert_element_type x4 -> x6, other arithmetic: 14.7 us -> 19.2 us  [quarter(): return (cut(self.mine) + cut(self.other)).astype(jnp.bfloat16)]
  transfers between devices with their start and end apart: 47 -> 54, of which waited for: 21 -> 19; matrix products, arithmetic and copies ran while one was open for 11% -> 13% of each run, Pallas kernels for 41% -> 42%
where the time goes in v7:
time: 510 us; the launch traced here: 502 us
  Pallas kernels  224 us (44%)
  waiting for transfers between devices  121 us (24%)
  other arithmetic  52.3 us (10%)
  starting transfers between devices  50.2 us (10%)
  local copies, waits for them, and re-layouts  38.5 us (8%)
  between operations  15.6 us (3%)
    ppermute x53, waiting for transfers between devices, swap(): lax.ppermute(value, axis, [(i, i ^ mask) for i in range(lax.axis_size(axi...  121 us
    pallas_call x4, Pallas kernels, attn_bwd(): pl.pallas_call(functools.partial(bwd_kernel, rows=rows, seq_len=seq_len,...  65.7 us
    ppermute x53, starting transfers between devices, swap(): lax.ppermute(value, axis, [(i, i ^ mask) for i in range(lax.axis_size(axi...  50.2 us
    pallas_call x1, Pallas kernels, mid_b(): pl.pallas_call(mid_b_kernel, out_shape=(low(rows, width), low(rows, width...  45.5 us
    pallas_call x1, Pallas kernels, mid_a(): pl.pallas_call(functools.partial(mid_a_kernel, masks=masks), out_shape=(f...  39.7 us
    pallas_call x2, Pallas kernels, attn_fwd(): pl.pallas_call(functools.partial(fwd_kernel, rows=rows, seq_len=seq_len,...  33.2 us
    convert_element_type x6, other arithmetic, quarter(): return (cut(self.mine) + cut(self.other)).astype(jnp.bfloat16)  19.2 us
    pallas_call x1, Pallas kernels, qkv_gx(): pl.pallas_call(gx_kernel, out_shape=jax.ShapeDtypeStruct((total, width),...  14.2 us
  transfers between devices with their start and end apart: 54, of which 19 were waited for; matrix products, arithmetic and copies ran while one was open for 13% of the time, Pallas kernels for 42%

profile of v7, /device:TPU:0, one launch (start us, length us, event | category | flops | bytes accessed | tf_op | source)
XLA Modules:
  0.0 502.0 jit_solution(15485432169263576130)
XLA Ops:
  12.5 3.1 collective-permute-start.2
  23.0 3.0 slice_reduce_fusion
  28.2 6.7 %collective-permute-done.3 = bf16[1,112,1024]{2,1,0:T(8,128)(2,1)S(1)} collective-permute-done((bf16[1,112,1024]{2,1,0:T(8,128)(2,1)S(1)}, bf16[1,112,1024]{2,1,0:T(8,128)(2,1)S(1)}, u32[]{:S(2)}, u32[]{:S(2)}) %collective-permute-start.3) | collective-permute-done | bytes 229408 | tf_op jit(solution)/shard_map/ppermute | solution.py:796
  36.7 3.7 collective-permute-done.1
  40.5 4.8 collective-permute-done.chip_ref
  51.8 21.9 %collective-permute-done.6 = bf16[1,160,1024]{2,1,0:T(8,128)(2,1)S(1)} collective-permute-done((bf16[1,160,1024]{2,1,0:T(8,128)(2,1)S(1)}, bf16[1,160,1024]{2,1,0:T(8,128)(2,1)S(1)}, u32[]{:S(2)}, u32[]{:S(2)}) %collective-permute-start.6) | collective-permute-done | bytes 327712 | tf_op jit(solution)/shard_map/ppermute | solution.py:796
  78.3 7.3 %collective-permute-done.10.refs_8_ = bf16[2,112,1024]{2,1,0:T(8,128)(2,1)S(1)} collective-permute-done((bf16[2,112,1024]{2,1,0:T(8,128)(2,1)S(1)}, bf16[2,112,1024]{2,1,0:T(8,128)(2,1)S(1)}, u32[]{:S(2)}, u32[]{:S(2)}) %collective-permute-start.10) | collective-permute-done | bytes 458784 | tf_op jit(solution)/shard_map/ppermute | solution.py:796
  99.3 13.2 %qkv_fwd.1 = (bf16[1024,1024]{1,0:T(8,128)(2,1)}, bf16[1024,1024]{1,0:T(8,128)(2,1)}, bf16[1024,1024]{1,0:T(8,128)(2,1)}, bf16[1024,1024]{1,0:T(8,128)(2,1)}, bf...) custom-call(s32[3]{0:T(128)} %pad_add_fusion.1.ids_ref, ...), custom_call_target="tpu_custom_call" | custom-call | flops 1048576 | bytes 65536 | tf_op jit(solution)/shard_map/qkv_fwd/pallas_call | solution.py:524
  112.5 16.6 %attn_fwd.2 = (bf16[1024,1024]{1,0:T(8,128)(2,1)}, f32[8,1024,128]{2,1,0:T(8,128)}) custom-call(s32[1]{0:T(128)} %dynamic_slice.189.len_ref, bf16[1024,1024]{1,0:T(8,128)(2,1)} %get-tuple-element.129.q_ref, bf16[1024,1024]{1,0:T(8,128)(2,1)} %get-tuple-element.122.k_ref, bf16[1024,1024]{1,0:T(8,128)(2,1)} %get-tuple-element.123.v_ref, ...), custom_call_target="tpu_custom_call" | custom-call | flops 1048576 | bytes 65536 | tf_op jit(solution)/shard_map/attn_fwd/pallas_call | solution.py:360
  131.9 16.6 %attn_fwd.3 = (bf16[1024,1024]{1,0:T(8,128)(2,1)}, f32[8,1024,128]{2,1,0:T(8,128)}) custom-call(s32[1]{0:T(128)} %dynamic_slice.189.len_ref, bf16[1024,1024]{1,0:T(8,128)(2,1)} %get-tuple-element.129.q_ref, bf16[1024,1024]{1,0:T(8,128)(2,1)} %get-tuple-element.122.k_ref, ...), custom_call_target="tpu_custom_call", output_to_operand_aliasing={{0}: (5, {}), {1}: (6, {})} | custom-call | flops 1048576 | bytes 65536 | tf_op jit(solution)/shard_map/attn_fwd/pallas_call | solution.py:360
  148.5 22.8 %collective-permute-done.23.chip_ref = bf16[2,256,1024]{2,1,0:T(8,128)(2,1)S(1)} collective-permute-done((bf16[2,256,1024]{2,1,0:T(8,128)(2,1)}, bf16[2,256,1024]{2,1,0:T(8,128)(2,1)S(1)}, u32[]{:S(2)}, u32[]{:S(2)}) %collective-permute-start.23) | collective-permute-done | bytes 1048608 | tf_op jit(solution)/shard_map/ppermute | solution.py:796
  171.4 4.4 collective-permute-done.22.refs_6_
  176.5 4.2 collective-permute-done.24.core_ref
  182.5 39.7 %mid_a.1 = (f32[1024,1024]{1,0:T(8,128)}, f32[1024,1024]{1,0:T(8,128)}, f32[1024,1024]{1,0:T(8,128)}, bf16[1024,1024]{1,0:T(8,128)(2,1)}, bf16[1024,1024]{1,0:T(...) custom-call(s32[3]{0:T(128)} %pad_add_fusion.1.ids_ref, ...), custom_call_target="tpu_custom_call" | custom-call | flops 1048576 | bytes 65536 | tf_op jit(solution)/shard_map/mid_a/pallas_call | solution.py:659
  222.3 45.5 %mid_b.1 = (bf16[1024,1024]{1,0:T(8,128)(2,1)}, bf16[1024,1024]{1,0:T(8,128)(2,1)}, bf16[1024,1024]{1,0:T(8,128)(2,1)}, bf16[16,160,1024]{2,1,0:T(8,128)(2,1)}, bf16[16,160,1024]{2,1,0:T(8,128)(2,1)}) custom-call(s32[3]{0:T(128)} %pad_add_fusion.1.ids_ref, f32[8,1024]{1,0:T(8,128)} %get-tuple-element.119.gain_ref, ...), custom_call_target="tpu_custom_call" | custom-call | flops 1048576 | bytes 65536 | tf_op jit(solution)/shard_map/mid_b/pallas_call | solution.py:727
  267.9 4.1 fusion.6
  274.9 16.5 %attn_bwd.4 = (bf16[1024,1024]{1,0:T(8,128)(2,1)}, bf16[1024,1024]{1,0:T(8,128)(2,1)}, bf16[1024,1024]{1,0:T(8,128)(2,1)}, f32[4,2048]{1,0:T(4,128)}) custom-call(s32[1]{0:T(128)} %dynamic_slice.189.len_ref, bf16[1024,1024]{1,0:T(8,128)(2,1)} %get-tuple-element.129.q_ref, bf16[1024,1024]{1,0:T(8,128)(2,1)} %get-tuple-element.122.k_ref, ...), custom_call_target="tpu_custom_call" | custom-call | flops 1048576 | bytes 65536 | tf_op jit(solution)/shard_map/attn_bwd/pallas_call | solution.py:439
  293.8 5.5 %add_convert_fusion.2 = (bf16[4,1,1,160,1024]{4,3,0,2,1:T(8,128)(2,1)S(1)}, bf16[4,1,1,160,1024]{4,3,0,2,1:T(8,128)(2,1)S(1)}, bf16[4,160,1024]{2,1,0:T(8,128)(2,1)S(1)}) fusion(s32[]{:T(128)S(6)} %select_n.182, s32[]{:T(128)S(6)} %select_n.180, bf16[4,2,2,160,1024]{4,3,2,1,0:T(8,128)(2,1)} %bitcast.133, s32[]{:T(128)S(6)} %select_n.176, s32[]{:T(128)S(6)} %select_n.178, ...), kind=kLoop, calls=%fused_computation.2 | loop fusion | flops 7864320 | bytes 11796496 | tf_op jit(solution)/shard_map/convert_element_type | solution.py:847
  306.7 3.2 fusion
  313.6 16.3 %attn_bwd.5 = (bf16[1024,1024]{1,0:T(8,128)(2,1)}, bf16[1024,1024]{1,0:T(8,128)(2,1)}, bf16[1024,1024]{1,0:T(8,128)(2,1)}, f32[4,2048]{1,0:T(4,128)}) custom-call(s32[1]{0:T(128)} %dynamic_slice.189.len_ref, bf16[1024,1024]{1,0:T(8,128)(2,1)} %get-tuple-element.129.q_ref, ...), custom_call_target="tpu_custom_call", output_to_operand_aliasing={{0}: (8, {}), {1}: (9, {}), {2}: (10, {})} | custom-call | flops 1048576 | bytes 65536 | tf_op jit(solution)/shard_map/attn_bwd/pallas_call | solution.py:439
  338.9 16.5 %attn_bwd.6 = (bf16[1024,1024]{1,0:T(8,128)(2,1)}, bf16[1024,1024]{1,0:T(8,128)(2,1)}, bf16[1024,1024]{1,0:T(8,128)(2,1)}, f32[4,2048]{1,0:T(4,128)}) custom-call(s32[1]{0:T(128)} %dynamic_slice.189.len_ref, bf16[1024,1024]{1,0:T(8,128)(2,1)} %get-tuple-element.129.q_ref, ...), custom_call_target="tpu_custom_call", output_to_operand_aliasing={{0}: (8, {}), {1}: (9, {}), {2}: (10, {})} | custom-call | flops 1048576 | bytes 65536 | tf_op jit(solution)/shard_map/attn_bwd/pallas_call | solution.py:439
  357.7 4.1 collective-permute-start.38
  362.1 16.4 %attn_bwd.7 = (bf16[1024,1024]{1,0:T(8,128)(2,1)}, bf16[1024,1024]{1,0:T(8,128)(2,1)}, bf16[1024,1024]{1,0:T(8,128)(2,1)}, f32[4,2048]{1,0:T(4,128)}) custom-call(s32[1]{0:T(128)} %dynamic_slice.189.len_ref, bf16[1024,1024]{1,0:T(8,128)(2,1)} %get-tuple-element.129.q_ref, ...), custom_call_target="tpu_custom_call", output_to_operand_aliasing={{0}: (8, {}), {1}: (9, {}), {2}: (10, {})} | custom-call | flops 1048576 | bytes 65536 | tf_op jit(solution)/shard_map/attn_bwd/pallas_call | solution.py:439
  381.7 12.3 %qkv_gw.1 = (bf16[16,112,1024]{2,1,0:T(8,128)(2,1)}, bf16[16,112,1024]{2,1,0:T(8,128)(2,1)}) custom-call(s32[3]{0:T(128)} %pad_add_fusion.1.ids_ref, bf16[1024,1024]{1,0:T(8,128)(2,1)} %get-tuple-element.184.h_ref, bf16[1024,1024]{1,0:T(8,128)(2,1)} %get-tuple-element.185.dq_ref, bf16[1024,1024]{1,0:T(8,128)(2,1)} %get-tuple-element.186.dk_ref, ...), custom_call_target="tpu_custom_call" | custom-call | flops 1048576 | bytes 65536 | tf_op jit(solution)/shard_map/qkv_gw/pallas_call | solution.py:761
  394.2 3.6 collective-permute-start.41
  400.2 14.2 %qkv_gx.1 = bf16[1024,1024]{1,0:T(8,128)(2,1)} custom-call(bf16[1024,1024]{1,0:T(8,128)(2,1)} %get-tuple-element.120.x_hbm.x_ref, bf16[1024,1024]{1,0:T(8,128)(2,1)} %get-tuple-element.190.gb_ref, bf16[1024,1024]{1,0:T(8,128)(2,1)} %get-tuple-element.185.dq_ref, bf16[1024,1024]{1,0:T(8,128)(2,1)} %get-tuple-element.186.dk_ref, ...), custom_call_target="tpu_custom_call" | custom-call | flops 1048576 | bytes 65536 | tf_op jit(solution)/shard_map/qkv_gx/pallas_call | solution.py:785
  414.5 3.2 add_convert_fusion.12
  423.6 6.5 %collective-permute-done.44 = bf16[2,112,1024]{2,1,0:T(8,128)(2,1)S(1)} collective-permute-done((bf16[2,112,1024]{2,1,0:T(8,128)(2,1)S(1)}, bf16[2,112,1024]{2,1,0:T(8,128)(2,1)S(1)}, u32[]{:S(2)}, u32[]{:S(2)}) %collective-permute-start.44) | collective-permute-done | bytes 458784 | tf_op jit(solution)/shard_map/ppermute | solution.py:796
  434.3 17.4 %collective-permute-done.47 = bf16[4,112,1024]{2,1,0:T(8,128)(2,1)S(1)} collective-permute-done((bf16[4,112,1024]{2,1,0:T(8,128)(2,1)S(1)}, bf16[4,112,1024]{2,1,0:T(8,128)(2,1)S(1)}, u32[]{:S(2)}, u32[]{:S(2)}) %collective-permute-start.47) | collective-permute-done | bytes 917536 | tf_op jit(solution)/shard_map/ppermute | solution.py:796
  461.8 5.3 %collective-permute-done.48 = bf16[112,1024]{1,0:T(8,128)(2,1)} collective-permute-done((bf16[112,1024]{1,0:T(8,128)(2,1)}, bf16[112,1024]{1,0:T(8,128)(2,1)}, u32[]{:S(2)}, u32[]{:S(2)}) %collective-permute-start.48) | collective-permute-done | bytes 229408 | tf_op jit(solution)/shard_map/ppermute | solution.py:796
  467.0 7.5 %collective-permute-done.49 = bf16[112,1024]{1,0:T(8,128)(2,1)} collective-permute-done((bf16[112,1024]{1,0:T(8,128)(2,1)}, bf16[112,1024]{1,0:T(8,128)(2,1)}, u32[]{:S(2)}, u32[]{:S(2)}) %collective-permute-start.49) | collective-permute-done | bytes 229408 | tf_op jit(solution)/shard_map/ppermute | solution.py:796
  474.6 3.2 collective-permute-done.51
  (282 shorter events, 117.0 us)
Async XLA Ops:
  7.2 215.1 %all-gather.3.cloned.1.call-start = ((), (), s32[]{:S(2)}) async-start(), calls=%async_computation | async-start | bytes 8650752 | tf_op jit(solution)/shard_map/all_gather | solution.py:933
  20.5 24.8 %collective-permute-start = (bf16[2,256,1024]{2,1,0:T(8,128)(2,1)}, bf16[2,256,1024]{2,1,0:T(8,128)(2,1)S(1)}, u32[]{:S(2)}, u32[]{:S(2)}) collective-permute-start(bf16[2,256,1024]{2,1,0:T(8,128)(2,1)} %constant_dynamic-slice_fusion.11), channel_id=1, source_target_pairs={{0,2},{1,3},{2,0},{3,1},{4,6},{5,7},{6,4},{7,5},{8,10},{9,11},{10,... | collective-permute-start | bytes 3145736 | tf_op jit(solution)/shard_map/ppermute | solution.py:796
  45.3 28.5 %collective-permute-start.7 = (bf16[4,112,1024]{2,1,0:T(8,128)(2,1)S(1)}, bf16[4,112,1024]{2,1,0:T(8,128)(2,1)S(1)}, u32[]{:S(2)}, u32[]{:S(2)}) collective-permute-start(bf16[4,112,1024]{2,1,0:T(8,128)(2,1)S(1)} %pad_maximum_fusion.6.refs_0_), channel_id=1, source_target_pairs={{0,2},{1,3},{2,0},{3,1},{4,6},{5,7},{6,4},{7,5},{8,10},{9,11},{10,... | collective-permute-start | bytes 2752520 | tf_op jit(solution)/shard_map/ppermute | solution.py:796
  46.8 27.0 %collective-permute-start.8 = (bf16[4,112,1024]{2,1,0:T(8,128)(2,1)S(1)}, bf16[4,112,1024]{2,1,0:T(8,128)(2,1)}, u32[]{:S(2)}, u32[]{:S(2)}) collective-permute-start(bf16[4,112,1024]{2,1,0:T(8,128)(2,1)S(1)} %pad_maximum_fusion.6.refs_0_), channel_id=1, source_target_pairs={{0,4},{4,0},{8,12},{12,8},{16,20},{20,16},{24,28},{28,24},{1,5},{5... | collective-permute-start | bytes 2752520 | tf_op jit(solution)/shard_map/ppermute | solution.py:796
  48.3 29.0 %collective-permute-start.5 = (bf16[4,112,1024]{2,1,0:T(8,128)(2,1)S(1)}, bf16[4,112,1024]{2,1,0:T(8,128)(2,1)S(1)}, u32[]{:S(2)}, u32[]{:S(2)}) collective-permute-start(bf16[4,112,1024]{2,1,0:T(8,128)(2,1)S(1)} %pad_maximum_fusion.6.refs_0_), channel_id=1, source_target_pairs={{0,1},{1,0},{2,3},{3,2},{4,5},{5,4},{6,7},{7,6},{8,9},{9,8},{10,11... | collective-permute-start | bytes 2752520 | tf_op jit(solution)/shard_map/ppermute | solution.py:796
  48.3 25.4 %collective-permute-start.6 = (bf16[1,160,1024]{2,1,0:T(8,128)(2,1)S(1)}, bf16[1,160,1024]{2,1,0:T(8,128)(2,1)S(1)}, u32[]{:S(2)}, u32[]{:S(2)}) collective-permute-start(bf16[1,160,1024]{2,1,0:T(8,128)(2,1)S(1)} %maximum_bitcast_fusion), channel_id=1, source_target_pairs={{0,16},{4,20},{8,24},{12,28},{16,0},{20,4},{24,8},{28,12},{1,17},{... | collective-permute-start | bytes 983048 | tf_op jit(solution)/shard_map/ppermute | solution.py:796
  49.9 26.1 %collective-permute-start.11 = (bf16[1,160,1024]{2,1,0:T(8,128)(2,1)S(1)}, bf16[1,160,1024]{2,1,0:T(8,128)(2,1)S(1)}, u32[]{:S(2)}, u32[]{:S(2)}) collective-permute-start(bf16[1,160,1024]{2,1,0:T(8,128)(2,1)S(1)} %maximum_bitcast_fusion), channel_id=1, source_target_pairs={{0,24},{4,28},{8,16},{12,20},{16,8},{20,12},{24,0},{28,4},{1,25},{... | collective-permute-start | bytes 983048 | tf_op jit(solution)/shard_map/ppermute | solution.py:796
  87.8 41.3 %collective-permute-start.17 = (bf16[4,160,1024]{2,1,0:T(8,128)(2,1)S(1)}, bf16[4,160,1024]{2,1,0:T(8,128)(2,1)S(1)}, u32[]{:S(2)}, u32[]{:S(2)}) collective-permute-start(bf16[4,160,1024]{2,1,0:T(8,128)(2,1)S(1)} %pad_maximum_fusion.refs_0_), channel_id=1, source_target_pairs={{0,1},{1,0},{2,3},{3,2},{4,5},{5,4},{6,7},{7,6},{8,9},{9,8},{10,11... | collective-permute-start | bytes 3932168 | tf_op jit(solution)/shard_map/ppermute | solution.py:796
  88.3 40.8 %collective-permute-start.18 = (bf16[4,160,1024]{2,1,0:T(8,128)(2,1)S(1)}, bf16[4,160,1024]{2,1,0:T(8,128)(2,1)}, u32[]{:S(2)}, u32[]{:S(2)}) collective-permute-start(bf16[4,160,1024]{2,1,0:T(8,128)(2,1)S(1)} %pad_maximum_fusion.refs_0_), channel_id=1, source_target_pairs={{0,2},{1,3},{2,0},{3,1},{4,6},{5,7},{6,4},{7,5},{8,10},{9,11},{10,... | collective-permute-start | bytes 3932168 | tf_op jit(solution)/shard_map/ppermute | solution.py:796
  91.3 37.8 %collective-permute-start.19 = (bf16[4,160,1024]{2,1,0:T(8,128)(2,1)S(1)}, bf16[4,160,1024]{2,1,0:T(8,128)(2,1)}, u32[]{:S(2)}, u32[]{:S(2)}) collective-permute-start(bf16[4,160,1024]{2,1,0:T(8,128)(2,1)S(1)} %pad_maximum_fusion.refs_0_), channel_id=1, source_target_pairs={{0,4},{4,0},{8,12},{12,8},{16,20},{20,16},{24,28},{28,24},{1,5},{5... | collective-permute-start | bytes 3932168 | tf_op jit(solution)/shard_map/ppermute | solution.py:796
  129.1 42.2 %collective-permute-start.20 = (bf16[4,160,1024]{2,1,0:T(8,128)(2,1)}, bf16[4,160,1024]{2,1,0:T(8,128)(2,1)}, u32[]{:S(2)}, u32[]{:S(2)}) collective-permute-start(bf16[4,160,1024]{2,1,0:T(8,128)(2,1)} %collective-permute-done.18.refs_2_), channel_id=1, source_target_pairs={{0,1},{1,0},{2,3},{3,2},{4,5},{5,4},{6,7},{7,6},{8,9},{9,8},{10,11... | collective-permute-start | bytes 3932168 | tf_op jit(solution)/shard_map/ppermute | solution.py:796
  129.3 42.0 %collective-permute-start.21 = (bf16[4,160,1024]{2,1,0:T(8,128)(2,1)}, bf16[4,160,1024]{2,1,0:T(8,128)(2,1)}, u32[]{:S(2)}, u32[]{:S(2)}) collective-permute-start(bf16[4,160,1024]{2,1,0:T(8,128)(2,1)} %collective-permute-done.19.refs_4_), channel_id=1, source_target_pairs={{0,1},{1,0},{2,3},{3,2},{4,5},{5,4},{6,7},{7,6},{8,9},{9,8},{10,11... | collective-permute-start | bytes 3932168 | tf_op jit(solution)/shard_map/ppermute | solution.py:796
  129.7 46.1 %collective-permute-start.22 = (bf16[4,160,1024]{2,1,0:T(8,128)(2,1)}, bf16[4,160,1024]{2,1,0:T(8,128)(2,1)}, u32[]{:S(2)}, u32[]{:S(2)}) collective-permute-start(bf16[4,160,1024]{2,1,0:T(8,128)(2,1)} %collective-permute-done.18.refs_2_), channel_id=1, source_target_pairs={{0,4},{4,0},{8,12},{12,8},{16,20},{20,16},{24,28},{28,24},{1,5},{5... | collective-permute-start | bytes 3932168 | tf_op jit(solution)/shard_map/ppermute | solution.py:796
  131.3 40.1 %collective-permute-start.23 = (bf16[2,256,1024]{2,1,0:T(8,128)(2,1)}, bf16[2,256,1024]{2,1,0:T(8,128)(2,1)S(1)}, u32[]{:S(2)}, u32[]{:S(2)}) collective-permute-start(bf16[2,256,1024]{2,1,0:T(8,128)(2,1)} %constant_dynamic-slice_fusion.8), channel_id=1, source_target_pairs={{0,2},{1,3},{2,0},{3,1},{4,6},{5,7},{6,4},{7,5},{8,10},{9,11},{10,... | collective-permute-start | bytes 3145736 | tf_op jit(solution)/shard_map/ppermute | solution.py:796
  222.2 45.6 %collective-permute-start.26 = (bf16[4,2,2,128,1024]{4,3,2,1,0:T(8,128)(2,1)}, bf16[4,2,2,128,1024]{4,3,2,1,0:T(8,128)(2,1)}, u32[]{:S(2)}, u32[]{:S(2)}) collective-permute-start(bf16[4,2,2,128,1024]{4,3,2,1,0:T(8,128)(2,1)} %bitcast.152), channel_id=1, source_target_pairs={{0,1},{1,0},{2,3},{3,2},{4,5},{5,4},{6,7},{7,6},{8,9},{9,8},{10,11... | collective-permute-start | bytes 12582920 | tf_op jit(solution)/shard_map/ppermute | solution.py:796
  272.3 33.2 %collective-permute-start.28 = (bf16[4,128,1024]{2,1,0:T(8,128)(2,1)}, bf16[4,128,1024]{2,1,0:T(8,128)(2,1)}, u32[]{:S(2)}, u32[]{:S(2)}) collective-permute-start(bf16[4,128,1024]{2,1,0:T(8,128)(2,1)} %get-tuple-element.216), channel_id=1, source_target_pairs={{0,4},{4,0},{8,12},{12,8},{16,20},{20,16},{24,28},{28,24},{1,5},{5... | collective-permute-start | bytes 3145736 | tf_op jit(solution)/shard_map/ppermute | solution.py:796
  274.5 55.3 %collective-permute-start.29 = (bf16[2,256,1024]{2,1,0:T(8,128)(2,1)}, bf16[2,256,1024]{2,1,0:T(8,128)(2,1)}, u32[]{:S(2)}, u32[]{:S(2)}) collective-permute-start(bf16[2,256,1024]{2,1,0:T(8,128)(2,1)} %constant_dynamic-slice_fusion.4), channel_id=1, source_target_pairs={{0,2},{1,3},{2,0},{3,1},{4,6},{5,7},{6,4},{7,5},{8,10},{9,11},{10,... | collective-permute-start | bytes 3145736 | tf_op jit(solution)/shard_map/ppermute | solution.py:796
  300.3 29.6 %collective-permute-start.30 = (bf16[2,160,1024]{2,1,0:T(8,128)(2,1)}, bf16[2,160,1024]{2,1,0:T(8,128)(2,1)}, u32[]{:S(2)}, u32[]{:S(2)}) collective-permute-start(bf16[2,160,1024]{2,1,0:T(8,128)(2,1)} %get-tuple-element.226), channel_id=1, source_target_pairs={{0,2},{1,3},{2,0},{3,1},{4,6},{5,7},{6,4},{7,5},{8,10},{9,11},{10,... | collective-permute-start | bytes 1966088 | tf_op jit(solution)/shard_map/ppermute | solution.py:796
  302.0 27.9 %collective-permute-start.31 = (bf16[2,160,1024]{2,1,0:T(8,128)(2,1)S(1)}, bf16[2,160,1024]{2,1,0:T(8,128)(2,1)}, u32[]{:S(2)}, u32[]{:S(2)}) collective-permute-start(bf16[2,160,1024]{2,1,0:T(8,128)(2,1)S(1)} %get-tuple-element.225), channel_id=1, source_target_pairs={{0,4},{4,0},{8,12},{12,8},{16,20},{20,16},{24,28},{28,24},{1,5},{5... | collective-permute-start | bytes 1966088 | tf_op jit(solution)/shard_map/ppermute | solution.py:796
  305.5 49.9 %collective-permute-start.34 = (bf16[4,128,1024]{2,1,0:T(8,128)(2,1)}, bf16[4,128,1024]{2,1,0:T(8,128)(2,1)}, u32[]{:S(2)}, u32[]{:S(2)}) collective-permute-start(bf16[4,128,1024]{2,1,0:T(8,128)(2,1)} %fusion.7), channel_id=1, source_target_pairs={{0,4},{4,0},{8,12},{12,8},{16,20},{20,16},{24,28},{28,24},{1,5},{5... | collective-permute-start | bytes 3145736 | tf_op jit(solution)/shard_map/ppermute | solution.py:796
  309.8 45.6 %collective-permute-start.33 = (bf16[4,128,1024]{2,1,0:T(8,128)(2,1)}, bf16[4,128,1024]{2,1,0:T(8,128)(2,1)}, u32[]{:S(2)}, u32[]{:S(2)}) collective-permute-start(bf16[4,128,1024]{2,1,0:T(8,128)(2,1)} %fusion), channel_id=1, source_target_pairs={{0,2},{1,3},{2,0},{3,1},{4,6},{5,7},{6,4},{7,5},{8,10},{9,11},{10,... | collective-permute-start | bytes 3145736 | tf_op jit(solution)/shard_map/ppermute | solution.py:796
  336.3 42.3 %collective-permute-start.36 = (bf16[4,160,1024]{2,1,0:T(8,128)(2,1)}, bf16[4,160,1024]{2,1,0:T(8,128)(2,1)S(1)}, u32[]{:S(2)}, u32[]{:S(2)}) collective-permute-start(bf16[4,160,1024]{2,1,0:T(8,128)(2,1)} %fusion.12), channel_id=1, source_target_pairs={{0,4},{4,0},{8,12},{12,8},{16,20},{20,16},{24,28},{28,24},{1,5},{5... | collective-permute-start | bytes 3932168 | tf_op jit(solution)/shard_map/ppermute | solution.py:796
  337.8 40.8 %collective-permute-start.35 = (bf16[4,160,1024]{2,1,0:T(8,128)(2,1)}, bf16[4,160,1024]{2,1,0:T(8,128)(2,1)}, u32[]{:S(2)}, u32[]{:S(2)}) collective-permute-start(bf16[4,160,1024]{2,1,0:T(8,128)(2,1)} %copy-done.16), channel_id=1, source_target_pairs={{0,2},{1,3},{2,0},{3,1},{4,6},{5,7},{6,4},{7,5},{8,10},{9,11},{10,... | collective-permute-start | bytes 3932168 | tf_op jit(solution)/shard_map/ppermute | solution.py:796
  357.7 24.0 %collective-permute-start.37 = (bf16[128,1024]{1,0:T(8,128)(2,1)S(1)}, bf16[128,1024]{1,0:T(8,128)(2,1)S(1)}, u32[]{:S(2)}, u32[]{:S(2)}) collective-permute-start(bf16[128,1024]{1,0:T(8,128)(2,1)S(1)} %get-tuple-element.229), channel_id=1, source_target_pairs={{0,8},{4,12},{8,0},{12,4},{16,24},{20,28},{24,16},{28,20},{1,9},{5... | collective-permute-start | bytes 786440 | tf_op jit(solution)/shard_map/ppermute | solution.py:796
  357.7 24.0 %collective-permute-start.38 = (bf16[128,1024]{1,0:T(8,128)(2,1)S(1)}, bf16[128,1024]{1,0:T(8,128)(2,1)S(1)}, u32[]{:S(2)}, u32[]{:S(2)}) collective-permute-start(bf16[128,1024]{1,0:T(8,128)(2,1)S(1)} %get-tuple-element.228), channel_id=1, source_target_pairs={{0,16},{4,20},{8,24},{12,28},{16,0},{20,4},{24,8},{28,12},{1,17},{... | collective-permute-start | bytes 786440 | tf_op jit(solution)/shard_map/ppermute | solution.py:796
  394.1 20.4 %collective-permute-start.40 = (bf16[4,2,2,112,1024]{4,3,2,1,0:T(8,128)(2,1)}, bf16[4,2,2,112,1024]{4,3,2,1,0:T(8,128)(2,1)}, u32[]{:S(2)}, u32[]{:S(2)}) collective-permute-start(bf16[4,2,2,112,1024]{4,3,2,1,0:T(8,128)(2,1)} %bitcast.153), channel_id=1, source_target_pairs={{0,1},{1,0},{2,3},{3,2},{4,5},{5,4},{6,7},{7,6},{8,9},{9,8},{10,11... | collective-permute-start | bytes 11010056 | tf_op jit(solution)/shard_map/ppermute | solution.py:796
  394.2 29.4 %collective-permute-start.41 = (bf16[160,1024]{1,0:T(8,128)(2,1)}, bf16[160,1024]{1,0:T(8,128)(2,1)}, u32[]{:S(2)}, u32[]{:S(2)}) collective-permute-start(bf16[160,1024]{1,0:T(8,128)(2,1)} %get-tuple-element.223), channel_id=1, source_target_pairs={{0,8},{4,12},{8,0},{12,4},{16,24},{20,28},{24,16},{28,20},{1,9},{5... | collective-permute-start | bytes 983048 | tf_op jit(solution)/shard_map/ppermute | solution.py:796
  397.8 25.9 %collective-permute-start.42 = (bf16[160,1024]{1,0:T(8,128)(2,1)}, bf16[160,1024]{1,0:T(8,128)(2,1)}, u32[]{:S(2)}, u32[]{:S(2)}) collective-permute-start(bf16[160,1024]{1,0:T(8,128)(2,1)} %get-tuple-element.222), channel_id=1, source_target_pairs={{0,16},{4,20},{8,24},{12,28},{16,0},{20,4},{24,8},{28,12},{1,17},{... | collective-permute-start | bytes 983048 | tf_op jit(solution)/shard_map/ppermute | solution.py:796
  398.8 24.8 %collective-permute-start.43 = (bf16[160,1024]{1,0:T(8,128)(2,1)S(1)}, bf16[160,1024]{1,0:T(8,128)(2,1)}, u32[]{:S(2)}, u32[]{:S(2)}) collective-permute-start(bf16[160,1024]{1,0:T(8,128)(2,1)S(1)} %get-tuple-element.221), channel_id=1, source_target_pairs={{0,24},{4,28},{8,16},{12,20},{16,8},{20,12},{24,0},{28,4},{1,25},{... | collective-permute-start | bytes 983048 | tf_op jit(solution)/shard_map/ppermute | solution.py:796
  430.4 21.2 %collective-permute-start.47 = (bf16[4,112,1024]{2,1,0:T(8,128)(2,1)S(1)}, bf16[4,112,1024]{2,1,0:T(8,128)(2,1)S(1)}, u32[]{:S(2)}, u32[]{:S(2)}) collective-permute-start(bf16[4,112,1024]{2,1,0:T(8,128)(2,1)S(1)} %fusion.14), channel_id=1, source_target_pairs={{0,4},{4,0},{8,12},{12,8},{16,20},{20,16},{24,28},{28,24},{1,5},{5... | collective-permute-start | bytes 2752520 | tf_op jit(solution)/shard_map/ppermute | solution.py:796
  431.2 21.0 %collective-permute-start.46 = (bf16[4,112,1024]{2,1,0:T(8,128)(2,1)S(1)}, bf16[4,112,1024]{2,1,0:T(8,128)(2,1)S(1)}, u32[]{:S(2)}, u32[]{:S(2)}) collective-permute-start(bf16[4,112,1024]{2,1,0:T(8,128)(2,1)S(1)} %fusion.13), channel_id=1, source_target_pairs={{0,2},{1,3},{2,0},{3,1},{4,6},{5,7},{6,4},{7,5},{8,10},{9,11},{10,... | collective-permute-start | bytes 2752520 | tf_op jit(solution)/shard_map/ppermute | solution.py:796
  454.7 23.1 %collective-permute-start.51 = (bf16[2,256,1024]{2,1,0:T(8,128)(2,1)}, bf16[2,256,1024]{2,1,0:T(8,128)(2,1)}, u32[]{:S(2)}, u32[]{:S(2)}) collective-permute-start(bf16[2,256,1024]{2,1,0:T(8,128)(2,1)} %constant_dynamic-slice_fusion.1), channel_id=1, source_target_pairs={{0,2},{1,3},{2,0},{3,1},{4,6},{5,7},{6,4},{7,5},{8,10},{9,11},{10,... | collective-permute-start | bytes 3145736 | tf_op jit(solution)/shard_map/ppermute | solution.py:796
  (68 other events, 799.9 us)
Sparse Core Ops, SparseCore 0:
  87.2 97.5 all-gather.2

commit v8 on v6

--- a/solution.py
+++ b/solution.py
@@ -290,7 +290,7 @@
 LOG2E = 1.4426950408889634
 LN2 = 0.6931471805599453
 LIMIT = 58 << 20
-LIGHT = pl.CostEstimate(flops=1 << 20, bytes_accessed=1 << 16, transcendentals=0)
+LIGHT = pl.CostEstimate(flops=1, bytes_accessed=1, transcendentals=0)
 
 def _dot(a, b, dims=(((1,), (0,)), ((), ()))):
     return lax.dot_general(a, b, dims, preferred_element_type=jnp.float32)
@@ -597,13 +597,14 @@
 
 def mid_a_kernel(ids_ref, x_hbm, o_hbm, g4_ref, chip_ref, core_ref, gain_ref, *refs, masks):
     gathered = refs[:len(masks)]
-    (mixed_out, acc_out, gh2_out, h2_out, h2t_out, gm_out, wo_out, gw_out,
+    (mixed_out, acc_out, gh2_out, h2_out, h2t_out, gm_out, wo_out, keep_out, send_out,
      xs, os, wo, ws_in, ws_back, mixed, h2, h2t, acc, gh2, gm, st_in, st_back, sems) = refs[len(masks):]
     flat = ids_ref[1]
     rows, width = xs.shape
     half, own = st_back.shape[2], width // (2 * st_in.shape[0])
-    def emit(src, which, dst_rows, lead=slice(None), src_rows=slice(None), lanes=slice(None)):
-        pltpu.make_async_copy(src.at[lead, :, src_rows, lanes], gw_out.at[lead, :, dst_rows, lanes], sems.at[which]).start()
+    core = flat & 1
+    def emit(src, which, **at):
+        by_core(core, keep_out, send_out, src, sem=sems.at[which], **at)
     loads = [pltpu.make_async_copy(x_hbm, xs, sems.at[0]), pltpu.make_async_copy(o_hbm, os, sems.at[1])]
     for load in loads:
         load.start()
@@ -657,8 +658,8 @@
     stack = half + ff // width * (width // shards)
     return pl.pallas_call(
         functools.partial(mid_a_kernel, masks=masks),
-        out_shape=(full(rows, width), full(rows, width), full(rows, width), low(rows, width), low(width, rows), low(rows, width), low(width, width), low(shards // 2, 2, stack, width)),
-        in_specs=[SM] + [ANY] * 5 + [VM] + [ANY] * len(gathered), out_specs=[ANY] * 8,
+        out_shape=(full(rows, width), full(rows, width), full(rows, width), low(rows, width), low(width, rows), low(rows, width), low(width, width), low(shards // 2, stack, width), low(shards // 2, stack, width)),
+        in_specs=[SM] + [ANY] * 5 + [VM] + [ANY] * len(gathered), out_specs=[ANY] * 9,
         scratch_shapes=[vm(rows, width), vm(rows, width), vm(width, width), vm(width, ff), vm(ff, width), vf(rows, width), vm(rows, width), vm(width, rows),
                         vf(rows, width), vf(rows, width), vm(rows, width), vm(shards // 2, 2, stack - half, width), vm(shards // 2, 2, half, width), pltpu.SemaphoreType.DMA((10,))],
         compiler_params=pltpu.CompilerParams(vmem_limit_bytes=LIMIT),
@@ -948,59 +949,70 @@
     g2.corner, g_chip = tie((attended, g2.pieces[3], g2.pieces[5]), g2.corner, g_chip)
     g2.take(g2.corner, 6)
     g_core = send_core(g4, g_chip, me)
-    *state, gw_a = mid_a(ids, x, attended, g4, (g_chip, g_core), gains, *g2.all_pieces(), ff)
-    r_a = lax.psum_scatter(gw_a.reshape(-1, width), both, scatter_dimension=0, tiled=True)
+    *state, keep3, send3 = mid_a(ids, x, attended, g4, (g_chip, g_core), gains, *g2.all_pieces(), ff)
+    sc3 = Scatter(keep3, send3, pos, True)
     out, gb, g_att, keep2, send2 = mid_b(ids, gains, state, attended, full3, ff)
-    sc2 = Scatter(keep2, send2, pos, True)
+    sc3.other, = tie(gb, sc3.other)
+    sc3.fold()
+    send2, = tie(sc3.own, send2)
+    sc2 = Scatter(keep2, send2, pos, False)
     out4 = out.reshape(parts, rows, width)
+    out4, = tie(sc3.own, out4)
     out_chip = send_chip(out4, me)
     count = pairs // 4
     back = lambda first, g, prev: attn_bwd(length, q, k, v, g, attended, lse, t_back, first, count, prev)
+    g_att, = tie(sc3.own, g_att)
     dq, dk, dv, off0 = back(0, g_att, None)
     sc2.other, = tie(off0, sc2.other)
     sc2.fold()
-    g_att, = tie((sc2.own, sc2.to_x, sc2.to_y), g_att)
+    sc3.came_y, = tie(sc2.own, sc3.came_y)
+    sc3.turn()
+    g_att, = tie(sc3.sent, g_att)
     dq, dk, dv, off1 = back(count, g_att, (dq, dk, dv))
-    sc2.came_y, = tie(off1, sc2.came_y)
+    sc2.came_x, sc2.came_y = tie((off1, out_chip), sc2.came_x, sc2.came_y)
     sc2.turn()
+    out4_in, out_chip = tie(sc2.sent, out4, out_chip)
+    out_core = send_core(out4_in, out_chip, me)
     g_att, = tie(sc2.sent, g_att)
     dq, dk, dv, off2 = back(2 * count, g_att, (dq, dk, dv))
     cols = 128 * count
-    keep, send = qkv_gw(ids, hidden, dq, dk, dv, bucket_rows, (), shards, 0, 3 * cols)
+    sc3.came_x, sc3.came_y = tie((off2, out_core), sc3.came_x, sc3.came_y)
+    h_in, = tie((sc3.came_x, sc3.came_y), hidden)
+    keep, send = qkv_gw(ids, h_in, dq, dk, dv, bucket_rows, (), shards, 0, 3 * cols)
+    sc3.came_x, sc2.came_x, sc2.came_y = tie(keep, sc3.came_x, sc2.came_x, sc2.came_y)
+    sc3.column()
+    sc2.column()
+    g_att, send = tie((sc3.mine, sc2.mine), g_att, send)
     sc1 = Scatter(keep, send, pos, False)
-    sc2.came_x, sc2.came_y = tie(keep, sc2.came_x, sc2.came_y)
-    sc2.column()
-    g_att, = tie((sc2.mine, out_chip), g_att)
-    out4_in, out_chip = tie(sc2.mine, out4, out_chip)
-    out_core = send_core(out4_in, out_chip, me)
     dq, dk, dv, off3 = back(3 * count, g_att, (dq, dk, dv))
-    sc1.other, = tie((off3, out_core), sc1.other)
+    sc1.other, = tie(off3, sc1.other)
     sc1.fold()
-    h_in, = tie(sc1.own, hidden)
+    h_in, = tie((sc1.own, sc3.came), hidden)
     keep, send = qkv_gw(ids, h_in, dq, dk, dv, bucket_rows, (off0, off1, off2, off3), shards, 3 * cols, cols)
     sc0 = Scatter(keep, send, pos, False)
     gb_in, = tie(keep, gb)
     gx = qkv_gx(x, gb_in, dq, dk, dv, gains, w_qkv)
+    sc1.came_x, sc1.came_y = tie(gx, sc1.came_x, sc1.came_y)
+    sc1.turn()
+    gx, = tie(sc1.sent, gx)
     gx4 = gx.reshape(parts, rows, width)
     gx_chip = send_chip(gx4, me)
-    sc1.came_x, sc1.came_y = tie((gx, sc2.came), sc1.came_x, sc1.came_y)
-    sc1.turn()
-    sc0.other, r_a = tie(sc1.sent, sc0.other, r_a)
+    sc0.other, = tie((sc1.sent, sc2.came), sc0.other)
     sc0.fold()
     out4, out_chip, out_core = tie(sc0.own, out4, out_chip, out_core)
     layer_out = place(out4, out_chip, out_core, me)
-    sc0.came_x, sc0.came_y = tie(layer_out, sc0.came_x, sc0.came_y)
+    sc1.came_x, sc1.came_y = tie(layer_out, sc1.came_x, sc1.came_y)
+    sc1.column()
+    sc0.came_x, sc0.came_y = tie(sc1.mine, sc0.came_x, sc0.came_y)
     sc0.turn()
     sc2.came = list(tie(sc0.sent, *sc2.came))
-    r2, r_a = sc2.result(), up(r_a)
-    sc1.came_x, sc1.came_y = tie((r2, sc0.sent), sc1.came_x, sc1.came_y)
-    sc1.column()
-    sc0.came_x, sc0.came_y = tie(sc1.came[0], sc0.came_x, sc0.came_y)
+    sc3.came = list(tie(sc0.sent, *sc3.came))
+    r2, r_a = sc2.result(), sc3.result()
+    sc0.came_x, sc0.came_y = tie((r2, sc1.came[0]), sc0.came_x, sc0.came_y)
     sc0.column()
-    gx4, gx_chip = tie((sc0.came[0], sc1.came), gx4, gx_chip)
+    gx4, gx_chip = tie((sc0.mine, sc1.came, sc0.came[0]), gx4, gx_chip)
     gx_core = send_core(gx4, gx_chip, me)
     input_grad = place(gx4, gx_chip, gx_core, me)
-    sc1.came = list(tie(sc0.came[0], *sc1.came))
     sc0.came = list(tie(input_grad, *sc0.came))
     r1, r0 = sc1.result(), sc0.result()
     join = lambda v: jnp.concatenate([v[i:i + own] for i in range(0, v.shape[0], own)], 1).reshape(own, shards, 1, half)

time: 556 us -> 552 us (level)
  waiting for transfers between devices: 171 us -> 137 us
  starting transfers between devices: 49.5 us -> 76.1 us
  other arithmetic: 44.8 us -> 52 us
    ppermute x53 -> x61, waiting for transfers between devices: 171 us -> 137 us  [swap(): lax.ppermute(value, axis, [(i, i ^ mask) for i in range(lax.axis_size(axi...]
    ppermute x53 -> x61, starting transfers between devices: 49.4 us -> 76.1 us  [swap(): lax.ppermute(value, axis, [(i, i ^ mask) for i in range(lax.axis_size(axi...]
    convert_element_type x4 -> x8, other arithmetic: 13.6 us -> 15.5 us  [quarter(): return (cut(self.mine) + cut(self.other)).astype(jnp.bfloat16)]
  transfers between devices with their start and end apart: 55 -> 62, of which waited for: 21 -> 24; matrix products, arithmetic and copies ran while one was open for 13% -> 12% of each run, Pallas kernels for 41% -> 42%
where the time goes in v8:
time: 552 us; the launch traced here: 544 us
  Pallas kernels  226 us (41%)
  waiting for transfers between devices  137 us (25%)
  starting transfers between devices  76.1 us (14%)
  other arithmetic  52 us (9%)
  local copies, waits for them, and re-layouts  37.7 us (7%)
  between operations  15.5 us (3%)
    ppermute x61, waiting for transfers between devices, swap(): lax.ppermute(value, axis, [(i, i ^ mask) for i in range(lax.axis_size(axi...  137 us
    ppermute x61, starting transfers between devices, swap(): lax.ppermute(value, axis, [(i, i ^ mask) for i in range(lax.axis_size(axi...  76.1 us
    pallas_call x4, Pallas kernels, attn_bwd(): pl.pallas_call(functools.partial(bwd_kernel, rows=rows, seq_len=seq_len,...  65.6 us
    pallas_call x1, Pallas kernels, mid_b(): pl.pallas_call(mid_b_kernel, out_shape=(low(rows, width), low(rows, width...  45.5 us
    pallas_call x1, Pallas kernels, mid_a(): pl.pallas_call(functools.partial(mid_a_kernel, masks=masks), out_shape=(f...  39.7 us
    pallas_call x2, Pallas kernels, attn_fwd(): pl.pallas_call(functools.partial(fwd_kernel, rows=rows, seq_len=seq_len,...  33.3 us
    convert_element_type x8, other arithmetic, quarter(): return (cut(self.mine) + cut(self.other)).astype(jnp.bfloat16)  15.5 us
    pallas_call x2, Pallas kernels, qkv_gw(): pl.pallas_call(gw_kernel, out_shape=(half, half), grid=(1,), in_specs=[SM...  14.6 us
  transfers between devices with their start and end apart: 62, of which 24 were waited for; matrix products, arithmetic and copies ran while one was open for 12% of the time, Pallas kernels for 42%

profile of v8, /device:TPU:0, one launch (start us, length us, event | category | flops | bytes accessed | tf_op | source)
XLA Modules:
  0.0 544.1 jit_solution(13817400737720066042)
XLA Ops:
  28.2 6.8 %collective-permute-done.3 = bf16[1,112,1024]{2,1,0:T(8,128)(2,1)} collective-permute-done((bf16[1,112,1024]{2,1,0:T(8,128)(2,1)S(1)}, bf16[1,112,1024]{2,1,0:T(8,128)(2,1)}, u32[]{:S(2)}, u32[]{:S(2)}) %collective-permute-start.3) | collective-permute-done | bytes 229408 | tf_op jit(solution)/shard_map/ppermute | solution.py:799
  36.2 4.2 collective-permute-done.1
  40.4 4.8 collective-permute-done.chip_ref
  51.8 21.9 %collective-permute-done.6 = bf16[1,160,1024]{2,1,0:T(8,128)(2,1)S(1)} collective-permute-done((bf16[1,160,1024]{2,1,0:T(8,128)(2,1)S(1)}, bf16[1,160,1024]{2,1,0:T(8,128)(2,1)S(1)}, u32[]{:S(2)}, u32[]{:S(2)}) %collective-permute-start.6) | collective-permute-done | bytes 327712 | tf_op jit(solution)/shard_map/ppermute | solution.py:799
  78.2 7.3 %collective-permute-done.10.refs_8_ = bf16[2,112,1024]{2,1,0:T(8,128)(2,1)S(1)} collective-permute-done((bf16[2,112,1024]{2,1,0:T(8,128)(2,1)S(1)}, bf16[2,112,1024]{2,1,0:T(8,128)(2,1)S(1)}, u32[]{:S(2)}, u32[]{:S(2)}) %collective-permute-start.10) | collective-permute-done | bytes 458784 | tf_op jit(solution)/shard_map/ppermute | solution.py:799
  99.2 13.2 %qkv_fwd.1 = (bf16[1024,1024]{1,0:T(8,128)(2,1)}, bf16[1024,1024]{1,0:T(8,128)(2,1)}, bf16[1024,1024]{1,0:T(8,128)(2,1)}, bf16[1024,1024]{1,0:T(8,128)(2,1)}, bf...) custom-call(s32[3]{0:T(128)} %pad_add_fusion.1.ids_ref, ...), custom_call_target="tpu_custom_call" | custom-call | flops 1 | bytes 1 | tf_op jit(solution)/shard_map/qkv_fwd/pallas_call | solution.py:524
  112.4 16.6 %attn_fwd.2 = (bf16[1024,1024]{1,0:T(8,128)(2,1)}, f32[8,1024,128]{2,1,0:T(8,128)}) custom-call(s32[1]{0:T(128)} %dynamic_slice.236.len_ref, bf16[1024,1024]{1,0:T(8,128)(2,1)} %get-tuple-element.140.q_ref, bf16[1024,1024]{1,0:T(8,128)(2,1)} %get-tuple-element.131.k_ref, bf16[1024,1024]{1,0:T(8,128)(2,1)} %get-tuple-element.132.v_ref, ...), custom_call_target="tpu_custom_call" | custom-call | flops 1 | bytes 1 | tf_op jit(solution)/shard_map/attn_fwd/pallas_call | solution.py:360
  131.8 16.6 %attn_fwd.3 = (bf16[1024,1024]{1,0:T(8,128)(2,1)}, f32[8,1024,128]{2,1,0:T(8,128)}) custom-call(s32[1]{0:T(128)} %dynamic_slice.236.len_ref, bf16[1024,1024]{1,0:T(8,128)(2,1)} %get-tuple-element.140.q_ref, bf16[1024,1024]{1,0:T(8,128)(2,1)} %get-tuple-element.131.k_ref, ...), custom_call_target="tpu_custom_call", output_to_operand_aliasing={{0}: (5, {}), {1}: (6, {})} | custom-call | flops 1 | bytes 1 | tf_op jit(solution)/shard_map/attn_fwd/pallas_call | solution.py:360
  148.5 22.8 %collective-permute-done.23.chip_ref = bf16[2,256,1024]{2,1,0:T(8,128)(2,1)S(1)} collective-permute-done((bf16[2,256,1024]{2,1,0:T(8,128)(2,1)}, bf16[2,256,1024]{2,1,0:T(8,128)(2,1)S(1)}, u32[]{:S(2)}, u32[]{:S(2)}) %collective-permute-start.23) | collective-permute-done | bytes 1048608 | tf_op jit(solution)/shard_map/ppermute | solution.py:799
  171.3 4.4 collective-permute-done.22.refs_6_
  176.5 4.2 collective-permute-done.24.core_ref
  182.4 39.7 %mid_a.1 = (f32[1024,1024]{1,0:T(8,128)}, f32[1024,1024]{1,0:T(8,128)}, f32[1024,1024]{1,0:T(8,128)}, bf16[1024,1024]{1,0:T(8,128)(2,1)}, bf16[1024,1024]{1,0:T(...) custom-call(s32[3]{0:T(128)} %pad_add_fusion.1.ids_ref, ...), custom_call_target="tpu_custom_call" | custom-call | flops 1 | bytes 1 | tf_op jit(solution)/shard_map/mid_a/pallas_call | solution.py:659
  222.3 45.5 %mid_b.1 = (bf16[1024,1024]{1,0:T(8,128)(2,1)}, bf16[1024,1024]{1,0:T(8,128)(2,1)}, bf16[1024,1024]{1,0:T(8,128)(2,1)}, bf16[16,160,1024]{2,1,0:T(8,128)(2,1)}, bf16[16,160,1024]{2,1,0:T(8,128)(2,1)}) custom-call(s32[3]{0:T(128)} %pad_add_fusion.1.ids_ref, f32[8,1024]{1,0:T(8,128)} %get-tuple-element.133.gain_ref, ...), custom_call_target="tpu_custom_call" | custom-call | flops 1 | bytes 1 | tf_op jit(solution)/shard_map/mid_b/pallas_call | solution.py:727
  267.8 4.1 fusion.6
  274.9 16.6 %attn_bwd.4 = (bf16[1024,1024]{1,0:T(8,128)(2,1)}, bf16[1024,1024]{1,0:T(8,128)(2,1)}, bf16[1024,1024]{1,0:T(8,128)(2,1)}, f32[4,2048]{1,0:T(4,128)}) custom-call(s32[1]{0:T(128)} %dynamic_slice.236.len_ref, bf16[1024,1024]{1,0:T(8,128)(2,1)} %get-tuple-element.140.q_ref, bf16[1024,1024]{1,0:T(8,128)(2,1)} %get-tuple-element.131.k_ref, ...), custom_call_target="tpu_custom_call" | custom-call | flops 1 | bytes 1 | tf_op jit(solution)/shard_map/attn_bwd/pallas_call | solution.py:439
  296.8 5.3 add_convert_fusion.4
  302.2 3.5 fusion
  309.9 16.2 %attn_bwd.5 = (bf16[1024,1024]{1,0:T(8,128)(2,1)}, bf16[1024,1024]{1,0:T(8,128)(2,1)}, bf16[1024,1024]{1,0:T(8,128)(2,1)}, f32[4,2048]{1,0:T(4,128)}) custom-call(s32[1]{0:T(128)} %dynamic_slice.236.len_ref, bf16[1024,1024]{1,0:T(8,128)(2,1)} %get-tuple-element.140.q_ref, ...), custom_call_target="tpu_custom_call", output_to_operand_aliasing={{0}: (8, {}), {1}: (9, {}), {2}: (10, {})} | custom-call | flops 1 | bytes 1 | tf_op jit(solution)/shard_map/attn_bwd/pallas_call | solution.py:439
  328.5 17.3 %collective-permute-done.30 = bf16[2,160,1024]{2,1,0:T(8,128)(2,1)S(1)} collective-permute-done((bf16[2,160,1024]{2,1,0:T(8,128)(2,1)S(1)}, bf16[2,160,1024]{2,1,0:T(8,128)(2,1)S(1)}, u32[]{:S(2)}, u32[]{:S(2)}) %collective-permute-start.30) | collective-permute-done | bytes 655392 | tf_op jit(solution)/shard_map/ppermute | solution.py:799
  353.5 16.4 %attn_bwd.6 = (bf16[1024,1024]{1,0:T(8,128)(2,1)}, bf16[1024,1024]{1,0:T(8,128)(2,1)}, bf16[1024,1024]{1,0:T(8,128)(2,1)}, f32[4,2048]{1,0:T(4,128)}) custom-call(s32[1]{0:T(128)} %dynamic_slice.236.len_ref, bf16[1024,1024]{1,0:T(8,128)(2,1)} %get-tuple-element.140.q_ref, ...), custom_call_target="tpu_custom_call", output_to_operand_aliasing={{0}: (8, {}), {1}: (9, {}), {2}: (10, {})} | custom-call | flops 1 | bytes 1 | tf_op jit(solution)/shard_map/attn_bwd/pallas_call | solution.py:439
  369.9 9.4 %qkv_gw.2 = (bf16[16,96,768]{2,1,0:T(8,128)(2,1)}, bf16[16,96,768]{2,1,0:T(8,128)(2,1)}) custom-call(s32[3]{0:T(128)} %pad_add_fusion.1.ids_ref, bf16[1024,1024]{1,0:T(8,128)(2,1)} %get-tuple-element.201.h_ref, bf16[1024,1024]{1,0:T(8,128)(2,1)} %get-tuple-element.189.dq_ref.refs_0_, bf16[1024,1024]{1,0:T(8,128)(2,1)} %get-tuple-element.190.dk_ref.refs_1_, ...), custom_call_target="tpu_custom_call" | custom-call | flops 1 | bytes 1 | tf_op jit(solution)/shard_map/qkv_gw/pallas_call | solution.py:764
  386.3 16.5 %attn_bwd.7 = (bf16[1024,1024]{1,0:T(8,128)(2,1)}, bf16[1024,1024]{1,0:T(8,128)(2,1)}, bf16[1024,1024]{1,0:T(8,128)(2,1)}, f32[4,2048]{1,0:T(4,128)}) custom-call(s32[1]{0:T(128)} %dynamic_slice.236.len_ref, bf16[1024,1024]{1,0:T(8,128)(2,1)} %get-tuple-element.140.q_ref, ...), custom_call_target="tpu_custom_call", output_to_operand_aliasing={{0}: (8, {}), {1}: (9, {}), {2}: (10, {})} | custom-call | flops 1 | bytes 1 | tf_op jit(solution)/shard_map/attn_bwd/pallas_call | solution.py:439
  403.1 4.1 collective-permute-start.39
  411.5 5.0 collective-permute-done.38
  416.5 9.5 %collective-permute-done.39 = bf16[128,1024]{1,0:T(8,128)(2,1)} collective-permute-done((bf16[128,1024]{1,0:T(8,128)(2,1)}, bf16[128,1024]{1,0:T(8,128)(2,1)}, u32[]{:S(2)}, u32[]{:S(2)}) %collective-permute-start.39) | collective-permute-done | bytes 262176 | tf_op jit(solution)/shard_map/ppermute | solution.py:799
  426.0 5.1 qkv_gw.3
  431.3 14.2 %qkv_gx.1 = bf16[1024,1024]{1,0:T(8,128)(2,1)} custom-call(bf16[1024,1024]{1,0:T(8,128)(2,1)} %get-tuple-element.134.x_hbm.x_ref, bf16[1024,1024]{1,0:T(8,128)(2,1)} %get-tuple-element.206.gb_ref, bf16[1024,1024]{1,0:T(8,128)(2,1)} %get-tuple-element.202.dq_ref, bf16[1024,1024]{1,0:T(8,128)(2,1)} %get-tuple-element.203.dk_ref, ...), custom_call_target="tpu_custom_call" | custom-call | flops 1 | bytes 1 | tf_op jit(solution)/shard_map/qkv_gx/pallas_call | solution.py:788
  453.9 3.7 collective-permute-done.45
  461.2 3.5 collective-permute-done.48
  468.4 12.4 %collective-permute-start.51 = (bf16[96,768]{1,0:T(8,128)(2,1)S(1)}, bf16[96,768]{1,0:T(8,128)(2,1)S(1)}, u32[]{:S(2)}, u32[]{:S(2)}) collective-permute-start(bf16[96,768]{1,0:T(8,128)(2,1)S(1)} %get-tuple-element.261), channel_id=1, source_target_pairs={{0,8},{4,12},{8,0},{12,4},{16,24},{20,28},{24,16},{28,20},{1,9},{5... | collective-permute-start | bytes 442376 | tf_op jit(solution)/shard_map/ppermute | solution.py:799
  485.7 7.4 %collective-permute-done.54 = bf16[96,768]{1,0:T(8,128)(2,1)S(1)} collective-permute-done((bf16[96,768]{1,0:T(8,128)(2,1)S(1)}, bf16[96,768]{1,0:T(8,128)(2,1)S(1)}, u32[]{:S(2)}, u32[]{:S(2)}) %collective-permute-start.54) | collective-permute-done | bytes 147488 | tf_op jit(solution)/shard_map/ppermute | solution.py:799
  500.7 11.4 %collective-permute-start.56 = (bf16[112,256]{1,0:T(8,128)(2,1)}, bf16[112,256]{1,0:T(8,128)(2,1)}, u32[]{:S(2)}, u32[]{:S(2)}) collective-permute-start(bf16[112,256]{1,0:T(8,128)(2,1)} %get-tuple-element.275), channel_id=1, source_target_pairs={{0,8},{4,12},{8,0},{12,4},{16,24},{20,28},{24,16},{28,20},{1,9},{5... | collective-permute-start | bytes 172040 | tf_op jit(solution)/shard_map/ppermute | solution.py:799
  (309 shorter events, 139.0 us)
Async XLA Ops:
  7.2 215.1 %all-gather.3.cloned.1.call-start = ((), (), s32[]{:S(2)}) async-start(), calls=%async_computation | async-start | bytes 8650752 | tf_op jit(solution)/shard_map/all_gather | solution.py:936
  20.4 24.8 %collective-permute-start = (bf16[2,256,1024]{2,1,0:T(8,128)(2,1)}, bf16[2,256,1024]{2,1,0:T(8,128)(2,1)S(1)}, u32[]{:S(2)}, u32[]{:S(2)}) collective-permute-start(bf16[2,256,1024]{2,1,0:T(8,128)(2,1)} %constant_dynamic-slice_fusion.11), channel_id=1, source_target_pairs={{0,2},{1,3},{2,0},{3,1},{4,6},{5,7},{6,4},{7,5},{8,10},{9,11},{10,... | collective-permute-start | bytes 3145736 | tf_op jit(solution)/shard_map/ppermute | solution.py:799
  45.2 28.5 %collective-permute-start.7 = (bf16[4,112,1024]{2,1,0:T(8,128)(2,1)S(1)}, bf16[4,112,1024]{2,1,0:T(8,128)(2,1)S(1)}, u32[]{:S(2)}, u32[]{:S(2)}) collective-permute-start(bf16[4,112,1024]{2,1,0:T(8,128)(2,1)S(1)} %pad_maximum_fusion.8.refs_0_), channel_id=1, source_target_pairs={{0,2},{1,3},{2,0},{3,1},{4,6},{5,7},{6,4},{7,5},{8,10},{9,11},{10,... | collective-permute-start | bytes 2752520 | tf_op jit(solution)/shard_map/ppermute | solution.py:799
  46.7 27.0 %collective-permute-start.8 = (bf16[4,112,1024]{2,1,0:T(8,128)(2,1)S(1)}, bf16[4,112,1024]{2,1,0:T(8,128)(2,1)}, u32[]{:S(2)}, u32[]{:S(2)}) collective-permute-start(bf16[4,112,1024]{2,1,0:T(8,128)(2,1)S(1)} %pad_maximum_fusion.8.refs_0_), channel_id=1, source_target_pairs={{0,4},{4,0},{8,12},{12,8},{16,20},{20,16},{24,28},{28,24},{1,5},{5... | collective-permute-start | bytes 2752520 | tf_op jit(solution)/shard_map/ppermute | solution.py:799
  48.2 29.0 %collective-permute-start.5 = (bf16[4,112,1024]{2,1,0:T(8,128)(2,1)S(1)}, bf16[4,112,1024]{2,1,0:T(8,128)(2,1)S(1)}, u32[]{:S(2)}, u32[]{:S(2)}) collective-permute-start(bf16[4,112,1024]{2,1,0:T(8,128)(2,1)S(1)} %pad_maximum_fusion.8.refs_0_), channel_id=1, source_target_pairs={{0,1},{1,0},{2,3},{3,2},{4,5},{5,4},{6,7},{7,6},{8,9},{9,8},{10,11... | collective-permute-start | bytes 2752520 | tf_op jit(solution)/shard_map/ppermute | solution.py:799
  48.2 25.4 %collective-permute-start.6 = (bf16[1,160,1024]{2,1,0:T(8,128)(2,1)S(1)}, bf16[1,160,1024]{2,1,0:T(8,128)(2,1)S(1)}, u32[]{:S(2)}, u32[]{:S(2)}) collective-permute-start(bf16[1,160,1024]{2,1,0:T(8,128)(2,1)S(1)} %maximum_bitcast_fusion), channel_id=1, source_target_pairs={{0,16},{4,20},{8,24},{12,28},{16,0},{20,4},{24,8},{28,12},{1,17},{... | collective-permute-start | bytes 983048 | tf_op jit(solution)/shard_map/ppermute | solution.py:799
  49.9 26.1 %collective-permute-start.11 = (bf16[1,160,1024]{2,1,0:T(8,128)(2,1)S(1)}, bf16[1,160,1024]{2,1,0:T(8,128)(2,1)S(1)}, u32[]{:S(2)}, u32[]{:S(2)}) collective-permute-start(bf16[1,160,1024]{2,1,0:T(8,128)(2,1)S(1)} %maximum_bitcast_fusion), channel_id=1, source_target_pairs={{0,24},{4,28},{8,16},{12,20},{16,8},{20,12},{24,0},{28,4},{1,25},{... | collective-permute-start | bytes 983048 | tf_op jit(solution)/shard_map/ppermute | solution.py:799
  87.7 41.3 %collective-permute-start.17 = (bf16[4,160,1024]{2,1,0:T(8,128)(2,1)S(1)}, bf16[4,160,1024]{2,1,0:T(8,128)(2,1)S(1)}, u32[]{:S(2)}, u32[]{:S(2)}) collective-permute-start(bf16[4,160,1024]{2,1,0:T(8,128)(2,1)S(1)} %pad_maximum_fusion.refs_0_), channel_id=1, source_target_pairs={{0,1},{1,0},{2,3},{3,2},{4,5},{5,4},{6,7},{7,6},{8,9},{9,8},{10,11... | collective-permute-start | bytes 3932168 | tf_op jit(solution)/shard_map/ppermute | solution.py:799
  88.2 40.8 %collective-permute-start.18 = (bf16[4,160,1024]{2,1,0:T(8,128)(2,1)S(1)}, bf16[4,160,1024]{2,1,0:T(8,128)(2,1)}, u32[]{:S(2)}, u32[]{:S(2)}) collective-permute-start(bf16[4,160,1024]{2,1,0:T(8,128)(2,1)S(1)} %pad_maximum_fusion.refs_0_), channel_id=1, source_target_pairs={{0,2},{1,3},{2,0},{3,1},{4,6},{5,7},{6,4},{7,5},{8,10},{9,11},{10,... | collective-permute-start | bytes 3932168 | tf_op jit(solution)/shard_map/ppermute | solution.py:799
  91.2 37.8 %collective-permute-start.19 = (bf16[4,160,1024]{2,1,0:T(8,128)(2,1)S(1)}, bf16[4,160,1024]{2,1,0:T(8,128)(2,1)}, u32[]{:S(2)}, u32[]{:S(2)}) collective-permute-start(bf16[4,160,1024]{2,1,0:T(8,128)(2,1)S(1)} %pad_maximum_fusion.refs_0_), channel_id=1, source_target_pairs={{0,4},{4,0},{8,12},{12,8},{16,20},{20,16},{24,28},{28,24},{1,5},{5... | collective-permute-start | bytes 3932168 | tf_op jit(solution)/shard_map/ppermute | solution.py:799
  129.1 42.2 %collective-permute-start.20 = (bf16[4,160,1024]{2,1,0:T(8,128)(2,1)}, bf16[4,160,1024]{2,1,0:T(8,128)(2,1)}, u32[]{:S(2)}, u32[]{:S(2)}) collective-permute-start(bf16[4,160,1024]{2,1,0:T(8,128)(2,1)} %collective-permute-done.18.refs_2_), channel_id=1, source_target_pairs={{0,1},{1,0},{2,3},{3,2},{4,5},{5,4},{6,7},{7,6},{8,9},{9,8},{10,11... | collective-permute-start | bytes 3932168 | tf_op jit(solution)/shard_map/ppermute | solution.py:799
  129.3 42.0 %collective-permute-start.21 = (bf16[4,160,1024]{2,1,0:T(8,128)(2,1)}, bf16[4,160,1024]{2,1,0:T(8,128)(2,1)}, u32[]{:S(2)}, u32[]{:S(2)}) collective-permute-start(bf16[4,160,1024]{2,1,0:T(8,128)(2,1)} %collective-permute-done.19.refs_4_), channel_id=1, source_target_pairs={{0,1},{1,0},{2,3},{3,2},{4,5},{5,4},{6,7},{7,6},{8,9},{9,8},{10,11... | collective-permute-start | bytes 3932168 | tf_op jit(solution)/shard_map/ppermute | solution.py:799
  129.7 46.1 %collective-permute-start.22 = (bf16[4,160,1024]{2,1,0:T(8,128)(2,1)}, bf16[4,160,1024]{2,1,0:T(8,128)(2,1)}, u32[]{:S(2)}, u32[]{:S(2)}) collective-permute-start(bf16[4,160,1024]{2,1,0:T(8,128)(2,1)} %collective-permute-done.18.refs_2_), channel_id=1, source_target_pairs={{0,4},{4,0},{8,12},{12,8},{16,20},{20,16},{24,28},{28,24},{1,5},{5... | collective-permute-start | bytes 3932168 | tf_op jit(solution)/shard_map/ppermute | solution.py:799
  131.3 40.1 %collective-permute-start.23 = (bf16[2,256,1024]{2,1,0:T(8,128)(2,1)}, bf16[2,256,1024]{2,1,0:T(8,128)(2,1)S(1)}, u32[]{:S(2)}, u32[]{:S(2)}) collective-permute-start(bf16[2,256,1024]{2,1,0:T(8,128)(2,1)} %constant_dynamic-slice_fusion.8), channel_id=1, source_target_pairs={{0,2},{1,3},{2,0},{3,1},{4,6},{5,7},{6,4},{7,5},{8,10},{9,11},{10,... | collective-permute-start | bytes 3145736 | tf_op jit(solution)/shard_map/ppermute | solution.py:799
  222.1 45.7 %collective-permute-start.26 = (bf16[4,2,2,128,1024]{4,3,2,1,0:T(8,128)(2,1)}, bf16[4,2,2,128,1024]{4,3,2,1,0:T(8,128)(2,1)}, u32[]{:S(2)}, u32[]{:S(2)}) collective-permute-start(bf16[4,2,2,128,1024]{4,3,2,1,0:T(8,128)(2,1)} %bitcast.197), channel_id=1, source_target_pairs={{0,1},{1,0},{2,3},{3,2},{4,5},{5,4},{6,7},{7,6},{8,9},{9,8},{10,11... | collective-permute-start | bytes 12582920 | tf_op jit(solution)/shard_map/ppermute | solution.py:799
  271.9 22.5 %collective-permute-start.27 = (bf16[4,2,2,160,1024]{4,3,2,1,0:T(8,128)(2,1)}, bf16[4,2,2,160,1024]{4,3,2,1,0:T(8,128)(2,1)S(1)}, u32[]{:S(2)}, u32[]{:S(2)}) collective-permute-start(bf16[4,2,2,160,1024]{4,3,2,1,0:T(8,128)(2,1)} %bitcast.196), channel_id=1, source_target_pairs={{0,1},{1,0},{2,3},{3,2},{4,5},{5,4},{6,7},{7,6},{8,9},{9,8},{10,11... | collective-permute-start | bytes 15728648 | tf_op jit(solution)/shard_map/ppermute | solution.py:799
  272.3 29.8 %collective-permute-start.28 = (bf16[4,128,1024]{2,1,0:T(8,128)(2,1)}, bf16[4,128,1024]{2,1,0:T(8,128)(2,1)}, u32[]{:S(2)}, u32[]{:S(2)}) collective-permute-start(bf16[4,128,1024]{2,1,0:T(8,128)(2,1)} %get-tuple-element.240), channel_id=1, source_target_pairs={{0,4},{4,0},{8,12},{12,8},{16,20},{20,16},{24,28},{28,24},{1,5},{5... | collective-permute-start | bytes 3145736 | tf_op jit(solution)/shard_map/ppermute | solution.py:799
  273.7 54.7 %collective-permute-start.29 = (bf16[2,256,1024]{2,1,0:T(8,128)(2,1)}, bf16[2,256,1024]{2,1,0:T(8,128)(2,1)}, u32[]{:S(2)}, u32[]{:S(2)}) collective-permute-start(bf16[2,256,1024]{2,1,0:T(8,128)(2,1)} %constant_dynamic-slice_fusion.5), channel_id=1, source_target_pairs={{0,2},{1,3},{2,0},{3,1},{4,6},{5,7},{6,4},{7,5},{8,10},{9,11},{10,... | collective-permute-start | bytes 3145736 | tf_op jit(solution)/shard_map/ppermute | solution.py:799
  305.7 64.2 %collective-permute-start.34 = (bf16[4,128,1024]{2,1,0:T(8,128)(2,1)}, bf16[4,128,1024]{2,1,0:T(8,128)(2,1)}, u32[]{:S(2)}, u32[]{:S(2)}) collective-permute-start(bf16[4,128,1024]{2,1,0:T(8,128)(2,1)} %fusion.7), channel_id=1, source_target_pairs={{0,4},{4,0},{8,12},{12,8},{16,20},{20,16},{24,28},{28,24},{1,5},{5... | collective-permute-start | bytes 3145736 | tf_op jit(solution)/shard_map/ppermute | solution.py:799
  307.2 62.7 %collective-permute-start.33 = (bf16[4,128,1024]{2,1,0:T(8,128)(2,1)}, bf16[4,128,1024]{2,1,0:T(8,128)(2,1)}, u32[]{:S(2)}, u32[]{:S(2)}) collective-permute-start(bf16[4,128,1024]{2,1,0:T(8,128)(2,1)} %fusion), channel_id=1, source_target_pairs={{0,2},{1,3},{2,0},{3,1},{4,6},{5,7},{6,4},{7,5},{8,10},{9,11},{10,... | collective-permute-start | bytes 3145736 | tf_op jit(solution)/shard_map/ppermute | solution.py:799
  308.4 37.4 %collective-permute-start.30 = (bf16[2,160,1024]{2,1,0:T(8,128)(2,1)S(1)}, bf16[2,160,1024]{2,1,0:T(8,128)(2,1)S(1)}, u32[]{:S(2)}, u32[]{:S(2)}) collective-permute-start(bf16[2,160,1024]{2,1,0:T(8,128)(2,1)S(1)} %get-tuple-element.253), channel_id=1, source_target_pairs={{0,2},{1,3},{2,0},{3,1},{4,6},{5,7},{6,4},{7,5},{8,10},{9,11},{10,... | collective-permute-start | bytes 1966088 | tf_op jit(solution)/shard_map/ppermute | solution.py:799
  309.4 36.4 %collective-permute-start.31 = (bf16[2,160,1024]{2,1,0:T(8,128)(2,1)S(1)}, bf16[2,160,1024]{2,1,0:T(8,128)(2,1)}, u32[]{:S(2)}, u32[]{:S(2)}) collective-permute-start(bf16[2,160,1024]{2,1,0:T(8,128)(2,1)S(1)} %get-tuple-element.252), channel_id=1, source_target_pairs={{0,4},{4,0},{8,12},{12,8},{16,20},{20,16},{24,28},{28,24},{1,5},{5... | collective-permute-start | bytes 1966088 | tf_op jit(solution)/shard_map/ppermute | solution.py:799
  348.5 30.9 %collective-permute-start.36 = (bf16[4,160,1024]{2,1,0:T(8,128)(2,1)}, bf16[4,160,1024]{2,1,0:T(8,128)(2,1)S(1)}, u32[]{:S(2)}, u32[]{:S(2)}) collective-permute-start(bf16[4,160,1024]{2,1,0:T(8,128)(2,1)} %pad_maximum_fusion.2), channel_id=1, source_target_pairs={{0,4},{4,0},{8,12},{12,8},{16,20},{20,16},{24,28},{28,24},{1,5},{5... | collective-permute-start | bytes 3932168 | tf_op jit(solution)/shard_map/ppermute | solution.py:799
  350.2 29.2 %collective-permute-start.35 = (bf16[4,160,1024]{2,1,0:T(8,128)(2,1)}, bf16[4,160,1024]{2,1,0:T(8,128)(2,1)}, u32[]{:S(2)}, u32[]{:S(2)}) collective-permute-start(bf16[4,160,1024]{2,1,0:T(8,128)(2,1)} %pad_maximum_fusion.1), channel_id=1, source_target_pairs={{0,2},{1,3},{2,0},{3,1},{4,6},{5,7},{6,4},{7,5},{8,10},{9,11},{10,... | collective-permute-start | bytes 3932168 | tf_op jit(solution)/shard_map/ppermute | solution.py:799
  385.9 21.5 %collective-permute-start.37 = (bf16[4,2,2,96,768]{4,3,2,1,0:T(8,128)(2,1)}, bf16[4,2,2,96,768]{4,3,2,1,0:T(8,128)(2,1)S(1)}, u32[]{:S(2)}, u32[]{:S(2)}) collective-permute-start(bf16[4,2,2,96,768]{4,3,2,1,0:T(8,128)(2,1)} %bitcast.32), channel_id=1, source_target_pairs={{0,1},{1,0},{2,3},{3,2},{4,5},{5,4},{6,7},{7,6},{8,9},{9,8},{10,11... | collective-permute-start | bytes 7077896 | tf_op jit(solution)/shard_map/ppermute | solution.py:799
  403.1 22.9 %collective-permute-start.39 = (bf16[128,1024]{1,0:T(8,128)(2,1)}, bf16[128,1024]{1,0:T(8,128)(2,1)}, u32[]{:S(2)}, u32[]{:S(2)}) collective-permute-start(bf16[128,1024]{1,0:T(8,128)(2,1)} %get-tuple-element.255), channel_id=1, source_target_pairs={{0,16},{4,20},{8,24},{12,28},{16,0},{20,4},{24,8},{28,12},{1,17},{... | collective-permute-start | bytes 786440 | tf_op jit(solution)/shard_map/ppermute | solution.py:799
  408.8 36.6 %collective-permute-start.41 = (bf16[2,96,768]{2,1,0:T(8,128)(2,1)}, bf16[2,96,768]{2,1,0:T(8,128)(2,1)S(1)}, u32[]{:S(2)}, u32[]{:S(2)}) collective-permute-start(bf16[2,96,768]{2,1,0:T(8,128)(2,1)} %get-tuple-element.265), channel_id=1, source_target_pairs={{0,2},{1,3},{2,0},{3,1},{4,6},{5,7},{6,4},{7,5},{8,10},{9,11},{10,... | collective-permute-start | bytes 884744 | tf_op jit(solution)/shard_map/ppermute | solution.py:799
  410.0 38.0 %collective-permute-start.42 = (bf16[2,96,768]{2,1,0:T(8,128)(2,1)}, bf16[2,96,768]{2,1,0:T(8,128)(2,1)S(1)}, u32[]{:S(2)}, u32[]{:S(2)}) collective-permute-start(bf16[2,96,768]{2,1,0:T(8,128)(2,1)} %get-tuple-element.264), channel_id=1, source_target_pairs={{0,4},{4,0},{8,12},{12,8},{16,20},{20,16},{24,28},{28,24},{1,5},{5... | collective-permute-start | bytes 884744 | tf_op jit(solution)/shard_map/ppermute | solution.py:799
  416.5 35.4 %collective-permute-start.43 = (bf16[160,1024]{1,0:T(8,128)(2,1)}, bf16[160,1024]{1,0:T(8,128)(2,1)}, u32[]{:S(2)}, u32[]{:S(2)}) collective-permute-start(bf16[160,1024]{1,0:T(8,128)(2,1)} %get-tuple-element.250), channel_id=1, source_target_pairs={{0,8},{4,12},{8,0},{12,4},{16,24},{20,28},{24,16},{28,20},{1,9},{5... | collective-permute-start | bytes 983048 | tf_op jit(solution)/shard_map/ppermute | solution.py:799
  426.0 26.3 %collective-permute-start.44 = (bf16[160,1024]{1,0:T(8,128)(2,1)}, bf16[160,1024]{1,0:T(8,128)(2,1)}, u32[]{:S(2)}, u32[]{:S(2)}) collective-permute-start(bf16[160,1024]{1,0:T(8,128)(2,1)} %get-tuple-element.249), channel_id=1, source_target_pairs={{0,16},{4,20},{8,24},{12,28},{16,0},{20,4},{24,8},{28,12},{1,17},{... | collective-permute-start | bytes 983048 | tf_op jit(solution)/shard_map/ppermute | solution.py:799
  431.2 26.5 %collective-permute-start.46 = (bf16[4,2,2,112,256]{4,3,2,1,0:T(8,128)(2,1)}, bf16[4,2,2,112,256]{4,3,2,1,0:T(8,128)(2,1)S(1)}, u32[]{:S(2)}, u32[]{:S(2)}) collective-permute-start(bf16[4,2,2,112,256]{4,3,2,1,0:T(8,128)(2,1)} %bitcast.198), channel_id=1, source_target_pairs={{0,1},{1,0},{2,3},{3,2},{4,5},{5,4},{6,7},{7,6},{8,9},{9,8},{10,11... | collective-permute-start | bytes 2752520 | tf_op jit(solution)/shard_map/ppermute | solution.py:799
  452.3 62.3 %collective-permute-start.57 = (bf16[2,256,1024]{2,1,0:T(8,128)(2,1)}, bf16[2,256,1024]{2,1,0:T(8,128)(2,1)}, u32[]{:S(2)}, u32[]{:S(2)}) collective-permute-start(bf16[2,256,1024]{2,1,0:T(8,128)(2,1)} %constant_dynamic-slice_fusion), channel_id=1, source_target_pairs={{0,2},{1,3},{2,0},{3,1},{4,6},{5,7},{6,4},{7,5},{8,10},{9,11},{10,... | collective-permute-start | bytes 3145736 | tf_op jit(solution)/shard_map/ppermute | solution.py:799
  (72 other events, 848.4 us)
Sparse Core Ops, SparseCore 0:
  87.2 97.5 all-gather.2

commit v9 on v7

--- a/solution.py
+++ b/solution.py
@@ -952,7 +952,7 @@
     sc3.other, = tie(gb, sc3.other)
     sc3.fold()
     send2, = tie(sc3.own, send2)
-    sc2 = Scatter(keep2, send2, pos, False)
+    sc2 = Scatter(keep2, send2, pos, True)
     out4 = out.reshape(parts, rows, width)
     out4, = tie(sc3.own, out4)
     out_chip = send_chip(out4, me)
@@ -992,7 +992,12 @@
     sc2.came = list(tie(sc1.sent, *sc2.came))
     sc3.came = list(tie(sc1.sent, *sc3.came))
     r2, r_a = sc2.result(), sc3.result()
-    sc1.came_x, sc1.came_y = tie(r2, sc1.came_x, sc1.came_y)
+    join = lambda v: jnp.concatenate([v[i:i + own] for i in range(0, v.shape[0], own)], 1).reshape(own, shards, 1, half)
+    g_in = jnp.concatenate([join(r_a[half:]), join(r2[half + own:])], 2).reshape(w_in.shape)
+    g_back = jnp.concatenate([r_a[:half], r2[:half]], 0)
+    g_out = r2[half:half + own]
+    g_gain2 = jnp.sum(up(low(w_in)) * g_in, axis=1) / up(low(norm2_gain))
+    sc1.came_x, sc1.came_y, g_in, g_back, g_out, g_gain2 = lax.optimization_barrier((sc1.came_x, sc1.came_y, g_in, g_back, g_out, g_gain2))
     sc1.column()
     gx, = tie(sc1.mine, gx)
     gx4 = gx.reshape(parts, rows, width)
@@ -1002,14 +1007,10 @@
     input_grad = place(gx4, gx_chip, gx_core, me)
     sc1.came = list(tie(input_grad, *sc1.came))
     r1 = sc1.result()
-    join = lambda v: jnp.concatenate([v[i:i + own] for i in range(0, v.shape[0], own)], 1).reshape(own, shards, 1, half)
-    g_in = jnp.concatenate([join(r_a[half:]), join(r2[half + own:])], 2).reshape(w_in.shape)
-    g_back = jnp.concatenate([r_a[:half], r2[:half]], 0)
     prod = up(shard1[:3 * own]) * r1[:3 * own]
     g_gain1 = jnp.sum(prod[:own] + prod[own:2 * own] + prod[2 * own:], axis=1) / up(low(norm1_gain))
-    g_gain2 = jnp.sum(up(low(w_in)) * g_in, axis=1) / up(low(norm2_gain))
     return (layer_out.reshape(tokens.shape), input_grad.reshape(tokens.shape), g_gain1, r1[:own], r1[own:2 * own], r1[2 * own:3 * own],
-            r2[half:half + own], r1[3 * own, :HEADS], g_gain2, g_in, g_back)
+            g_out, r1[3 * own, :HEADS], g_gain2, g_in, g_back)
 
 
 def local_any(shape, tokens, *rest):

time: 510 us -> 497 us (0.975)
  local copies, waits for them, and re-layouts: 38.5 us -> 28.8 us
    ppermute x53 -> x52, starting transfers between devices: 50.2 us -> 47.7 us  [swap(): lax.ppermute(value, axis, [(i, i ^ mask) for i in range(lax.axis_size(axi...]
    ppermute x53 -> x52, waiting for transfers between devices: 121 us -> 123 us  [swap(): lax.ppermute(value, axis, [(i, i ^ mask) for i in range(lax.axis_size(axi...]
  transfers between devices with their start and end apart: 54 -> 53, of which waited for: 19 -> 22; matrix products, arithmetic and copies ran while one was open for 13% -> 12% of each run, Pallas kernels for 42% -> 43%
where the time goes in v9:
time: 497 us; the launch traced here: 489 us
  Pallas kernels  224 us (45%)
  waiting for transfers between devices  123 us (25%)
  other arithmetic  50.4 us (10%)
  starting transfers between devices  47.8 us (10%)
  local copies, waits for them, and re-layouts  28.8 us (6%)
  between operations  15.6 us (3%)
    ppermute x52, waiting for transfers between devices, swap(): lax.ppermute(value, axis, [(i, i ^ mask) for i in range(lax.axis_size(axi...  123 us
    pallas_call x4, Pallas kernels, attn_bwd(): pl.pallas_call(functools.partial(bwd_kernel, rows=rows, seq_len=seq_len,...  65.9 us
    ppermute x52, starting transfers between devices, swap(): lax.ppermute(value, axis, [(i, i ^ mask) for i in range(lax.axis_size(axi...  47.7 us
    pallas_call x1, Pallas kernels, mid_b(): pl.pallas_call(mid_b_kernel, out_shape=(low(rows, width), low(rows, width...  45.1 us
    pallas_call x1, Pallas kernels, mid_a(): pl.pallas_call(functools.partial(mid_a_kernel, masks=masks), out_shape=(f...  39.7 us
    pallas_call x2, Pallas kernels, attn_fwd(): pl.pallas_call(functools.partial(fwd_kernel, rows=rows, seq_len=seq_len,...  33.3 us
    convert_element_type x6, other arithmetic, quarter(): return (cut(self.mine) + cut(self.other)).astype(jnp.bfloat16)  20 us
    pallas_call x1, Pallas kernels, qkv_gx(): pl.pallas_call(gx_kernel, out_shape=jax.ShapeDtypeStruct((total, width),...  14.3 us
  transfers between devices with their start and end apart: 53, of which 22 were waited for; matrix products, arithmetic and copies ran while one was open for 12% of the time, Pallas kernels for 43%

profile of v9, /device:TPU:0, one launch (start us, length us, event | category | flops | bytes accessed | tf_op | source)
XLA Modules:
  0.0 489.1 jit_solution(5546899110281178113)
XLA Ops:
  12.5 3.1 collective-permute-start.2
  23.0 3.0 slice_reduce_fusion
  28.2 6.7 %collective-permute-done.3 = bf16[1,112,1024]{2,1,0:T(8,128)(2,1)S(1)} collective-permute-done((bf16[1,112,1024]{2,1,0:T(8,128)(2,1)S(1)}, bf16[1,112,1024]{2,1,0:T(8,128)(2,1)S(1)}, u32[]{:S(2)}, u32[]{:S(2)}) %collective-permute-start.3) | collective-permute-done | bytes 229408 | tf_op jit(solution)/shard_map/ppermute | solution.py:796
  36.7 3.7 collective-permute-done.1
  40.5 4.8 collective-permute-done.chip_ref
  51.8 21.9 %collective-permute-done.6 = bf16[1,160,1024]{2,1,0:T(8,128)(2,1)S(1)} collective-permute-done((bf16[1,160,1024]{2,1,0:T(8,128)(2,1)S(1)}, bf16[1,160,1024]{2,1,0:T(8,128)(2,1)S(1)}, u32[]{:S(2)}, u32[]{:S(2)}) %collective-permute-start.6) | collective-permute-done | bytes 327712 | tf_op jit(solution)/shard_map/ppermute | solution.py:796
  78.3 7.3 %collective-permute-done.10.refs_8_ = bf16[2,112,1024]{2,1,0:T(8,128)(2,1)S(1)} collective-permute-done((bf16[2,112,1024]{2,1,0:T(8,128)(2,1)S(1)}, bf16[2,112,1024]{2,1,0:T(8,128)(2,1)S(1)}, u32[]{:S(2)}, u32[]{:S(2)}) %collective-permute-start.10) | collective-permute-done | bytes 458784 | tf_op jit(solution)/shard_map/ppermute | solution.py:796
  99.3 13.2 %qkv_fwd.1 = (bf16[1024,1024]{1,0:T(8,128)(2,1)}, bf16[1024,1024]{1,0:T(8,128)(2,1)}, bf16[1024,1024]{1,0:T(8,128)(2,1)}, bf16[1024,1024]{1,0:T(8,128)(2,1)}, bf...) custom-call(s32[3]{0:T(128)} %pad_add_fusion.1.ids_ref, ...), custom_call_target="tpu_custom_call" | custom-call | flops 1048576 | bytes 65536 | tf_op jit(solution)/shard_map/qkv_fwd/pallas_call | solution.py:524
  112.5 16.6 %attn_fwd.2 = (bf16[1024,1024]{1,0:T(8,128)(2,1)}, f32[8,1024,128]{2,1,0:T(8,128)}) custom-call(s32[1]{0:T(128)} %dynamic_slice.189.len_ref, bf16[1024,1024]{1,0:T(8,128)(2,1)} %get-tuple-element.133.q_ref, bf16[1024,1024]{1,0:T(8,128)(2,1)} %get-tuple-element.126.k_ref, bf16[1024,1024]{1,0:T(8,128)(2,1)} %get-tuple-element.127.v_ref, ...), custom_call_target="tpu_custom_call" | custom-call | flops 1048576 | bytes 65536 | tf_op jit(solution)/shard_map/attn_fwd/pallas_call | solution.py:360
  131.9 16.6 %attn_fwd.3 = (bf16[1024,1024]{1,0:T(8,128)(2,1)}, f32[8,1024,128]{2,1,0:T(8,128)}) custom-call(s32[1]{0:T(128)} %dynamic_slice.189.len_ref, bf16[1024,1024]{1,0:T(8,128)(2,1)} %get-tuple-element.133.q_ref, bf16[1024,1024]{1,0:T(8,128)(2,1)} %get-tuple-element.126.k_ref, ...), custom_call_target="tpu_custom_call", output_to_operand_aliasing={{0}: (5, {}), {1}: (6, {})} | custom-call | flops 1048576 | bytes 65536 | tf_op jit(solution)/shard_map/attn_fwd/pallas_call | solution.py:360
  148.5 22.8 %collective-permute-done.23.chip_ref = bf16[2,256,1024]{2,1,0:T(8,128)(2,1)S(1)} collective-permute-done((bf16[2,256,1024]{2,1,0:T(8,128)(2,1)}, bf16[2,256,1024]{2,1,0:T(8,128)(2,1)S(1)}, u32[]{:S(2)}, u32[]{:S(2)}) %collective-permute-start.23) | collective-permute-done | bytes 1048608 | tf_op jit(solution)/shard_map/ppermute | solution.py:796
  171.4 4.4 collective-permute-done.22.refs_6_
  176.5 4.2 collective-permute-done.24.core_ref
  182.5 39.7 %mid_a.1 = (f32[1024,1024]{1,0:T(8,128)}, f32[1024,1024]{1,0:T(8,128)}, f32[1024,1024]{1,0:T(8,128)}, bf16[1024,1024]{1,0:T(8,128)(2,1)}, bf16[1024,1024]{1,0:T(...) custom-call(s32[3]{0:T(128)} %pad_add_fusion.1.ids_ref, ...), custom_call_target="tpu_custom_call" | custom-call | flops 1048576 | bytes 65536 | tf_op jit(solution)/shard_map/mid_a/pallas_call | solution.py:659
  222.3 45.1 %mid_b.1 = (bf16[1024,1024]{1,0:T(8,128)(2,1)}, bf16[1024,1024]{1,0:T(8,128)(2,1)}, bf16[1024,1024]{1,0:T(8,128)(2,1)}, bf16[16,160,1024]{2,1,0:T(8,128)(2,1)}, bf16[16,160,1024]{2,1,0:T(8,128)(2,1)}) custom-call(s32[3]{0:T(128)} %pad_add_fusion.1.ids_ref, f32[8,1024]{1,0:T(8,128)} %get-tuple-element.123.gain_ref, ...), custom_call_target="tpu_custom_call" | custom-call | flops 1048576 | bytes 65536 | tf_op jit(solution)/shard_map/mid_b/pallas_call | solution.py:727
  267.5 4.7 fusion.8
  273.0 16.6 %attn_bwd.4 = (bf16[1024,1024]{1,0:T(8,128)(2,1)}, bf16[1024,1024]{1,0:T(8,128)(2,1)}, bf16[1024,1024]{1,0:T(8,128)(2,1)}, f32[4,2048]{1,0:T(4,128)}) custom-call(s32[1]{0:T(128)} %dynamic_slice.189.len_ref, bf16[1024,1024]{1,0:T(8,128)(2,1)} %get-tuple-element.133.q_ref, bf16[1024,1024]{1,0:T(8,128)(2,1)} %get-tuple-element.126.k_ref, ...), custom_call_target="tpu_custom_call" | custom-call | flops 1048576 | bytes 65536 | tf_op jit(solution)/shard_map/attn_bwd/pallas_call | solution.py:439
  289.7 4.8 fusion.4
  301.2 3.2 fusion.1
  305.4 16.3 %attn_bwd.5 = (bf16[1024,1024]{1,0:T(8,128)(2,1)}, bf16[1024,1024]{1,0:T(8,128)(2,1)}, bf16[1024,1024]{1,0:T(8,128)(2,1)}, f32[4,2048]{1,0:T(4,128)}) custom-call(s32[1]{0:T(128)} %dynamic_slice.189.len_ref, bf16[1024,1024]{1,0:T(8,128)(2,1)} %get-tuple-element.133.q_ref, ...), custom_call_target="tpu_custom_call", output_to_operand_aliasing={{0}: (8, {}), {1}: (9, {}), {2}: (10, {})} | custom-call | flops 1048576 | bytes 65536 | tf_op jit(solution)/shard_map/attn_bwd/pallas_call | solution.py:439
  321.6 3.0 fusion.5
  327.0 3.6 fusion
  335.0 16.5 %attn_bwd.6 = (bf16[1024,1024]{1,0:T(8,128)(2,1)}, bf16[1024,1024]{1,0:T(8,128)(2,1)}, bf16[1024,1024]{1,0:T(8,128)(2,1)}, f32[4,2048]{1,0:T(4,128)}) custom-call(s32[1]{0:T(128)} %dynamic_slice.189.len_ref, bf16[1024,1024]{1,0:T(8,128)(2,1)} %get-tuple-element.133.q_ref, ...), custom_call_target="tpu_custom_call", output_to_operand_aliasing={{0}: (8, {}), {1}: (9, {}), {2}: (10, {})} | custom-call | flops 1048576 | bytes 65536 | tf_op jit(solution)/shard_map/attn_bwd/pallas_call | solution.py:439
  354.5 3.2 collective-permute-start.37
  358.9 16.5 %attn_bwd.7 = (bf16[1024,1024]{1,0:T(8,128)(2,1)}, bf16[1024,1024]{1,0:T(8,128)(2,1)}, bf16[1024,1024]{1,0:T(8,128)(2,1)}, f32[4,2048]{1,0:T(4,128)}) custom-call(s32[1]{0:T(128)} %dynamic_slice.189.len_ref, bf16[1024,1024]{1,0:T(8,128)(2,1)} %get-tuple-element.133.q_ref, ...), custom_call_target="tpu_custom_call", output_to_operand_aliasing={{0}: (8, {}), {1}: (9, {}), {2}: (10, {})} | custom-call | flops 1048576 | bytes 65536 | tf_op jit(solution)/shard_map/attn_bwd/pallas_call | solution.py:439
  378.5 12.5 %qkv_gw.1 = (bf16[16,112,1024]{2,1,0:T(8,128)(2,1)}, bf16[16,112,1024]{2,1,0:T(8,128)(2,1)}) custom-call(s32[3]{0:T(128)} %pad_add_fusion.1.ids_ref, bf16[1024,1024]{1,0:T(8,128)(2,1)} %get-tuple-element.188.h_ref, bf16[1024,1024]{1,0:T(8,128)(2,1)} %get-tuple-element.189.dq_ref, bf16[1024,1024]{1,0:T(8,128)(2,1)} %get-tuple-element.190.dk_ref, ...), custom_call_target="tpu_custom_call" | custom-call | flops 1048576 | bytes 65536 | tf_op jit(solution)/shard_map/qkv_gw/pallas_call | solution.py:761
  396.5 14.3 %qkv_gx.1 = bf16[1024,1024]{1,0:T(8,128)(2,1)} custom-call(bf16[1024,1024]{1,0:T(8,128)(2,1)} %get-tuple-element.124.x_hbm.x_ref, bf16[1024,1024]{1,0:T(8,128)(2,1)} %get-tuple-element.194.gb_ref, bf16[1024,1024]{1,0:T(8,128)(2,1)} %get-tuple-element.189.dq_ref, bf16[1024,1024]{1,0:T(8,128)(2,1)} %get-tuple-element.190.dk_ref, ...), custom_call_target="tpu_custom_call" | custom-call | flops 1048576 | bytes 65536 | tf_op jit(solution)/shard_map/qkv_gx/pallas_call | solution.py:785
  410.8 3.3 add_convert_fusion.12
  437.6 12.4 %collective-permute-done.46 = bf16[4,112,1024]{2,1,0:T(8,128)(2,1)} collective-permute-done((bf16[4,112,1024]{2,1,0:T(8,128)(2,1)}, bf16[4,112,1024]{2,1,0:T(8,128)(2,1)}, u32[]{:S(2)}, u32[]{:S(2)}) %collective-permute-start.46) | collective-permute-done | bytes 917536 | tf_op jit(solution)/shard_map/ppermute | solution.py:796
  459.0 5.4 %collective-permute-done.47 = bf16[112,1024]{1,0:T(8,128)(2,1)S(1)} collective-permute-done((bf16[112,1024]{1,0:T(8,128)(2,1)S(1)}, bf16[112,1024]{1,0:T(8,128)(2,1)S(1)}, u32[]{:S(2)}, u32[]{:S(2)}) %collective-permute-start.47) | collective-permute-done | bytes 229408 | tf_op jit(solution)/shard_map/ppermute | solution.py:796
  464.4 8.6 %collective-permute-done.48 = bf16[112,1024]{1,0:T(8,128)(2,1)S(1)} collective-permute-done((bf16[112,1024]{1,0:T(8,128)(2,1)S(1)}, bf16[112,1024]{1,0:T(8,128)(2,1)S(1)}, u32[]{:S(2)}, u32[]{:S(2)}) %collective-permute-start.48) | collective-permute-done | bytes 229408 | tf_op jit(solution)/shard_map/ppermute | solution.py:796
  472.9 3.5 collective-permute-done.50
  (284 shorter events, 112.1 us)
Async XLA Ops:
  7.2 215.1 %all-gather.3.cloned.1.call-start = ((), (), s32[]{:S(2)}) async-start(), calls=%async_computation | async-start | bytes 8650752 | tf_op jit(solution)/shard_map/all_gather | solution.py:933
  20.5 24.8 %collective-permute-start = (bf16[2,256,1024]{2,1,0:T(8,128)(2,1)}, bf16[2,256,1024]{2,1,0:T(8,128)(2,1)S(1)}, u32[]{:S(2)}, u32[]{:S(2)}) collective-permute-start(bf16[2,256,1024]{2,1,0:T(8,128)(2,1)} %constant_dynamic-slice_fusion.11), channel_id=1, source_target_pairs={{0,2},{1,3},{2,0},{3,1},{4,6},{5,7},{6,4},{7,5},{8,10},{9,11},{10,... | collective-permute-start | bytes 3145736 | tf_op jit(solution)/shard_map/ppermute | solution.py:796
  45.3 28.5 %collective-permute-start.7 = (bf16[4,112,1024]{2,1,0:T(8,128)(2,1)S(1)}, bf16[4,112,1024]{2,1,0:T(8,128)(2,1)S(1)}, u32[]{:S(2)}, u32[]{:S(2)}) collective-permute-start(bf16[4,112,1024]{2,1,0:T(8,128)(2,1)S(1)} %pad_maximum_fusion.6.refs_0_), channel_id=1, source_target_pairs={{0,2},{1,3},{2,0},{3,1},{4,6},{5,7},{6,4},{7,5},{8,10},{9,11},{10,... | collective-permute-start | bytes 2752520 | tf_op jit(solution)/shard_map/ppermute | solution.py:796
  46.8 27.0 %collective-permute-start.8 = (bf16[4,112,1024]{2,1,0:T(8,128)(2,1)S(1)}, bf16[4,112,1024]{2,1,0:T(8,128)(2,1)}, u32[]{:S(2)}, u32[]{:S(2)}) collective-permute-start(bf16[4,112,1024]{2,1,0:T(8,128)(2,1)S(1)} %pad_maximum_fusion.6.refs_0_), channel_id=1, source_target_pairs={{0,4},{4,0},{8,12},{12,8},{16,20},{20,16},{24,28},{28,24},{1,5},{5... | collective-permute-start | bytes 2752520 | tf_op jit(solution)/shard_map/ppermute | solution.py:796
  48.3 29.0 %collective-permute-start.5 = (bf16[4,112,1024]{2,1,0:T(8,128)(2,1)S(1)}, bf16[4,112,1024]{2,1,0:T(8,128)(2,1)S(1)}, u32[]{:S(2)}, u32[]{:S(2)}) collective-permute-start(bf16[4,112,1024]{2,1,0:T(8,128)(2,1)S(1)} %pad_maximum_fusion.6.refs_0_), channel_id=1, source_target_pairs={{0,1},{1,0},{2,3},{3,2},{4,5},{5,4},{6,7},{7,6},{8,9},{9,8},{10,11... | collective-permute-start | bytes 2752520 | tf_op jit(solution)/shard_map/ppermute | solution.py:796
  48.3 25.4 %collective-permute-start.6 = (bf16[1,160,1024]{2,1,0:T(8,128)(2,1)S(1)}, bf16[1,160,1024]{2,1,0:T(8,128)(2,1)S(1)}, u32[]{:S(2)}, u32[]{:S(2)}) collective-permute-start(bf16[1,160,1024]{2,1,0:T(8,128)(2,1)S(1)} %maximum_bitcast_fusion), channel_id=1, source_target_pairs={{0,16},{4,20},{8,24},{12,28},{16,0},{20,4},{24,8},{28,12},{1,17},{... | collective-permute-start | bytes 983048 | tf_op jit(solution)/shard_map/ppermute | solution.py:796
  49.9 26.1 %collective-permute-start.11 = (bf16[1,160,1024]{2,1,0:T(8,128)(2,1)S(1)}, bf16[1,160,1024]{2,1,0:T(8,128)(2,1)S(1)}, u32[]{:S(2)}, u32[]{:S(2)}) collective-permute-start(bf16[1,160,1024]{2,1,0:T(8,128)(2,1)S(1)} %maximum_bitcast_fusion), channel_id=1, source_target_pairs={{0,24},{4,28},{8,16},{12,20},{16,8},{20,12},{24,0},{28,4},{1,25},{... | collective-permute-start | bytes 983048 | tf_op jit(solution)/shard_map/ppermute | solution.py:796
  87.8 41.3 %collective-permute-start.17 = (bf16[4,160,1024]{2,1,0:T(8,128)(2,1)S(1)}, bf16[4,160,1024]{2,1,0:T(8,128)(2,1)S(1)}, u32[]{:S(2)}, u32[]{:S(2)}) collective-permute-start(bf16[4,160,1024]{2,1,0:T(8,128)(2,1)S(1)} %pad_maximum_fusion.refs_0_), channel_id=1, source_target_pairs={{0,1},{1,0},{2,3},{3,2},{4,5},{5,4},{6,7},{7,6},{8,9},{9,8},{10,11... | collective-permute-start | bytes 3932168 | tf_op jit(solution)/shard_map/ppermute | solution.py:796
  88.3 40.8 %collective-permute-start.18 = (bf16[4,160,1024]{2,1,0:T(8,128)(2,1)S(1)}, bf16[4,160,1024]{2,1,0:T(8,128)(2,1)}, u32[]{:S(2)}, u32[]{:S(2)}) collective-permute-start(bf16[4,160,1024]{2,1,0:T(8,128)(2,1)S(1)} %pad_maximum_fusion.refs_0_), channel_id=1, source_target_pairs={{0,2},{1,3},{2,0},{3,1},{4,6},{5,7},{6,4},{7,5},{8,10},{9,11},{10,... | collective-permute-start | bytes 3932168 | tf_op jit(solution)/shard_map/ppermute | solution.py:796
  91.3 37.8 %collective-permute-start.19 = (bf16[4,160,1024]{2,1,0:T(8,128)(2,1)S(1)}, bf16[4,160,1024]{2,1,0:T(8,128)(2,1)}, u32[]{:S(2)}, u32[]{:S(2)}) collective-permute-start(bf16[4,160,1024]{2,1,0:T(8,128)(2,1)S(1)} %pad_maximum_fusion.refs_0_), channel_id=1, source_target_pairs={{0,4},{4,0},{8,12},{12,8},{16,20},{20,16},{24,28},{28,24},{1,5},{5... | collective-permute-start | bytes 3932168 | tf_op jit(solution)/shard_map/ppermute | solution.py:796
  129.1 42.2 %collective-permute-start.20 = (bf16[4,160,1024]{2,1,0:T(8,128)(2,1)}, bf16[4,160,1024]{2,1,0:T(8,128)(2,1)}, u32[]{:S(2)}, u32[]{:S(2)}) collective-permute-start(bf16[4,160,1024]{2,1,0:T(8,128)(2,1)} %collective-permute-done.18.refs_2_), channel_id=1, source_target_pairs={{0,1},{1,0},{2,3},{3,2},{4,5},{5,4},{6,7},{7,6},{8,9},{9,8},{10,11... | collective-permute-start | bytes 3932168 | tf_op jit(solution)/shard_map/ppermute | solution.py:796
  129.3 42.0 %collective-permute-start.21 = (bf16[4,160,1024]{2,1,0:T(8,128)(2,1)}, bf16[4,160,1024]{2,1,0:T(8,128)(2,1)}, u32[]{:S(2)}, u32[]{:S(2)}) collective-permute-start(bf16[4,160,1024]{2,1,0:T(8,128)(2,1)} %collective-permute-done.19.refs_4_), channel_id=1, source_target_pairs={{0,1},{1,0},{2,3},{3,2},{4,5},{5,4},{6,7},{7,6},{8,9},{9,8},{10,11... | collective-permute-start | bytes 3932168 | tf_op jit(solution)/shard_map/ppermute | solution.py:796
  129.7 46.1 %collective-permute-start.22 = (bf16[4,160,1024]{2,1,0:T(8,128)(2,1)}, bf16[4,160,1024]{2,1,0:T(8,128)(2,1)}, u32[]{:S(2)}, u32[]{:S(2)}) collective-permute-start(bf16[4,160,1024]{2,1,0:T(8,128)(2,1)} %collective-permute-done.18.refs_2_), channel_id=1, source_target_pairs={{0,4},{4,0},{8,12},{12,8},{16,20},{20,16},{24,28},{28,24},{1,5},{5... | collective-permute-start | bytes 3932168 | tf_op jit(solution)/shard_map/ppermute | solution.py:796
  131.3 40.1 %collective-permute-start.23 = (bf16[2,256,1024]{2,1,0:T(8,128)(2,1)}, bf16[2,256,1024]{2,1,0:T(8,128)(2,1)S(1)}, u32[]{:S(2)}, u32[]{:S(2)}) collective-permute-start(bf16[2,256,1024]{2,1,0:T(8,128)(2,1)} %constant_dynamic-slice_fusion.8), channel_id=1, source_target_pairs={{0,2},{1,3},{2,0},{3,1},{4,6},{5,7},{6,4},{7,5},{8,10},{9,11},{10,... | collective-permute-start | bytes 3145736 | tf_op jit(solution)/shard_map/ppermute | solution.py:796
  222.2 45.3 %collective-permute-start.26 = (bf16[4,2,2,128,1024]{4,3,2,1,0:T(8,128)(2,1)}, bf16[4,2,2,128,1024]{4,3,2,1,0:T(8,128)(2,1)}, u32[]{:S(2)}, u32[]{:S(2)}) collective-permute-start(bf16[4,2,2,128,1024]{4,3,2,1,0:T(8,128)(2,1)} %bitcast.146), channel_id=1, source_target_pairs={{0,1},{1,0},{2,3},{3,2},{4,5},{5,4},{6,7},{7,6},{8,9},{9,8},{10,11... | collective-permute-start | bytes 12582920 | tf_op jit(solution)/shard_map/ppermute | solution.py:796
  272.6 28.1 %collective-permute-start.28 = (bf16[4,128,1024]{2,1,0:T(8,128)(2,1)}, bf16[4,128,1024]{2,1,0:T(8,128)(2,1)}, u32[]{:S(2)}, u32[]{:S(2)}) collective-permute-start(bf16[4,128,1024]{2,1,0:T(8,128)(2,1)} %get-tuple-element.223), channel_id=1, source_target_pairs={{0,4},{4,0},{8,12},{12,8},{16,20},{20,16},{24,28},{28,24},{1,5},{5... | collective-permute-start | bytes 3145736 | tf_op jit(solution)/shard_map/ppermute | solution.py:796
  294.4 32.6 %collective-permute-start.30 = (bf16[4,160,1024]{2,1,0:T(8,128)(2,1)}, bf16[4,160,1024]{2,1,0:T(8,128)(2,1)}, u32[]{:S(2)}, u32[]{:S(2)}) collective-permute-start(bf16[4,160,1024]{2,1,0:T(8,128)(2,1)} %get-tuple-element.221), channel_id=1, source_target_pairs={{0,4},{4,0},{8,12},{12,8},{16,20},{20,16},{24,28},{28,24},{1,5},{5... | collective-permute-start | bytes 3932168 | tf_op jit(solution)/shard_map/ppermute | solution.py:796
  297.1 27.5 %collective-permute-start.29 = (bf16[2,256,1024]{2,1,0:T(8,128)(2,1)}, bf16[2,256,1024]{2,1,0:T(8,128)(2,1)}, u32[]{:S(2)}, u32[]{:S(2)}) collective-permute-start(bf16[2,256,1024]{2,1,0:T(8,128)(2,1)} %constant_dynamic-slice_fusion.4), channel_id=1, source_target_pairs={{0,2},{1,3},{2,0},{3,1},{4,6},{5,7},{6,4},{7,5},{8,10},{9,11},{10,... | collective-permute-start | bytes 3145736 | tf_op jit(solution)/shard_map/ppermute | solution.py:796
  300.7 50.8 %collective-permute-start.33 = (bf16[4,128,1024]{2,1,0:T(8,128)(2,1)}, bf16[4,128,1024]{2,1,0:T(8,128)(2,1)}, u32[]{:S(2)}, u32[]{:S(2)}) collective-permute-start(bf16[4,128,1024]{2,1,0:T(8,128)(2,1)} %fusion.9), channel_id=1, source_target_pairs={{0,4},{4,0},{8,12},{12,8},{16,20},{20,16},{24,28},{28,24},{1,5},{5... | collective-permute-start | bytes 3145736 | tf_op jit(solution)/shard_map/ppermute | solution.py:796
  304.5 47.0 %collective-permute-start.32 = (bf16[4,128,1024]{2,1,0:T(8,128)(2,1)}, bf16[4,128,1024]{2,1,0:T(8,128)(2,1)}, u32[]{:S(2)}, u32[]{:S(2)}) collective-permute-start(bf16[4,128,1024]{2,1,0:T(8,128)(2,1)} %fusion.1), channel_id=1, source_target_pairs={{0,2},{1,3},{2,0},{3,1},{4,6},{5,7},{6,4},{7,5},{8,10},{9,11},{10,... | collective-permute-start | bytes 3145736 | tf_op jit(solution)/shard_map/ppermute | solution.py:796
  333.0 43.6 %collective-permute-start.35 = (bf16[4,160,1024]{2,1,0:T(8,128)(2,1)}, bf16[4,160,1024]{2,1,0:T(8,128)(2,1)S(1)}, u32[]{:S(2)}, u32[]{:S(2)}) collective-permute-start(bf16[4,160,1024]{2,1,0:T(8,128)(2,1)} %fusion.5), channel_id=1, source_target_pairs={{0,4},{4,0},{8,12},{12,8},{16,20},{20,16},{24,28},{28,24},{1,5},{5... | collective-permute-start | bytes 3932168 | tf_op jit(solution)/shard_map/ppermute | solution.py:796
  334.1 42.6 %collective-permute-start.34 = (bf16[4,160,1024]{2,1,0:T(8,128)(2,1)}, bf16[4,160,1024]{2,1,0:T(8,128)(2,1)S(1)}, u32[]{:S(2)}, u32[]{:S(2)}) collective-permute-start(bf16[4,160,1024]{2,1,0:T(8,128)(2,1)} %fusion), channel_id=1, source_target_pairs={{0,2},{1,3},{2,0},{3,1},{4,6},{5,7},{6,4},{7,5},{8,10},{9,11},{10,... | collective-permute-start | bytes 3932168 | tf_op jit(solution)/shard_map/ppermute | solution.py:796
  354.5 24.0 %collective-permute-start.36 = (bf16[128,1024]{1,0:T(8,128)(2,1)S(1)}, bf16[128,1024]{1,0:T(8,128)(2,1)S(1)}, u32[]{:S(2)}, u32[]{:S(2)}) collective-permute-start(bf16[128,1024]{1,0:T(8,128)(2,1)S(1)} %get-tuple-element.234), channel_id=1, source_target_pairs={{0,8},{4,12},{8,0},{12,4},{16,24},{20,28},{24,16},{28,20},{1,9},{5... | collective-permute-start | bytes 786440 | tf_op jit(solution)/shard_map/ppermute | solution.py:796
  354.5 24.0 %collective-permute-start.37 = (bf16[128,1024]{1,0:T(8,128)(2,1)S(1)}, bf16[128,1024]{1,0:T(8,128)(2,1)S(1)}, u32[]{:S(2)}, u32[]{:S(2)}) collective-permute-start(bf16[128,1024]{1,0:T(8,128)(2,1)S(1)} %get-tuple-element.233), channel_id=1, source_target_pairs={{0,16},{4,20},{8,24},{12,28},{16,0},{20,4},{24,8},{28,12},{1,17},{... | collective-permute-start | bytes 786440 | tf_op jit(solution)/shard_map/ppermute | solution.py:796
  357.6 20.9 %collective-permute-start.38 = (bf16[128,1024]{1,0:T(8,128)(2,1)S(1)}, bf16[128,1024]{1,0:T(8,128)(2,1)S(1)}, u32[]{:S(2)}, u32[]{:S(2)}) collective-permute-start(bf16[128,1024]{1,0:T(8,128)(2,1)S(1)} %get-tuple-element.232), channel_id=1, source_target_pairs={{0,24},{4,28},{8,16},{12,20},{16,8},{20,12},{24,0},{28,4},{1,25},{... | collective-permute-start | bytes 786440 | tf_op jit(solution)/shard_map/ppermute | solution.py:796
  391.0 19.7 %collective-permute-start.39 = (bf16[4,2,2,112,1024]{4,3,2,1,0:T(8,128)(2,1)}, bf16[4,2,2,112,1024]{4,3,2,1,0:T(8,128)(2,1)}, u32[]{:S(2)}, u32[]{:S(2)}) collective-permute-start(bf16[4,2,2,112,1024]{4,3,2,1,0:T(8,128)(2,1)} %bitcast.147), channel_id=1, source_target_pairs={{0,1},{1,0},{2,3},{3,2},{4,5},{5,4},{6,7},{7,6},{8,9},{9,8},{10,11... | collective-permute-start | bytes 11010056 | tf_op jit(solution)/shard_map/ppermute | solution.py:796
  391.1 32.5 %collective-permute-start.40 = (bf16[160,1024]{1,0:T(8,128)(2,1)}, bf16[160,1024]{1,0:T(8,128)(2,1)}, u32[]{:S(2)}, u32[]{:S(2)}) collective-permute-start(bf16[160,1024]{1,0:T(8,128)(2,1)} %get-tuple-element.230), channel_id=1, source_target_pairs={{0,8},{4,12},{8,0},{12,4},{16,24},{20,28},{24,16},{28,20},{1,9},{5... | collective-permute-start | bytes 983048 | tf_op jit(solution)/shard_map/ppermute | solution.py:796
  394.0 29.6 %collective-permute-start.41 = (bf16[160,1024]{1,0:T(8,128)(2,1)}, bf16[160,1024]{1,0:T(8,128)(2,1)}, u32[]{:S(2)}, u32[]{:S(2)}) collective-permute-start(bf16[160,1024]{1,0:T(8,128)(2,1)} %get-tuple-element.229), channel_id=1, source_target_pairs={{0,16},{4,20},{8,24},{12,28},{16,0},{20,4},{24,8},{28,12},{1,17},{... | collective-permute-start | bytes 983048 | tf_op jit(solution)/shard_map/ppermute | solution.py:796
  395.3 28.3 %collective-permute-start.42 = (bf16[160,1024]{1,0:T(8,128)(2,1)}, bf16[160,1024]{1,0:T(8,128)(2,1)}, u32[]{:S(2)}, u32[]{:S(2)}) collective-permute-start(bf16[160,1024]{1,0:T(8,128)(2,1)} %get-tuple-element.228), channel_id=1, source_target_pairs={{0,24},{4,28},{8,16},{12,20},{16,8},{20,12},{24,0},{28,4},{1,25},{... | collective-permute-start | bytes 983048 | tf_op jit(solution)/shard_map/ppermute | solution.py:796
  428.8 21.2 %collective-permute-start.46 = (bf16[4,112,1024]{2,1,0:T(8,128)(2,1)}, bf16[4,112,1024]{2,1,0:T(8,128)(2,1)}, u32[]{:S(2)}, u32[]{:S(2)}) collective-permute-start(bf16[4,112,1024]{2,1,0:T(8,128)(2,1)} %fusion.14), channel_id=1, source_target_pairs={{0,4},{4,0},{8,12},{12,8},{16,20},{20,16},{24,28},{28,24},{1,5},{5... | collective-permute-start | bytes 2752520 | tf_op jit(solution)/shard_map/ppermute | solution.py:796
  430.7 20.9 %collective-permute-start.45 = (bf16[4,112,1024]{2,1,0:T(8,128)(2,1)}, bf16[4,112,1024]{2,1,0:T(8,128)(2,1)}, u32[]{:S(2)}, u32[]{:S(2)}) collective-permute-start(bf16[4,112,1024]{2,1,0:T(8,128)(2,1)} %fusion.13), channel_id=1, source_target_pairs={{0,2},{1,3},{2,0},{3,1},{4,6},{5,7},{6,4},{7,5},{8,10},{9,11},{10,... | collective-permute-start | bytes 2752520 | tf_op jit(solution)/shard_map/ppermute | solution.py:796
  453.9 22.5 %collective-permute-start.50 = (bf16[2,256,1024]{2,1,0:T(8,128)(2,1)S(1)}, bf16[2,256,1024]{2,1,0:T(8,128)(2,1)S(1)}, u32[]{:S(2)}, u32[]{:S(2)}) collective-permute-start(bf16[2,256,1024]{2,1,0:T(8,128)(2,1)S(1)} %constant_dynamic-slice_fusion.1), channel_id=1, source_target_pairs={{0,2},{1,3},{2,0},{3,1},{4,6},{5,7},{6,4},{7,5},{8,10},{9,11},{10,... | collective-permute-start | bytes 3145736 | tf_op jit(solution)/shard_map/ppermute | solution.py:796
  (71 other events, 743.6 us)
Sparse Core Ops, SparseCore 0:
  87.2 97.5 all-gather.2

commit v10 on v9

--- a/solution.py
+++ b/solution.py
@@ -933,7 +933,7 @@
     full3 = lax.all_gather(shard3, both, axis=0, tiled=False)
     x, hidden, q, k, v, w_qkv, gains, t, t_back = qkv_fwd(ids, x4, (x_chip, x_core), *g1.all_pieces(), bucket_rows, HEADS)
     pairs = HEADS // 2
-    att = attn_fwd(length, q, k, v, t, 0, pairs // 2)
+    att = attn_fwd(length, q, k, v, t, 0, 3)
     g2.take(g2.own, 0)
     g2.x, g2.y = tie((att[0], g2.pieces[1]), g2.x, g2.y)
     g2.corner_y()
@@ -942,7 +942,7 @@
     g2.take(g2.x, 2)
     g2.take(g2.y, 4)
     q_in, = tie((g2.x, g2.y), q)
-    attended, lse = attn_fwd(length, q_in, k, v, t, pairs // 2, pairs // 2, att)
+    attended, lse = attn_fwd(length, q_in, k, v, t, 3, pairs - 3, att)
     g2.corner, g_chip = tie((attended, g2.pieces[3], g2.pieces[5]), g2.corner, g_chip)
     g2.take(g2.corner, 6)
     g_core = send_core(g4, g_chip, me)
@@ -1005,7 +1005,7 @@
     gx_chip, = tie(sc1.came, gx_chip)
     gx_core = send_core(gx4, gx_chip, me)
     input_grad = place(gx4, gx_chip, gx_core, me)
-    sc1.came = list(tie(input_grad, *sc1.came))
+    sc1.came = list(tie(gx_chip, *sc1.came))
     r1 = sc1.result()
     prod = up(shard1[:3 * own]) * r1[:3 * own]
     g_gain1 = jnp.sum(prod[:own] + prod[own:2 * own] + prod[2 * own:], axis=1) / up(low(norm1_gain))

time: 497 us -> 494 us (level)
  waiting for transfers between devices: 123 us -> 117 us
    ppermute x52, waiting for transfers between devices: 123 us -> 117 us  [swap(): lax.ppermute(value, axis, [(i, i ^ mask) for i in range(lax.axis_size(axi...]
  transfers between devices with their start and end apart: 53 -> 53, of which waited for: 22 -> 23; matrix products, arithmetic and copies ran while one was open for 12% -> 13% of each run, Pallas kernels for 43% -> 43%
where the time goes in v10:
time: 494 us; the launch traced here: 487 us
  Pallas kernels  224 us (45%)
  waiting for transfers between devices  117 us (24%)
  other arithmetic  50.4 us (10%)
  starting transfers between devices  49.7 us (10%)
  local copies, waits for them, and re-layouts  30.3 us (6%)
  between operations  15.6 us (3%)
    ppermute x52, waiting for transfers between devices, swap(): lax.ppermute(value, axis, [(i, i ^ mask) for i in range(lax.axis_size(axi...  117 us
    pallas_call x4, Pallas kernels, attn_bwd(): pl.pallas_call(functools.partial(bwd_kernel, rows=rows, seq_len=seq_len,...  65.9 us
    ppermute x52, starting transfers between devices, swap(): lax.ppermute(value, axis, [(i, i ^ mask) for i in range(lax.axis_size(axi...  49.7 us
    pallas_call x1, Pallas kernels, mid_b(): pl.pallas_call(mid_b_kernel, out_shape=(low(rows, width), low(rows, width...  45.1 us
    pallas_call x1, Pallas kernels, mid_a(): pl.pallas_call(functools.partial(mid_a_kernel, masks=masks), out_shape=(f...  39.9 us
    pallas_call x2, Pallas kernels, attn_fwd(): pl.pallas_call(functools.partial(fwd_kernel, rows=rows, seq_len=seq_len,...  33.3 us
    convert_element_type x6, other arithmetic, quarter(): return (cut(self.mine) + cut(self.other)).astype(jnp.bfloat16)  20 us
    pallas_call x1, Pallas kernels, qkv_gx(): pl.pallas_call(gx_kernel, out_shape=jax.ShapeDtypeStruct((total, width),...  14.3 us
  transfers between devices with their start and end apart: 53, of which 23 were waited for; matrix products, arithmetic and copies ran while one was open for 13% of the time, Pallas kernels for 43%

profile of v10, /device:TPU:0, one launch (start us, length us, event | category | flops | bytes accessed | tf_op | source)
XLA Modules:
  0.0 486.9 jit_solution(7994002889694717416)
XLA Ops:
  12.5 3.1 collective-permute-start.2
  23.0 3.0 slice_reduce_fusion
  28.2 6.7 %collective-permute-done.3 = bf16[1,112,1024]{2,1,0:T(8,128)(2,1)S(1)} collective-permute-done((bf16[1,112,1024]{2,1,0:T(8,128)(2,1)S(1)}, bf16[1,112,1024]{2,1,0:T(8,128)(2,1)S(1)}, u32[]{:S(2)}, u32[]{:S(2)}) %collective-permute-start.3) | collective-permute-done | bytes 229408 | tf_op jit(solution)/shard_map/ppermute | solution.py:796
  36.7 3.7 collective-permute-done.1
  40.5 4.8 collective-permute-done.chip_ref
  51.8 21.9 %collective-permute-done.6 = bf16[1,160,1024]{2,1,0:T(8,128)(2,1)S(1)} collective-permute-done((bf16[1,160,1024]{2,1,0:T(8,128)(2,1)S(1)}, bf16[1,160,1024]{2,1,0:T(8,128)(2,1)S(1)}, u32[]{:S(2)}, u32[]{:S(2)}) %collective-permute-start.6) | collective-permute-done | bytes 327712 | tf_op jit(solution)/shard_map/ppermute | solution.py:796
  78.3 7.3 %collective-permute-done.10.refs_8_ = bf16[2,112,1024]{2,1,0:T(8,128)(2,1)S(1)} collective-permute-done((bf16[2,112,1024]{2,1,0:T(8,128)(2,1)S(1)}, bf16[2,112,1024]{2,1,0:T(8,128)(2,1)S(1)}, u32[]{:S(2)}, u32[]{:S(2)}) %collective-permute-start.10) | collective-permute-done | bytes 458784 | tf_op jit(solution)/shard_map/ppermute | solution.py:796
  99.3 13.2 %qkv_fwd.1 = (bf16[1024,1024]{1,0:T(8,128)(2,1)}, bf16[1024,1024]{1,0:T(8,128)(2,1)}, bf16[1024,1024]{1,0:T(8,128)(2,1)}, bf16[1024,1024]{1,0:T(8,128)(2,1)}, bf...) custom-call(s32[3]{0:T(128)} %pad_add_fusion.1.ids_ref, ...), custom_call_target="tpu_custom_call" | custom-call | flops 1048576 | bytes 65536 | tf_op jit(solution)/shard_map/qkv_fwd/pallas_call | solution.py:524
  112.5 13.2 %attn_fwd.2 = (bf16[1024,1024]{1,0:T(8,128)(2,1)}, f32[8,1024,128]{2,1,0:T(8,128)}) custom-call(s32[1]{0:T(128)} %dynamic_slice.189.len_ref, bf16[1024,1024]{1,0:T(8,128)(2,1)} %get-tuple-element.133.q_ref, bf16[1024,1024]{1,0:T(8,128)(2,1)} %get-tuple-element.126.k_ref, bf16[1024,1024]{1,0:T(8,128)(2,1)} %get-tuple-element.127.v_ref, ...), custom_call_target="tpu_custom_call" | custom-call | flops 1048576 | bytes 65536 | tf_op jit(solution)/shard_map/attn_fwd/pallas_call | solution.py:360
  131.5 20.1 %attn_fwd.3 = (bf16[1024,1024]{1,0:T(8,128)(2,1)}, f32[8,1024,128]{2,1,0:T(8,128)}) custom-call(s32[1]{0:T(128)} %dynamic_slice.189.len_ref, bf16[1024,1024]{1,0:T(8,128)(2,1)} %get-tuple-element.133.q_ref, bf16[1024,1024]{1,0:T(8,128)(2,1)} %get-tuple-element.126.k_ref, ...), custom_call_target="tpu_custom_call", output_to_operand_aliasing={{0}: (5, {}), {1}: (6, {})} | custom-call | flops 1048576 | bytes 65536 | tf_op jit(solution)/shard_map/attn_fwd/pallas_call | solution.py:360
  151.6 19.3 %collective-permute-done.23.chip_ref = bf16[2,256,1024]{2,1,0:T(8,128)(2,1)S(1)} collective-permute-done((bf16[2,256,1024]{2,1,0:T(8,128)(2,1)}, bf16[2,256,1024]{2,1,0:T(8,128)(2,1)S(1)}, u32[]{:S(2)}, u32[]{:S(2)}) %collective-permute-start.23) | collective-permute-done | bytes 1048608 | tf_op jit(solution)/shard_map/ppermute | solution.py:796
  170.9 3.4 collective-permute-done.22.refs_6_
  175.0 3.8 collective-permute-done.24.core_ref
  180.2 39.9 %mid_a.1 = (f32[1024,1024]{1,0:T(8,128)}, f32[1024,1024]{1,0:T(8,128)}, f32[1024,1024]{1,0:T(8,128)}, bf16[1024,1024]{1,0:T(8,128)(2,1)}, bf16[1024,1024]{1,0:T(...) custom-call(s32[3]{0:T(128)} %pad_add_fusion.1.ids_ref, ...), custom_call_target="tpu_custom_call" | custom-call | flops 1048576 | bytes 65536 | tf_op jit(solution)/shard_map/mid_a/pallas_call | solution.py:659
  220.3 45.1 %mid_b.1 = (bf16[1024,1024]{1,0:T(8,128)(2,1)}, bf16[1024,1024]{1,0:T(8,128)(2,1)}, bf16[1024,1024]{1,0:T(8,128)(2,1)}, bf16[16,160,1024]{2,1,0:T(8,128)(2,1)}, bf16[16,160,1024]{2,1,0:T(8,128)(2,1)}) custom-call(s32[3]{0:T(128)} %pad_add_fusion.1.ids_ref, f32[8,1024]{1,0:T(8,128)} %get-tuple-element.123.gain_ref, ...), custom_call_target="tpu_custom_call" | custom-call | flops 1048576 | bytes 65536 | tf_op jit(solution)/shard_map/mid_b/pallas_call | solution.py:727
  265.4 4.7 fusion.8
  273.0 16.6 %attn_bwd.4 = (bf16[1024,1024]{1,0:T(8,128)(2,1)}, bf16[1024,1024]{1,0:T(8,128)(2,1)}, bf16[1024,1024]{1,0:T(8,128)(2,1)}, f32[4,2048]{1,0:T(4,128)}) custom-call(s32[1]{0:T(128)} %dynamic_slice.189.len_ref, bf16[1024,1024]{1,0:T(8,128)(2,1)} %get-tuple-element.133.q_ref, bf16[1024,1024]{1,0:T(8,128)(2,1)} %get-tuple-element.126.k_ref, ...), custom_call_target="tpu_custom_call" | custom-call | flops 1048576 | bytes 65536 | tf_op jit(solution)/shard_map/attn_bwd/pallas_call | solution.py:439
  289.7 4.8 fusion.4
  300.2 3.2 fusion.1
  305.4 16.3 %attn_bwd.5 = (bf16[1024,1024]{1,0:T(8,128)(2,1)}, bf16[1024,1024]{1,0:T(8,128)(2,1)}, bf16[1024,1024]{1,0:T(8,128)(2,1)}, f32[4,2048]{1,0:T(4,128)}) custom-call(s32[1]{0:T(128)} %dynamic_slice.189.len_ref, bf16[1024,1024]{1,0:T(8,128)(2,1)} %get-tuple-element.133.q_ref, ...), custom_call_target="tpu_custom_call", output_to_operand_aliasing={{0}: (8, {}), {1}: (9, {}), {2}: (10, {})} | custom-call | flops 1048576 | bytes 65536 | tf_op jit(solution)/shard_map/attn_bwd/pallas_call | solution.py:439
  321.7 3.0 fusion.5
  326.5 3.6 fusion
  333.4 16.5 %attn_bwd.6 = (bf16[1024,1024]{1,0:T(8,128)(2,1)}, bf16[1024,1024]{1,0:T(8,128)(2,1)}, bf16[1024,1024]{1,0:T(8,128)(2,1)}, f32[4,2048]{1,0:T(4,128)}) custom-call(s32[1]{0:T(128)} %dynamic_slice.189.len_ref, bf16[1024,1024]{1,0:T(8,128)(2,1)} %get-tuple-element.133.q_ref, ...), custom_call_target="tpu_custom_call", output_to_operand_aliasing={{0}: (8, {}), {1}: (9, {}), {2}: (10, {})} | custom-call | flops 1048576 | bytes 65536 | tf_op jit(solution)/shard_map/attn_bwd/pallas_call | solution.py:439
  352.9 3.5 collective-permute-start.37
  357.3 16.5 %attn_bwd.7 = (bf16[1024,1024]{1,0:T(8,128)(2,1)}, bf16[1024,1024]{1,0:T(8,128)(2,1)}, bf16[1024,1024]{1,0:T(8,128)(2,1)}, f32[4,2048]{1,0:T(4,128)}) custom-call(s32[1]{0:T(128)} %dynamic_slice.189.len_ref, bf16[1024,1024]{1,0:T(8,128)(2,1)} %get-tuple-element.133.q_ref, ...), custom_call_target="tpu_custom_call", output_to_operand_aliasing={{0}: (8, {}), {1}: (9, {}), {2}: (10, {})} | custom-call | flops 1048576 | bytes 65536 | tf_op jit(solution)/shard_map/attn_bwd/pallas_call | solution.py:439
  377.7 12.5 %qkv_gw.1 = (bf16[16,112,1024]{2,1,0:T(8,128)(2,1)}, bf16[16,112,1024]{2,1,0:T(8,128)(2,1)}) custom-call(s32[3]{0:T(128)} %pad_add_fusion.1.ids_ref, bf16[1024,1024]{1,0:T(8,128)(2,1)} %get-tuple-element.188.h_ref, bf16[1024,1024]{1,0:T(8,128)(2,1)} %get-tuple-element.189.dq_ref, bf16[1024,1024]{1,0:T(8,128)(2,1)} %get-tuple-element.190.dk_ref, ...), custom_call_target="tpu_custom_call" | custom-call | flops 1048576 | bytes 65536 | tf_op jit(solution)/shard_map/qkv_gw/pallas_call | solution.py:761
  395.2 14.3 %qkv_gx.1 = bf16[1024,1024]{1,0:T(8,128)(2,1)} custom-call(bf16[1024,1024]{1,0:T(8,128)(2,1)} %get-tuple-element.124.x_hbm.x_ref, bf16[1024,1024]{1,0:T(8,128)(2,1)} %get-tuple-element.194.gb_ref, bf16[1024,1024]{1,0:T(8,128)(2,1)} %get-tuple-element.189.dq_ref, bf16[1024,1024]{1,0:T(8,128)(2,1)} %get-tuple-element.190.dk_ref, ...), custom_call_target="tpu_custom_call" | custom-call | flops 1048576 | bytes 65536 | tf_op jit(solution)/shard_map/qkv_gx/pallas_call | solution.py:785
  409.5 3.3 add_convert_fusion.12
  436.5 12.3 %collective-permute-done.46 = bf16[4,112,1024]{2,1,0:T(8,128)(2,1)} collective-permute-done((bf16[4,112,1024]{2,1,0:T(8,128)(2,1)}, bf16[4,112,1024]{2,1,0:T(8,128)(2,1)}, u32[]{:S(2)}, u32[]{:S(2)}) %collective-permute-start.46) | collective-permute-done | bytes 917536 | tf_op jit(solution)/shard_map/ppermute | solution.py:796
  457.9 5.4 %collective-permute-done.47 = bf16[112,1024]{1,0:T(8,128)(2,1)S(1)} collective-permute-done((bf16[112,1024]{1,0:T(8,128)(2,1)S(1)}, bf16[112,1024]{1,0:T(8,128)(2,1)S(1)}, u32[]{:S(2)}, u32[]{:S(2)}) %collective-permute-start.47) | collective-permute-done | bytes 229408 | tf_op jit(solution)/shard_map/ppermute | solution.py:796
  463.3 8.6 %collective-permute-done.48 = bf16[112,1024]{1,0:T(8,128)(2,1)S(1)} collective-permute-done((bf16[112,1024]{1,0:T(8,128)(2,1)S(1)}, bf16[112,1024]{1,0:T(8,128)(2,1)S(1)}, u32[]{:S(2)}, u32[]{:S(2)}) %collective-permute-start.48) | collective-permute-done | bytes 229408 | tf_op jit(solution)/shard_map/ppermute | solution.py:796
  471.8 3.5 collective-permute-done.50
  (284 shorter events, 114.5 us)
Async XLA Ops:
  7.2 213.1 %all-gather.3.cloned.1.call-start = ((), (), s32[]{:S(2)}) async-start(), calls=%async_computation | async-start | bytes 8650752 | tf_op jit(solution)/shard_map/all_gather | solution.py:933
  20.5 24.8 %collective-permute-start = (bf16[2,256,1024]{2,1,0:T(8,128)(2,1)}, bf16[2,256,1024]{2,1,0:T(8,128)(2,1)S(1)}, u32[]{:S(2)}, u32[]{:S(2)}) collective-permute-start(bf16[2,256,1024]{2,1,0:T(8,128)(2,1)} %constant_dynamic-slice_fusion.11), channel_id=1, source_target_pairs={{0,2},{1,3},{2,0},{3,1},{4,6},{5,7},{6,4},{7,5},{8,10},{9,11},{10,... | collective-permute-start | bytes 3145736 | tf_op jit(solution)/shard_map/ppermute | solution.py:796
  45.3 28.5 %collective-permute-start.7 = (bf16[4,112,1024]{2,1,0:T(8,128)(2,1)S(1)}, bf16[4,112,1024]{2,1,0:T(8,128)(2,1)S(1)}, u32[]{:S(2)}, u32[]{:S(2)}) collective-permute-start(bf16[4,112,1024]{2,1,0:T(8,128)(2,1)S(1)} %pad_maximum_fusion.6.refs_0_), channel_id=1, source_target_pairs={{0,2},{1,3},{2,0},{3,1},{4,6},{5,7},{6,4},{7,5},{8,10},{9,11},{10,... | collective-permute-start | bytes 2752520 | tf_op jit(solution)/shard_map/ppermute | solution.py:796
  46.8 27.0 %collective-permute-start.8 = (bf16[4,112,1024]{2,1,0:T(8,128)(2,1)S(1)}, bf16[4,112,1024]{2,1,0:T(8,128)(2,1)}, u32[]{:S(2)}, u32[]{:S(2)}) collective-permute-start(bf16[4,112,1024]{2,1,0:T(8,128)(2,1)S(1)} %pad_maximum_fusion.6.refs_0_), channel_id=1, source_target_pairs={{0,4},{4,0},{8,12},{12,8},{16,20},{20,16},{24,28},{28,24},{1,5},{5... | collective-permute-start | bytes 2752520 | tf_op jit(solution)/shard_map/ppermute | solution.py:796
  48.3 29.0 %collective-permute-start.5 = (bf16[4,112,1024]{2,1,0:T(8,128)(2,1)S(1)}, bf16[4,112,1024]{2,1,0:T(8,128)(2,1)S(1)}, u32[]{:S(2)}, u32[]{:S(2)}) collective-permute-start(bf16[4,112,1024]{2,1,0:T(8,128)(2,1)S(1)} %pad_maximum_fusion.6.refs_0_), channel_id=1, source_target_pairs={{0,1},{1,0},{2,3},{3,2},{4,5},{5,4},{6,7},{7,6},{8,9},{9,8},{10,11... | collective-permute-start | bytes 2752520 | tf_op jit(solution)/shard_map/ppermute | solution.py:796
  48.3 25.4 %collective-permute-start.6 = (bf16[1,160,1024]{2,1,0:T(8,128)(2,1)S(1)}, bf16[1,160,1024]{2,1,0:T(8,128)(2,1)S(1)}, u32[]{:S(2)}, u32[]{:S(2)}) collective-permute-start(bf16[1,160,1024]{2,1,0:T(8,128)(2,1)S(1)} %maximum_bitcast_fusion), channel_id=1, source_target_pairs={{0,16},{4,20},{8,24},{12,28},{16,0},{20,4},{24,8},{28,12},{1,17},{... | collective-permute-start | bytes 983048 | tf_op jit(solution)/shard_map/ppermute | solution.py:796
  49.9 26.1 %collective-permute-start.11 = (bf16[1,160,1024]{2,1,0:T(8,128)(2,1)S(1)}, bf16[1,160,1024]{2,1,0:T(8,128)(2,1)S(1)}, u32[]{:S(2)}, u32[]{:S(2)}) collective-permute-start(bf16[1,160,1024]{2,1,0:T(8,128)(2,1)S(1)} %maximum_bitcast_fusion), channel_id=1, source_target_pairs={{0,24},{4,28},{8,16},{12,20},{16,8},{20,12},{24,0},{28,4},{1,25},{... | collective-permute-start | bytes 983048 | tf_op jit(solution)/shard_map/ppermute | solution.py:796
  87.8 37.9 %collective-permute-start.17 = (bf16[4,160,1024]{2,1,0:T(8,128)(2,1)S(1)}, bf16[4,160,1024]{2,1,0:T(8,128)(2,1)S(1)}, u32[]{:S(2)}, u32[]{:S(2)}) collective-permute-start(bf16[4,160,1024]{2,1,0:T(8,128)(2,1)S(1)} %pad_maximum_fusion.refs_0_), channel_id=1, source_target_pairs={{0,1},{1,0},{2,3},{3,2},{4,5},{5,4},{6,7},{7,6},{8,9},{9,8},{10,11... | collective-permute-start | bytes 3932168 | tf_op jit(solution)/shard_map/ppermute | solution.py:796
  88.3 37.5 %collective-permute-start.18 = (bf16[4,160,1024]{2,1,0:T(8,128)(2,1)S(1)}, bf16[4,160,1024]{2,1,0:T(8,128)(2,1)}, u32[]{:S(2)}, u32[]{:S(2)}) collective-permute-start(bf16[4,160,1024]{2,1,0:T(8,128)(2,1)S(1)} %pad_maximum_fusion.refs_0_), channel_id=1, source_target_pairs={{0,2},{1,3},{2,0},{3,1},{4,6},{5,7},{6,4},{7,5},{8,10},{9,11},{10,... | collective-permute-start | bytes 3932168 | tf_op jit(solution)/shard_map/ppermute | solution.py:796
  91.3 36.6 %collective-permute-start.19 = (bf16[4,160,1024]{2,1,0:T(8,128)(2,1)S(1)}, bf16[4,160,1024]{2,1,0:T(8,128)(2,1)}, u32[]{:S(2)}, u32[]{:S(2)}) collective-permute-start(bf16[4,160,1024]{2,1,0:T(8,128)(2,1)S(1)} %pad_maximum_fusion.refs_0_), channel_id=1, source_target_pairs={{0,4},{4,0},{8,12},{12,8},{16,20},{20,16},{24,28},{28,24},{1,5},{5... | collective-permute-start | bytes 3932168 | tf_op jit(solution)/shard_map/ppermute | solution.py:796
  127.9 43.0 %collective-permute-start.20 = (bf16[4,160,1024]{2,1,0:T(8,128)(2,1)}, bf16[4,160,1024]{2,1,0:T(8,128)(2,1)}, u32[]{:S(2)}, u32[]{:S(2)}) collective-permute-start(bf16[4,160,1024]{2,1,0:T(8,128)(2,1)} %collective-permute-done.18.refs_2_), channel_id=1, source_target_pairs={{0,1},{1,0},{2,3},{3,2},{4,5},{5,4},{6,7},{7,6},{8,9},{9,8},{10,11... | collective-permute-start | bytes 3932168 | tf_op jit(solution)/shard_map/ppermute | solution.py:796
  127.9 43.0 %collective-permute-start.21 = (bf16[4,160,1024]{2,1,0:T(8,128)(2,1)}, bf16[4,160,1024]{2,1,0:T(8,128)(2,1)}, u32[]{:S(2)}, u32[]{:S(2)}) collective-permute-start(bf16[4,160,1024]{2,1,0:T(8,128)(2,1)} %collective-permute-done.19.refs_4_), channel_id=1, source_target_pairs={{0,1},{1,0},{2,3},{3,2},{4,5},{5,4},{6,7},{7,6},{8,9},{9,8},{10,11... | collective-permute-start | bytes 3932168 | tf_op jit(solution)/shard_map/ppermute | solution.py:796
  128.4 45.9 %collective-permute-start.22 = (bf16[4,160,1024]{2,1,0:T(8,128)(2,1)}, bf16[4,160,1024]{2,1,0:T(8,128)(2,1)}, u32[]{:S(2)}, u32[]{:S(2)}) collective-permute-start(bf16[4,160,1024]{2,1,0:T(8,128)(2,1)} %collective-permute-done.18.refs_2_), channel_id=1, source_target_pairs={{0,4},{4,0},{8,12},{12,8},{16,20},{20,16},{24,28},{28,24},{1,5},{5... | collective-permute-start | bytes 3932168 | tf_op jit(solution)/shard_map/ppermute | solution.py:796
  130.9 39.9 %collective-permute-start.23 = (bf16[2,256,1024]{2,1,0:T(8,128)(2,1)}, bf16[2,256,1024]{2,1,0:T(8,128)(2,1)S(1)}, u32[]{:S(2)}, u32[]{:S(2)}) collective-permute-start(bf16[2,256,1024]{2,1,0:T(8,128)(2,1)} %constant_dynamic-slice_fusion.8), channel_id=1, source_target_pairs={{0,2},{1,3},{2,0},{3,1},{4,6},{5,7},{6,4},{7,5},{8,10},{9,11},{10,... | collective-permute-start | bytes 3145736 | tf_op jit(solution)/shard_map/ppermute | solution.py:796
  220.1 45.3 %collective-permute-start.26 = (bf16[4,2,2,128,1024]{4,3,2,1,0:T(8,128)(2,1)}, bf16[4,2,2,128,1024]{4,3,2,1,0:T(8,128)(2,1)}, u32[]{:S(2)}, u32[]{:S(2)}) collective-permute-start(bf16[4,2,2,128,1024]{4,3,2,1,0:T(8,128)(2,1)} %bitcast.146), channel_id=1, source_target_pairs={{0,1},{1,0},{2,3},{3,2},{4,5},{5,4},{6,7},{7,6},{8,9},{9,8},{10,11... | collective-permute-start | bytes 12582920 | tf_op jit(solution)/shard_map/ppermute | solution.py:796
  270.2 19.5 %collective-permute-start.27 = (bf16[4,2,2,160,1024]{4,3,2,1,0:T(8,128)(2,1)}, bf16[4,2,2,160,1024]{4,3,2,1,0:T(8,128)(2,1)}, u32[]{:S(2)}, u32[]{:S(2)}) collective-permute-start(bf16[4,2,2,160,1024]{4,3,2,1,0:T(8,128)(2,1)} %bitcast.145), channel_id=1, source_target_pairs={{0,1},{1,0},{2,3},{3,2},{4,5},{5,4},{6,7},{7,6},{8,9},{9,8},{10,11... | collective-permute-start | bytes 15728648 | tf_op jit(solution)/shard_map/ppermute | solution.py:796
  270.6 27.6 %collective-permute-start.28 = (bf16[4,128,1024]{2,1,0:T(8,128)(2,1)}, bf16[4,128,1024]{2,1,0:T(8,128)(2,1)}, u32[]{:S(2)}, u32[]{:S(2)}) collective-permute-start(bf16[4,128,1024]{2,1,0:T(8,128)(2,1)} %get-tuple-element.223), channel_id=1, source_target_pairs={{0,4},{4,0},{8,12},{12,8},{16,20},{20,16},{24,28},{28,24},{1,5},{5... | collective-permute-start | bytes 3145736 | tf_op jit(solution)/shard_map/ppermute | solution.py:796
  294.5 32.0 %collective-permute-start.30 = (bf16[4,160,1024]{2,1,0:T(8,128)(2,1)}, bf16[4,160,1024]{2,1,0:T(8,128)(2,1)}, u32[]{:S(2)}, u32[]{:S(2)}) collective-permute-start(bf16[4,160,1024]{2,1,0:T(8,128)(2,1)} %get-tuple-element.221), channel_id=1, source_target_pairs={{0,4},{4,0},{8,12},{12,8},{16,20},{20,16},{24,28},{28,24},{1,5},{5... | collective-permute-start | bytes 3932168 | tf_op jit(solution)/shard_map/ppermute | solution.py:796
  295.5 29.2 %collective-permute-start.29 = (bf16[2,256,1024]{2,1,0:T(8,128)(2,1)}, bf16[2,256,1024]{2,1,0:T(8,128)(2,1)}, u32[]{:S(2)}, u32[]{:S(2)}) collective-permute-start(bf16[2,256,1024]{2,1,0:T(8,128)(2,1)} %constant_dynamic-slice_fusion.4), channel_id=1, source_target_pairs={{0,2},{1,3},{2,0},{3,1},{4,6},{5,7},{6,4},{7,5},{8,10},{9,11},{10,... | collective-permute-start | bytes 3145736 | tf_op jit(solution)/shard_map/ppermute | solution.py:796
  298.2 51.7 %collective-permute-start.33 = (bf16[4,128,1024]{2,1,0:T(8,128)(2,1)}, bf16[4,128,1024]{2,1,0:T(8,128)(2,1)}, u32[]{:S(2)}, u32[]{:S(2)}) collective-permute-start(bf16[4,128,1024]{2,1,0:T(8,128)(2,1)} %fusion.9), channel_id=1, source_target_pairs={{0,4},{4,0},{8,12},{12,8},{16,20},{20,16},{24,28},{28,24},{1,5},{5... | collective-permute-start | bytes 3145736 | tf_op jit(solution)/shard_map/ppermute | solution.py:796
  303.4 46.5 %collective-permute-start.32 = (bf16[4,128,1024]{2,1,0:T(8,128)(2,1)}, bf16[4,128,1024]{2,1,0:T(8,128)(2,1)}, u32[]{:S(2)}, u32[]{:S(2)}) collective-permute-start(bf16[4,128,1024]{2,1,0:T(8,128)(2,1)} %fusion.1), channel_id=1, source_target_pairs={{0,2},{1,3},{2,0},{3,1},{4,6},{5,7},{6,4},{7,5},{8,10},{9,11},{10,... | collective-permute-start | bytes 3145736 | tf_op jit(solution)/shard_map/ppermute | solution.py:796
  332.5 43.4 %collective-permute-start.35 = (bf16[4,160,1024]{2,1,0:T(8,128)(2,1)}, bf16[4,160,1024]{2,1,0:T(8,128)(2,1)S(1)}, u32[]{:S(2)}, u32[]{:S(2)}) collective-permute-start(bf16[4,160,1024]{2,1,0:T(8,128)(2,1)} %fusion.5), channel_id=1, source_target_pairs={{0,4},{4,0},{8,12},{12,8},{16,20},{20,16},{24,28},{28,24},{1,5},{5... | collective-permute-start | bytes 3932168 | tf_op jit(solution)/shard_map/ppermute | solution.py:796
  333.4 42.4 %collective-permute-start.34 = (bf16[4,160,1024]{2,1,0:T(8,128)(2,1)}, bf16[4,160,1024]{2,1,0:T(8,128)(2,1)S(1)}, u32[]{:S(2)}, u32[]{:S(2)}) collective-permute-start(bf16[4,160,1024]{2,1,0:T(8,128)(2,1)} %fusion), channel_id=1, source_target_pairs={{0,2},{1,3},{2,0},{3,1},{4,6},{5,7},{6,4},{7,5},{8,10},{9,11},{10,... | collective-permute-start | bytes 3932168 | tf_op jit(solution)/shard_map/ppermute | solution.py:796
  352.9 24.8 %collective-permute-start.36 = (bf16[128,1024]{1,0:T(8,128)(2,1)S(1)}, bf16[128,1024]{1,0:T(8,128)(2,1)S(1)}, u32[]{:S(2)}, u32[]{:S(2)}) collective-permute-start(bf16[128,1024]{1,0:T(8,128)(2,1)S(1)} %get-tuple-element.234), channel_id=1, source_target_pairs={{0,8},{4,12},{8,0},{12,4},{16,24},{20,28},{24,16},{28,20},{1,9},{5... | collective-permute-start | bytes 786440 | tf_op jit(solution)/shard_map/ppermute | solution.py:796
  352.9 24.8 %collective-permute-start.37 = (bf16[128,1024]{1,0:T(8,128)(2,1)S(1)}, bf16[128,1024]{1,0:T(8,128)(2,1)S(1)}, u32[]{:S(2)}, u32[]{:S(2)}) collective-permute-start(bf16[128,1024]{1,0:T(8,128)(2,1)S(1)} %get-tuple-element.233), channel_id=1, source_target_pairs={{0,16},{4,20},{8,24},{12,28},{16,0},{20,4},{24,8},{28,12},{1,17},{... | collective-permute-start | bytes 786440 | tf_op jit(solution)/shard_map/ppermute | solution.py:796
  356.4 21.3 %collective-permute-start.38 = (bf16[128,1024]{1,0:T(8,128)(2,1)S(1)}, bf16[128,1024]{1,0:T(8,128)(2,1)S(1)}, u32[]{:S(2)}, u32[]{:S(2)}) collective-permute-start(bf16[128,1024]{1,0:T(8,128)(2,1)S(1)} %get-tuple-element.232), channel_id=1, source_target_pairs={{0,24},{4,28},{8,16},{12,20},{16,8},{20,12},{24,0},{28,4},{1,25},{... | collective-permute-start | bytes 786440 | tf_op jit(solution)/shard_map/ppermute | solution.py:796
  390.3 32.2 %collective-permute-start.40 = (bf16[160,1024]{1,0:T(8,128)(2,1)}, bf16[160,1024]{1,0:T(8,128)(2,1)}, u32[]{:S(2)}, u32[]{:S(2)}) collective-permute-start(bf16[160,1024]{1,0:T(8,128)(2,1)} %get-tuple-element.230), channel_id=1, source_target_pairs={{0,8},{4,12},{8,0},{12,4},{16,24},{20,28},{24,16},{28,20},{1,9},{5... | collective-permute-start | bytes 983048 | tf_op jit(solution)/shard_map/ppermute | solution.py:796
  392.8 29.8 %collective-permute-start.41 = (bf16[160,1024]{1,0:T(8,128)(2,1)}, bf16[160,1024]{1,0:T(8,128)(2,1)}, u32[]{:S(2)}, u32[]{:S(2)}) collective-permute-start(bf16[160,1024]{1,0:T(8,128)(2,1)} %get-tuple-element.229), channel_id=1, source_target_pairs={{0,16},{4,20},{8,24},{12,28},{16,0},{20,4},{24,8},{28,12},{1,17},{... | collective-permute-start | bytes 983048 | tf_op jit(solution)/shard_map/ppermute | solution.py:796
  393.9 28.7 %collective-permute-start.42 = (bf16[160,1024]{1,0:T(8,128)(2,1)}, bf16[160,1024]{1,0:T(8,128)(2,1)}, u32[]{:S(2)}, u32[]{:S(2)}) collective-permute-start(bf16[160,1024]{1,0:T(8,128)(2,1)} %get-tuple-element.228), channel_id=1, source_target_pairs={{0,24},{4,28},{8,16},{12,20},{16,8},{20,12},{24,0},{28,4},{1,25},{... | collective-permute-start | bytes 983048 | tf_op jit(solution)/shard_map/ppermute | solution.py:796
  427.6 21.2 %collective-permute-start.46 = (bf16[4,112,1024]{2,1,0:T(8,128)(2,1)}, bf16[4,112,1024]{2,1,0:T(8,128)(2,1)}, u32[]{:S(2)}, u32[]{:S(2)}) collective-permute-start(bf16[4,112,1024]{2,1,0:T(8,128)(2,1)} %fusion.14), channel_id=1, source_target_pairs={{0,4},{4,0},{8,12},{12,8},{16,20},{20,16},{24,28},{28,24},{1,5},{5... | collective-permute-start | bytes 2752520 | tf_op jit(solution)/shard_map/ppermute | solution.py:796
  429.6 20.9 %collective-permute-start.45 = (bf16[4,112,1024]{2,1,0:T(8,128)(2,1)}, bf16[4,112,1024]{2,1,0:T(8,128)(2,1)}, u32[]{:S(2)}, u32[]{:S(2)}) collective-permute-start(bf16[4,112,1024]{2,1,0:T(8,128)(2,1)} %fusion.13), channel_id=1, source_target_pairs={{0,2},{1,3},{2,0},{3,1},{4,6},{5,7},{6,4},{7,5},{8,10},{9,11},{10,... | collective-permute-start | bytes 2752520 | tf_op jit(solution)/shard_map/ppermute | solution.py:796
  452.8 22.5 %collective-permute-start.50 = (bf16[2,256,1024]{2,1,0:T(8,128)(2,1)S(1)}, bf16[2,256,1024]{2,1,0:T(8,128)(2,1)S(1)}, u32[]{:S(2)}, u32[]{:S(2)}) collective-permute-start(bf16[2,256,1024]{2,1,0:T(8,128)(2,1)S(1)} %constant_dynamic-slice_fusion.1), channel_id=1, source_target_pairs={{0,2},{1,3},{2,0},{3,1},{4,6},{5,7},{6,4},{7,5},{8,10},{9,11},{10,... | collective-permute-start | bytes 3145736 | tf_op jit(solution)/shard_map/ppermute | solution.py:796
  (71 other events, 788.0 us)
Sparse Core Ops, SparseCore 0:
  87.2 96.9 all-gather.2

commit v11 on v10

--- a/solution.py
+++ b/solution.py
@@ -911,8 +911,10 @@
     x4, g4 = tokens.reshape(parts, rows, width), cotangent.reshape(parts, rows, width)
     bucket_rows = jnp.stack([jnp.pad(buckets, (0, 1), constant_values=-1), jnp.pad(buckets[::-1], (0, 1), constant_values=-1)])
 
-    g1 = Gather(shard1)
-    x_chip = send_chip(x4, me)
+    x_far = lax.dynamic_slice_in_dim(x4, 2 * (1 - me // 2), 2, 0)
+    shard1_in, = tie(x_far, shard1)
+    x_chip = swap(x_far, "seq", 2)
+    g1 = Gather(shard1_in)
     g2 = Gather(shard2)
     g1.fill()
     g1.own, = tie((x_chip, g2.sent[1], shard3), g1.own)

time: 494 us -> 494 us (level)
  transfers between devices with their start and end apart: 53 -> 53, of which waited for: 23 -> 23; matrix products, arithmetic and copies ran while one was open for 13% -> 12% of each run, Pallas kernels for 43% -> 43%
where the time goes in v11:
time: 494 us; the launch traced here: 487 us
  Pallas kernels  224 us (45%)
  waiting for transfers between devices  117 us (24%)
  other arithmetic  50.4 us (10%)
  starting transfers between devices  49.7 us (10%)
  local copies, waits for them, and re-layouts  30.3 us (6%)
  between operations  15.6 us (3%)
    ppermute x52, waiting for transfers between devices, swap(): lax.ppermute(value, axis, [(i, i ^ mask) for i in range(lax.axis_size(axi...  117 us
    pallas_call x4, Pallas kernels, attn_bwd(): pl.pallas_call(functools.partial(bwd_kernel, rows=rows, seq_len=seq_len,...  65.9 us
    ppermute x52, starting transfers between devices, swap(): lax.ppermute(value, axis, [(i, i ^ mask) for i in range(lax.axis_size(axi...  49.7 us
    pallas_call x1, Pallas kernels, mid_b(): pl.pallas_call(mid_b_kernel, out_shape=(low(rows, width), low(rows, width...  45.1 us
    pallas_call x1, Pallas kernels, mid_a(): pl.pallas_call(functools.partial(mid_a_kernel, masks=masks), out_shape=(f...  39.9 us
    pallas_call x2, Pallas kernels, attn_fwd(): pl.pallas_call(functools.partial(fwd_kernel, rows=rows, seq_len=seq_len,...  33.3 us
    convert_element_type x6, other arithmetic, quarter(): return (cut(self.mine) + cut(self.other)).astype(jnp.bfloat16)  20 us
    pallas_call x1, Pallas kernels, qkv_gx(): pl.pallas_call(gx_kernel, out_shape=jax.ShapeDtypeStruct((total, width),...  14.3 us
  transfers between devices with their start and end apart: 53, of which 23 were waited for; matrix products, arithmetic and copies ran while one was open for 12% of the time, Pallas kernels for 43%

profile of v11, /device:TPU:0, one launch (start us, length us, event | category | flops | bytes accessed | tf_op | source)
XLA Modules:
  0.0 486.9 jit_solution(11044263241938123536)
XLA Ops:
  14.8 3.1 collective-permute-start.2
  23.0 3.0 slice_reduce_fusion
  28.2 9.0 %collective-permute-done.3 = bf16[1,112,1024]{2,1,0:T(8,128)(2,1)S(1)} collective-permute-done((bf16[1,112,1024]{2,1,0:T(8,128)(2,1)S(1)}, bf16[1,112,1024]{2,1,0:T(8,128)(2,1)S(1)}, u32[]{:S(2)}, u32[]{:S(2)}) %collective-permute-start.3) | collective-permute-done | bytes 229408 | tf_op jit(solution)/shard_map/ppermute | solution.py:796
  40.6 4.7 collective-permute-done.chip_ref
  51.8 21.9 %collective-permute-done.6 = bf16[1,160,1024]{2,1,0:T(8,128)(2,1)S(1)} collective-permute-done((bf16[1,160,1024]{2,1,0:T(8,128)(2,1)S(1)}, bf16[1,160,1024]{2,1,0:T(8,128)(2,1)S(1)}, u32[]{:S(2)}, u32[]{:S(2)}) %collective-permute-start.6) | collective-permute-done | bytes 327712 | tf_op jit(solution)/shard_map/ppermute | solution.py:796
  78.3 7.3 %collective-permute-done.10.refs_8_ = bf16[2,112,1024]{2,1,0:T(8,128)(2,1)S(1)} collective-permute-done((bf16[2,112,1024]{2,1,0:T(8,128)(2,1)S(1)}, bf16[2,112,1024]{2,1,0:T(8,128)(2,1)S(1)}, u32[]{:S(2)}, u32[]{:S(2)}) %collective-permute-start.10) | collective-permute-done | bytes 458784 | tf_op jit(solution)/shard_map/ppermute | solution.py:796
  99.3 13.2 %qkv_fwd.1 = (bf16[1024,1024]{1,0:T(8,128)(2,1)}, bf16[1024,1024]{1,0:T(8,128)(2,1)}, bf16[1024,1024]{1,0:T(8,128)(2,1)}, bf16[1024,1024]{1,0:T(8,128)(2,1)}, bf...) custom-call(s32[3]{0:T(128)} %pad_add_fusion.1.ids_ref, ...), custom_call_target="tpu_custom_call" | custom-call | flops 1048576 | bytes 65536 | tf_op jit(solution)/shard_map/qkv_fwd/pallas_call | solution.py:524
  112.5 13.2 %attn_fwd.2 = (bf16[1024,1024]{1,0:T(8,128)(2,1)}, f32[8,1024,128]{2,1,0:T(8,128)}) custom-call(s32[1]{0:T(128)} %dynamic_slice.189.len_ref, bf16[1024,1024]{1,0:T(8,128)(2,1)} %get-tuple-element.135.q_ref, bf16[1024,1024]{1,0:T(8,128)(2,1)} %get-tuple-element.128.k_ref, bf16[1024,1024]{1,0:T(8,128)(2,1)} %get-tuple-element.129.v_ref, ...), custom_call_target="tpu_custom_call" | custom-call | flops 1048576 | bytes 65536 | tf_op jit(solution)/shard_map/attn_fwd/pallas_call | solution.py:360
  131.5 20.1 %attn_fwd.3 = (bf16[1024,1024]{1,0:T(8,128)(2,1)}, f32[8,1024,128]{2,1,0:T(8,128)}) custom-call(s32[1]{0:T(128)} %dynamic_slice.189.len_ref, bf16[1024,1024]{1,0:T(8,128)(2,1)} %get-tuple-element.135.q_ref, bf16[1024,1024]{1,0:T(8,128)(2,1)} %get-tuple-element.128.k_ref, ...), custom_call_target="tpu_custom_call", output_to_operand_aliasing={{0}: (5, {}), {1}: (6, {})} | custom-call | flops 1048576 | bytes 65536 | tf_op jit(solution)/shard_map/attn_fwd/pallas_call | solution.py:360
  151.6 19.3 %collective-permute-done.23.chip_ref = bf16[2,256,1024]{2,1,0:T(8,128)(2,1)S(1)} collective-permute-done((bf16[2,256,1024]{2,1,0:T(8,128)(2,1)}, bf16[2,256,1024]{2,1,0:T(8,128)(2,1)S(1)}, u32[]{:S(2)}, u32[]{:S(2)}) %collective-permute-start.23) | collective-permute-done | bytes 1048608 | tf_op jit(solution)/shard_map/ppermute | solution.py:796
  170.9 3.4 collective-permute-done.22.refs_6_
  175.0 3.8 collective-permute-done.24.core_ref
  180.3 39.9 %mid_a.1 = (f32[1024,1024]{1,0:T(8,128)}, f32[1024,1024]{1,0:T(8,128)}, f32[1024,1024]{1,0:T(8,128)}, bf16[1024,1024]{1,0:T(8,128)(2,1)}, bf16[1024,1024]{1,0:T(...) custom-call(s32[3]{0:T(128)} %pad_add_fusion.1.ids_ref, ...), custom_call_target="tpu_custom_call" | custom-call | flops 1048576 | bytes 65536 | tf_op jit(solution)/shard_map/mid_a/pallas_call | solution.py:659
  220.3 45.1 %mid_b.1 = (bf16[1024,1024]{1,0:T(8,128)(2,1)}, bf16[1024,1024]{1,0:T(8,128)(2,1)}, bf16[1024,1024]{1,0:T(8,128)(2,1)}, bf16[16,160,1024]{2,1,0:T(8,128)(2,1)}, bf16[16,160,1024]{2,1,0:T(8,128)(2,1)}) custom-call(s32[3]{0:T(128)} %pad_add_fusion.1.ids_ref, f32[8,1024]{1,0:T(8,128)} %get-tuple-element.125.gain_ref, ...), custom_call_target="tpu_custom_call" | custom-call | flops 1048576 | bytes 65536 | tf_op jit(solution)/shard_map/mid_b/pallas_call | solution.py:727
  265.5 4.7 fusion.8
  273.1 16.6 %attn_bwd.4 = (bf16[1024,1024]{1,0:T(8,128)(2,1)}, bf16[1024,1024]{1,0:T(8,128)(2,1)}, bf16[1024,1024]{1,0:T(8,128)(2,1)}, f32[4,2048]{1,0:T(4,128)}) custom-call(s32[1]{0:T(128)} %dynamic_slice.189.len_ref, bf16[1024,1024]{1,0:T(8,128)(2,1)} %get-tuple-element.135.q_ref, bf16[1024,1024]{1,0:T(8,128)(2,1)} %get-tuple-element.128.k_ref, ...), custom_call_target="tpu_custom_call" | custom-call | flops 1048576 | bytes 65536 | tf_op jit(solution)/shard_map/attn_bwd/pallas_call | solution.py:439
  289.8 4.8 fusion.4
  295.6 2.6 fusion.9
  300.2 3.2 fusion.1
  305.5 16.3 %attn_bwd.5 = (bf16[1024,1024]{1,0:T(8,128)(2,1)}, bf16[1024,1024]{1,0:T(8,128)(2,1)}, bf16[1024,1024]{1,0:T(8,128)(2,1)}, f32[4,2048]{1,0:T(4,128)}) custom-call(s32[1]{0:T(128)} %dynamic_slice.189.len_ref, bf16[1024,1024]{1,0:T(8,128)(2,1)} %get-tuple-element.135.q_ref, ...), custom_call_target="tpu_custom_call", output_to_operand_aliasing={{0}: (8, {}), {1}: (9, {}), {2}: (10, {})} | custom-call | flops 1048576 | bytes 65536 | tf_op jit(solution)/shard_map/attn_bwd/pallas_call | solution.py:439
  321.7 3.0 fusion.5
  326.5 3.6 fusion
  333.5 16.5 %attn_bwd.6 = (bf16[1024,1024]{1,0:T(8,128)(2,1)}, bf16[1024,1024]{1,0:T(8,128)(2,1)}, bf16[1024,1024]{1,0:T(8,128)(2,1)}, f32[4,2048]{1,0:T(4,128)}) custom-call(s32[1]{0:T(128)} %dynamic_slice.189.len_ref, bf16[1024,1024]{1,0:T(8,128)(2,1)} %get-tuple-element.135.q_ref, ...), custom_call_target="tpu_custom_call", output_to_operand_aliasing={{0}: (8, {}), {1}: (9, {}), {2}: (10, {})} | custom-call | flops 1048576 | bytes 65536 | tf_op jit(solution)/shard_map/attn_bwd/pallas_call | solution.py:439
  352.9 3.4 collective-permute-start.37
  357.3 16.5 %attn_bwd.7 = (bf16[1024,1024]{1,0:T(8,128)(2,1)}, bf16[1024,1024]{1,0:T(8,128)(2,1)}, bf16[1024,1024]{1,0:T(8,128)(2,1)}, f32[4,2048]{1,0:T(4,128)}) custom-call(s32[1]{0:T(128)} %dynamic_slice.189.len_ref, bf16[1024,1024]{1,0:T(8,128)(2,1)} %get-tuple-element.135.q_ref, ...), custom_call_target="tpu_custom_call", output_to_operand_aliasing={{0}: (8, {}), {1}: (9, {}), {2}: (10, {})} | custom-call | flops 1048576 | bytes 65536 | tf_op jit(solution)/shard_map/attn_bwd/pallas_call | solution.py:439
  377.7 12.5 %qkv_gw.1 = (bf16[16,112,1024]{2,1,0:T(8,128)(2,1)}, bf16[16,112,1024]{2,1,0:T(8,128)(2,1)}) custom-call(s32[3]{0:T(128)} %pad_add_fusion.1.ids_ref, bf16[1024,1024]{1,0:T(8,128)(2,1)} %get-tuple-element.190.h_ref, bf16[1024,1024]{1,0:T(8,128)(2,1)} %get-tuple-element.191.dq_ref, bf16[1024,1024]{1,0:T(8,128)(2,1)} %get-tuple-element.192.dk_ref, ...), custom_call_target="tpu_custom_call" | custom-call | flops 1048576 | bytes 65536 | tf_op jit(solution)/shard_map/qkv_gw/pallas_call | solution.py:761
  395.2 14.3 %qkv_gx.1 = bf16[1024,1024]{1,0:T(8,128)(2,1)} custom-call(bf16[1024,1024]{1,0:T(8,128)(2,1)} %get-tuple-element.126.x_hbm.x_ref, bf16[1024,1024]{1,0:T(8,128)(2,1)} %get-tuple-element.196.gb_ref, bf16[1024,1024]{1,0:T(8,128)(2,1)} %get-tuple-element.191.dq_ref, bf16[1024,1024]{1,0:T(8,128)(2,1)} %get-tuple-element.192.dk_ref, ...), custom_call_target="tpu_custom_call" | custom-call | flops 1048576 | bytes 65536 | tf_op jit(solution)/shard_map/qkv_gx/pallas_call | solution.py:785
  409.5 3.3 add_convert_fusion.12
  436.5 12.3 %collective-permute-done.46 = bf16[4,112,1024]{2,1,0:T(8,128)(2,1)} collective-permute-done((bf16[4,112,1024]{2,1,0:T(8,128)(2,1)}, bf16[4,112,1024]{2,1,0:T(8,128)(2,1)}, u32[]{:S(2)}, u32[]{:S(2)}) %collective-permute-start.46) | collective-permute-done | bytes 917536 | tf_op jit(solution)/shard_map/ppermute | solution.py:796
  457.9 5.3 %collective-permute-done.47 = bf16[112,1024]{1,0:T(8,128)(2,1)S(1)} collective-permute-done((bf16[112,1024]{1,0:T(8,128)(2,1)S(1)}, bf16[112,1024]{1,0:T(8,128)(2,1)S(1)}, u32[]{:S(2)}, u32[]{:S(2)}) %collective-permute-start.47) | collective-permute-done | bytes 229408 | tf_op jit(solution)/shard_map/ppermute | solution.py:796
  463.3 8.6 %collective-permute-done.48 = bf16[112,1024]{1,0:T(8,128)(2,1)S(1)} collective-permute-done((bf16[112,1024]{1,0:T(8,128)(2,1)S(1)}, bf16[112,1024]{1,0:T(8,128)(2,1)S(1)}, u32[]{:S(2)}, u32[]{:S(2)}) %collective-permute-start.48) | collective-permute-done | bytes 229408 | tf_op jit(solution)/shard_map/ppermute | solution.py:796
  471.9 3.4 collective-permute-done.50
  (284 shorter events, 113.5 us)
Async XLA Ops:
  7.2 213.1 %all-gather.3.cloned.1.call-start = ((), (), s32[]{:S(2)}) async-start(), calls=%async_computation | async-start | bytes 8650752 | tf_op jit(solution)/shard_map/all_gather | solution.py:935
  20.5 24.8 %collective-permute-start = (bf16[2,256,1024]{2,1,0:T(8,128)(2,1)}, bf16[2,256,1024]{2,1,0:T(8,128)(2,1)S(1)}, u32[]{:S(2)}, u32[]{:S(2)}) collective-permute-start(bf16[2,256,1024]{2,1,0:T(8,128)(2,1)} %constant_dynamic-slice_fusion.11), channel_id=1, source_target_pairs={{0,2},{1,3},{2,0},{3,1},{4,6},{5,7},{6,4},{7,5},{8,10},{9,11},{10,... | collective-permute-start | bytes 3145736 | tf_op jit(solution)/shard_map/ppermute | solution.py:796
  45.3 28.5 %collective-permute-start.7 = (bf16[4,112,1024]{2,1,0:T(8,128)(2,1)S(1)}, bf16[4,112,1024]{2,1,0:T(8,128)(2,1)S(1)}, u32[]{:S(2)}, u32[]{:S(2)}) collective-permute-start(bf16[4,112,1024]{2,1,0:T(8,128)(2,1)S(1)} %pad_maximum_fusion.6.refs_0_), channel_id=1, source_target_pairs={{0,2},{1,3},{2,0},{3,1},{4,6},{5,7},{6,4},{7,5},{8,10},{9,11},{10,... | collective-permute-start | bytes 2752520 | tf_op jit(solution)/shard_map/ppermute | solution.py:796
  46.8 27.0 %collective-permute-start.8 = (bf16[4,112,1024]{2,1,0:T(8,128)(2,1)S(1)}, bf16[4,112,1024]{2,1,0:T(8,128)(2,1)}, u32[]{:S(2)}, u32[]{:S(2)}) collective-permute-start(bf16[4,112,1024]{2,1,0:T(8,128)(2,1)S(1)} %pad_maximum_fusion.6.refs_0_), channel_id=1, source_target_pairs={{0,4},{4,0},{8,12},{12,8},{16,20},{20,16},{24,28},{28,24},{1,5},{5... | collective-permute-start | bytes 2752520 | tf_op jit(solution)/shard_map/ppermute | solution.py:796
  48.3 29.0 %collective-permute-start.5 = (bf16[4,112,1024]{2,1,0:T(8,128)(2,1)S(1)}, bf16[4,112,1024]{2,1,0:T(8,128)(2,1)S(1)}, u32[]{:S(2)}, u32[]{:S(2)}) collective-permute-start(bf16[4,112,1024]{2,1,0:T(8,128)(2,1)S(1)} %pad_maximum_fusion.6.refs_0_), channel_id=1, source_target_pairs={{0,1},{1,0},{2,3},{3,2},{4,5},{5,4},{6,7},{7,6},{8,9},{9,8},{10,11... | collective-permute-start | bytes 2752520 | tf_op jit(solution)/shard_map/ppermute | solution.py:796
  48.3 25.4 %collective-permute-start.6 = (bf16[1,160,1024]{2,1,0:T(8,128)(2,1)S(1)}, bf16[1,160,1024]{2,1,0:T(8,128)(2,1)S(1)}, u32[]{:S(2)}, u32[]{:S(2)}) collective-permute-start(bf16[1,160,1024]{2,1,0:T(8,128)(2,1)S(1)} %maximum_bitcast_fusion), channel_id=1, source_target_pairs={{0,16},{4,20},{8,24},{12,28},{16,0},{20,4},{24,8},{28,12},{1,17},{... | collective-permute-start | bytes 983048 | tf_op jit(solution)/shard_map/ppermute | solution.py:796
  49.9 26.1 %collective-permute-start.11 = (bf16[1,160,1024]{2,1,0:T(8,128)(2,1)S(1)}, bf16[1,160,1024]{2,1,0:T(8,128)(2,1)S(1)}, u32[]{:S(2)}, u32[]{:S(2)}) collective-permute-start(bf16[1,160,1024]{2,1,0:T(8,128)(2,1)S(1)} %maximum_bitcast_fusion), channel_id=1, source_target_pairs={{0,24},{4,28},{8,16},{12,20},{16,8},{20,12},{24,0},{28,4},{1,25},{... | collective-permute-start | bytes 983048 | tf_op jit(solution)/shard_map/ppermute | solution.py:796
  87.8 37.9 %collective-permute-start.17 = (bf16[4,160,1024]{2,1,0:T(8,128)(2,1)S(1)}, bf16[4,160,1024]{2,1,0:T(8,128)(2,1)S(1)}, u32[]{:S(2)}, u32[]{:S(2)}) collective-permute-start(bf16[4,160,1024]{2,1,0:T(8,128)(2,1)S(1)} %pad_maximum_fusion.refs_0_), channel_id=1, source_target_pairs={{0,1},{1,0},{2,3},{3,2},{4,5},{5,4},{6,7},{7,6},{8,9},{9,8},{10,11... | collective-permute-start | bytes 3932168 | tf_op jit(solution)/shard_map/ppermute | solution.py:796
  88.3 37.5 %collective-permute-start.18 = (bf16[4,160,1024]{2,1,0:T(8,128)(2,1)S(1)}, bf16[4,160,1024]{2,1,0:T(8,128)(2,1)}, u32[]{:S(2)}, u32[]{:S(2)}) collective-permute-start(bf16[4,160,1024]{2,1,0:T(8,128)(2,1)S(1)} %pad_maximum_fusion.refs_0_), channel_id=1, source_target_pairs={{0,2},{1,3},{2,0},{3,1},{4,6},{5,7},{6,4},{7,5},{8,10},{9,11},{10,... | collective-permute-start | bytes 3932168 | tf_op jit(solution)/shard_map/ppermute | solution.py:796
  91.3 36.6 %collective-permute-start.19 = (bf16[4,160,1024]{2,1,0:T(8,128)(2,1)S(1)}, bf16[4,160,1024]{2,1,0:T(8,128)(2,1)}, u32[]{:S(2)}, u32[]{:S(2)}) collective-permute-start(bf16[4,160,1024]{2,1,0:T(8,128)(2,1)S(1)} %pad_maximum_fusion.refs_0_), channel_id=1, source_target_pairs={{0,4},{4,0},{8,12},{12,8},{16,20},{20,16},{24,28},{28,24},{1,5},{5... | collective-permute-start | bytes 3932168 | tf_op jit(solution)/shard_map/ppermute | solution.py:796
  127.9 43.0 %collective-permute-start.20 = (bf16[4,160,1024]{2,1,0:T(8,128)(2,1)}, bf16[4,160,1024]{2,1,0:T(8,128)(2,1)}, u32[]{:S(2)}, u32[]{:S(2)}) collective-permute-start(bf16[4,160,1024]{2,1,0:T(8,128)(2,1)} %collective-permute-done.18.refs_2_), channel_id=1, source_target_pairs={{0,1},{1,0},{2,3},{3,2},{4,5},{5,4},{6,7},{7,6},{8,9},{9,8},{10,11... | collective-permute-start | bytes 3932168 | tf_op jit(solution)/shard_map/ppermute | solution.py:796
  127.9 43.0 %collective-permute-start.21 = (bf16[4,160,1024]{2,1,0:T(8,128)(2,1)}, bf16[4,160,1024]{2,1,0:T(8,128)(2,1)}, u32[]{:S(2)}, u32[]{:S(2)}) collective-permute-start(bf16[4,160,1024]{2,1,0:T(8,128)(2,1)} %collective-permute-done.19.refs_4_), channel_id=1, source_target_pairs={{0,1},{1,0},{2,3},{3,2},{4,5},{5,4},{6,7},{7,6},{8,9},{9,8},{10,11... | collective-permute-start | bytes 3932168 | tf_op jit(solution)/shard_map/ppermute | solution.py:796
  128.4 45.9 %collective-permute-start.22 = (bf16[4,160,1024]{2,1,0:T(8,128)(2,1)}, bf16[4,160,1024]{2,1,0:T(8,128)(2,1)}, u32[]{:S(2)}, u32[]{:S(2)}) collective-permute-start(bf16[4,160,1024]{2,1,0:T(8,128)(2,1)} %collective-permute-done.18.refs_2_), channel_id=1, source_target_pairs={{0,4},{4,0},{8,12},{12,8},{16,20},{20,16},{24,28},{28,24},{1,5},{5... | collective-permute-start | bytes 3932168 | tf_op jit(solution)/shard_map/ppermute | solution.py:796
  131.0 39.9 %collective-permute-start.23 = (bf16[2,256,1024]{2,1,0:T(8,128)(2,1)}, bf16[2,256,1024]{2,1,0:T(8,128)(2,1)S(1)}, u32[]{:S(2)}, u32[]{:S(2)}) collective-permute-start(bf16[2,256,1024]{2,1,0:T(8,128)(2,1)} %constant_dynamic-slice_fusion.8), channel_id=1, source_target_pairs={{0,2},{1,3},{2,0},{3,1},{4,6},{5,7},{6,4},{7,5},{8,10},{9,11},{10,... | collective-permute-start | bytes 3145736 | tf_op jit(solution)/shard_map/ppermute | solution.py:796
  220.1 45.3 %collective-permute-start.26 = (bf16[4,2,2,128,1024]{4,3,2,1,0:T(8,128)(2,1)}, bf16[4,2,2,128,1024]{4,3,2,1,0:T(8,128)(2,1)}, u32[]{:S(2)}, u32[]{:S(2)}) collective-permute-start(bf16[4,2,2,128,1024]{4,3,2,1,0:T(8,128)(2,1)} %bitcast.146), channel_id=1, source_target_pairs={{0,1},{1,0},{2,3},{3,2},{4,5},{5,4},{6,7},{7,6},{8,9},{9,8},{10,11... | collective-permute-start | bytes 12582920 | tf_op jit(solution)/shard_map/ppermute | solution.py:796
  270.2 19.5 %collective-permute-start.27 = (bf16[4,2,2,160,1024]{4,3,2,1,0:T(8,128)(2,1)}, bf16[4,2,2,160,1024]{4,3,2,1,0:T(8,128)(2,1)}, u32[]{:S(2)}, u32[]{:S(2)}) collective-permute-start(bf16[4,2,2,160,1024]{4,3,2,1,0:T(8,128)(2,1)} %bitcast.145), channel_id=1, source_target_pairs={{0,1},{1,0},{2,3},{3,2},{4,5},{5,4},{6,7},{7,6},{8,9},{9,8},{10,11... | collective-permute-start | bytes 15728648 | tf_op jit(solution)/shard_map/ppermute | solution.py:796
  270.6 27.6 %collective-permute-start.28 = (bf16[4,128,1024]{2,1,0:T(8,128)(2,1)}, bf16[4,128,1024]{2,1,0:T(8,128)(2,1)}, u32[]{:S(2)}, u32[]{:S(2)}) collective-permute-start(bf16[4,128,1024]{2,1,0:T(8,128)(2,1)} %get-tuple-element.225), channel_id=1, source_target_pairs={{0,4},{4,0},{8,12},{12,8},{16,20},{20,16},{24,28},{28,24},{1,5},{5... | collective-permute-start | bytes 3145736 | tf_op jit(solution)/shard_map/ppermute | solution.py:796
  294.5 32.0 %collective-permute-start.30 = (bf16[4,160,1024]{2,1,0:T(8,128)(2,1)}, bf16[4,160,1024]{2,1,0:T(8,128)(2,1)}, u32[]{:S(2)}, u32[]{:S(2)}) collective-permute-start(bf16[4,160,1024]{2,1,0:T(8,128)(2,1)} %get-tuple-element.223), channel_id=1, source_target_pairs={{0,4},{4,0},{8,12},{12,8},{16,20},{20,16},{24,28},{28,24},{1,5},{5... | collective-permute-start | bytes 3932168 | tf_op jit(solution)/shard_map/ppermute | solution.py:796
  295.6 29.2 %collective-permute-start.29 = (bf16[2,256,1024]{2,1,0:T(8,128)(2,1)}, bf16[2,256,1024]{2,1,0:T(8,128)(2,1)}, u32[]{:S(2)}, u32[]{:S(2)}) collective-permute-start(bf16[2,256,1024]{2,1,0:T(8,128)(2,1)} %constant_dynamic-slice_fusion.4), channel_id=1, source_target_pairs={{0,2},{1,3},{2,0},{3,1},{4,6},{5,7},{6,4},{7,5},{8,10},{9,11},{10,... | collective-permute-start | bytes 3145736 | tf_op jit(solution)/shard_map/ppermute | solution.py:796
  298.2 51.7 %collective-permute-start.33 = (bf16[4,128,1024]{2,1,0:T(8,128)(2,1)}, bf16[4,128,1024]{2,1,0:T(8,128)(2,1)}, u32[]{:S(2)}, u32[]{:S(2)}) collective-permute-start(bf16[4,128,1024]{2,1,0:T(8,128)(2,1)} %fusion.9), channel_id=1, source_target_pairs={{0,4},{4,0},{8,12},{12,8},{16,20},{20,16},{24,28},{28,24},{1,5},{5... | collective-permute-start | bytes 3145736 | tf_op jit(solution)/shard_map/ppermute | solution.py:796
  303.4 46.5 %collective-permute-start.32 = (bf16[4,128,1024]{2,1,0:T(8,128)(2,1)}, bf16[4,128,1024]{2,1,0:T(8,128)(2,1)}, u32[]{:S(2)}, u32[]{:S(2)}) collective-permute-start(bf16[4,128,1024]{2,1,0:T(8,128)(2,1)} %fusion.1), channel_id=1, source_target_pairs={{0,2},{1,3},{2,0},{3,1},{4,6},{5,7},{6,4},{7,5},{8,10},{9,11},{10,... | collective-permute-start | bytes 3145736 | tf_op jit(solution)/shard_map/ppermute | solution.py:796
  332.5 43.4 %collective-permute-start.35 = (bf16[4,160,1024]{2,1,0:T(8,128)(2,1)}, bf16[4,160,1024]{2,1,0:T(8,128)(2,1)S(1)}, u32[]{:S(2)}, u32[]{:S(2)}) collective-permute-start(bf16[4,160,1024]{2,1,0:T(8,128)(2,1)} %fusion.5), channel_id=1, source_target_pairs={{0,4},{4,0},{8,12},{12,8},{16,20},{20,16},{24,28},{28,24},{1,5},{5... | collective-permute-start | bytes 3932168 | tf_op jit(solution)/shard_map/ppermute | solution.py:796
  333.5 42.4 %collective-permute-start.34 = (bf16[4,160,1024]{2,1,0:T(8,128)(2,1)}, bf16[4,160,1024]{2,1,0:T(8,128)(2,1)S(1)}, u32[]{:S(2)}, u32[]{:S(2)}) collective-permute-start(bf16[4,160,1024]{2,1,0:T(8,128)(2,1)} %fusion), channel_id=1, source_target_pairs={{0,2},{1,3},{2,0},{3,1},{4,6},{5,7},{6,4},{7,5},{8,10},{9,11},{10,... | collective-permute-start | bytes 3932168 | tf_op jit(solution)/shard_map/ppermute | solution.py:796
  352.9 24.8 %collective-permute-start.36 = (bf16[128,1024]{1,0:T(8,128)(2,1)S(1)}, bf16[128,1024]{1,0:T(8,128)(2,1)S(1)}, u32[]{:S(2)}, u32[]{:S(2)}) collective-permute-start(bf16[128,1024]{1,0:T(8,128)(2,1)S(1)} %get-tuple-element.236), channel_id=1, source_target_pairs={{0,8},{4,12},{8,0},{12,4},{16,24},{20,28},{24,16},{28,20},{1,9},{5... | collective-permute-start | bytes 786440 | tf_op jit(solution)/shard_map/ppermute | solution.py:796
  352.9 24.8 %collective-permute-start.37 = (bf16[128,1024]{1,0:T(8,128)(2,1)S(1)}, bf16[128,1024]{1,0:T(8,128)(2,1)S(1)}, u32[]{:S(2)}, u32[]{:S(2)}) collective-permute-start(bf16[128,1024]{1,0:T(8,128)(2,1)S(1)} %get-tuple-element.235), channel_id=1, source_target_pairs={{0,16},{4,20},{8,24},{12,28},{16,0},{20,4},{24,8},{28,12},{1,17},{... | collective-permute-start | bytes 786440 | tf_op jit(solution)/shard_map/ppermute | solution.py:796
  356.4 21.3 %collective-permute-start.38 = (bf16[128,1024]{1,0:T(8,128)(2,1)S(1)}, bf16[128,1024]{1,0:T(8,128)(2,1)S(1)}, u32[]{:S(2)}, u32[]{:S(2)}) collective-permute-start(bf16[128,1024]{1,0:T(8,128)(2,1)S(1)} %get-tuple-element.234), channel_id=1, source_target_pairs={{0,24},{4,28},{8,16},{12,20},{16,8},{20,12},{24,0},{28,4},{1,25},{... | collective-permute-start | bytes 786440 | tf_op jit(solution)/shard_map/ppermute | solution.py:796
  390.4 32.2 %collective-permute-start.40 = (bf16[160,1024]{1,0:T(8,128)(2,1)}, bf16[160,1024]{1,0:T(8,128)(2,1)}, u32[]{:S(2)}, u32[]{:S(2)}) collective-permute-start(bf16[160,1024]{1,0:T(8,128)(2,1)} %get-tuple-element.232), channel_id=1, source_target_pairs={{0,8},{4,12},{8,0},{12,4},{16,24},{20,28},{24,16},{28,20},{1,9},{5... | collective-permute-start | bytes 983048 | tf_op jit(solution)/shard_map/ppermute | solution.py:796
  392.8 29.8 %collective-permute-start.41 = (bf16[160,1024]{1,0:T(8,128)(2,1)}, bf16[160,1024]{1,0:T(8,128)(2,1)}, u32[]{:S(2)}, u32[]{:S(2)}) collective-permute-start(bf16[160,1024]{1,0:T(8,128)(2,1)} %get-tuple-element.231), channel_id=1, source_target_pairs={{0,16},{4,20},{8,24},{12,28},{16,0},{20,4},{24,8},{28,12},{1,17},{... | collective-permute-start | bytes 983048 | tf_op jit(solution)/shard_map/ppermute | solution.py:796
  393.9 28.7 %collective-permute-start.42 = (bf16[160,1024]{1,0:T(8,128)(2,1)}, bf16[160,1024]{1,0:T(8,128)(2,1)}, u32[]{:S(2)}, u32[]{:S(2)}) collective-permute-start(bf16[160,1024]{1,0:T(8,128)(2,1)} %get-tuple-element.230), channel_id=1, source_target_pairs={{0,24},{4,28},{8,16},{12,20},{16,8},{20,12},{24,0},{28,4},{1,25},{... | collective-permute-start | bytes 983048 | tf_op jit(solution)/shard_map/ppermute | solution.py:796
  427.6 21.2 %collective-permute-start.46 = (bf16[4,112,1024]{2,1,0:T(8,128)(2,1)}, bf16[4,112,1024]{2,1,0:T(8,128)(2,1)}, u32[]{:S(2)}, u32[]{:S(2)}) collective-permute-start(bf16[4,112,1024]{2,1,0:T(8,128)(2,1)} %fusion.14), channel_id=1, source_target_pairs={{0,4},{4,0},{8,12},{12,8},{16,20},{20,16},{24,28},{28,24},{1,5},{5... | collective-permute-start | bytes 2752520 | tf_op jit(solution)/shard_map/ppermute | solution.py:796
  429.6 20.9 %collective-permute-start.45 = (bf16[4,112,1024]{2,1,0:T(8,128)(2,1)}, bf16[4,112,1024]{2,1,0:T(8,128)(2,1)}, u32[]{:S(2)}, u32[]{:S(2)}) collective-permute-start(bf16[4,112,1024]{2,1,0:T(8,128)(2,1)} %fusion.13), channel_id=1, source_target_pairs={{0,2},{1,3},{2,0},{3,1},{4,6},{5,7},{6,4},{7,5},{8,10},{9,11},{10,... | collective-permute-start | bytes 2752520 | tf_op jit(solution)/shard_map/ppermute | solution.py:796
  452.8 22.5 %collective-permute-start.50 = (bf16[2,256,1024]{2,1,0:T(8,128)(2,1)S(1)}, bf16[2,256,1024]{2,1,0:T(8,128)(2,1)S(1)}, u32[]{:S(2)}, u32[]{:S(2)}) collective-permute-start(bf16[2,256,1024]{2,1,0:T(8,128)(2,1)S(1)} %constant_dynamic-slice_fusion.1), channel_id=1, source_target_pairs={{0,2},{1,3},{2,0},{3,1},{4,6},{5,7},{6,4},{7,5},{8,10},{9,11},{10,... | collective-permute-start | bytes 3145736 | tf_op jit(solution)/shard_map/ppermute | solution.py:796
  (71 other events, 795.4 us)
Sparse Core Ops, SparseCore 0:
  87.2 96.9 all-gather.2
